TPU v7x, 32 devices: a whole 2x2x4 slice. The times are simulated.
32 devices in a mesh: grp: 2 (over y), mesh: 4 (over z), tm: 2 (over x), rep: 2 (over core).
Axes of the slice: x: 2, y: 2, z: 4, core: 2. Of those that a mesh axis runs over, the one named last changes fastest.
Arguments:
- right_side: float32 [4, 128, 64, 128], P(('grp', 'tm'), ('mesh', 'rep')), parts along dimension 0, may hold values from -25 to 25
- kappa_sq: float32 [256, 64], P(('grp', 'mesh', 'rep')), parts along dimension 0, may hold values from 0.25 to 4
- time_coupling: float32 [2], P('grp'), parts along dimension 0, may hold values from 0.15 to 0.45
- near_stiffness: float32 [128, 64, 384], P(('mesh', 'rep')), may hold values from -0.16 to 0.16, as said below
- far_stiffness: float32 [8, 64, 1536], P(('mesh', 'rep')), may hold values from -0.16 to 0.16, as said below
- near_columns: int32 [128, 6], P(('mesh', 'rep')), may hold values from 0 to 15, as said below
- face_blocks: int32 [8, 6, 4], P(('mesh', 'rep')), may hold values from 0 to 15, as said below
- face_counts: int32 [8, 6], P(('mesh', 'rep')), may hold values from 0 to 4, as said below
Outputs:
- solution_field: float32 [4, 128, 64, 128], P(('grp', 'tm'), ('mesh', 'rep')), parts along dimension 0
- residual: float32 [4, 128, 64, 128], P(('grp', 'tm'), ('mesh', 'rep')), parts along dimension 0
There are 2 independent parts, one for each index of `grp`. A program takes and returns all parts, laid end to end along the dimension named above; an argument that names none is the same for every part. Nothing has to cross between parts.
Inputs may be any that keep to these rules, and one draw needn't show every extreme that they name: face_counts[n(p, e), e'] = face_counts[p, e]; every partition sends 4 blocks toward at least one direction. `face_blocks`: the 4 blocks of one partition and direction are distinct. `near_columns`: for j < 3, slot 2j over the block rows of a partition is a permutation of its local blocks and slot 2j + 1 is the inverse permutation. `near_stiffness`: for j < 3, the block in slot 2j + 1 of block row b is the transpose of the block in slot 2j of the block row that slot 2j + 1 of b names. `far_stiffness`: G[n(p, e), e' * 4 + f] is the transpose of G[p, e * 4 + f].
All inputs are finite; a program needn't handle non-finite values.
Results may differ from a plain program's by a relative error of at most 0.00016.
Values sent between devices are 32-bit elements; how exact they have to be, the bound alone decides.
No kernel may reach another device: no remote copies, remote signals or barrier semaphores. Data moves between devices by JAX's collectives and lax.ppermute only.
A program may use at most 64 MiB of HBM per device.

v0:
```python
import jax
import jax.numpy as jnp
from jax import lax
from jax.sharding import PartitionSpec as P

ITERS = 2


def from_behind(block, axis, distance):
    devices = range(lax.axis_size(axis))
    route = [((i - distance) % len(devices), i) for i in devices]
    return lax.ppermute(block, axis, route)


def with_halo(value, sides, width):
    for axis, dim in sides:
        peers, length = (lax.axis_size(axis), value.shape[dim])
        up = [(i, (i + 1) % peers) for i in range(peers - 1)]
        down = [(j, i) for i, j in up]
        last = lax.slice_in_dim(value, length - width, length, axis=dim)
        initial = lax.slice_in_dim(value, 0, width, axis=dim)
        before = lax.ppermute(last, axis, up)
        after = lax.ppermute(initial, axis, down)
        value = jnp.concatenate([before, value, after], axis=dim)
    return value


def spatial(
    vector, kappa_sq, near_stiffness, far_stiffness, near_columns, face_blocks, face_counts
):
    hours_n, blocks_n, node_width, probes = vector.shape
    face_slots = face_blocks.shape[2]
    partitions = lax.axis_size(("mesh", "rep"))
    stride = partitions // 4 + 1
    offsets = (1, -1, 2, -2, stride, -stride)
    slot_blocks = face_blocks[0].reshape(-1)
    active = (jnp.arange(face_slots)[None, :] < face_counts[0][:, None]).astype(jnp.float32)
    outgoing = jnp.take(vector, slot_blocks, axis=1).reshape(
        hours_n, 6, face_slots, node_width, probes
    )
    outgoing = outgoing * active[None, :, :, None, None]
    arrived = []
    for heading in range(6):
        arrived.append(from_behind(outgoing[:, heading ^ 1], ("mesh", "rep"), -offsets[heading]))
    received = jnp.stack(arrived, axis=1).reshape(hours_n, 6 * face_slots, node_width, probes)
    nearby = jnp.take(vector, near_columns.reshape(-1), axis=1).reshape(
        hours_n, blocks_n, -1, probes
    )
    result = (3.0 + kappa_sq)[None, :, :, None] * vector
    result = result + jnp.einsum(
        "nik,hnkp->hnip",
        near_stiffness,
        nearby,
        precision=lax.Precision.HIGHEST,
        preferred_element_type=jnp.float32,
    )
    far_blocks = far_stiffness[0].reshape(node_width, 6 * face_slots, node_width)
    far_terms = jnp.einsum(
        "iqk,hqkp->hqip",
        far_blocks,
        received,
        precision=lax.Precision.HIGHEST,
        preferred_element_type=jnp.float32,
    )
    landing = (slot_blocks[None, :] == jnp.arange(blocks_n)[:, None]).astype(jnp.float32)
    result = result + jnp.einsum(
        "nq,hqip->hnip",
        landing,
        far_terms,
        precision=lax.Precision.HIGHEST,
        preferred_element_type=jnp.float32,
    )
    return result


def operate(
    vector,
    kappa_sq,
    time_coupling,
    near_stiffness,
    far_stiffness,
    near_columns,
    face_blocks,
    face_counts,
):
    product = spatial(
        vector, kappa_sq, near_stiffness, far_stiffness, near_columns, face_blocks, face_counts
    )
    padded = with_halo(product, (("tm", 0),), 1)
    return product - time_coupling[0] * (padded[:-2] + padded[2:])


def two_products(residual, applied):
    return lax.psum(
        (jnp.sum(residual * residual, axis=(0, 1, 2)), jnp.sum(residual * applied, axis=(0, 1, 2))),
        ("mesh", "tm", "rep"),
    )


def shards(
    right_side,
    kappa_sq,
    time_coupling,
    near_stiffness,
    far_stiffness,
    near_columns,
    face_blocks,
    face_counts,
):

    def apply_operator(vector):
        return operate(
            vector,
            kappa_sq,
            time_coupling,
            near_stiffness,
            far_stiffness,
            near_columns,
            face_blocks,
            face_counts,
        )

    solution_field = jnp.zeros_like(right_side)
    residual = right_side
    applied = apply_operator(residual)
    norm_now, product = two_products(residual, applied)
    step_size = norm_now / product
    direction = residual
    applied_dir = applied
    for iteration in range(ITERS):
        solution_field = solution_field + step_size * direction
        residual = residual - step_size * applied_dir
        if iteration + 1 < ITERS:
            applied = apply_operator(residual)
            norm_next, product = two_products(residual, applied)
            beta_ratio = norm_next / norm_now
            step_size = norm_next / (product - beta_ratio * norm_next / step_size)
            direction = residual + beta_ratio * direction
            applied_dir = applied + beta_ratio * applied_dir
            norm_now = norm_next
    return (solution_field, residual)


def solution(mesh):
    placed = (
        P(("grp", "tm"), ("mesh", "rep"), None, None),
        P(("grp", "mesh", "rep"), None),
        P("grp"),
        P(("mesh", "rep"), None, None),
        P(("mesh", "rep"), None, None),
        P(("mesh", "rep"), None),
        P(("mesh", "rep"), None, None),
        P(("mesh", "rep"), None),
    )
    return jax.shard_map(
        shards,
        mesh=mesh,
        in_specs=placed,
        out_specs=(
            P(("grp", "tm"), ("mesh", "rep"), None, None),
            P(("grp", "tm"), ("mesh", "rep"), None, None),
        ),
        check_vma=False,
    )
```

profile of v0, /device:TPU:0, one launch (start us, length us, event | category | flops | bytes accessed | tf_op | source)
XLA Modules:
  0.0 164.5 jit_solution(14381647301428617906)
XLA Ops:
  0.6 0.0 copy-start
  0.6 0.9 copy.19
  1.5 0.1 reshape_squeeze.8
  1.6 0.5 copy-done.8
  2.1 0.7 fusion.15
  2.9 0.8 copy.18
  3.6 0.1 reshape.135
  3.7 0.0 copy-start.4
  3.8 1.7 %gather_fusion.1 = f32[24,64,128]{2,1,0:T(8,128)S(1)} fusion(f32[16,64,128]{2,1,0:T(8,128)} %bitcast.116, s32[1024]{0:T(1024)S(1)} %get-tuple-element.30), kind=kCustom, calls=%fused_computation.1.clone | custom fusion | bytes 1572960 | tf_op jit(solution)/shard_map/jit(_take)/gather | solution.py:38
  5.5 0.0 copy-start.1
  5.5 0.1 bitcast_select_fusion.3
  5.6 0.1 broadcast_multiply_fusion.1
  5.7 0.8 slice_bitcast_fusion.6
  6.5 2.5 %collective-permute-start.5 = (f32[1,4,64,128]{3,2,1,0:T(8,128)S(1)}, f32[1,4,64,128]{3,2,1,0:T(8,128)}, u32[]{:S(2)}, u32[]{:S(2)}) collective-permute-start(f32[1,4,64,128]{3,2,1,0:T(8,128)S(1)} %get-tuple-element.22), channel_id=1, source_target_pairs={{9,0},{12,1},{13,4},{0,5},{1,8},{4,9},{5,12},{8,13},{11,2},{14,3},... | collective-permute-start | bytes 393224 | tf_op jit(solution)/shard_map/ppermute | solution.py:12
  9.0 1.0 collective-permute-start.4
  10.0 2.2 %collective-permute-start.3 = (f32[1,4,64,128]{3,2,1,0:T(8,128)}, f32[1,4,64,128]{3,2,1,0:T(8,128)}, u32[]{:S(2)}, u32[]{:S(2)}) collective-permute-start(f32[1,4,64,128]{3,2,1,0:T(8,128)} %get-tuple-element.24), channel_id=1, source_target_pairs={{12,0},{13,1},{0,4},{1,5},{4,8},{5,9},{8,12},{9,13},{14,2},{15,3},... | collective-permute-start | bytes 393224 | tf_op jit(solution)/shard_map/ppermute | solution.py:12
  12.2 2.0 %collective-permute-start.2 = (f32[1,4,64,128]{3,2,1,0:T(8,128)}, f32[1,4,64,128]{3,2,1,0:T(8,128)}, u32[]{:S(2)}, u32[]{:S(2)}) collective-permute-start(f32[1,4,64,128]{3,2,1,0:T(8,128)} %get-tuple-element.25), channel_id=1, source_target_pairs={{4,0},{5,1},{8,4},{9,5},{12,8},{13,9},{0,12},{1,13},{6,2},{7,3},{1... | collective-permute-start | bytes 393224 | tf_op jit(solution)/shard_map/ppermute | solution.py:12
  14.2 0.7 collective-permute-start
  14.9 0.2 reshape_squeeze.9
  15.1 2.4 %gather_fusion = f32[96,64,128]{2,1,0:T(8,128)} fusion(f32[16,64,128]{2,1,0:T(8,128)S(1)} %bitcast.117, s32[1024]{0:T(1024)S(1)} %get-tuple-element.31), kind=kCustom, calls=%fused_computation.clone | custom fusion | bytes 6291840 | tf_op jit(solution)/shard_map/jit(_take)/gather | solution.py:46
  17.5 2.2 %bitcast_select_fusion.1 = f32[1,96,64,128]{3,2,1,0:T(8,128)S(1)} fusion(f32[96,64,128]{2,1,0:T(8,128)} %gather_fusion, pred[96]{0:T(512)(128)(4,1)S(1)} %compare_and_fusion.1), kind=kLoop, calls=%fused_computation.5 | loop fusion | flops 786432 | bytes 6291552 | tf_op jit(solution)/shard_map/jit(_take)/select_n | solution.py:46
  19.7 3.2 %collective-permute-done = f32[1,4,64,128]{3,2,1,0:T(8,128)} collective-permute-done((f32[1,4,64,128]{3,2,1,0:T(8,128)}, f32[1,4,64,128]{3,2,1,0:T(8,128)}, u32[]{:S(2)}, u32[]{:S(2)}) %collective-permute-start) | collective-permute-done | bytes 131104 | tf_op jit(solution)/shard_map/ppermute | solution.py:12
  22.9 1.4 collective-permute-start.1
  24.3 0.9 bitcast_dynamic-update-slice_fusion.11
  25.2 4.2 %collective-permute-done.1 = f32[1,4,64,128]{3,2,1,0:T(8,128)S(1)} collective-permute-done((f32[1,4,64,128]{3,2,1,0:T(8,128)S(1)}, f32[1,4,64,128]{3,2,1,0:T(8,128)S(1)}, u32[]{:S(2)}, u32[]{:S(2)}) %collective-permute-start.1) | collective-permute-done | bytes 131104 | tf_op jit(solution)/shard_map/ppermute | solution.py:12
  29.4 0.0 collective-permute-done.2
  29.4 0.9 bitcast_dynamic-update-slice_fusion.9
  30.3 0.0 collective-permute-done.3
  30.3 0.9 bitcast_dynamic-update-slice_fusion.8
  31.3 0.9 bitcast_dynamic-update-slice_fusion.7
  32.2 0.9 bitcast_dynamic-update-slice_fusion.6
  33.1 0.9 convolution_bitcast_fusion.1
  34.1 0.9 fusion.6
  34.9 2.6 %fusion.1 = f32[1,16,64,128]{3,2,1,0:T(8,128)S(1)} fusion(f32[16,384,128]{2,1,0:T(8,128)S(1)} %bitcast.121, f32[16,64,384]{2,1,0:T(8,128)S(1)} %copy-done, f32[64,128,16]{1,2,0:T(8,128)S(1)} %fusion.6, f32[1,16,64,128]{3,2,1,0:T(8,128)S(1)} %copy-done.1, f32[16,64]{1,0:T(8,128)S(1)} %broadcast_add_fusion), kind=kOutput, calls=%fused_computation.11 | convolution fusion | flops 604372992 | bytes 6295552 | tf_op jit(solution)/shard_map/nik,hnkp->hnip/dot_general | solution.py:50
  37.5 1.3 collective-permute-start.7
  38.8 4.6 %collective-permute-start.6 = (f32[1,16,64,128]{3,2,1,0:T(8,128)S(1)}, f32[1,16,64,128]{3,2,1,0:T(8,128)S(1)}, u32[]{:S(2)}, u32[]{:S(2)}) collective-permute-start(f32[1,16,64,128]{3,2,1,0:T(8,128)S(1)} %fusion.1), channel_id=1, source_target_pairs={{0,2},{1,3},{4,6},{5,7},{8,10},{9,11},{12,14},{13,15},{16,18},{17,... | collective-permute-start | bytes 1572872 | tf_op jit(solution)/shard_map/ppermute | solution.py:22
  44.1 6.0 %collective-permute-done.7 = f32[1,16,64,128]{3,2,1,0:T(8,128)S(1)} collective-permute-done((f32[1,16,64,128]{3,2,1,0:T(8,128)S(1)}, f32[1,16,64,128]{3,2,1,0:T(8,128)S(1)}, u32[]{:S(2)}, u32[]{:S(2)}) %collective-permute-start.7) | collective-permute-done | bytes 524320 | tf_op jit(solution)/shard_map/ppermute | solution.py:23
  50.1 1.2 collective-permute-done.6
  51.3 1.0 multiply_reduce_fusion.2
  52.3 32.0 %all-reduce.1 = (f32[128]{0:T(128)S(1)}, f32[128]{0:T(128)S(1)}) all-reduce(f32[128]{0:T(128)S(1)} %get-tuple-element.7, f32[128]{0:T(128)S(1)} %get-tuple-element.6), channel_id=1, replica_groups=mesh['grp'=2,'mesh'=4,'tm'=2,'rep'=2] {'mesh','tm','rep'}, use_global_device_ids=true, to_apply=%region_1.2 | all-reduce | flops 256 | bytes 2048 | tf_op jit(solution)/shard_map/psum | solution.py:94
  84.2 1.1 multiply_subtract_fusion.2
  85.3 1.6 gather_fusion.3
  87.0 2.4 %gather_fusion.2 = f32[96,64,128]{2,1,0:T(8,128)} fusion(f32[16,64,128]{2,1,0:T(8,128)S(1)} %bitcast.119, s32[1024]{0:T(1024)S(1)} %get-tuple-element.31), kind=kCustom, calls=%fused_computation.2.clone | custom fusion | bytes 6291840 | tf_op jit(solution)/shard_map/jit(_take)/gather | solution.py:46
  89.4 1.4 bitcast_select_fusion.2
  90.8 0.1 broadcast_multiply_fusion
  90.9 0.1 slice_bitcast_fusion
  91.0 0.1 collective-permute-start.13
  91.0 2.6 %collective-permute-start.12 = (f32[1,4,64,128]{3,2,1,0:T(8,128)S(1)}, f32[1,4,64,128]{3,2,1,0:T(8,128)S(1)}, u32[]{:S(2)}, u32[]{:S(2)}) collective-permute-start(f32[1,4,64,128]{3,2,1,0:T(8,128)S(1)} %get-tuple-element.17), channel_id=1, source_target_pairs={{5,0},{8,1},{9,4},{12,5},{13,8},{0,9},{1,12},{4,13},{7,2},{10,3},{... | collective-permute-start | bytes 393224 | tf_op jit(solution)/shard_map/ppermute | solution.py:12
  93.7 3.8 %collective-permute-start.10 = (f32[1,4,64,128]{3,2,1,0:T(8,128)S(1)}, f32[1,4,64,128]{3,2,1,0:T(8,128)S(1)}, u32[]{:S(2)}, u32[]{:S(2)}) collective-permute-start(f32[1,4,64,128]{3,2,1,0:T(8,128)S(1)} %get-tuple-element.19), channel_id=1, source_target_pairs={{4,0},{5,1},{8,4},{9,5},{12,8},{13,9},{0,12},{1,13},{6,2},{7,3},{1... | collective-permute-start | bytes 393224 | tf_op jit(solution)/shard_map/ppermute | solution.py:12
  97.5 0.3 bitcast_select_fusion
  97.8 5.5 %collective-permute-done.8 = f32[1,4,64,128]{3,2,1,0:T(8,128)S(1)} collective-permute-done((f32[1,4,64,128]{3,2,1,0:T(8,128)S(1)}, f32[1,4,64,128]{3,2,1,0:T(8,128)S(1)}, u32[]{:S(2)}, u32[]{:S(2)}) %collective-permute-start.8) | collective-permute-done | bytes 131104 | tf_op jit(solution)/shard_map/ppermute | solution.py:12
  103.3 2.1 %collective-permute-start.9 = (f32[1,4,64,128]{3,2,1,0:T(8,128)S(1)}, f32[1,4,64,128]{3,2,1,0:T(8,128)S(1)}, u32[]{:S(2)}, u32[]{:S(2)}) collective-permute-start(f32[1,4,64,128]{3,2,1,0:T(8,128)S(1)} %get-tuple-element.20), channel_id=1, source_target_pairs={{13,0},{0,1},{1,4},{4,5},{5,8},{8,9},{9,12},{12,13},{15,2},{2,3},{... | collective-permute-start | bytes 393224 | tf_op jit(solution)/shard_map/ppermute | solution.py:12
  105.5 4.3 %collective-permute-done.9 = f32[1,4,64,128]{3,2,1,0:T(8,128)S(1)} collective-permute-done((f32[1,4,64,128]{3,2,1,0:T(8,128)S(1)}, f32[1,4,64,128]{3,2,1,0:T(8,128)S(1)}, u32[]{:S(2)}, u32[]{:S(2)}) %collective-permute-start.9) | collective-permute-done | bytes 131104 | tf_op jit(solution)/shard_map/ppermute | solution.py:12
  109.9 0.9 convolution_bitcast_fusion
  110.9 0.9 fusion.4
  111.7 0.0 copy-start.3
  111.8 2.6 %fusion.3 = f32[1,16,64,128]{3,2,1,0:T(8,128)S(1)} fusion(f32[16,384,128]{2,1,0:T(8,128)S(1)} %bitcast.120, f32[16,64,384]{2,1,0:T(8,128)S(1)} %copy-done, f32[64,128,16]{1,2,0:T(8,128)S(1)} %fusion.4, f32[1,16,64,128]{3,2,1,0:T(8,128)S(1)} %multiply_subtract_fusion.2, f32[16,64]{1,0:T(8,128)S(1)} %broadcast_add_fusion), kind=kOutput, calls=%fused_computation.13 | convolution fusion | flops 604372992 | bytes 6295552 | tf_op jit(solution)/shard_map/nik,hnkp->hnip/dot_general | solution.py:50
  114.4 1.3 collective-permute-start.15
  115.7 4.6 %collective-permute-start.14 = (f32[1,16,64,128]{3,2,1,0:T(8,128)S(1)}, f32[1,16,64,128]{3,2,1,0:T(8,128)S(1)}, u32[]{:S(2)}, u32[]{:S(2)}) collective-permute-start(f32[1,16,64,128]{3,2,1,0:T(8,128)S(1)} %fusion.3), channel_id=1, source_target_pairs={{0,2},{1,3},{4,6},{5,7},{8,10},{9,11},{12,14},{13,15},{16,18},{17,... | collective-permute-start | bytes 1572872 | tf_op jit(solution)/shard_map/ppermute | solution.py:22
  120.3 7.4 %collective-permute-done.15 = f32[1,16,64,128]{3,2,1,0:T(8,128)S(1)} collective-permute-done((f32[1,16,64,128]{3,2,1,0:T(8,128)S(1)}, f32[1,16,64,128]{3,2,1,0:T(8,128)S(1)}, u32[]{:S(2)}, u32[]{:S(2)}) %collective-permute-start.15) | collective-permute-done | bytes 524320 | tf_op jit(solution)/shard_map/ppermute | solution.py:23
  127.7 1.2 collective-permute-done.14
  128.9 1.0 multiply_reduce_fusion
  129.9 32.4 %all-reduce = (f32[128]{0:T(128)S(1)}, f32[128]{0:T(128)S(1)}) all-reduce(f32[128]{0:T(128)S(1)} %get-tuple-element.5, f32[128]{0:T(128)S(1)} %get-tuple-element.4), channel_id=1, replica_groups=mesh['grp'=2,'mesh'=4,'tm'=2,'rep'=2] {'mesh','tm','rep'}, use_global_device_ids=true, to_apply=%region_5.8 | all-reduce | flops 256 | bytes 2048 | tf_op jit(solution)/shard_map/psum | solution.py:94
  162.3 2.2 %multiply_subtract_fusion = (f32[1,16,64,128]{3,2,1,0:T(8,128)}, f32[1,16,64,128]{3,2,1,0:T(8,128)}) fusion(f32[1,16,64,128]{3,2,1,0:T(8,128)S(1)} %multiply_subtract_fusion.2, f32[1,16,64,128]{3,2,1,0:T(8,128)} %get-tuple-element.14, f32[1,16,64,128]{3,2,1,0:T(8,128)S(1)} %copy-done.3, f32[128]{0:T(128)S(1)} %get-tuple-element.13, ...), kind=kLoop, calls=%fused_computation.22 | loop fusion | flops 1179648 | bytes 3147264 | tf_op jit(solution)/shard_map/sub | solution.py:132
  (48 shorter events, 0.2 us)
Async XLA Ops:
  0.6 34.3 %copy-start = (f32[16,64,384]{2,1,0:T(8,128)S(1)}, f32[16,64,384]{2,1,0:T(8,128)}, u32[]{:S(2)}) copy-start(f32[16,64,384]{2,1,0:T(8,128)} %param.15) | copy-start | bytes 4718596
  1.6 0.5 copy-start.8
  1.6 4.0 %copy-start.11 = (pred[24]{0:T(512)(128)(4,1)}, pred[24]{0:T(512)(128)(4,1)S(1)}, u32[]{:S(2)}) copy-start(pred[24]{0:T(512)(128)(4,1)S(1)} %compare_and_fusion) | copy-start | bytes 76
  3.7 1.9 %copy-start.7 = (s32[1024]{0:T(1024)}, s32[1024]{0:T(1024)S(1)}, u32[]{:S(2)}) copy-start(s32[1024]{0:T(1024)S(1)} %get-tuple-element.30) | copy-start | bytes 12292
  3.7 11.2 %copy-start.4 = (f32[1,64,1536]{2,1,0:T(8,128)S(1)}, f32[1,64,1536]{2,1,0:T(8,128)}, u32[]{:S(2)}) copy-start(f32[1,64,1536]{2,1,0:T(8,128)} %param.16) | copy-start | bytes 1179652
  5.5 9.6 %copy-start.1 = (f32[1,16,64,128]{3,2,1,0:T(8,128)S(1)}, f32[1,16,64,128]{3,2,1,0:T(8,128)}, u32[]{:S(2)}) copy-start(f32[1,16,64,128]{3,2,1,0:T(8,128)} %param.12) | copy-start | bytes 1572868
  6.5 25.7 %collective-permute-start.5 = (f32[1,4,64,128]{3,2,1,0:T(8,128)S(1)}, f32[1,4,64,128]{3,2,1,0:T(8,128)}, u32[]{:S(2)}, u32[]{:S(2)}) collective-permute-start(f32[1,4,64,128]{3,2,1,0:T(8,128)S(1)} %get-tuple-element.22), channel_id=1, source_target_pairs={{9,0},{12,1},{13,4},{0,5},{1,8},{4,9},{5,12},{8,13},{11,2},{14,3},... | collective-permute-start | bytes 393224 | tf_op jit(solution)/shard_map/ppermute | solution.py:12
  9.0 22.3 %collective-permute-start.4 = (f32[1,4,64,128]{3,2,1,0:T(8,128)S(1)}, f32[1,4,64,128]{3,2,1,0:T(8,128)}, u32[]{:S(2)}, u32[]{:S(2)}) collective-permute-start(f32[1,4,64,128]{3,2,1,0:T(8,128)S(1)} %get-tuple-element.23), channel_id=1, source_target_pairs={{5,0},{8,1},{9,4},{12,5},{13,8},{0,9},{1,12},{4,13},{7,2},{10,3},{... | collective-permute-start | bytes 393224 | tf_op jit(solution)/shard_map/ppermute | solution.py:12
  10.0 20.3 %collective-permute-start.3 = (f32[1,4,64,128]{3,2,1,0:T(8,128)}, f32[1,4,64,128]{3,2,1,0:T(8,128)}, u32[]{:S(2)}, u32[]{:S(2)}) collective-permute-start(f32[1,4,64,128]{3,2,1,0:T(8,128)} %get-tuple-element.24), channel_id=1, source_target_pairs={{12,0},{13,1},{0,4},{1,5},{4,8},{5,9},{8,12},{9,13},{14,2},{15,3},... | collective-permute-start | bytes 393224 | tf_op jit(solution)/shard_map/ppermute | solution.py:12
  12.2 17.2 %collective-permute-start.2 = (f32[1,4,64,128]{3,2,1,0:T(8,128)}, f32[1,4,64,128]{3,2,1,0:T(8,128)}, u32[]{:S(2)}, u32[]{:S(2)}) collective-permute-start(f32[1,4,64,128]{3,2,1,0:T(8,128)} %get-tuple-element.25), channel_id=1, source_target_pairs={{4,0},{5,1},{8,4},{9,5},{12,8},{13,9},{0,12},{1,13},{6,2},{7,3},{1... | collective-permute-start | bytes 393224 | tf_op jit(solution)/shard_map/ppermute | solution.py:12
  14.2 8.7 %collective-permute-start = (f32[1,4,64,128]{3,2,1,0:T(8,128)}, f32[1,4,64,128]{3,2,1,0:T(8,128)}, u32[]{:S(2)}, u32[]{:S(2)}) collective-permute-start(f32[1,4,64,128]{3,2,1,0:T(8,128)} %get-tuple-element.27), channel_id=1, source_target_pairs={{1,0},{4,1},{5,4},{8,5},{9,8},{12,9},{13,12},{0,13},{3,2},{6,3},{7... | collective-permute-start | bytes 393224 | tf_op jit(solution)/shard_map/ppermute | solution.py:12
  14.9 2.6 %copy-start.13 = (pred[96]{0:T(512)(128)(4,1)}, pred[96]{0:T(512)(128)(4,1)S(1)}, u32[]{:S(2)}) copy-start(pred[96]{0:T(512)(128)(4,1)S(1)} %compare_and_fusion.1) | copy-start | bytes 292
  17.5 2.2 %copy-start.6 = (f32[16,64]{1,0:T(8,128)S(1)}, f32[16,64]{1,0:T(8,128)}, u32[]{:S(2)}) copy-start(f32[16,64]{1,0:T(8,128)} %param.13) | copy-start | bytes 12292
  17.5 5.4 %copy-start.5 = (f32[1,4,64,128]{3,2,1,0:T(8,128)S(1)}, f32[1,4,64,128]{3,2,1,0:T(8,128)}, u32[]{:S(2)}) copy-start(f32[1,4,64,128]{3,2,1,0:T(8,128)} %get-tuple-element.26) | copy-start | bytes 393220
  19.7 14.3 %copy-start.9 = (s32[24]{0:T(128)S(1)}, s32[24]{0:T(128)}, u32[]{:S(2)}) copy-start(s32[24]{0:T(128)} %copy-done.8) | copy-start | bytes 292
  22.9 6.5 %collective-permute-start.1 = (f32[1,4,64,128]{3,2,1,0:T(8,128)S(1)}, f32[1,4,64,128]{3,2,1,0:T(8,128)S(1)}, u32[]{:S(2)}, u32[]{:S(2)}) collective-permute-start(f32[1,4,64,128]{3,2,1,0:T(8,128)S(1)} %copy-done.5), channel_id=1, source_target_pairs={{13,0},{0,1},{1,4},{4,5},{5,8},{8,9},{9,12},{12,13},{15,2},{2,3},{... | collective-permute-start | bytes 393224 | tf_op jit(solution)/shard_map/ppermute | solution.py:12
  37.5 12.6 %collective-permute-start.7 = (f32[1,16,64,128]{3,2,1,0:T(8,128)S(1)}, f32[1,16,64,128]{3,2,1,0:T(8,128)S(1)}, u32[]{:S(2)}, u32[]{:S(2)}) collective-permute-start(f32[1,16,64,128]{3,2,1,0:T(8,128)S(1)} %fusion.1), channel_id=1, source_target_pairs={{2,0},{3,1},{6,4},{7,5},{10,8},{11,9},{14,12},{15,13},{18,16},{19,... | collective-permute-start | bytes 1572872 | tf_op jit(solution)/shard_map/ppermute | solution.py:23
  38.8 12.5 %collective-permute-start.6 = (f32[1,16,64,128]{3,2,1,0:T(8,128)S(1)}, f32[1,16,64,128]{3,2,1,0:T(8,128)S(1)}, u32[]{:S(2)}, u32[]{:S(2)}) collective-permute-start(f32[1,16,64,128]{3,2,1,0:T(8,128)S(1)} %fusion.1), channel_id=1, source_target_pairs={{0,2},{1,3},{4,6},{5,7},{8,10},{9,11},{12,14},{13,15},{16,18},{17,... | collective-permute-start | bytes 1572872 | tf_op jit(solution)/shard_map/ppermute | solution.py:22
  87.0 2.4 %copy-start.12 = (pred[24]{0:T(512)(128)(4,1)S(1)}, pred[24]{0:T(512)(128)(4,1)}, u32[]{:S(2)}) copy-start(pred[24]{0:T(512)(128)(4,1)} %copy-done.11) | copy-start | bytes 76
  89.4 8.1 %copy-start.2 = (f32[96,64,128]{2,1,0:T(8,128)S(1)}, f32[96,64,128]{2,1,0:T(8,128)}, u32[]{:S(2)}) copy-start(f32[96,64,128]{2,1,0:T(8,128)} %gather_fusion.2) | copy-start | bytes 9437188
  89.4 8.1 %copy-start.14 = (pred[96]{0:T(512)(128)(4,1)S(1)}, pred[96]{0:T(512)(128)(4,1)}, u32[]{:S(2)}) copy-start(pred[96]{0:T(512)(128)(4,1)} %copy-done.13) | copy-start | bytes 292
  91.0 18.9 %collective-permute-start.13 = (f32[1,4,64,128]{3,2,1,0:T(8,128)S(1)}, f32[1,4,64,128]{3,2,1,0:T(8,128)S(1)}, u32[]{:S(2)}, u32[]{:S(2)}) collective-permute-start(f32[1,4,64,128]{3,2,1,0:T(8,128)S(1)} %get-tuple-element.16), channel_id=1, source_target_pairs={{9,0},{12,1},{13,4},{0,5},{1,8},{4,9},{5,12},{8,13},{11,2},{14,3},... | collective-permute-start | bytes 393224 | tf_op jit(solution)/shard_map/ppermute | solution.py:12
  91.0 18.8 %collective-permute-start.12 = (f32[1,4,64,128]{3,2,1,0:T(8,128)S(1)}, f32[1,4,64,128]{3,2,1,0:T(8,128)S(1)}, u32[]{:S(2)}, u32[]{:S(2)}) collective-permute-start(f32[1,4,64,128]{3,2,1,0:T(8,128)S(1)} %get-tuple-element.17), channel_id=1, source_target_pairs={{5,0},{8,1},{9,4},{12,5},{13,8},{0,9},{1,12},{4,13},{7,2},{10,3},{... | collective-permute-start | bytes 393224 | tf_op jit(solution)/shard_map/ppermute | solution.py:12
  93.7 16.2 %collective-permute-start.11 = (f32[1,4,64,128]{3,2,1,0:T(8,128)S(1)}, f32[1,4,64,128]{3,2,1,0:T(8,128)S(1)}, u32[]{:S(2)}, u32[]{:S(2)}) collective-permute-start(f32[1,4,64,128]{3,2,1,0:T(8,128)S(1)} %get-tuple-element.18), channel_id=1, source_target_pairs={{12,0},{13,1},{0,4},{1,5},{4,8},{5,9},{8,12},{9,13},{14,2},{15,3},... | collective-permute-start | bytes 393224 | tf_op jit(solution)/shard_map/ppermute | solution.py:12
  93.7 16.2 %collective-permute-start.10 = (f32[1,4,64,128]{3,2,1,0:T(8,128)S(1)}, f32[1,4,64,128]{3,2,1,0:T(8,128)S(1)}, u32[]{:S(2)}, u32[]{:S(2)}) collective-permute-start(f32[1,4,64,128]{3,2,1,0:T(8,128)S(1)} %get-tuple-element.19), channel_id=1, source_target_pairs={{4,0},{5,1},{8,4},{9,5},{12,8},{13,9},{0,12},{1,13},{6,2},{7,3},{1... | collective-permute-start | bytes 393224 | tf_op jit(solution)/shard_map/ppermute | solution.py:12
  97.5 5.9 %collective-permute-start.8 = (f32[1,4,64,128]{3,2,1,0:T(8,128)S(1)}, f32[1,4,64,128]{3,2,1,0:T(8,128)S(1)}, u32[]{:S(2)}, u32[]{:S(2)}) collective-permute-start(f32[1,4,64,128]{3,2,1,0:T(8,128)S(1)} %get-tuple-element.21), channel_id=1, source_target_pairs={{1,0},{4,1},{5,4},{8,5},{9,8},{12,9},{13,12},{0,13},{3,2},{6,3},{7... | collective-permute-start | bytes 393224 | tf_op jit(solution)/shard_map/ppermute | solution.py:12
  97.8 13.1 %copy-start.10 = (s32[24]{0:T(128)S(1)}, s32[24]{0:T(128)}, u32[]{:S(2)}) copy-start(s32[24]{0:T(128)} %copy-done.8) | copy-start | bytes 292
  103.3 6.5 %collective-permute-start.9 = (f32[1,4,64,128]{3,2,1,0:T(8,128)S(1)}, f32[1,4,64,128]{3,2,1,0:T(8,128)S(1)}, u32[]{:S(2)}, u32[]{:S(2)}) collective-permute-start(f32[1,4,64,128]{3,2,1,0:T(8,128)S(1)} %get-tuple-element.20), channel_id=1, source_target_pairs={{13,0},{0,1},{1,4},{4,5},{5,8},{8,9},{9,12},{12,13},{15,2},{2,3},{... | collective-permute-start | bytes 393224 | tf_op jit(solution)/shard_map/ppermute | solution.py:12
  111.7 50.6 %copy-start.3 = (f32[1,16,64,128]{3,2,1,0:T(8,128)S(1)}, f32[1,16,64,128]{3,2,1,0:T(8,128)}, u32[]{:S(2)}) copy-start(f32[1,16,64,128]{3,2,1,0:T(8,128)} %get-tuple-element.15) | copy-start | bytes 1572868
  114.4 13.3 %collective-permute-start.15 = (f32[1,16,64,128]{3,2,1,0:T(8,128)S(1)}, f32[1,16,64,128]{3,2,1,0:T(8,128)S(1)}, u32[]{:S(2)}, u32[]{:S(2)}) collective-permute-start(f32[1,16,64,128]{3,2,1,0:T(8,128)S(1)} %fusion.3), channel_id=1, source_target_pairs={{2,0},{3,1},{6,4},{7,5},{10,8},{11,9},{14,12},{15,13},{18,16},{19,... | collective-permute-start | bytes 1572872 | tf_op jit(solution)/shard_map/ppermute | solution.py:23
  115.7 13.2 %collective-permute-start.14 = (f32[1,16,64,128]{3,2,1,0:T(8,128)S(1)}, f32[1,16,64,128]{3,2,1,0:T(8,128)S(1)}, u32[]{:S(2)}, u32[]{:S(2)}) collective-permute-start(f32[1,16,64,128]{3,2,1,0:T(8,128)S(1)} %fusion.3), channel_id=1, source_target_pairs={{0,2},{1,3},{4,6},{5,7},{8,10},{9,11},{12,14},{13,15},{16,18},{17,... | collective-permute-start | bytes 1572872 | tf_op jit(solution)/shard_map/ppermute | solution.py:22
where the time goes:
time: 165 us
  blocking collectives  64.4 us (39%)
  waiting for transfers between devices  33.1 us (20%)
  starting transfers between devices  30.1 us (18%)
  local copies, waits for them, and re-layouts  16.1 us (10%)
  other arithmetic  10.3 us (6%)
  matrix products  8.76 us (5%)
  between operations  1.73 us (1%)
    psum x2, blocking collectives, two_products(): lax.psum((jnp.sum(residual * residual, axis=(0, 1, 2)), jnp.sum(residual...  64.4 us
    ppermute x12, starting transfers between devices, from_behind(): return lax.ppermute(block, axis, route)  18.3 us
    ppermute x12, waiting for transfers between devices, from_behind(): return lax.ppermute(block, axis, route)  17.3 us
    ppermute x2, waiting for transfers between devices, with_halo(): after = lax.ppermute(initial, axis, down)  13.4 us
    ppermute x2, starting transfers between devices, with_halo(): before = lax.ppermute(last, axis, up)  9.21 us
    unnamed x42, local copies, waits for them, and re-layouts  5.93 us
    dot_general x2, matrix products, spatial(): jnp.einsum('nik,hnkp->hnip', near_stiffness, nearby, precision=lax.Precis...  5.2 us
    gather x2, local copies, waits for them, and re-layouts, spatial(): jnp.take(vector, near_columns.reshape(-1), axis=1)  4.79 us
  transfers between devices with their start and end apart: 16, of which 8 were waited for; matrix products, arithmetic and copies ran while one was open for 5% of the time, Pallas kernels for 0%

commit v1 on v0

v1 whole, which is shorter than its diff:
```python
import functools

import jax
import jax.numpy as jnp
from jax import lax
from jax.experimental import pallas as pl
from jax.experimental.pallas import tpu as pltpu
from jax.sharding import PartitionSpec as P

SPACE = ("mesh", "rep")
F32 = jnp.float32
BF16 = jnp.bfloat16


def vmem():
    return pl.BlockSpec(memory_space=pltpu.VMEM)


def smem():
    return pl.BlockSpec(memory_space=pltpu.SMEM)


def struct(*shape, dtype=F32):
    return jax.ShapeDtypeStruct(shape, dtype)


def call(body, outs, ins, *args):
    return pl.pallas_call(
        body,
        out_shape=outs,
        in_specs=ins,
        out_specs=jax.tree.map(lambda _: vmem(), outs),
        compiler_params=pltpu.CompilerParams(vmem_limit_bytes=48 << 20),
    )(*args)


def halves(value):
    high = value.astype(BF16)
    return high, (value - high.astype(F32)).astype(BF16)


def triple_left(value):
    high, low = halves(value)
    return jnp.concatenate([high, low, high], axis=1)


def triple_right(value):
    high, low = halves(value)
    return jnp.concatenate([high, high, low], axis=0)


def product(left, right):
    return jnp.dot(triple_left(left), triple_right(right), preferred_element_type=F32)


def pack_body(faces, field, *outs):
    for e, out in enumerate(outs):
        for f in range(out.shape[0]):
            out[f] = field[faces[0, f, e]]


def near_body(columns, kappa, stiffness, field, out, high, low, diagonal):
    blocks, width, _ = field.shape
    slots = columns.shape[0]
    diagonal[...] = jnp.transpose(kappa[...])
    for b in range(blocks):
        high[b], low[b] = halves(field[b])
    for b in range(blocks):
        total = (3.0 + diagonal[:, b : b + 1]) * field[b]
        index = [columns[k, b] for k in range(slots)]
        highs = jnp.concatenate([high[i] for i in index], axis=0)
        lows = jnp.concatenate([low[i] for i in index], axis=0)
        left_high, left_low = halves(stiffness[b])
        total += jnp.dot(left_high, highs, preferred_element_type=F32)
        total += jnp.dot(left_low, highs, preferred_element_type=F32)
        total += jnp.dot(left_high, lows, preferred_element_type=F32)
        out[b] = total


def near(columns, kappa, stiffness, field):
    return pl.pallas_call(
        near_body,
        out_shape=struct(*field.shape),
        in_specs=[smem(), vmem(), vmem(), vmem()],
        out_specs=vmem(),
        scratch_shapes=[
            pltpu.VMEM(field.shape, BF16),
            pltpu.VMEM(field.shape, BF16),
            pltpu.VMEM((kappa.shape[1], kappa.shape[0]), F32),
        ],
        compiler_params=pltpu.CompilerParams(vmem_limit_bytes=48 << 20),
    )(columns, kappa, stiffness, field)


def far_body(headings, slots, pack, faces, counts, stiffness, start, *refs):
    arrived, (out, *packed) = refs[:headings], refs[headings:]
    width = start.shape[1]
    out[...] = start[...]
    for e in range(headings):
        for f in range(slots):

            @pl.when(f < counts[0, e])
            def _(e=e, f=f):
                q = e * slots + f
                block = faces[0, f, e]
                left = stiffness[0, :, q * width : (q + 1) * width]
                out[block] += product(left, arrived[e][f])

    if pack:
        pack_body(faces, out, *packed)


def exchange(outgoing, offsets):
    count = lax.axis_size(SPACE)
    arrived = [None] * len(offsets)
    for e in sorted(range(len(offsets)), key=lambda e: -abs(offsets[e])):
        route = [(i, (i + offsets[e]) % count) for i in range(count)]
        arrived[e ^ 1] = lax.ppermute(outgoing[e], SPACE, route)
    return arrived


def rotations(value, axes):
    count = lax.axis_size(axes)
    return [
        lax.ppermute(value, axes, [(i, (i + d) % count) for i in range(count)])
        for d in range(1, count)
    ]


def total_over(value, axes):
    if lax.axis_size(axes) > 4:
        return lax.psum(value, axes)
    return functools.reduce(jnp.add, [value, *rotations(value, axes)])


def hour_rows(coupling, hour, hours, power):
    row = [jnp.where(hour == s, 1.0, 0.0) for s in range(hours)]
    for _ in range(power):
        edge = [0.0, *row, 0.0]
        row = [edge[s + 1] - coupling * (edge[s] + edge[s + 2]) for s in range(hours)]
    return [
        functools.reduce(
            jnp.add,
            [
                jnp.where(lax.rem(hour + hours - d, hours) == s, row[s], 0.0)
                for s in range(hours)
            ],
        )
        for d in range(hours)
    ]


def mix(weights, fields, b):
    return functools.reduce(jnp.add, [w * field[b] for w, field in zip(weights, fields)])


def moments_body(hours, coupling, hour, right, second, *refs):
    first, out = refs[:hours], refs[hours]
    once = hour_rows(coupling[0], hour[0], hours, 1)
    thrice = hour_rows(coupling[0], hour[0], hours, 3)
    sums = [jnp.zeros(right.shape[1:], F32) for _ in range(4)]
    for b in range(right.shape[0]):
        start = right[b]
        image = mix(once, first, b)
        sums[0] += start * start
        sums[1] += start * image
        sums[2] += image * image
        sums[3] += mix(thrice, first, b) * second[b]
    rows = [jnp.sum(s, axis=0, keepdims=True) for s in sums]
    out[...] = jnp.concatenate(rows + rows, axis=0)


def finish_body(hours, parts, coupling, hour, right, *refs):
    sums, refs = refs[:parts], refs[parts:]
    first, second, (solution, residual) = refs[:hours], refs[hours:-2], refs[-2:]
    once = hour_rows(coupling[0], hour[0], hours, 1)
    twice = hour_rows(coupling[0], hour[0], hours, 2)
    moment = functools.reduce(jnp.add, [s[...] for s in sums])
    m0, m1, m2, m3 = (moment[k : k + 1] for k in range(4))
    alpha = m0 / m1
    norm = alpha * alpha * m2 - m0
    lift = 1.0 + norm / m0
    step = norm / (lift * lift * m1 - 2.0 * lift * alpha * m2 + alpha * alpha * m3)
    on_right = alpha + step * lift
    on_first = step * alpha
    for b in range(right.shape[0]):
        start = right[b]
        image = mix(once, first, b)
        solution[b] = on_right * start - on_first * image
        residual[b] = start - on_right * image + on_first * mix(twice, second, b)


def shards(
    right_side,
    kappa_sq,
    time_coupling,
    near_stiffness,
    far_stiffness,
    near_columns,
    face_blocks,
    face_counts,
):
    right = right_side.reshape(right_side.shape[1:])
    hours = lax.axis_size("tm")
    hour = lax.axis_index("tm").reshape(1)
    headings, slots = face_blocks.shape[1:]
    stride = lax.axis_size(SPACE) // 4 + 1
    offsets = (1, -1, 2, -2, stride, -stride)
    faces = jnp.swapaxes(face_blocks, 1, 2)
    columns = jnp.swapaxes(near_columns, 0, 1)
    face = struct(slots, *right.shape[1:])
    outgoing = call(pack_body, [face] * headings, [smem(), vmem()], faces, right)

    def far(start, arrived, pack):
        body = functools.partial(far_body, headings, slots, pack)
        outs = [struct(*right.shape)] + [face] * (headings if pack else 0)
        ins = [smem(), smem()] + [vmem()] * (2 + headings)
        return call(body, outs, ins, faces, face_counts, far_stiffness, start, *arrived)

    arrived = exchange(outgoing, offsets)
    start = near(columns, kappa_sq, near_stiffness, right)
    first, *outgoing = far(start, arrived, True)
    arrived = exchange(outgoing, offsets)
    first_hours = [first, *rotations(first, "tm")]
    start = near(columns, kappa_sq, near_stiffness, first)
    (second,) = far(start, arrived, False)
    second_hours = [second, *rotations(second, "tm")]

    moments = call(
        functools.partial(moments_body, hours),
        struct(8, right.shape[2]),
        [smem(), smem()] + [vmem()] * (2 + hours),
        time_coupling,
        hour,
        right,
        second,
        *first_hours,
    )
    moments = total_over(moments, ("tm", "rep"))
    if lax.axis_size("mesh") > 4:
        sums = [lax.psum(moments, "mesh")]
    else:
        sums = [moments, *rotations(moments, "mesh")]
    solution_field, residual = call(
        functools.partial(finish_body, hours, len(sums)),
        [struct(*right.shape)] * 2,
        [smem(), smem()] + [vmem()] * (1 + len(sums) + 2 * hours),
        time_coupling,
        hour,
        right,
        *sums,
        *first_hours,
        *second_hours,
    )
    return (solution_field[None], residual[None])


def solution(mesh):
    placed = (
        P(("grp", "tm"), SPACE, None, None),
        P(("grp", "mesh", "rep"), None),
        P("grp"),
        P(SPACE, None, None),
        P(SPACE, None, None),
        P(SPACE, None),
        P(SPACE, None, None),
        P(SPACE, None),
    )
    return jax.shard_map(
        shards,
        mesh=mesh,
        in_specs=placed,
        out_specs=(
            P(("grp", "tm"), SPACE, None, None),
            P(("grp", "tm"), SPACE, None, None),
        ),
        check_vma=False,
    )
```

time: 165 us -> 75.3 us (0.46)
  blocking collectives: 64.4 us -> 0 us
  Pallas kernels: 0 us -> 12.6 us
  local copies, waits for them, and re-layouts: 16.1 us -> 5.57 us
  other arithmetic: 10.3 us -> 0.01 us
  starting transfers between devices: 30.1 us -> 20.4 us
  matrix products: 8.76 us -> 0 us
    psum x2 -> x0, blocking collectives: 64.4 us -> none  [two_products(): lax.psum((jnp.sum(residual * residual, axis=(0, 1, 2)), jnp.sum(residual...]
    pallas_call x0 -> x7, Pallas kernels: none -> 12.6 us  [the longest x5 9.28 us: call(): pl.pallas_call(body, out_shape=outs, in_specs=ins, out_specs=jax.tree.map...]
    ppermute x16 -> x20, starting transfers between devices: 30.1 us -> 20.4 us  [the longest x12 12.3 us: exchange(): arrived[e ^ 1] = lax.ppermute(outgoing[e], SPACE, route)]
    dot_general x6 -> x0, matrix products: 8.76 us -> none  [the longest x2 5.2 us: spatial(): jnp.einsum('nik,hnkp->hnip', near_stiffness, nearby, precision=lax.Precis...]
    gather x4 -> x0, local copies, waits for them, and re-layouts: 8.1 us -> none  [the longest x2 4.79 us: spatial(): jnp.take(vector, near_columns.reshape(-1), axis=1)]
    select_n x6 -> x0, other arithmetic: 4.01 us -> none  [the longest x3 2.49 us: spatial(): jnp.take(vector, near_columns.reshape(-1), axis=1)]
    sub x2 -> x0, other arithmetic: 3.33 us -> none  [shards(): residual = residual - step_size * applied_dir]
    reduce_sum x2 -> x0, other arithmetic: 1.94 us -> none  [two_products(): jnp.sum(residual * applied, axis=(0, 1, 2))]
  transfers between devices with their start and end apart: 16 -> 20, of which waited for: 8 -> 10; matrix products, arithmetic and copies ran while one was open for 5% -> 0% of each run, Pallas kernels for 0% -> 10%
where the time goes in v1:
time: 75.3 us; the launch traced here: 74.3 us
  waiting for transfers between devices  34.4 us (46%)
  starting transfers between devices  20.4 us (27%)
  Pallas kernels  12.6 us (17%)
  local copies, waits for them, and re-layouts  5.57 us (7%)
  between operations  1.42 us (2%)
    ppermute x12, waiting for transfers between devices, exchange(): arrived[e ^ 1] = lax.ppermute(outgoing[e], SPACE, route)  21.8 us
    ppermute x8, waiting for transfers between devices, rotations(): lax.ppermute(value, axes, [(i, (i + d) % count) for i in range(count)])  12.5 us
    ppermute x12, starting transfers between devices, exchange(): arrived[e ^ 1] = lax.ppermute(outgoing[e], SPACE, route)  12.3 us
    pallas_call x5, Pallas kernels, call(): pl.pallas_call(body, out_shape=outs, in_specs=ins, out_specs=jax.tree.map...  9.28 us
    ppermute x8, starting transfers between devices, rotations(): lax.ppermute(value, axes, [(i, (i + d) % count) for i in range(count)])  8.09 us
    unnamed x22, local copies, waits for them, and re-layouts  5.57 us
    pallas_call x2, Pallas kernels, near(): pl.pallas_call(near_body, out_shape=struct(*field.shape), in_specs=[smem(...  3.28 us
  transfers between devices with their start and end apart: 20, of which 10 were waited for; matrix products, arithmetic and copies ran while one was open for 0% of the time, Pallas kernels for 10%

profile of v1, /device:TPU:0, one launch (start us, length us, event | category | flops | bytes accessed | tf_op | source)
XLA Modules:
  0.0 74.3 jit_solution(14944601364105488234)
XLA Ops:
  0.6 0.0 copy-start
  0.6 1.0 %copy-done = f32[1,16,64,128]{3,2,1,0:T(8,128)S(1)} copy-done((f32[1,16,64,128]{3,2,1,0:T(8,128)S(1)}, f32[1,16,64,128]{3,2,1,0:T(8,128)}, u32[]{:S(2)}) %copy-start) | copy-done | bytes 524312
  1.7 0.0 copy-start.7
  1.7 0.7 copy-done.7
  2.4 0.0 copy-start.5
  2.4 0.0 copy-start.8
  2.4 0.0 copy-start.10
  2.4 0.6 shard_map.96
  3.0 4.5 %collective-permute-start = (f32[4,64,128]{2,1,0:T(8,128)S(1)}, f32[4,64,128]{2,1,0:T(8,128)S(1)}, u32[]{:S(2)}, u32[]{:S(2)}) collective-permute-start(f32[4,64,128]{2,1,0:T(8,128)S(1)} %get-tuple-element.17), channel_id=1, source_target_pairs={{0,13},{1,0},{4,1},{5,4},{8,5},{9,8},{12,9},{13,12},{2,15},{3,2},{... | collective-permute-start | bytes 393224 | tf_op jit(solution)/shard_map/ppermute | solution.py:118
  7.5 0.0 collective-permute-start.1
  7.5 1.1 %collective-permute-start.2 = (f32[4,64,128]{2,1,0:T(8,128)S(1)}, f32[4,64,128]{2,1,0:T(8,128)S(1)}, u32[]{:S(2)}, u32[]{:S(2)}) collective-permute-start(f32[4,64,128]{2,1,0:T(8,128)S(1)} %get-tuple-element.19), channel_id=1, source_target_pairs={{0,12},{1,13},{4,0},{5,1},{8,4},{9,5},{12,8},{13,9},{2,14},{3,15},... | collective-permute-start | bytes 393224 | tf_op jit(solution)/shard_map/ppermute | solution.py:118
  8.6 1.0 %collective-permute-start.3 = (f32[4,64,128]{2,1,0:T(8,128)S(1)}, f32[4,64,128]{2,1,0:T(8,128)S(1)}, u32[]{:S(2)}, u32[]{:S(2)}) collective-permute-start(f32[4,64,128]{2,1,0:T(8,128)S(1)} %get-tuple-element.20), channel_id=1, source_target_pairs={{0,4},{1,5},{4,8},{5,9},{8,12},{9,13},{12,0},{13,1},{2,6},{3,7},{6... | collective-permute-start | bytes 393224 | tf_op jit(solution)/shard_map/ppermute | solution.py:118
  9.6 1.8 %collective-permute-start.4 = (f32[4,64,128]{2,1,0:T(8,128)S(1)}, f32[4,64,128]{2,1,0:T(8,128)S(1)}, u32[]{:S(2)}, u32[]{:S(2)}) collective-permute-start(f32[4,64,128]{2,1,0:T(8,128)S(1)} %get-tuple-element.21), channel_id=1, source_target_pairs={{0,9},{1,12},{4,13},{5,0},{8,1},{9,4},{12,5},{13,8},{2,11},{3,14},... | collective-permute-start | bytes 393224 | tf_op jit(solution)/shard_map/ppermute | solution.py:118
  11.4 0.0 collective-permute-done.refs_0_
  11.4 0.0 collective-permute-start.5
  11.4 1.0 %copy-done.1 = f32[1,16,64,128]{3,2,1,0:T(8,128)S(1)} copy-done((f32[1,16,64,128]{3,2,1,0:T(8,128)S(1)}, f32[1,16,64,128]{3,2,1,0:T(8,128)}, u32[]{:S(2)}) %copy-start.1) | copy-done | bytes 524312
  12.4 1.4 %copy-done.3 = f32[16,64,384]{2,1,0:T(8,128)S(1)} copy-done((f32[16,64,384]{2,1,0:T(8,128)S(1)}, f32[16,64,384]{2,1,0:T(8,128)}, u32[]{:S(2)}) %copy-start.3) | copy-done | bytes 1572888
  13.8 0.7 copy-done.6
  14.5 0.7 copy-done.9
  15.2 1.6 %shard_map.95.start = f32[16,64,128]{2,1,0:T(8,128)S(1)} custom-call(s32[6,16]{1,0:T(8,128)S(1)} %bitcast.13, f32[16,64]{1,0:T(8,128)S(1)} %copy-done.6, f32[16,64,384]{2,1,0:T(8,128)S(1)} %copy-done.3, f32[16,64,128]{2,1,0:T(8,128)S(1)} %bitcast.7), custom_call_target="tpu_custom_call" | custom-call | tf_op jit(solution)/shard_map/pallas_call | solution.py:81
  16.9 0.0 collective-permute-done.1.refs_1_
  16.9 0.0 collective-permute-done.2.refs_2_
  16.9 0.0 collective-permute-done.3.refs_3_
  16.9 0.6 collective-permute-done.4.refs_4_
  17.5 8.0 %collective-permute-done.5.refs_5_ = f32[4,64,128]{2,1,0:T(8,128)S(1)} collective-permute-done((f32[4,64,128]{2,1,0:T(8,128)S(1)}, f32[4,64,128]{2,1,0:T(8,128)S(1)}, u32[]{:S(2)}, u32[]{:S(2)}) %collective-permute-start.5) | collective-permute-done | bytes 131104 | tf_op jit(solution)/shard_map/ppermute | solution.py:118
  25.5 0.0 copy-done.5
  25.5 0.0 copy-done.8
  25.5 0.0 copy-done.10
  25.5 3.6 %shard_map.97 = (f32[16,64,128]{2,1,0:T(8,128)S(1)}, f32[4,64,128]{2,1,0:T(8,128)S(1)}, f32[4,64,128]{2,1,0:T(8,128)S(1)}, f32[4,64,128]{2,1,0:T(8,128)S(1)}, f3...) custom-call(s32[1,4,6]{2,1,0:T(4,128)S(1)} %bitcast.11, s32[1,6]{1,0:T(1,128)S(1)} %copy-done.10, ...), custom_call_target="tpu_custom_call" | custom-call | tf_op jit(solution)/shard_map/pallas_call | solution.py:28
  29.1 0.2 collective-permute-start.6
  29.3 0.4 collective-permute-start.7
  29.7 1.5 %collective-permute-start.12 = (f32[16,64,128]{2,1,0:T(8,128)S(1)}, f32[16,64,128]{2,1,0:T(8,128)S(1)}, u32[]{:S(2)}, u32[]{:S(2)}) collective-permute-start(f32[16,64,128]{2,1,0:T(8,128)S(1)} %get-tuple-element.23.field.refs_0_.refs_4_), channel_id=1, source_target_pairs={{0,2},{2,0},{1,3},{3,1},{4,6},{6,4},{5,7},{7,5},{8,10},{10,8},{9,1... | collective-permute-start | bytes 1572872 | tf_op jit(solution)/shard_map/ppermute | solution.py:125
  31.2 1.6 %collective-permute-start.8 = (f32[4,64,128]{2,1,0:T(8,128)S(1)}, f32[4,64,128]{2,1,0:T(8,128)S(1)}, u32[]{:S(2)}, u32[]{:S(2)}) collective-permute-start(f32[4,64,128]{2,1,0:T(8,128)S(1)} %get-tuple-element.26), channel_id=1, source_target_pairs={{0,12},{1,13},{4,0},{5,1},{8,4},{9,5},{12,8},{13,9},{2,14},{3,15},... | collective-permute-start | bytes 393224 | tf_op jit(solution)/shard_map/ppermute | solution.py:118
  32.7 0.4 collective-permute-start.9
  33.2 0.0 collective-permute-done.6.refs_0_
  33.2 1.4 %collective-permute-start.10 = (f32[4,64,128]{2,1,0:T(8,128)S(1)}, f32[4,64,128]{2,1,0:T(8,128)S(1)}, u32[]{:S(2)}, u32[]{:S(2)}) collective-permute-start(f32[4,64,128]{2,1,0:T(8,128)S(1)} %get-tuple-element.28), channel_id=1, source_target_pairs={{0,9},{1,12},{4,13},{5,0},{8,1},{9,4},{12,5},{13,8},{2,11},{3,14},... | collective-permute-start | bytes 393224 | tf_op jit(solution)/shard_map/ppermute | solution.py:118
  34.5 2.0 %collective-permute-done.7.refs_1_ = f32[4,64,128]{2,1,0:T(8,128)S(1)} collective-permute-done((f32[4,64,128]{2,1,0:T(8,128)S(1)}, f32[4,64,128]{2,1,0:T(8,128)S(1)}, u32[]{:S(2)}, u32[]{:S(2)}) %collective-permute-start.7) | collective-permute-done | bytes 131104 | tf_op jit(solution)/shard_map/ppermute | solution.py:118
  36.5 0.0 collective-permute-start.11
  36.5 0.0 copy-done.4
  36.5 1.6 %shard_map.98.start = f32[16,64,128]{2,1,0:T(8,128)S(1)} custom-call(s32[6,16]{1,0:T(8,128)S(1)} %bitcast.14, f32[16,64]{1,0:T(8,128)S(1)} %copy-done.6, f32[16,64,384]{2,1,0:T(8,128)S(1)} %copy-done.4, f32[16,64,128]{2,1,0:T(8,128)S(1)} %get-tuple-element.23.field.refs_0_.refs_4_), custom_call_target="tpu_custom_call" | custom-call | tf_op jit(solution)/shard_map/pallas_call | solution.py:81
  38.1 0.0 copy-start.2
  38.2 3.0 %collective-permute-done.8.refs_2_ = f32[4,64,128]{2,1,0:T(8,128)S(1)} collective-permute-done((f32[4,64,128]{2,1,0:T(8,128)S(1)}, f32[4,64,128]{2,1,0:T(8,128)S(1)}, u32[]{:S(2)}, u32[]{:S(2)}) %collective-permute-start.8) | collective-permute-done | bytes 131104 | tf_op jit(solution)/shard_map/ppermute | solution.py:118
  41.2 0.0 collective-permute-done.9.refs_3_
  41.2 0.8 %collective-permute-done.10.refs_4_ = f32[4,64,128]{2,1,0:T(8,128)S(1)} collective-permute-done((f32[4,64,128]{2,1,0:T(8,128)S(1)}, f32[4,64,128]{2,1,0:T(8,128)S(1)}, u32[]{:S(2)}, u32[]{:S(2)}) %collective-permute-start.10) | collective-permute-done | bytes 131104 | tf_op jit(solution)/shard_map/ppermute | solution.py:118
  42.0 7.4 %collective-permute-done.11.refs_5_ = f32[4,64,128]{2,1,0:T(8,128)S(1)} collective-permute-done((f32[4,64,128]{2,1,0:T(8,128)S(1)}, f32[4,64,128]{2,1,0:T(8,128)S(1)}, u32[]{:S(2)}, u32[]{:S(2)}) %collective-permute-start.11) | collective-permute-done | bytes 131104 | tf_op jit(solution)/shard_map/ppermute | solution.py:118
  49.4 3.5 %shard_map.99.second.refs_6_ = f32[16,64,128]{2,1,0:T(8,128)S(1)} custom-call(s32[1,4,6]{2,1,0:T(4,128)S(1)} %bitcast.12, s32[1,6]{1,0:T(1,128)S(1)} %copy-done.10, f32[1,64,1536]{2,1,0:T(8,128)S(1)} %copy-done.5, f32[16,64,128]{2,1,0:T(8,128)S(1)} %shard_map.98.start, f32[4,64,128]{2,1,0:T(8,128)S(1)} %collective-permute-done.6.refs_0_, ...), custom_call_target="tpu_custom_call" | custom-call | tf_op jit(solution)/shard_map/pallas_call | solution.py:28
  53.0 0.6 collective-permute-start.19
  54.2 0.0 collective-permute-done.12.refs_1_.refs_5_
  54.2 0.0 copy-done.2
  54.3 0.3 shard_map.100
  54.6 0.1 collective-permute-start.15
  54.6 1.6 %collective-permute-start.14 = (f32[8,128]{1,0:T(8,128)S(1)}, f32[8,128]{1,0:T(8,128)S(1)}, u32[]{:S(2)}, u32[]{:S(2)}) collective-permute-start(f32[8,128]{1,0:T(8,128)S(1)} %shard_map.100), channel_id=1, source_target_pairs={{0,2},{1,3},{2,0},{3,1},{4,6},{5,7},{6,4},{7,5},{8,10},{9,11},{10,... | collective-permute-start | bytes 12296 | tf_op jit(solution)/shard_map/ppermute | solution.py:125
  56.2 0.2 collective-permute-start.13
  56.4 6.7 %collective-permute-done.15 = f32[8,128]{1,0:T(8,128)S(1)} collective-permute-done((f32[8,128]{1,0:T(8,128)S(1)}, f32[8,128]{1,0:T(8,128)S(1)}, u32[]{:S(2)}, u32[]{:S(2)}) %collective-permute-start.15) | collective-permute-done | bytes 4128 | tf_op jit(solution)/shard_map/ppermute | solution.py:125
  63.1 2.0 %collective-permute-done.14 = f32[8,128]{1,0:T(8,128)S(1)} collective-permute-done((f32[8,128]{1,0:T(8,128)S(1)}, f32[8,128]{1,0:T(8,128)S(1)}, u32[]{:S(2)}, u32[]{:S(2)}) %collective-permute-start.14) | collective-permute-done | bytes 4128 | tf_op jit(solution)/shard_map/ppermute | solution.py:125
  65.1 0.0 collective-permute-done.13
  65.1 1.7 %collective-permute-start.18 = (f32[8,128]{1,0:T(8,128)S(1)}, f32[8,128]{1,0:T(8,128)S(1)}, u32[]{:S(2)}, u32[]{:S(2)}) collective-permute-start(f32[8,128]{1,0:T(8,128)S(1)} %add_add_fusion.refs_0_), channel_id=1, source_target_pairs={{0,12},{4,0},{8,4},{12,8},{1,13},{5,1},{9,5},{13,9},{2,14},{6,2},{... | collective-permute-start | bytes 12296 | tf_op jit(solution)/shard_map/ppermute | solution.py:125
  66.8 0.9 %collective-permute-start.17 = (f32[8,128]{1,0:T(8,128)S(1)}, f32[8,128]{1,0:T(8,128)S(1)}, u32[]{:S(2)}, u32[]{:S(2)}) collective-permute-start(f32[8,128]{1,0:T(8,128)S(1)} %add_add_fusion.refs_0_), channel_id=1, source_target_pairs={{0,8},{4,12},{8,0},{12,4},{1,9},{5,13},{9,1},{13,5},{2,10},{6,14},... | collective-permute-start | bytes 12296 | tf_op jit(solution)/shard_map/ppermute | solution.py:125
  67.7 1.6 %collective-permute-start.16 = (f32[8,128]{1,0:T(8,128)S(1)}, f32[8,128]{1,0:T(8,128)S(1)}, u32[]{:S(2)}, u32[]{:S(2)}) collective-permute-start(f32[8,128]{1,0:T(8,128)S(1)} %add_add_fusion.refs_0_), channel_id=1, source_target_pairs={{0,4},{4,8},{8,12},{12,0},{1,5},{5,9},{9,13},{13,1},{2,6},{6,10},{... | collective-permute-start | bytes 12296 | tf_op jit(solution)/shard_map/ppermute | solution.py:125
  69.3 0.0 collective-permute-done.18.refs_3_
  69.3 2.0 %collective-permute-done.17.refs_2_ = f32[8,128]{1,0:T(8,128)S(1)} collective-permute-done((f32[8,128]{1,0:T(8,128)S(1)}, f32[8,128]{1,0:T(8,128)S(1)}, u32[]{:S(2)}, u32[]{:S(2)}) %collective-permute-start.17) | collective-permute-done | bytes 4128 | tf_op jit(solution)/shard_map/ppermute | solution.py:125
  71.3 1.8 %collective-permute-done.16.refs_1_ = f32[8,128]{1,0:T(8,128)S(1)} collective-permute-done((f32[8,128]{1,0:T(8,128)S(1)}, f32[8,128]{1,0:T(8,128)S(1)}, u32[]{:S(2)}, u32[]{:S(2)}) %collective-permute-start.16) | collective-permute-done | bytes 4128 | tf_op jit(solution)/shard_map/ppermute | solution.py:125
  73.1 0.0 collective-permute-done.19.refs_7_
  73.1 1.2 %shard_map.101 = (f32[16,64,128]{2,1,0:T(8,128)}, f32[16,64,128]{2,1,0:T(8,128)}) custom-call(f32[1]{0:T(128)S(6)} %copy.10.coupling, s32[1]{0:T(128)} %bitcast.hour, f32[16,64,128]{2,1,0:T(8,128)S(1)} %bitcast.9, f32[8,128]{1,0:T(8,128)S(1)} %add_add_fusion.refs_0_, f32[8,128]{1,0:T(8,128)S(1)} %collective-permute-done.16.refs_1_, ...), custom_call_target="tpu_custom_call" | custom-call | tf_op jit(solution)/shard_map/pallas_call | solution.py:28
  (6 shorter events, 0.0 us)
Async XLA Ops:
  0.6 1.0 %copy-start = (f32[1,16,64,128]{3,2,1,0:T(8,128)S(1)}, f32[1,16,64,128]{3,2,1,0:T(8,128)}, u32[]{:S(2)}) copy-start(f32[1,16,64,128]{3,2,1,0:T(8,128)} %param.8) | copy-start | bytes 1572868
  1.7 0.7 copy-start.7
  2.4 23.1 %copy-start.5 = (f32[1,64,1536]{2,1,0:T(8,128)S(1)}, f32[1,64,1536]{2,1,0:T(8,128)}, u32[]{:S(2)}) copy-start(f32[1,64,1536]{2,1,0:T(8,128)} %stiffness.7) | copy-start | bytes 1179652
  2.4 23.1 %copy-start.8 = (s32[1,6,4]{1,2,0:T(4,128)S(1)}, s32[1,6,4]{1,2,0:T(4,128)}, u32[]{:S(2)}) copy-start(s32[1,6,4]{1,2,0:T(4,128)} %param.14) | copy-start | bytes 292
  2.4 23.1 %copy-start.10 = (s32[1,6]{1,0:T(1,128)S(1)}, s32[1,6]{1,0:T(1,128)}, u32[]{:S(2)}) copy-start(s32[1,6]{1,0:T(1,128)} %counts.3) | copy-start | bytes 76
  3.0 8.4 %collective-permute-start = (f32[4,64,128]{2,1,0:T(8,128)S(1)}, f32[4,64,128]{2,1,0:T(8,128)S(1)}, u32[]{:S(2)}, u32[]{:S(2)}) collective-permute-start(f32[4,64,128]{2,1,0:T(8,128)S(1)} %get-tuple-element.17), channel_id=1, source_target_pairs={{0,13},{1,0},{4,1},{5,4},{8,5},{9,8},{12,9},{13,12},{2,15},{3,2},{... | collective-permute-start | bytes 393224 | tf_op jit(solution)/shard_map/ppermute | solution.py:118
  7.5 9.3 %collective-permute-start.1 = (f32[4,64,128]{2,1,0:T(8,128)S(1)}, f32[4,64,128]{2,1,0:T(8,128)S(1)}, u32[]{:S(2)}, u32[]{:S(2)}) collective-permute-start(f32[4,64,128]{2,1,0:T(8,128)S(1)} %get-tuple-element.18), channel_id=1, source_target_pairs={{0,1},{1,4},{4,5},{5,8},{8,9},{9,12},{12,13},{13,0},{2,3},{3,6},{6... | collective-permute-start | bytes 393224 | tf_op jit(solution)/shard_map/ppermute | solution.py:118
  7.5 9.3 %collective-permute-start.2 = (f32[4,64,128]{2,1,0:T(8,128)S(1)}, f32[4,64,128]{2,1,0:T(8,128)S(1)}, u32[]{:S(2)}, u32[]{:S(2)}) collective-permute-start(f32[4,64,128]{2,1,0:T(8,128)S(1)} %get-tuple-element.19), channel_id=1, source_target_pairs={{0,12},{1,13},{4,0},{5,1},{8,4},{9,5},{12,8},{13,9},{2,14},{3,15},... | collective-permute-start | bytes 393224 | tf_op jit(solution)/shard_map/ppermute | solution.py:118
  8.6 8.3 %collective-permute-start.3 = (f32[4,64,128]{2,1,0:T(8,128)S(1)}, f32[4,64,128]{2,1,0:T(8,128)S(1)}, u32[]{:S(2)}, u32[]{:S(2)}) collective-permute-start(f32[4,64,128]{2,1,0:T(8,128)S(1)} %get-tuple-element.20), channel_id=1, source_target_pairs={{0,4},{1,5},{4,8},{5,9},{8,12},{9,13},{12,0},{13,1},{2,6},{3,7},{6... | collective-permute-start | bytes 393224 | tf_op jit(solution)/shard_map/ppermute | solution.py:118
  9.6 7.9 %collective-permute-start.4 = (f32[4,64,128]{2,1,0:T(8,128)S(1)}, f32[4,64,128]{2,1,0:T(8,128)S(1)}, u32[]{:S(2)}, u32[]{:S(2)}) collective-permute-start(f32[4,64,128]{2,1,0:T(8,128)S(1)} %get-tuple-element.21), channel_id=1, source_target_pairs={{0,9},{1,12},{4,13},{5,0},{8,1},{9,4},{12,5},{13,8},{2,11},{3,14},... | collective-permute-start | bytes 393224 | tf_op jit(solution)/shard_map/ppermute | solution.py:118
  11.4 14.1 %collective-permute-start.5 = (f32[4,64,128]{2,1,0:T(8,128)S(1)}, f32[4,64,128]{2,1,0:T(8,128)S(1)}, u32[]{:S(2)}, u32[]{:S(2)}) collective-permute-start(f32[4,64,128]{2,1,0:T(8,128)S(1)} %get-tuple-element.22), channel_id=1, source_target_pairs={{0,5},{1,8},{4,9},{5,12},{8,13},{9,0},{12,1},{13,4},{2,7},{3,10},{... | collective-permute-start | bytes 393224 | tf_op jit(solution)/shard_map/ppermute | solution.py:118
  11.4 1.0 %copy-start.1 = (f32[1,16,64,128]{3,2,1,0:T(8,128)S(1)}, f32[1,16,64,128]{3,2,1,0:T(8,128)}, u32[]{:S(2)}) copy-start(f32[1,16,64,128]{3,2,1,0:T(8,128)} %param.8) | copy-start | bytes 1572868
  12.4 1.4 %copy-start.3 = (f32[16,64,384]{2,1,0:T(8,128)S(1)}, f32[16,64,384]{2,1,0:T(8,128)}, u32[]{:S(2)}) copy-start(f32[16,64,384]{2,1,0:T(8,128)} %stiffness.6) | copy-start | bytes 4718596
  13.8 0.7 copy-start.6
  14.5 0.7 copy-start.9
  15.2 21.3 %copy-start.4 = (f32[16,64,384]{2,1,0:T(8,128)S(1)}, f32[16,64,384]{2,1,0:T(8,128)}, u32[]{:S(2)}) copy-start(f32[16,64,384]{2,1,0:T(8,128)} %stiffness.6) | copy-start | bytes 4718596
  29.1 4.1 %collective-permute-start.6 = (f32[4,64,128]{2,1,0:T(8,128)S(1)}, f32[4,64,128]{2,1,0:T(8,128)S(1)}, u32[]{:S(2)}, u32[]{:S(2)}) collective-permute-start(f32[4,64,128]{2,1,0:T(8,128)S(1)} %get-tuple-element.24), channel_id=1, source_target_pairs={{0,13},{1,0},{4,1},{5,4},{8,5},{9,8},{12,9},{13,12},{2,15},{3,2},{... | collective-permute-start | bytes 393224 | tf_op jit(solution)/shard_map/ppermute | solution.py:118
  29.3 7.2 %collective-permute-start.7 = (f32[4,64,128]{2,1,0:T(8,128)S(1)}, f32[4,64,128]{2,1,0:T(8,128)S(1)}, u32[]{:S(2)}, u32[]{:S(2)}) collective-permute-start(f32[4,64,128]{2,1,0:T(8,128)S(1)} %get-tuple-element.25), channel_id=1, source_target_pairs={{0,1},{1,4},{4,5},{5,8},{8,9},{9,12},{12,13},{13,0},{2,3},{3,6},{6... | collective-permute-start | bytes 393224 | tf_op jit(solution)/shard_map/ppermute | solution.py:118
  29.7 24.6 %collective-permute-start.12 = (f32[16,64,128]{2,1,0:T(8,128)S(1)}, f32[16,64,128]{2,1,0:T(8,128)S(1)}, u32[]{:S(2)}, u32[]{:S(2)}) collective-permute-start(f32[16,64,128]{2,1,0:T(8,128)S(1)} %get-tuple-element.23.field.refs_0_.refs_4_), channel_id=1, source_target_pairs={{0,2},{2,0},{1,3},{3,1},{4,6},{6,4},{5,7},{7,5},{8,10},{10,8},{9,1... | collective-permute-start | bytes 1572872 | tf_op jit(solution)/shard_map/ppermute | solution.py:125
  31.2 10.0 %collective-permute-start.8 = (f32[4,64,128]{2,1,0:T(8,128)S(1)}, f32[4,64,128]{2,1,0:T(8,128)S(1)}, u32[]{:S(2)}, u32[]{:S(2)}) collective-permute-start(f32[4,64,128]{2,1,0:T(8,128)S(1)} %get-tuple-element.26), channel_id=1, source_target_pairs={{0,12},{1,13},{4,0},{5,1},{8,4},{9,5},{12,8},{13,9},{2,14},{3,15},... | collective-permute-start | bytes 393224 | tf_op jit(solution)/shard_map/ppermute | solution.py:118
  32.7 8.4 %collective-permute-start.9 = (f32[4,64,128]{2,1,0:T(8,128)S(1)}, f32[4,64,128]{2,1,0:T(8,128)S(1)}, u32[]{:S(2)}, u32[]{:S(2)}) collective-permute-start(f32[4,64,128]{2,1,0:T(8,128)S(1)} %get-tuple-element.27), channel_id=1, source_target_pairs={{0,4},{1,5},{4,8},{5,9},{8,12},{9,13},{12,0},{13,1},{2,6},{3,7},{6... | collective-permute-start | bytes 393224 | tf_op jit(solution)/shard_map/ppermute | solution.py:118
  33.2 8.8 %collective-permute-start.10 = (f32[4,64,128]{2,1,0:T(8,128)S(1)}, f32[4,64,128]{2,1,0:T(8,128)S(1)}, u32[]{:S(2)}, u32[]{:S(2)}) collective-permute-start(f32[4,64,128]{2,1,0:T(8,128)S(1)} %get-tuple-element.28), channel_id=1, source_target_pairs={{0,9},{1,12},{4,13},{5,0},{8,1},{9,4},{12,5},{13,8},{2,11},{3,14},... | collective-permute-start | bytes 393224 | tf_op jit(solution)/shard_map/ppermute | solution.py:118
  36.5 12.9 %collective-permute-start.11 = (f32[4,64,128]{2,1,0:T(8,128)S(1)}, f32[4,64,128]{2,1,0:T(8,128)S(1)}, u32[]{:S(2)}, u32[]{:S(2)}) collective-permute-start(f32[4,64,128]{2,1,0:T(8,128)S(1)} %get-tuple-element.29), channel_id=1, source_target_pairs={{0,5},{1,8},{4,9},{5,12},{8,13},{9,0},{12,1},{13,4},{2,7},{3,10},{... | collective-permute-start | bytes 393224 | tf_op jit(solution)/shard_map/ppermute | solution.py:118
  38.1 16.1 %copy-start.2 = (f32[1,16,64,128]{3,2,1,0:T(8,128)S(1)}, f32[1,16,64,128]{3,2,1,0:T(8,128)}, u32[]{:S(2)}) copy-start(f32[1,16,64,128]{3,2,1,0:T(8,128)} %param.8) | copy-start | bytes 1572868
  53.0 20.1 %collective-permute-start.19 = (f32[16,64,128]{2,1,0:T(8,128)S(1)}, f32[16,64,128]{2,1,0:T(8,128)S(1)}, u32[]{:S(2)}, u32[]{:S(2)}) collective-permute-start(f32[16,64,128]{2,1,0:T(8,128)S(1)} %shard_map.99.second.refs_6_), channel_id=1, source_target_pairs={{0,2},{2,0},{1,3},{3,1},{4,6},{6,4},{5,7},{7,5},{8,10},{10,8},{9,1... | collective-permute-start | bytes 1572872 | tf_op jit(solution)/shard_map/ppermute | solution.py:125
  54.6 8.5 %collective-permute-start.15 = (f32[8,128]{1,0:T(8,128)S(1)}, f32[8,128]{1,0:T(8,128)S(1)}, u32[]{:S(2)}, u32[]{:S(2)}) collective-permute-start(f32[8,128]{1,0:T(8,128)S(1)} %shard_map.100), channel_id=1, source_target_pairs={{0,3},{1,0},{2,1},{3,2},{4,7},{5,4},{6,5},{7,6},{8,11},{9,8},{10,9... | collective-permute-start | bytes 12296 | tf_op jit(solution)/shard_map/ppermute | solution.py:125
  54.6 10.4 %collective-permute-start.14 = (f32[8,128]{1,0:T(8,128)S(1)}, f32[8,128]{1,0:T(8,128)S(1)}, u32[]{:S(2)}, u32[]{:S(2)}) collective-permute-start(f32[8,128]{1,0:T(8,128)S(1)} %shard_map.100), channel_id=1, source_target_pairs={{0,2},{1,3},{2,0},{3,1},{4,6},{5,7},{6,4},{7,5},{8,10},{9,11},{10,... | collective-permute-start | bytes 12296 | tf_op jit(solution)/shard_map/ppermute | solution.py:125
  56.2 8.9 %collective-permute-start.13 = (f32[8,128]{1,0:T(8,128)S(1)}, f32[8,128]{1,0:T(8,128)S(1)}, u32[]{:S(2)}, u32[]{:S(2)}) collective-permute-start(f32[8,128]{1,0:T(8,128)S(1)} %shard_map.100), channel_id=1, source_target_pairs={{0,1},{1,2},{2,3},{3,0},{4,5},{5,6},{6,7},{7,4},{8,9},{9,10},{10,1... | collective-permute-start | bytes 12296 | tf_op jit(solution)/shard_map/ppermute | solution.py:125
  65.1 4.2 %collective-permute-start.18 = (f32[8,128]{1,0:T(8,128)S(1)}, f32[8,128]{1,0:T(8,128)S(1)}, u32[]{:S(2)}, u32[]{:S(2)}) collective-permute-start(f32[8,128]{1,0:T(8,128)S(1)} %add_add_fusion.refs_0_), channel_id=1, source_target_pairs={{0,12},{4,0},{8,4},{12,8},{1,13},{5,1},{9,5},{13,9},{2,14},{6,2},{... | collective-permute-start | bytes 12296 | tf_op jit(solution)/shard_map/ppermute | solution.py:125
  66.8 4.5 %collective-permute-start.17 = (f32[8,128]{1,0:T(8,128)S(1)}, f32[8,128]{1,0:T(8,128)S(1)}, u32[]{:S(2)}, u32[]{:S(2)}) collective-permute-start(f32[8,128]{1,0:T(8,128)S(1)} %add_add_fusion.refs_0_), channel_id=1, source_target_pairs={{0,8},{4,12},{8,0},{12,4},{1,9},{5,13},{9,1},{13,5},{2,10},{6,14},... | collective-permute-start | bytes 12296 | tf_op jit(solution)/shard_map/ppermute | solution.py:125
  67.7 5.4 %collective-permute-start.16 = (f32[8,128]{1,0:T(8,128)S(1)}, f32[8,128]{1,0:T(8,128)S(1)}, u32[]{:S(2)}, u32[]{:S(2)}) collective-permute-start(f32[8,128]{1,0:T(8,128)S(1)} %add_add_fusion.refs_0_), channel_id=1, source_target_pairs={{0,4},{4,8},{8,12},{12,0},{1,5},{5,9},{9,13},{13,1},{2,6},{6,10},{... | collective-permute-start | bytes 12296 | tf_op jit(solution)/shard_map/ppermute | solution.py:125

commit v2 on v1

v2 whole, which is shorter than its diff:
```python
import functools

import jax
import jax.numpy as jnp
from jax import lax
from jax.experimental import pallas as pl
from jax.experimental.pallas import tpu as pltpu
from jax.sharding import PartitionSpec as P

SPACE = ("mesh", "rep")
F32 = jnp.float32
BF16 = jnp.bfloat16
EARLY = (0, 2, 4)


def struct(*shape, dtype=F32):
    return jax.ShapeDtypeStruct(shape, dtype)


def call(body, outs, scalars, vectors, scratch=()):
    spaces = [pltpu.SMEM] * len(scalars) + [pltpu.VMEM] * len(vectors)
    return pl.pallas_call(
        body,
        out_shape=outs,
        in_specs=[pl.BlockSpec(memory_space=space) for space in spaces],
        out_specs=jax.tree.map(lambda _: pl.BlockSpec(memory_space=pltpu.VMEM), outs),
        scratch_shapes=scratch,
        compiler_params=pltpu.CompilerParams(vmem_limit_bytes=40 << 20),
    )(*scalars, *vectors)


def total(values):
    return functools.reduce(jnp.add, values)


def halves(value):
    high = value.astype(BF16)
    return high, (value - high.astype(F32)).astype(BF16)


def group_of(shape, hours):
    lanes = shape[-1]
    return lax.broadcasted_iota(jnp.int32, shape, len(shape) - 1) // (lanes // hours)


def turned(value, places, hours):
    width = value.shape[-1] // hours
    result = value
    for k in range(1, hours):
        result = jnp.where(places == k, pltpu.roll(value, k * width, value.ndim - 1), result)
    return result


def pack_lanes(hours, hour, field, outs):
    group = group_of(field.shape[1:], hours)
    for r, out in enumerate(outs):
        target = lax.rem(hour + r + 1, hours)
        for j in range(out.shape[0]):
            packed = None
            for i in range(hours):
                part = turned(field[j * hours + i], lax.rem(i - target + hours, hours), hours)
                packed = part if i == 0 else jnp.where(group == i, part, packed)
            out[j] = packed


def merge_lanes(hours, hour, own, packs, block):
    group = group_of(own.shape, hours)
    for r, pack in enumerate(packs):
        source = lax.rem(hour + hours - r - 1, hours)
        part = pack[block // hours]
        part = turned(part, lax.rem(source - block % hours + hours, hours), hours)
        own = jnp.where(group == source, part, own)
    return own


def couple(hours, coupling, value):
    lanes = value.shape[-1]
    width = lanes // hours
    before, after = (pltpu.roll(value, d, value.ndim - 1) for d in (width, lanes - width))
    if hours == 2:
        return value - coupling * before
    group = group_of(value.shape, hours)
    sides = jnp.where(group > 0, before, 0.0) + jnp.where(group < hours - 1, after, 0.0)
    return value - coupling * sides


def pack_faces(faces, field, headings, outs):
    for e, out in zip(headings, outs):
        for f in range(out.shape[0]):
            out[f] = field[faces[0, f, e]]


def far_product(stiffness, q, block):
    high, low = halves(block)
    right = jnp.concatenate([high, high, low], axis=0)
    return jnp.dot(stiffness[q], right, preferred_element_type=F32)


def landing(faces, counts, e, f, spare):
    return jnp.where(f < counts[0, e], faces[0, f, e], spare)


def open_body(hours, faces, hour, field, *outs):
    split = len(EARLY)
    pack_faces(faces, field, EARLY, outs[:split])
    pack_lanes(hours, hour[0], field, outs[split:])


def turn_body(hours, faces, hour, field, *refs):
    packs, out, faces_out = refs[: hours - 1], refs[hours - 1], refs[hours:]
    for b in range(field.shape[0]):
        out[b] = merge_lanes(hours, hour[0], field[b], packs, b)
    pack_faces(faces, out, [e ^ 1 for e in EARLY], faces_out)


def split_body(stiffness, out):
    width = stiffness.shape[1]
    for q in range(out.shape[0]):
        high, low = halves(stiffness[0, :, q * width : (q + 1) * width])
        out[q] = jnp.concatenate([high, low, high], axis=1)


def near_body(count, columns, kappa, stiffness, *refs):
    fields, outs, (high, low, diagonal) = refs[:count], refs[count:-3], refs[-3:]
    blocks = stiffness.shape[0]
    slots = columns.shape[0]
    lanes = fields[0].shape[2]
    diagonal[...] = jnp.transpose(kappa[...])
    for n, field in enumerate(fields):
        part = slice(n * lanes, (n + 1) * lanes)
        for b in range(blocks):
            high[b, :, part], low[b, :, part] = halves(field[b])
    for b in range(blocks):
        index = [columns[k, b] for k in range(slots)]
        highs = jnp.concatenate([high[i] for i in index], axis=0)
        lows = jnp.concatenate([low[i] for i in index], axis=0)
        left_high, left_low = halves(stiffness[b])
        near = jnp.dot(left_high, highs, preferred_element_type=F32)
        near += jnp.dot(left_low, highs, preferred_element_type=F32)
        near += jnp.dot(left_high, lows, preferred_element_type=F32)
        weight = 3.0 + diagonal[:, b : b + 1]
        for n, (field, out) in enumerate(zip(fields, outs)):
            out[b] = near[:, n * lanes : (n + 1) * lanes] + weight * field[b]


def near(columns, kappa, stiffness, fields):
    blocks, width, lanes = fields[0].shape
    return call(
        functools.partial(near_body, len(fields)),
        [struct(*field.shape) for field in fields],
        [columns],
        [kappa, stiffness, *fields],
        [
            pltpu.VMEM((blocks, width, lanes * len(fields)), BF16),
            pltpu.VMEM((blocks, width, lanes * len(fields)), BF16),
            pltpu.VMEM((width, blocks), F32),
        ],
    )


def early_products(stiffness, arrived, out):
    slots = arrived[0].shape[0]
    for n, e in enumerate(EARLY):
        for f in range(slots):
            out[n * slots + f] = far_product(stiffness, (e ^ 1) * slots + f, arrived[n][f])


def early_body(hours, hour, stiffness, *refs):
    count = len(EARLY)
    arrived, (out, *packs) = refs[:count], refs[count:]
    early_products(stiffness, arrived, out)
    pack_lanes(hours, hour[0], out, packs)


def gather_far(hours, faces, counts, hour, stiffness, own, packs, arrived, near_part, field):
    blocks = near_part.shape[0]
    slots = arrived[0].shape[0]
    for b in range(blocks):
        field[b] = near_part[b]
    for n, e in enumerate(EARLY):
        for f in range(slots):
            q = n * slots + f
            block = landing(faces, counts, e ^ 1, f, blocks)
            field[block] += merge_lanes(hours, hour[0], own[q], packs, q)
            block = landing(faces, counts, e, f, blocks)
            field[block] += far_product(stiffness, e * slots + f, arrived[n][f])


def middle_body(hours, faces, counts, hour, coupling, stiffness, near_part, own, *refs):
    count, turns = len(EARLY), hours - 1
    packs, arrived = refs[:turns], refs[turns : turns + count]
    first, image, *rest, field = refs[turns + count :]
    faces_out, image_packs, first_packs = (
        rest[:count],
        rest[count : count + turns],
        rest[count + turns :],
    )
    gather_far(hours, faces, counts, hour, stiffness, own, packs, arrived, near_part, field)
    for b in range(first.shape[0]):
        once = couple(hours, coupling[0], field[b])
        first[b] = once
        image[b] = couple(hours, coupling[0], once)
    pack_lanes(hours, hour[0], image, image_packs)
    pack_faces(faces, image, EARLY, faces_out)
    pack_lanes(hours, hour[0], first, first_packs)


def moments_body(hours, faces, counts, hour, right, first, second, own, out):
    slots = own.shape[0] // len(EARLY)
    sums = [jnp.zeros(right.shape[1:], F32) for _ in range(4)]
    for b in range(right.shape[0]):
        start, image = right[b], first[b]
        sums[0] += start * start
        sums[1] += start * image
        sums[2] += image * image
        sums[3] += image * second[b]
    for n, e in enumerate(EARLY):
        for f in range(slots):
            weight = jnp.where(f < counts[0, e ^ 1], 2.0, 0.0)
            sums[3] += weight * (first[faces[0, f, e ^ 1]] * own[n * slots + f])
    rows = jnp.concatenate([jnp.sum(s, axis=0, keepdims=True) for s in sums] * 2, axis=0)
    width = rows.shape[1] // hours
    rows = total([rows] + [pltpu.roll(rows, k * width, 1) for k in range(1, hours)])
    out[...] = jnp.where(group_of(rows.shape, hours) == hour[0], rows, 0.0)


def close_body(hours, parts, faces, counts, hour, stiffness, right, first, near_part, own, *refs):
    count, turns = len(EARLY), hours - 1
    sums, refs = refs[:parts], refs[parts:]
    first_packs, packs, arrived = refs[:turns], refs[turns : 2 * turns], refs[2 * turns :][:count]
    solution, residual, field = refs[2 * turns + count :]
    moment = total([s[...] for s in sums])
    m0, m1, m2, m3 = (moment[k : k + 1] for k in range(4))
    alpha = m0 / m1
    norm = alpha * alpha * m2 - m0
    lift = 1.0 + norm / m0
    step = norm / (lift * lift * m1 - 2.0 * lift * alpha * m2 + alpha * alpha * m3)
    on_right = alpha + step * lift
    on_first = step * alpha
    gather_far(hours, faces, counts, hour, stiffness, own, packs, arrived, near_part, field)
    for b in range(right.shape[0]):
        start = right[b]
        image = merge_lanes(hours, hour[0], first[b], first_packs, b)
        solution[b] = on_right * start - on_first * image
        residual[b] = start - on_right * image + on_first * field[b]


def shifted(value, axes, sizes, steps):
    route = []
    for source in range(functools.reduce(lambda a, b: a * b, sizes)):
        rest, target, scale = source, 0, 1
        for size, step in reversed(list(zip(sizes, steps))):
            rest, place = divmod(rest, size)
            target += (place + step) % size * scale
            scale *= size
        route.append((source, target))
    return lax.ppermute(value, axes, route)


def send_faces(outgoing, headings, offsets):
    count = lax.axis_size(SPACE)
    return [shifted(v, SPACE, (count,), (offsets[e],)) for v, e in zip(outgoing, headings)]


def send_lanes(packs):
    hours = lax.axis_size("tm")
    return [shifted(v, ("tm",), (hours,), (r + 1,)) for r, v in enumerate(packs)]


def everyone(value, axes):
    sizes = [lax.axis_size(axis) for axis in axes]
    size = functools.reduce(lambda a, b: a * b, sizes)
    if size > 4:
        return [lax.psum(value, axes)]
    steps = [[]]
    for n in sizes:
        steps = [s + [k] for s in steps for k in range(n)]
    return [value] + [shifted(value, axes, sizes, s) for s in steps[1:]]


def shards(
    right_side,
    kappa_sq,
    time_coupling,
    near_stiffness,
    far_stiffness,
    near_columns,
    face_blocks,
    face_counts,
):
    right = right_side.reshape(right_side.shape[1:])
    blocks, width, lanes = right.shape
    hours = lax.axis_size("tm")
    hour = lax.axis_index("tm").reshape(1)
    headings, slots = face_blocks.shape[1:]
    stride = lax.axis_size(SPACE) // 4 + 1
    offsets = (1, -1, 2, -2, stride, -stride)
    late = [e ^ 1 for e in EARLY]
    faces = jnp.swapaxes(face_blocks, 1, 2)
    columns = jnp.swapaxes(near_columns, 0, 1)
    counts = face_counts
    field = struct(*right.shape)
    face = [struct(slots, width, lanes)] * len(EARLY)
    pack = [struct(blocks // hours, width, lanes)] * (hours - 1)
    product = struct(len(EARLY) * slots, width, lanes)
    product_pack = [struct(product.shape[0] // hours, width, lanes)] * (hours - 1)
    spare = [pltpu.VMEM((blocks + 1, width, lanes), F32)]

    def body(function, *sizes):
        return functools.partial(function, hours, *sizes)

    def unpack(values, *sizes):
        values, result = list(values), []
        for n in sizes:
            result.append(values[:n])
            values = values[n:]
        return result

    outs = call(body(open_body), face + pack, [faces, hour], [right])
    outgoing, packs = unpack(outs, len(face), len(pack))
    packs = send_lanes(packs)
    early = send_faces(outgoing, EARLY, offsets)
    probe_right, *outgoing = call(
        body(turn_body), [field] + face, [faces, hour], [right, *packs]
    )
    arrived = send_faces(outgoing, late, offsets)
    stiffness = call(
        split_body, struct(headings * slots, width, 3 * width, dtype=BF16), [], [far_stiffness]
    )
    (near_part,) = near(columns, kappa_sq, near_stiffness, [probe_right])
    own, *packs = call(
        body(early_body), [product] + product_pack, [hour], [stiffness, *early]
    )
    packs = send_lanes(packs)
    outs = call(
        body(middle_body),
        [field, field] + face + pack + pack,
        [faces, counts, hour, time_coupling],
        [stiffness, near_part, own, *packs, *arrived],
        spare,
    )
    (first, image), outgoing, packs, first_packs = unpack(
        outs, 2, len(face), len(pack), len(pack)
    )

    packs = send_lanes(packs)
    early = send_faces(outgoing, EARLY, offsets)
    hour_image, *outgoing = call(body(turn_body), [field] + face, [faces, hour], [image, *packs])
    arrived = send_faces(outgoing, late, offsets)
    first_packs = send_lanes(first_packs)
    near_probe, near_hour = near(columns, kappa_sq, near_stiffness, [image, hour_image])
    own, *packs = call(
        body(early_body), [product] + product_pack, [hour], [stiffness, *early]
    )
    sums = call(
        body(moments_body),
        struct(8, lanes),
        [faces, counts, hour],
        [probe_right, first, near_probe, own],
    )
    sums = everyone(total(everyone(sums, ("tm", "rep"))), ("mesh",))
    packs = send_lanes(packs)
    solution_field, residual = call(
        body(close_body, len(sums)),
        [field, field],
        [faces, counts, hour],
        [stiffness, right, first, near_hour, own, *sums, *first_packs, *packs, *arrived],
        spare,
    )
    return (solution_field[None], residual[None])


def solution(mesh):
    placed = (
        P(("grp", "tm"), SPACE, None, None),
        P(("grp", "mesh", "rep"), None),
        P("grp"),
        P(SPACE, None, None),
        P(SPACE, None, None),
        P(SPACE, None),
        P(SPACE, None, None),
        P(SPACE, None),
    )
    return jax.shard_map(
        shards,
        mesh=mesh,
        in_specs=placed,
        out_specs=(
            P(("grp", "tm"), SPACE, None, None),
            P(("grp", "tm"), SPACE, None, None),
        ),
        check_vma=False,
    )
```

time: 75.3 us -> 75.2 us (level); the launches traced: 74.3 us -> 75 us
  starting transfers between devices: 20.4 us -> 24.5 us
  local copies, waits for them, and re-layouts: 5.57 us -> 2.74 us
    ppermute x20 -> x23, starting transfers between devices: 20.4 us -> 24.5 us  [shifted(): return lax.ppermute(value, axes, route)]
    unnamed x22 -> x18, local copies, waits for them, and re-layouts: 5.57 us -> 2.74 us
    pallas_call x7 -> x11, Pallas kernels: 12.6 us -> 12.2 us  [call(): pl.pallas_call(body, out_shape=outs, in_specs=[pl.BlockSpec(memory_space=...]
    ppermute x20 -> x23, waiting for transfers between devices: 34.4 us -> 34.1 us  [shifted(): return lax.ppermute(value, axes, route)]
  transfers between devices with their start and end apart: 20 -> 23, of which waited for: 10 -> 14; matrix products, arithmetic and copies ran while one was open for 0% -> 0% of each run, Pallas kernels for 10% -> 10%
where the time goes in v2:
time: 75.2 us; the launch traced here: 75 us
  waiting for transfers between devices  34.1 us (45%)
  starting transfers between devices  24.5 us (33%)
  Pallas kernels  12.2 us (16%)
  local copies, waits for them, and re-layouts  2.74 us (4%)
  between operations  1.48 us (2%)
    ppermute x23, waiting for transfers between devices, shifted(): return lax.ppermute(value, axes, route)  34.1 us
    ppermute x23, starting transfers between devices, shifted(): return lax.ppermute(value, axes, route)  24.5 us
    pallas_call x11, Pallas kernels, call(): pl.pallas_call(body, out_shape=outs, in_specs=[pl.BlockSpec(memory_space=...  12.2 us
    unnamed x18, local copies, waits for them, and re-layouts  2.74 us
  transfers between devices with their start and end apart: 23, of which 14 were waited for; matrix products, arithmetic and copies ran while one was open for 0% of the time, Pallas kernels for 10%

profile of v2, /device:TPU:0, one launch (start us, length us, event | category | flops | bytes accessed | tf_op | source)
XLA Modules:
  0.0 75.0 jit_solution(6378093915403889082)
XLA Ops:
  0.7 1.0 %copy-done.1 = f32[1,16,64,128]{3,2,1,0:T(8,128)S(1)} copy-done((f32[1,16,64,128]{3,2,1,0:T(8,128)S(1)}, f32[1,16,64,128]{3,2,1,0:T(8,128)}, u32[]{:S(2)}) %copy-start.1) | copy-done | bytes 524312
  1.7 0.7 copy-done.4
  2.4 0.8 %shard_map.96 = (f32[4,64,128]{2,1,0:T(8,128)S(1)}, f32[4,64,128]{2,1,0:T(8,128)S(1)}, f32[4,64,128]{2,1,0:T(8,128)S(1)}, f32[8,64,128]{2,1,0:T(8,128)S(1)}) custom-call(s32[1,4,6]{2,1,0:T(4,128)S(1)} %bitcast.9, s32[1]{0:T(128)} %bitcast.1.hour, f32[16,64,128]{2,1,0:T(8,128)S(1)} %bitcast.6), custom_call_target="tpu_custom_call" | custom-call | tf_op jit(solution)/shard_map/pallas_call | solution.py:22
  3.1 3.0 %collective-permute-start = (f32[8,64,128]{2,1,0:T(8,128)S(1)}, f32[8,64,128]{2,1,0:T(8,128)S(1)}, u32[]{:S(2)}, u32[]{:S(2)}) collective-permute-start(f32[8,64,128]{2,1,0:T(8,128)S(1)} %get-tuple-element.29), channel_id=1, source_target_pairs={{0,2},{2,0},{1,3},{3,1},{4,6},{6,4},{5,7},{7,5},{8,10},{10,8},{9,1... | collective-permute-start | bytes 786440 | tf_op jit(solution)/shard_map/ppermute | solution.py:257
  6.2 0.0 collective-permute-start.1
  6.2 1.6 %collective-permute-start.2 = (f32[4,64,128]{2,1,0:T(8,128)S(1)}, f32[4,64,128]{2,1,0:T(8,128)S(1)}, u32[]{:S(2)}, u32[]{:S(2)}) collective-permute-start(f32[4,64,128]{2,1,0:T(8,128)S(1)} %get-tuple-element.32), channel_id=1, source_target_pairs={{0,4},{1,5},{4,8},{5,9},{8,12},{9,13},{12,0},{13,1},{2,6},{3,7},{6... | collective-permute-start | bytes 393224 | tf_op jit(solution)/shard_map/ppermute | solution.py:257
  7.8 2.6 %collective-permute-start.3 = (f32[4,64,128]{2,1,0:T(8,128)S(1)}, f32[4,64,128]{2,1,0:T(8,128)S(1)}, u32[]{:S(2)}, u32[]{:S(2)}) collective-permute-start(f32[4,64,128]{2,1,0:T(8,128)S(1)} %get-tuple-element.33), channel_id=1, source_target_pairs={{0,5},{1,8},{4,9},{5,12},{8,13},{9,0},{12,1},{13,4},{2,7},{3,10},{... | collective-permute-start | bytes 393224 | tf_op jit(solution)/shard_map/ppermute | solution.py:257
  10.3 1.0 %copy-done.3 = f32[1,64,1536]{2,1,0:T(8,128)S(1)} copy-done((f32[1,64,1536]{2,1,0:T(8,128)S(1)}, f32[1,64,1536]{2,1,0:T(8,128)}, u32[]{:S(2)}) %copy-start.3) | copy-done | bytes 393240
  11.3 0.2 shard_map.95.stiffness
  11.5 1.8 %collective-permute-done.1.refs_0_ = f32[4,64,128]{2,1,0:T(8,128)S(1)} collective-permute-done((f32[4,64,128]{2,1,0:T(8,128)S(1)}, f32[4,64,128]{2,1,0:T(8,128)S(1)}, u32[]{:S(2)}, u32[]{:S(2)}) %collective-permute-start.1) | collective-permute-done | bytes 131104 | tf_op jit(solution)/shard_map/ppermute | solution.py:257
  13.3 1.1 %collective-permute-done.2.refs_1_ = f32[4,64,128]{2,1,0:T(8,128)S(1)} collective-permute-done((f32[4,64,128]{2,1,0:T(8,128)S(1)}, f32[4,64,128]{2,1,0:T(8,128)S(1)}, u32[]{:S(2)}, u32[]{:S(2)}) %collective-permute-start.2) | collective-permute-done | bytes 131104 | tf_op jit(solution)/shard_map/ppermute | solution.py:257
  14.4 5.0 %collective-permute-done.3.refs_2_ = f32[4,64,128]{2,1,0:T(8,128)S(1)} collective-permute-done((f32[4,64,128]{2,1,0:T(8,128)S(1)}, f32[4,64,128]{2,1,0:T(8,128)S(1)}, u32[]{:S(2)}, u32[]{:S(2)}) %collective-permute-start.3) | collective-permute-done | bytes 131104 | tf_op jit(solution)/shard_map/ppermute | solution.py:257
  19.4 0.4 shard_map.99
  19.8 0.0 copy-start.8
  19.8 0.1 collective-permute-start.4
  19.9 0.0 collective-permute-done.refs_0_
  19.9 0.8 %shard_map.97 = (f32[16,64,128]{2,1,0:T(8,128)S(1)}, f32[4,64,128]{2,1,0:T(8,128)S(1)}, f32[4,64,128]{2,1,0:T(8,128)S(1)}, f32[4,64,128]{2,1,0:T(8,128)S(1)}) custom-call(s32[1,4,6]{2,1,0:T(4,128)S(1)} %bitcast.10, s32[1]{0:T(128)} %bitcast.1.hour, f32[16,64,128]{2,1,0:T(8,128)S(1)} %bitcast.7, f32[8,64,128]{2,1,0:T(8,128)S(1)} %collective-permute-done.refs_0_), custom_call_target="tpu_custom_call" | custom-call | tf_op jit(solution)/shard_map/pallas_call | solution.py:22
  20.7 0.1 collective-permute-start.5
  20.8 2.2 %collective-permute-start.6 = (f32[4,64,128]{2,1,0:T(8,128)S(1)}, f32[4,64,128]{2,1,0:T(8,128)S(1)}, u32[]{:S(2)}, u32[]{:S(2)}) collective-permute-start(f32[4,64,128]{2,1,0:T(8,128)S(1)} %get-tuple-element.37), channel_id=1, source_target_pairs={{0,12},{1,13},{4,0},{5,1},{8,4},{9,5},{12,8},{13,9},{2,14},{3,15},... | collective-permute-start | bytes 393224 | tf_op jit(solution)/shard_map/ppermute | solution.py:257
  23.0 0.0 collective-permute-start.7
  23.7 0.0 copy-done
  23.7 0.0 copy-done.6
  23.7 0.0 copy-done.7
  23.7 1.6 %shard_map.98.near_part = f32[16,64,128]{2,1,0:T(8,128)S(1)} custom-call(s32[6,16]{1,0:T(8,128)S(1)} %bitcast.15, f32[16,64]{1,0:T(8,128)S(1)} %copy-done.6, f32[16,64,384]{2,1,0:T(8,128)S(1)} %copy-done, f32[16,64,128]{2,1,0:T(8,128)S(1)} %get-tuple-element.30.refs_0_.right), custom_call_target="tpu_custom_call" | custom-call | tf_op jit(solution)/shard_map/pallas_call | solution.py:22
  25.4 0.2 collective-permute-done.4.refs_0_
  25.5 0.0 collective-permute-done.5.refs_1_
  25.5 1.6 %collective-permute-done.6.refs_2_ = f32[4,64,128]{2,1,0:T(8,128)S(1)} collective-permute-done((f32[4,64,128]{2,1,0:T(8,128)S(1)}, f32[4,64,128]{2,1,0:T(8,128)S(1)}, u32[]{:S(2)}, u32[]{:S(2)}) %collective-permute-start.6) | collective-permute-done | bytes 131104 | tf_op jit(solution)/shard_map/ppermute | solution.py:257
  27.2 2.0 %collective-permute-done.7.refs_3_ = f32[4,64,128]{2,1,0:T(8,128)S(1)} collective-permute-done((f32[4,64,128]{2,1,0:T(8,128)S(1)}, f32[4,64,128]{2,1,0:T(8,128)S(1)}, u32[]{:S(2)}, u32[]{:S(2)}) %collective-permute-start.7) | collective-permute-done | bytes 131104 | tf_op jit(solution)/shard_map/ppermute | solution.py:257
  29.2 1.6 %shard_map.100 = (f32[16,64,128]{2,1,0:T(8,128)S(1)}, f32[16,64,128]{2,1,0:T(8,128)S(1)}, f32[4,64,128]{2,1,0:T(8,128)S(1)}, f32[4,64,128]{2,1,0:T(8,128)S(1)}, ...) custom-call(s32[1,4,6]{2,1,0:T(4,128)S(1)} %bitcast.11, s32[1,6]{1,0:T(1,128)S(1)} %copy-done.8, ...), custom_call_target="tpu_custom_call" | custom-call | tf_op jit(solution)/shard_map/pallas_call | solution.py:22
  30.8 2.3 %collective-permute-start.8 = (f32[8,64,128]{2,1,0:T(8,128)S(1)}, f32[8,64,128]{2,1,0:T(8,128)S(1)}, u32[]{:S(2)}, u32[]{:S(2)}) collective-permute-start(f32[8,64,128]{2,1,0:T(8,128)S(1)} %get-tuple-element.41), channel_id=1, source_target_pairs={{0,2},{2,0},{1,3},{3,1},{4,6},{6,4},{5,7},{7,5},{8,10},{10,8},{9,1... | collective-permute-start | bytes 786440 | tf_op jit(solution)/shard_map/ppermute | solution.py:257
  33.1 0.0 collective-permute-start.9
  33.1 2.3 %collective-permute-start.10 = (f32[4,64,128]{2,1,0:T(8,128)S(1)}, f32[4,64,128]{2,1,0:T(8,128)S(1)}, u32[]{:S(2)}, u32[]{:S(2)}) collective-permute-start(f32[4,64,128]{2,1,0:T(8,128)S(1)} %get-tuple-element.45), channel_id=1, source_target_pairs={{0,4},{1,5},{4,8},{5,9},{8,12},{9,13},{12,0},{13,1},{2,6},{3,7},{6... | collective-permute-start | bytes 393224 | tf_op jit(solution)/shard_map/ppermute | solution.py:257
  35.4 1.7 %collective-permute-start.11 = (f32[4,64,128]{2,1,0:T(8,128)S(1)}, f32[4,64,128]{2,1,0:T(8,128)S(1)}, u32[]{:S(2)}, u32[]{:S(2)}) collective-permute-start(f32[4,64,128]{2,1,0:T(8,128)S(1)} %get-tuple-element.46), channel_id=1, source_target_pairs={{0,5},{1,8},{4,9},{5,12},{8,13},{9,0},{12,1},{13,4},{2,7},{3,10},{... | collective-permute-start | bytes 393224 | tf_op jit(solution)/shard_map/ppermute | solution.py:257
  37.1 0.1 collective-permute-start.18
  37.2 3.6 %collective-permute-done.9.refs_0_ = f32[4,64,128]{2,1,0:T(8,128)S(1)} collective-permute-done((f32[4,64,128]{2,1,0:T(8,128)S(1)}, f32[4,64,128]{2,1,0:T(8,128)S(1)}, u32[]{:S(2)}, u32[]{:S(2)}) %collective-permute-start.9) | collective-permute-done | bytes 131104 | tf_op jit(solution)/shard_map/ppermute | solution.py:257
  40.8 1.3 %collective-permute-done.10.refs_1_ = f32[4,64,128]{2,1,0:T(8,128)S(1)} collective-permute-done((f32[4,64,128]{2,1,0:T(8,128)S(1)}, f32[4,64,128]{2,1,0:T(8,128)S(1)}, u32[]{:S(2)}, u32[]{:S(2)}) %collective-permute-start.10) | collective-permute-done | bytes 131104 | tf_op jit(solution)/shard_map/ppermute | solution.py:257
  42.1 4.9 %collective-permute-done.11.refs_2_ = f32[4,64,128]{2,1,0:T(8,128)S(1)} collective-permute-done((f32[4,64,128]{2,1,0:T(8,128)S(1)}, f32[4,64,128]{2,1,0:T(8,128)S(1)}, u32[]{:S(2)}, u32[]{:S(2)}) %collective-permute-start.11) | collective-permute-done | bytes 131104 | tf_op jit(solution)/shard_map/ppermute | solution.py:257
  47.0 0.4 shard_map.103
  47.4 0.0 collective-permute-done.8.refs_0_
  47.4 0.8 %shard_map.101 = (f32[16,64,128]{2,1,0:T(8,128)S(1)}, f32[4,64,128]{2,1,0:T(8,128)S(1)}, f32[4,64,128]{2,1,0:T(8,128)S(1)}, f32[4,64,128]{2,1,0:T(8,128)S(1)}) custom-call(s32[1,4,6]{2,1,0:T(4,128)S(1)} %bitcast.12, s32[1]{0:T(128)} %bitcast.1.hour, f32[16,64,128]{2,1,0:T(8,128)S(1)} %get-tuple-element.40.field.refs_0_, ...), custom_call_target="tpu_custom_call" | custom-call | tf_op jit(solution)/shard_map/pallas_call | solution.py:22
  48.2 2.7 %shard_map.102 = (f32[16,64,128]{2,1,0:T(8,128)S(1)}, f32[16,64,128]{2,1,0:T(8,128)S(1)}) custom-call(s32[6,16]{1,0:T(8,128)S(1)} %bitcast.16, f32[16,64]{1,0:T(8,128)S(1)} %copy-done.6, f32[16,64,384]{2,1,0:T(8,128)S(1)} %copy-done, f32[16,64,128]{2,1,0:T(8,128)S(1)} %get-tuple-element.40.field.refs_0_, f32[16,64,128]{2,1,0:T(8,128)S(1)} %get-tuple-element.42.refs_1_), custom_call_target="tpu_custom_call" | custom-call | tf_op jit(solution)/shard_map/pallas_call | solution.py:22
  50.9 0.8 %shard_map.104 = f32[8,128]{1,0:T(8,128)S(1)} custom-call(s32[1,4,6]{2,1,0:T(4,128)S(1)} %bitcast.13, s32[1,6]{1,0:T(1,128)S(1)} %copy-done.8, s32[1]{0:T(128)} %bitcast.1.hour, f32[16,64,128]{2,1,0:T(8,128)S(1)} %get-tuple-element.30.refs_0_.right, f32[16,64,128]{2,1,0:T(8,128)S(1)} %get-tuple-element.39.first, ...), custom_call_target="tpu_custom_call" | custom-call | tf_op jit(solution)/shard_map/pallas_call | solution.py:22
  51.7 0.0 collective-permute-start.14
  51.8 0.4 collective-permute-start.13
  52.2 1.4 %collective-permute-start.12 = (f32[8,128]{1,0:T(8,128)S(1)}, f32[8,128]{1,0:T(8,128)S(1)}, u32[]{:S(2)}, u32[]{:S(2)}) collective-permute-start(f32[8,128]{1,0:T(8,128)S(1)} %shard_map.104), channel_id=1, source_target_pairs={{0,1},{1,0},{2,3},{3,2},{4,5},{5,4},{6,7},{7,6},{8,9},{9,8},{10,11... | collective-permute-start | bytes 12296 | tf_op jit(solution)/shard_map/ppermute | solution.py:257
  53.6 0.3 collective-permute-start.19
  54.0 0.8 %collective-permute-done.14 = f32[8,128]{1,0:T(8,128)S(1)} collective-permute-done((f32[8,128]{1,0:T(8,128)S(1)}, f32[8,128]{1,0:T(8,128)S(1)}, u32[]{:S(2)}, u32[]{:S(2)}) %collective-permute-start.14) | collective-permute-done | bytes 4128 | tf_op jit(solution)/shard_map/ppermute | solution.py:257
  54.8 0.0 collective-permute-start.20
  54.8 0.7 collective-permute-done.13
  55.5 0.1 collective-permute-start.21
  55.5 0.0 collective-permute-done.12
  55.5 0.0 collective-permute-start.22
  55.5 0.0 collective-permute-done.18.refs_4_
  55.5 2.0 %collective-permute-start.15 = (f32[8,128]{1,0:T(8,128)S(1)}, f32[8,128]{1,0:T(8,128)S(1)}, u32[]{:S(2)}, u32[]{:S(2)}) collective-permute-start(f32[8,128]{1,0:T(8,128)S(1)} %add_add_fusion.refs_0_), channel_id=1, source_target_pairs={{0,4},{4,8},{8,12},{12,0},{1,5},{5,9},{9,13},{13,1},{2,6},{6,10},{... | collective-permute-start | bytes 12296 | tf_op jit(solution)/shard_map/ppermute | solution.py:257
  57.6 6.4 %collective-permute-done.15.refs_1_ = f32[8,128]{1,0:T(8,128)S(1)} collective-permute-done((f32[8,128]{1,0:T(8,128)S(1)}, f32[8,128]{1,0:T(8,128)S(1)}, u32[]{:S(2)}, u32[]{:S(2)}) %collective-permute-start.15) | collective-permute-done | bytes 4128 | tf_op jit(solution)/shard_map/ppermute | solution.py:257
  63.9 3.7 %collective-permute-start.16 = (f32[8,128]{1,0:T(8,128)S(1)}, f32[8,128]{1,0:T(8,128)S(1)}, u32[]{:S(2)}, u32[]{:S(2)}) collective-permute-start(f32[8,128]{1,0:T(8,128)S(1)} %add_add_fusion.refs_0_), channel_id=1, source_target_pairs={{0,8},{4,12},{8,0},{12,4},{1,9},{5,13},{9,1},{13,5},{2,10},{6,14},... | collective-permute-start | bytes 12296 | tf_op jit(solution)/shard_map/ppermute | solution.py:257
  67.7 1.6 %collective-permute-done.16.refs_2_ = f32[8,128]{1,0:T(8,128)S(1)} collective-permute-done((f32[8,128]{1,0:T(8,128)S(1)}, f32[8,128]{1,0:T(8,128)S(1)}, u32[]{:S(2)}, u32[]{:S(2)}) %collective-permute-start.16) | collective-permute-done | bytes 4128 | tf_op jit(solution)/shard_map/ppermute | solution.py:257
  69.2 0.4 collective-permute-start.17
  69.7 3.2 %collective-permute-done.17.refs_3_ = f32[8,128]{1,0:T(8,128)S(1)} collective-permute-done((f32[8,128]{1,0:T(8,128)S(1)}, f32[8,128]{1,0:T(8,128)S(1)}, u32[]{:S(2)}, u32[]{:S(2)}) %collective-permute-start.17) | collective-permute-done | bytes 4128 | tf_op jit(solution)/shard_map/ppermute | solution.py:257
  72.9 0.0 collective-permute-done.19.refs_5_
  72.9 0.0 collective-permute-done.20.refs_6_
  72.9 0.0 collective-permute-done.21.refs_7_
  72.9 0.0 collective-permute-done.22.refs_8_
  72.9 2.1 %shard_map.105 = (f32[16,64,128]{2,1,0:T(8,128)}, f32[16,64,128]{2,1,0:T(8,128)}) custom-call(s32[1,4,6]{2,1,0:T(4,128)S(1)} %bitcast.14, s32[1,6]{1,0:T(1,128)S(1)} %copy-done.8, s32[1]{0:T(128)} %bitcast.1.hour, bf16[24,64,192]{2,1,0:T(8,128)(2,1)S(1)} %shard_map.95.stiffness, f32[16,64,128]{2,1,0:T(8,128)S(1)} %bitcast.8, ...), custom_call_target="tpu_custom_call" | custom-call | tf_op jit(solution)/shard_map/pallas_call | solution.py:22
  (12 shorter events, 0.0 us)
Async XLA Ops:
  0.6 19.3 %copy-start.5 = (s32[1,6,4]{1,2,0:T(4,128)S(1)}, s32[1,6,4]{1,2,0:T(4,128)}, u32[]{:S(2)}) copy-start(s32[1,6,4]{1,2,0:T(4,128)} %param.14) | copy-start | bytes 292
  0.6 1.0 %copy-start.1 = (f32[1,16,64,128]{3,2,1,0:T(8,128)S(1)}, f32[1,16,64,128]{3,2,1,0:T(8,128)}, u32[]{:S(2)}) copy-start(f32[1,16,64,128]{3,2,1,0:T(8,128)} %param.8) | copy-start | bytes 1572868
  1.7 0.7 copy-start.4
  2.4 17.6 %copy-start.2 = (f32[1,16,64,128]{3,2,1,0:T(8,128)S(1)}, f32[1,16,64,128]{3,2,1,0:T(8,128)}, u32[]{:S(2)}) copy-start(f32[1,16,64,128]{3,2,1,0:T(8,128)} %param.8) | copy-start | bytes 1572868
  3.1 16.8 %collective-permute-start = (f32[8,64,128]{2,1,0:T(8,128)S(1)}, f32[8,64,128]{2,1,0:T(8,128)S(1)}, u32[]{:S(2)}, u32[]{:S(2)}) collective-permute-start(f32[8,64,128]{2,1,0:T(8,128)S(1)} %get-tuple-element.29), channel_id=1, source_target_pairs={{0,2},{2,0},{1,3},{3,1},{4,6},{6,4},{5,7},{7,5},{8,10},{10,8},{9,1... | collective-permute-start | bytes 786440 | tf_op jit(solution)/shard_map/ppermute | solution.py:257
  6.2 7.1 %collective-permute-start.1 = (f32[4,64,128]{2,1,0:T(8,128)S(1)}, f32[4,64,128]{2,1,0:T(8,128)S(1)}, u32[]{:S(2)}, u32[]{:S(2)}) collective-permute-start(f32[4,64,128]{2,1,0:T(8,128)S(1)} %get-tuple-element.31), channel_id=1, source_target_pairs={{0,1},{1,4},{4,5},{5,8},{8,9},{9,12},{12,13},{13,0},{2,3},{3,6},{6... | collective-permute-start | bytes 393224 | tf_op jit(solution)/shard_map/ppermute | solution.py:257
  6.2 8.2 %collective-permute-start.2 = (f32[4,64,128]{2,1,0:T(8,128)S(1)}, f32[4,64,128]{2,1,0:T(8,128)S(1)}, u32[]{:S(2)}, u32[]{:S(2)}) collective-permute-start(f32[4,64,128]{2,1,0:T(8,128)S(1)} %get-tuple-element.32), channel_id=1, source_target_pairs={{0,4},{1,5},{4,8},{5,9},{8,12},{9,13},{12,0},{13,1},{2,6},{3,7},{6... | collective-permute-start | bytes 393224 | tf_op jit(solution)/shard_map/ppermute | solution.py:257
  7.8 15.9 %copy-start = (f32[16,64,384]{2,1,0:T(8,128)S(1)}, f32[16,64,384]{2,1,0:T(8,128)}, u32[]{:S(2)}) copy-start(f32[16,64,384]{2,1,0:T(8,128)} %stiffness.5) | copy-start | bytes 4718596
  7.8 11.6 %collective-permute-start.3 = (f32[4,64,128]{2,1,0:T(8,128)S(1)}, f32[4,64,128]{2,1,0:T(8,128)S(1)}, u32[]{:S(2)}, u32[]{:S(2)}) collective-permute-start(f32[4,64,128]{2,1,0:T(8,128)S(1)} %get-tuple-element.33), channel_id=1, source_target_pairs={{0,5},{1,8},{4,9},{5,12},{8,13},{9,0},{12,1},{13,4},{2,7},{3,10},{... | collective-permute-start | bytes 393224 | tf_op jit(solution)/shard_map/ppermute | solution.py:257
  10.3 1.0 %copy-start.3 = (f32[1,64,1536]{2,1,0:T(8,128)S(1)}, f32[1,64,1536]{2,1,0:T(8,128)}, u32[]{:S(2)}) copy-start(f32[1,64,1536]{2,1,0:T(8,128)} %stiffness.3) | copy-start | bytes 1179652
  11.3 12.4 %copy-start.6 = (f32[16,64]{1,0:T(8,128)S(1)}, f32[16,64]{1,0:T(8,128)}, u32[]{:S(2)}) copy-start(f32[16,64]{1,0:T(8,128)} %kappa.3) | copy-start | bytes 12292
  11.3 12.4 %copy-start.7 = (s32[16,6]{0,1:T(8,128)S(1)}, s32[16,6]{0,1:T(8,128)}, u32[]{:S(2)}) copy-start(s32[16,6]{0,1:T(8,128)} %param.13) | copy-start | bytes 1156
  19.8 9.4 %copy-start.8 = (s32[1,6]{1,0:T(1,128)S(1)}, s32[1,6]{1,0:T(1,128)}, u32[]{:S(2)}) copy-start(s32[1,6]{1,0:T(1,128)} %counts.5) | copy-start | bytes 76
  19.8 5.7 %collective-permute-start.4 = (f32[6,64,128]{2,1,0:T(8,128)S(1)}, f32[6,64,128]{2,1,0:T(8,128)S(1)}, u32[]{:S(2)}, u32[]{:S(2)}) collective-permute-start(f32[6,64,128]{2,1,0:T(8,128)S(1)} %get-tuple-element.35), channel_id=1, source_target_pairs={{0,2},{2,0},{1,3},{3,1},{4,6},{6,4},{5,7},{7,5},{8,10},{10,8},{9,1... | collective-permute-start | bytes 589832 | tf_op jit(solution)/shard_map/ppermute | solution.py:257
  20.7 4.8 %collective-permute-start.5 = (f32[4,64,128]{2,1,0:T(8,128)S(1)}, f32[4,64,128]{2,1,0:T(8,128)S(1)}, u32[]{:S(2)}, u32[]{:S(2)}) collective-permute-start(f32[4,64,128]{2,1,0:T(8,128)S(1)} %get-tuple-element.36), channel_id=1, source_target_pairs={{0,13},{1,0},{4,1},{5,4},{8,5},{9,8},{12,9},{13,12},{2,15},{3,2},{... | collective-permute-start | bytes 393224 | tf_op jit(solution)/shard_map/ppermute | solution.py:257
  20.8 6.3 %collective-permute-start.6 = (f32[4,64,128]{2,1,0:T(8,128)S(1)}, f32[4,64,128]{2,1,0:T(8,128)S(1)}, u32[]{:S(2)}, u32[]{:S(2)}) collective-permute-start(f32[4,64,128]{2,1,0:T(8,128)S(1)} %get-tuple-element.37), channel_id=1, source_target_pairs={{0,12},{1,13},{4,0},{5,1},{8,4},{9,5},{12,8},{13,9},{2,14},{3,15},... | collective-permute-start | bytes 393224 | tf_op jit(solution)/shard_map/ppermute | solution.py:257
  23.0 6.2 %collective-permute-start.7 = (f32[4,64,128]{2,1,0:T(8,128)S(1)}, f32[4,64,128]{2,1,0:T(8,128)S(1)}, u32[]{:S(2)}, u32[]{:S(2)}) collective-permute-start(f32[4,64,128]{2,1,0:T(8,128)S(1)} %get-tuple-element.38), channel_id=1, source_target_pairs={{0,9},{1,12},{4,13},{5,0},{8,1},{9,4},{12,5},{13,8},{2,11},{3,14},... | collective-permute-start | bytes 393224 | tf_op jit(solution)/shard_map/ppermute | solution.py:257
  30.8 16.7 %collective-permute-start.8 = (f32[8,64,128]{2,1,0:T(8,128)S(1)}, f32[8,64,128]{2,1,0:T(8,128)S(1)}, u32[]{:S(2)}, u32[]{:S(2)}) collective-permute-start(f32[8,64,128]{2,1,0:T(8,128)S(1)} %get-tuple-element.41), channel_id=1, source_target_pairs={{0,2},{2,0},{1,3},{3,1},{4,6},{6,4},{5,7},{7,5},{8,10},{10,8},{9,1... | collective-permute-start | bytes 786440 | tf_op jit(solution)/shard_map/ppermute | solution.py:257
  33.1 7.7 %collective-permute-start.9 = (f32[4,64,128]{2,1,0:T(8,128)S(1)}, f32[4,64,128]{2,1,0:T(8,128)S(1)}, u32[]{:S(2)}, u32[]{:S(2)}) collective-permute-start(f32[4,64,128]{2,1,0:T(8,128)S(1)} %get-tuple-element.44), channel_id=1, source_target_pairs={{0,1},{1,4},{4,5},{5,8},{8,9},{9,12},{12,13},{13,0},{2,3},{3,6},{6... | collective-permute-start | bytes 393224 | tf_op jit(solution)/shard_map/ppermute | solution.py:257
  33.1 9.0 %collective-permute-start.10 = (f32[4,64,128]{2,1,0:T(8,128)S(1)}, f32[4,64,128]{2,1,0:T(8,128)S(1)}, u32[]{:S(2)}, u32[]{:S(2)}) collective-permute-start(f32[4,64,128]{2,1,0:T(8,128)S(1)} %get-tuple-element.45), channel_id=1, source_target_pairs={{0,4},{1,5},{4,8},{5,9},{8,12},{9,13},{12,0},{13,1},{2,6},{3,7},{6... | collective-permute-start | bytes 393224 | tf_op jit(solution)/shard_map/ppermute | solution.py:257
  35.4 11.6 %collective-permute-start.11 = (f32[4,64,128]{2,1,0:T(8,128)S(1)}, f32[4,64,128]{2,1,0:T(8,128)S(1)}, u32[]{:S(2)}, u32[]{:S(2)}) collective-permute-start(f32[4,64,128]{2,1,0:T(8,128)S(1)} %get-tuple-element.46), channel_id=1, source_target_pairs={{0,5},{1,8},{4,9},{5,12},{8,13},{9,0},{12,1},{13,4},{2,7},{3,10},{... | collective-permute-start | bytes 393224 | tf_op jit(solution)/shard_map/ppermute | solution.py:257
  37.1 18.4 %collective-permute-start.18 = (f32[8,64,128]{2,1,0:T(8,128)S(1)}, f32[8,64,128]{2,1,0:T(8,128)S(1)}, u32[]{:S(2)}, u32[]{:S(2)}) collective-permute-start(f32[8,64,128]{2,1,0:T(8,128)S(1)} %get-tuple-element.49), channel_id=1, source_target_pairs={{0,2},{2,0},{1,3},{3,1},{4,6},{6,4},{5,7},{7,5},{8,10},{10,8},{9,1... | collective-permute-start | bytes 786440 | tf_op jit(solution)/shard_map/ppermute | solution.py:257
  51.7 3.0 %collective-permute-start.14 = (f32[8,128]{1,0:T(8,128)S(1)}, f32[8,128]{1,0:T(8,128)S(1)}, u32[]{:S(2)}, u32[]{:S(2)}) collective-permute-start(f32[8,128]{1,0:T(8,128)S(1)} %shard_map.104), channel_id=1, source_target_pairs={{0,3},{1,2},{2,1},{3,0},{4,7},{5,6},{6,5},{7,4},{8,11},{9,10},{10,... | collective-permute-start | bytes 12296 | tf_op jit(solution)/shard_map/ppermute | solution.py:257
  51.8 3.7 %collective-permute-start.13 = (f32[8,128]{1,0:T(8,128)S(1)}, f32[8,128]{1,0:T(8,128)S(1)}, u32[]{:S(2)}, u32[]{:S(2)}) collective-permute-start(f32[8,128]{1,0:T(8,128)S(1)} %shard_map.104), channel_id=1, source_target_pairs={{0,2},{1,3},{2,0},{3,1},{4,6},{5,7},{6,4},{7,5},{8,10},{9,11},{10,... | collective-permute-start | bytes 12296 | tf_op jit(solution)/shard_map/ppermute | solution.py:257
  52.2 3.3 %collective-permute-start.12 = (f32[8,128]{1,0:T(8,128)S(1)}, f32[8,128]{1,0:T(8,128)S(1)}, u32[]{:S(2)}, u32[]{:S(2)}) collective-permute-start(f32[8,128]{1,0:T(8,128)S(1)} %shard_map.104), channel_id=1, source_target_pairs={{0,1},{1,0},{2,3},{3,2},{4,5},{5,4},{6,7},{7,6},{8,9},{9,8},{10,11... | collective-permute-start | bytes 12296 | tf_op jit(solution)/shard_map/ppermute | solution.py:257
  53.6 19.2 %collective-permute-start.19 = (f32[6,64,128]{2,1,0:T(8,128)S(1)}, f32[6,64,128]{2,1,0:T(8,128)S(1)}, u32[]{:S(2)}, u32[]{:S(2)}) collective-permute-start(f32[6,64,128]{2,1,0:T(8,128)S(1)} %get-tuple-element.50), channel_id=1, source_target_pairs={{0,2},{2,0},{1,3},{3,1},{4,6},{6,4},{5,7},{7,5},{8,10},{10,8},{9,1... | collective-permute-start | bytes 589832 | tf_op jit(solution)/shard_map/ppermute | solution.py:257
  54.8 18.1 %collective-permute-start.20 = (f32[4,64,128]{2,1,0:T(8,128)S(1)}, f32[4,64,128]{2,1,0:T(8,128)S(1)}, u32[]{:S(2)}, u32[]{:S(2)}) collective-permute-start(f32[4,64,128]{2,1,0:T(8,128)S(1)} %get-tuple-element.51), channel_id=1, source_target_pairs={{0,13},{1,0},{4,1},{5,4},{8,5},{9,8},{12,9},{13,12},{2,15},{3,2},{... | collective-permute-start | bytes 393224 | tf_op jit(solution)/shard_map/ppermute | solution.py:257
  55.5 17.4 %collective-permute-start.21 = (f32[4,64,128]{2,1,0:T(8,128)S(1)}, f32[4,64,128]{2,1,0:T(8,128)S(1)}, u32[]{:S(2)}, u32[]{:S(2)}) collective-permute-start(f32[4,64,128]{2,1,0:T(8,128)S(1)} %get-tuple-element.52), channel_id=1, source_target_pairs={{0,12},{1,13},{4,0},{5,1},{8,4},{9,5},{12,8},{13,9},{2,14},{3,15},... | collective-permute-start | bytes 393224 | tf_op jit(solution)/shard_map/ppermute | solution.py:257
  55.5 17.4 %collective-permute-start.22 = (f32[4,64,128]{2,1,0:T(8,128)S(1)}, f32[4,64,128]{2,1,0:T(8,128)S(1)}, u32[]{:S(2)}, u32[]{:S(2)}) collective-permute-start(f32[4,64,128]{2,1,0:T(8,128)S(1)} %get-tuple-element.53), channel_id=1, source_target_pairs={{0,9},{1,12},{4,13},{5,0},{8,1},{9,4},{12,5},{13,8},{2,11},{3,14},... | collective-permute-start | bytes 393224 | tf_op jit(solution)/shard_map/ppermute | solution.py:257
  55.5 8.4 %collective-permute-start.15 = (f32[8,128]{1,0:T(8,128)S(1)}, f32[8,128]{1,0:T(8,128)S(1)}, u32[]{:S(2)}, u32[]{:S(2)}) collective-permute-start(f32[8,128]{1,0:T(8,128)S(1)} %add_add_fusion.refs_0_), channel_id=1, source_target_pairs={{0,4},{4,8},{8,12},{12,0},{1,5},{5,9},{9,13},{13,1},{2,6},{6,10},{... | collective-permute-start | bytes 12296 | tf_op jit(solution)/shard_map/ppermute | solution.py:257
  63.9 5.3 %collective-permute-start.16 = (f32[8,128]{1,0:T(8,128)S(1)}, f32[8,128]{1,0:T(8,128)S(1)}, u32[]{:S(2)}, u32[]{:S(2)}) collective-permute-start(f32[8,128]{1,0:T(8,128)S(1)} %add_add_fusion.refs_0_), channel_id=1, source_target_pairs={{0,8},{4,12},{8,0},{12,4},{1,9},{5,13},{9,1},{13,5},{2,10},{6,14},... | collective-permute-start | bytes 12296 | tf_op jit(solution)/shard_map/ppermute | solution.py:257
  69.2 3.6 %collective-permute-start.17 = (f32[8,128]{1,0:T(8,128)S(1)}, f32[8,128]{1,0:T(8,128)S(1)}, u32[]{:S(2)}, u32[]{:S(2)}) collective-permute-start(f32[8,128]{1,0:T(8,128)S(1)} %add_add_fusion.refs_0_), channel_id=1, source_target_pairs={{0,12},{4,0},{8,4},{12,8},{1,13},{5,1},{9,5},{13,9},{2,14},{6,2},{... | collective-permute-start | bytes 12296 | tf_op jit(solution)/shard_map/ppermute | solution.py:257

commit v3 on v2

--- a/solution.py
+++ b/solution.py
@@ -10,7 +10,7 @@
 SPACE = ("mesh", "rep")
 F32 = jnp.float32
 BF16 = jnp.bfloat16
-EARLY = (0, 2, 4)
+PLUS = 3
 
 
 def struct(*shape, dtype=F32):
@@ -85,9 +85,10 @@
 
 
 def pack_faces(faces, field, headings, outs):
-    for e, out in zip(headings, outs):
-        for f in range(out.shape[0]):
-            out[f] = field[faces[0, f, e]]
+    slots = faces.shape[1]
+    places = [out.at[k] for out in outs for k in range(out.shape[0])]
+    for m, place in enumerate(places):
+        place[...] = field[faces[0, m % slots, headings[m // slots]]]
 
 
 def far_product(stiffness, q, block):
@@ -100,17 +101,21 @@
     return jnp.where(f < counts[0, e], faces[0, f, e], spare)
 
 
-def open_body(hours, faces, hour, field, *outs):
-    split = len(EARLY)
-    pack_faces(faces, field, EARLY, outs[:split])
-    pack_lanes(hours, hour[0], field, outs[split:])
-
-
-def turn_body(hours, faces, hour, field, *refs):
-    packs, out, faces_out = refs[: hours - 1], refs[hours - 1], refs[hours:]
+def open_body(hours, faces, plan, hour, field, *outs):
+    pack_lanes(hours, hour[0], field, outs[: hours - 1])
+    pack_faces(faces, field, [plan[n] for n in range(PLUS)], outs[hours - 1 :])
+
+
+def turn_body(hours, extra, faces, plan, hour, field, _, *refs):
+    packs, refs = refs[: hours - 1], refs[hours - 1 :]
+    (out, *faces_out), others = refs[extra:], []
+    if extra:
+        others, faces_out = faces_out[: hours - 1], faces_out[hours - 1 :]
     for b in range(field.shape[0]):
         out[b] = merge_lanes(hours, hour[0], field[b], packs, b)
-    pack_faces(faces, out, [e ^ 1 for e in EARLY], faces_out)
+    pack_faces(faces, out, [plan[PLUS + n] ^ 1 for n in range(PLUS)], faces_out)
+    if extra:
+        pack_lanes(hours, hour[0], refs[0], others)
 
 
 def split_body(stiffness, out):
@@ -158,55 +163,47 @@
     )
 
 
-def early_products(stiffness, arrived, out):
-    slots = arrived[0].shape[0]
-    for n, e in enumerate(EARLY):
+def early_body(hours, plan, hour, stiffness, *refs):
+    arrived, (out, *packs) = refs[:PLUS], refs[PLUS + 2 :]
+    slots = out.shape[0] // PLUS
+    for n in range(PLUS):
         for f in range(slots):
-            out[n * slots + f] = far_product(stiffness, (e ^ 1) * slots + f, arrived[n][f])
-
-
-def early_body(hours, hour, stiffness, *refs):
-    count = len(EARLY)
-    arrived, (out, *packs) = refs[:count], refs[count:]
-    early_products(stiffness, arrived, out)
+            q = (plan[PLUS + n] ^ 1) * slots + f
+            out[n * slots + f] = far_product(stiffness, q, arrived[n][f])
     pack_lanes(hours, hour[0], out, packs)
 
 
-def gather_far(hours, faces, counts, hour, stiffness, own, packs, arrived, near_part, field):
+def gather_far(hours, faces, counts, plan, hour, stiffness, own, packs, arrived, near_part, field):
     blocks = near_part.shape[0]
-    slots = arrived[0].shape[0]
+    slots = own.shape[0] // PLUS
     for b in range(blocks):
         field[b] = near_part[b]
-    for n, e in enumerate(EARLY):
+    for n in range(PLUS):
+        e = plan[n]
         for f in range(slots):
             q = n * slots + f
-            block = landing(faces, counts, e ^ 1, f, blocks)
+            block = landing(faces, counts, plan[PLUS + n] ^ 1, f, blocks)
             field[block] += merge_lanes(hours, hour[0], own[q], packs, q)
             block = landing(faces, counts, e, f, blocks)
             field[block] += far_product(stiffness, e * slots + f, arrived[n][f])
 
 
-def middle_body(hours, faces, counts, hour, coupling, stiffness, near_part, own, *refs):
-    count, turns = len(EARLY), hours - 1
-    packs, arrived = refs[:turns], refs[turns : turns + count]
-    first, image, *rest, field = refs[turns + count :]
-    faces_out, image_packs, first_packs = (
-        rest[:count],
-        rest[count : count + turns],
-        rest[count + turns :],
-    )
-    gather_far(hours, faces, counts, hour, stiffness, own, packs, arrived, near_part, field)
+def middle_body(hours, faces, counts, plan, hour, coupling, stiffness, near_part, own, *refs):
+    turns = hours - 1
+    packs, arrived = refs[:turns], refs[turns : turns + PLUS]
+    first, image, *rest, field = refs[turns + PLUS :]
+    image_packs, faces_out = rest[:turns], rest[turns:]
+    gather_far(hours, faces, counts, plan, hour, stiffness, own, packs, arrived, near_part, field)
     for b in range(first.shape[0]):
         once = couple(hours, coupling[0], field[b])
         first[b] = once
         image[b] = couple(hours, coupling[0], once)
     pack_lanes(hours, hour[0], image, image_packs)
-    pack_faces(faces, image, EARLY, faces_out)
-    pack_lanes(hours, hour[0], first, first_packs)
-
-
-def moments_body(hours, faces, counts, hour, right, first, second, own, out):
-    slots = own.shape[0] // len(EARLY)
+    pack_faces(faces, image, [plan[n] for n in range(PLUS)], faces_out)
+
+
+def moments_body(hours, faces, counts, plan, hour, right, first, second, own, out):
+    slots = own.shape[0] // PLUS
     sums = [jnp.zeros(right.shape[1:], F32) for _ in range(4)]
     for b in range(right.shape[0]):
         start, image = right[b], first[b]
@@ -214,21 +211,24 @@
         sums[1] += start * image
         sums[2] += image * image
         sums[3] += image * second[b]
-    for n, e in enumerate(EARLY):
+    for n in range(PLUS):
+        e = plan[PLUS + n] ^ 1
         for f in range(slots):
-            weight = jnp.where(f < counts[0, e ^ 1], 2.0, 0.0)
-            sums[3] += weight * (first[faces[0, f, e ^ 1]] * own[n * slots + f])
+            weight = jnp.where(f < counts[0, e], 2.0, 0.0)
+            sums[3] += weight * (first[faces[0, f, e]] * own[n * slots + f])
     rows = jnp.concatenate([jnp.sum(s, axis=0, keepdims=True) for s in sums] * 2, axis=0)
     width = rows.shape[1] // hours
     rows = total([rows] + [pltpu.roll(rows, k * width, 1) for k in range(1, hours)])
     out[...] = jnp.where(group_of(rows.shape, hours) == hour[0], rows, 0.0)
 
 
-def close_body(hours, parts, faces, counts, hour, stiffness, right, first, near_part, own, *refs):
-    count, turns = len(EARLY), hours - 1
+def close_body(
+    hours, parts, faces, counts, plan, hour, stiffness, right, first, near_part, own, *refs
+):
+    turns = hours - 1
     sums, refs = refs[:parts], refs[parts:]
-    first_packs, packs, arrived = refs[:turns], refs[turns : 2 * turns], refs[2 * turns :][:count]
-    solution, residual, field = refs[2 * turns + count :]
+    first_packs, packs, arrived = refs[:turns], refs[turns : 2 * turns], refs[2 * turns :][:PLUS]
+    solution, residual, field = refs[2 * turns + PLUS :]
     moment = total([s[...] for s in sums])
     m0, m1, m2, m3 = (moment[k : k + 1] for k in range(4))
     alpha = m0 / m1
@@ -237,7 +237,7 @@
     step = norm / (lift * lift * m1 - 2.0 * lift * alpha * m2 + alpha * alpha * m3)
     on_right = alpha + step * lift
     on_first = step * alpha
-    gather_far(hours, faces, counts, hour, stiffness, own, packs, arrived, near_part, field)
+    gather_far(hours, faces, counts, plan, hour, stiffness, own, packs, arrived, near_part, field)
     for b in range(right.shape[0]):
         start = right[b]
         image = merge_lanes(hours, hour[0], first[b], first_packs, b)
@@ -257,9 +257,33 @@
     return lax.ppermute(value, axes, route)
 
 
-def send_faces(outgoing, headings, offsets):
-    count = lax.axis_size(SPACE)
-    return [shifted(v, SPACE, (count,), (offsets[e],)) for v, e in zip(outgoing, headings)]
+def paired(stride):
+    return stride == 3 and lax.axis_size("rep") == 2
+
+
+def face_plan(stride):
+    if not paired(stride):
+        return jnp.array([2, 0, 4, 2, 0, 4], jnp.int32)
+    odd = lax.axis_index("rep") == 1
+    near, long = jnp.where(odd, 0, 4), jnp.where(odd, 4, 0)
+    two = jnp.int32(2)
+    return jnp.stack([two, near, long, two, long, near]).astype(jnp.int32)
+
+
+def send_faces(outgoing, stride, sign):
+    mesh, rep = (lax.axis_size(axis) for axis in SPACE)
+    count = mesh * rep
+    if not paired(stride):
+        return [
+            shifted(v, SPACE, (count,), (sign * d,)) for v, d in zip(outgoing, (2, 1, stride))
+        ]
+    both, single = outgoing
+    slots = both.shape[0] // 2
+    hop = (1, 3) if sign > 0 else (-3, -1)
+    both = shifted(both, ("mesh",), (mesh,), (sign,))
+    single = lax.ppermute(single, SPACE, [(i, (i + hop[i % 2]) % count) for i in range(count)])
+    relayed = shifted(both[slots:], ("rep",), (rep,), (1,))
+    return [both, relayed, single]
 
 
 def send_lanes(packs):
@@ -294,68 +318,62 @@
     hour = lax.axis_index("tm").reshape(1)
     headings, slots = face_blocks.shape[1:]
     stride = lax.axis_size(SPACE) // 4 + 1
-    offsets = (1, -1, 2, -2, stride, -stride)
-    late = [e ^ 1 for e in EARLY]
     faces = jnp.swapaxes(face_blocks, 1, 2)
     columns = jnp.swapaxes(near_columns, 0, 1)
     counts = face_counts
+    plan = face_plan(stride)
     field = struct(*right.shape)
-    face = [struct(slots, width, lanes)] * len(EARLY)
+    sent = [2 * slots, slots] if paired(stride) else [slots] * PLUS
+    face = [struct(n, width, lanes) for n in sent]
     pack = [struct(blocks // hours, width, lanes)] * (hours - 1)
-    product = struct(len(EARLY) * slots, width, lanes)
+    product = struct(PLUS * slots, width, lanes)
     product_pack = [struct(product.shape[0] // hours, width, lanes)] * (hours - 1)
     spare = [pltpu.VMEM((blocks + 1, width, lanes), F32)]
+    turns = hours - 1
 
     def body(function, *sizes):
         return functools.partial(function, hours, *sizes)
 
-    def unpack(values, *sizes):
-        values, result = list(values), []
-        for n in sizes:
-            result.append(values[:n])
-            values = values[n:]
-        return result
-
-    outs = call(body(open_body), face + pack, [faces, hour], [right])
-    outgoing, packs = unpack(outs, len(face), len(pack))
-    packs = send_lanes(packs)
-    early = send_faces(outgoing, EARLY, offsets)
+    def early_products(early, after):
+        own, *packs = call(
+            body(early_body), [product] + product_pack, [plan, hour], [stiffness, *early, *after]
+        )
+        return own, packs
+
+    outs = call(body(open_body), pack + face, [faces, plan, hour], [right])
+    packs = send_lanes(outs[:turns])
+    early = send_faces(outs[turns:], stride, 1)
     probe_right, *outgoing = call(
-        body(turn_body), [field] + face, [faces, hour], [right, *packs]
-    )
-    arrived = send_faces(outgoing, late, offsets)
+        body(turn_body, 0), [field] + face, [faces, plan, hour], [right, early[-1], *packs]
+    )
+    arrived = send_faces(outgoing, stride, -1)
     stiffness = call(
         split_body, struct(headings * slots, width, 3 * width, dtype=BF16), [], [far_stiffness]
     )
     (near_part,) = near(columns, kappa_sq, near_stiffness, [probe_right])
-    own, *packs = call(
-        body(early_body), [product] + product_pack, [hour], [stiffness, *early]
-    )
+    own, packs = early_products(early, [near_part, arrived[-1]])
     packs = send_lanes(packs)
-    outs = call(
+    first, image, *outs = call(
         body(middle_body),
-        [field, field] + face + pack + pack,
-        [faces, counts, hour, time_coupling],
+        [field, field] + pack + face,
+        [faces, counts, plan, hour, time_coupling],
         [stiffness, near_part, own, *packs, *arrived],
         spare,
     )
-    (first, image), outgoing, packs, first_packs = unpack(
-        outs, 2, len(face), len(pack), len(pack)
-    )
-
-    packs = send_lanes(packs)
-    early = send_faces(outgoing, EARLY, offsets)
-    hour_image, *outgoing = call(body(turn_body), [field] + face, [faces, hour], [image, *packs])
-    arrived = send_faces(outgoing, late, offsets)
-    first_packs = send_lanes(first_packs)
+
+    packs = send_lanes(outs[:turns])
+    early = send_faces(outs[turns:], stride, 1)
+    hour_image, *outs = call(
+        body(turn_body, 1), [field] + pack + face, [faces, plan, hour], [image, early[-1], *packs, first]
+    )
+    first_packs = send_lanes(outs[:turns])
+    arrived = send_faces(outs[turns:], stride, -1)
     near_probe, near_hour = near(columns, kappa_sq, near_stiffness, [image, hour_image])
-    own, *packs = call(
-        body(early_body), [product] + product_pack, [hour], [stiffness, *early]
-    )
+    own, packs = early_products(early, [near_hour, arrived[-1]])
     sums = call(
         body(moments_body),
         struct(8, lanes),
-        [faces, counts, hour],
+        [faces, counts, plan, hour],
         [probe_right, first, near_probe, own],
     )
     sums = everyone(total(everyone(sums, ("tm", "rep"))), ("mesh",))
@@ -363,7 +381,7 @@
     solution_field, residual = call(
         body(close_body, len(sums)),
         [field, field],
-        [faces, counts, hour],
+        [faces, counts, plan, hour],
         [stiffness, right, first, near_hour, own, *sums, *first_packs, *packs, *arrived],
         spare,
     )

time: 75.2 us -> 77.3 us (1.028)
  Pallas kernels: 12.2 us -> 13.2 us
  starting transfers between devices: 24.5 us -> 25.5 us
    ppermute x23 -> x19, waiting for transfers between devices: 34.1 us -> 9.51 us  [shifted(): return lax.ppermute(value, axes, route)]
    ppermute x0 -> x4, waiting for transfers between devices: none -> 24.4 us  [send_faces(): lax.ppermute(single, SPACE, [(i, (i + hop[i % 2]) % count) for i in range...]
    ppermute x23 -> x19, starting transfers between devices: 24.5 us -> 25.5 us  [shifted(): return lax.ppermute(value, axes, route)]
    pallas_call x11, Pallas kernels: 12.2 us -> 13.2 us  [call(): pl.pallas_call(body, out_shape=outs, in_specs=[pl.BlockSpec(memory_space=...]
  transfers between devices with their start and end apart: 23 -> 23, of which waited for: 14 -> 9; matrix products, arithmetic and copies ran while one was open for 0% -> 0% of each run, Pallas kernels for 10% -> 11%
where the time goes in v3:
time: 77.3 us; the launch traced here: 77.1 us
  waiting for transfers between devices  33.9 us (44%)
  starting transfers between devices  25.5 us (33%)
  Pallas kernels  13.2 us (17%)
  local copies, waits for them, and re-layouts  2.97 us (4%)
  between operations  1.49 us (2%)
    ppermute x19, starting transfers between devices, shifted(): return lax.ppermute(value, axes, route)  25.5 us
    ppermute x4, waiting for transfers between devices, send_faces(): lax.ppermute(single, SPACE, [(i, (i + hop[i % 2]) % count) for i in range...  24.4 us
    pallas_call x11, Pallas kernels, call(): pl.pallas_call(body, out_shape=outs, in_specs=[pl.BlockSpec(memory_space=...  13.2 us
    ppermute x19, waiting for transfers between devices, shifted(): return lax.ppermute(value, axes, route)  9.51 us
    unnamed x18, local copies, waits for them, and re-layouts  2.85 us
  transfers between devices with their start and end apart: 23, of which 9 were waited for; matrix products, arithmetic and copies ran while one was open for 0% of the time, Pallas kernels for 11%

profile of v3, /device:TPU:0, one launch (start us, length us, event | category | flops | bytes accessed | tf_op | source)
XLA Modules:
  0.0 77.1 jit_solution(15382749271718526959)
XLA Ops:
  0.6 0.1 stack.13.plan
  0.7 1.1 %copy-done.1 = f32[1,16,64,128]{3,2,1,0:T(8,128)S(1)} copy-done((f32[1,16,64,128]{3,2,1,0:T(8,128)S(1)}, f32[1,16,64,128]{3,2,1,0:T(8,128)}, u32[]{:S(2)}) %copy-start.1) | copy-done | bytes 524312
  1.9 0.7 copy-done.4
  2.6 0.8 shard_map.96
  3.3 3.0 %collective-permute-start.1 = (f32[8,64,128]{2,1,0:T(8,128)S(1)}, f32[8,64,128]{2,1,0:T(8,128)S(1)}, u32[]{:S(2)}, u32[]{:S(2)}) collective-permute-start(f32[8,64,128]{2,1,0:T(8,128)S(1)} %get-tuple-element.26), channel_id=1, source_target_pairs={{0,2},{2,0},{1,3},{3,1},{4,6},{6,4},{5,7},{7,5},{8,10},{10,8},{9,1... | collective-permute-start | bytes 786440 | tf_op jit(solution)/shard_map/ppermute | solution.py:257
  6.3 1.6 %collective-permute-start.2 = (f32[8,64,128]{2,1,0:T(8,128)S(1)}, f32[8,64,128]{2,1,0:T(8,128)S(1)}, u32[]{:S(2)}, u32[]{:S(2)}) collective-permute-start(f32[8,64,128]{2,1,0:T(8,128)S(1)} %get-tuple-element.28), channel_id=1, source_target_pairs={{0,4},{4,8},{8,12},{12,0},{1,5},{5,9},{9,13},{13,1},{2,6},{6,10},{... | collective-permute-start | bytes 786440 | tf_op jit(solution)/shard_map/ppermute | solution.py:257
  7.9 0.0 collective-permute-start
  7.9 10.9 %collective-permute-done._.refs_2_ = f32[4,64,128]{2,1,0:T(8,128)S(1)} collective-permute-done((f32[4,64,128]{2,1,0:T(8,128)S(1)}, f32[4,64,128]{2,1,0:T(8,128)S(1)}, u32[]{:S(2)}, u32[]{:S(2)}) %collective-permute-start) | collective-permute-done | bytes 131104 | tf_op jit(solution)/shard_map/ppermute | solution.py:284
  18.8 0.0 collective-permute-done.1.refs_0_
  18.8 0.8 %shard_map.97 = (f32[16,64,128]{2,1,0:T(8,128)S(1)}, f32[8,64,128]{2,1,0:T(8,128)S(1)}, f32[4,64,128]{2,1,0:T(8,128)S(1)}) custom-call(s32[1,4,6]{2,1,0:T(4,128)S(1)} %bitcast.12, s32[6]{0:T(128)S(1)} %stack.13.plan, s32[1]{0:T(128)} %bitcast.3.hour, f32[16,64,128]{2,1,0:T(8,128)S(1)} %bitcast.9, f32[4,64,128]{2,1,0:T(8,128)S(1)} %collective-permute-done._.refs_2_, ...), custom_call_target="tpu_custom_call" | custom-call | tf_op jit(solution)/shard_map/pallas_call | solution.py:22
  19.6 1.6 %collective-permute-start.6 = (f32[8,64,128]{2,1,0:T(8,128)S(1)}, f32[8,64,128]{2,1,0:T(8,128)S(1)}, u32[]{:S(2)}, u32[]{:S(2)}) collective-permute-start(f32[8,64,128]{2,1,0:T(8,128)S(1)} %get-tuple-element.32), channel_id=1, source_target_pairs={{0,12},{4,0},{8,4},{12,8},{1,13},{5,1},{9,5},{13,9},{2,14},{6,2},{... | collective-permute-start | bytes 786440 | tf_op jit(solution)/shard_map/ppermute | solution.py:257
  21.2 0.0 collective-permute-start.4
  21.2 0.0 collective-permute-done.2.refs_0_
  21.2 0.6 collective-permute-start.3
  21.8 1.0 %copy-done.3 = f32[1,64,1536]{2,1,0:T(8,128)S(1)} copy-done((f32[1,64,1536]{2,1,0:T(8,128)S(1)}, f32[1,64,1536]{2,1,0:T(8,128)}, u32[]{:S(2)}) %copy-start.3) | copy-done | bytes 393240
  22.8 0.2 shard_map.95.stiffness
  23.0 1.6 %shard_map.98.refs_3_.near_part = f32[16,64,128]{2,1,0:T(8,128)S(1)} custom-call(s32[6,16]{1,0:T(8,128)S(1)} %bitcast.17, f32[16,64]{1,0:T(8,128)S(1)} %copy-done.6, f32[16,64,384]{2,1,0:T(8,128)S(1)} %copy-done, f32[16,64,128]{2,1,0:T(8,128)S(1)} %get-tuple-element.27.refs_0_.right), custom_call_target="tpu_custom_call" | custom-call | tf_op jit(solution)/shard_map/pallas_call | solution.py:22
  24.6 0.0 copy-start.8
  24.6 1.9 %collective-permute-done.4.refs_4_.refs_3_ = f32[4,64,128]{2,1,0:T(8,128)S(1)} collective-permute-done((f32[4,64,128]{2,1,0:T(8,128)S(1)}, f32[4,64,128]{2,1,0:T(8,128)S(1)}, u32[]{:S(2)}, u32[]{:S(2)}) %collective-permute-start.4) | collective-permute-done | bytes 131104 | tf_op jit(solution)/shard_map/ppermute | solution.py:284
  26.5 0.0 collective-permute-done.3.refs_1_
  26.5 1.0 %shard_map.99 = (f32[12,64,128]{2,1,0:T(8,128)S(1)}, f32[6,64,128]{2,1,0:T(8,128)S(1)}) custom-call(s32[6]{0:T(128)S(1)} %stack.13.plan, s32[1]{0:T(128)} %bitcast.3.hour, bf16[24,64,192]{2,1,0:T(8,128)(2,1)S(1)} %shard_map.95.stiffness, f32[8,64,128]{2,1,0:T(8,128)S(1)} %collective-permute-done.2.refs_0_, f32[4,64,128]{2,1,0:T(8,128)S(1)} %collective-permute-done.3.refs_1_, ...), custom_call_target="tpu_custom_call" | custom-call | tf_op jit(solution)/shard_map/pallas_call | solution.py:22
  27.5 0.6 collective-permute-start.5
  28.1 0.0 collective-permute-done.6.refs_1_
  28.1 2.0 %collective-permute-start.7 = (f32[4,64,128]{2,1,0:T(8,128)S(1)}, f32[4,64,128]{2,1,0:T(8,128)S(1)}, u32[]{:S(2)}, u32[]{:S(2)}) collective-permute-start(f32[4,64,128]{2,1,0:T(8,128)S(1)} %slice.17), channel_id=1, source_target_pairs={{0,1},{1,0},{2,3},{3,2},{4,5},{5,4},{6,7},{7,6},{8,9},{9,8},{10,11... | collective-permute-start | bytes 393224 | tf_op jit(solution)/shard_map/ppermute | solution.py:257
  30.8 3.2 %collective-permute-done.5.refs_0_ = f32[6,64,128]{2,1,0:T(8,128)S(1)} collective-permute-done((f32[6,64,128]{2,1,0:T(8,128)S(1)}, f32[6,64,128]{2,1,0:T(8,128)S(1)}, u32[]{:S(2)}, u32[]{:S(2)}) %collective-permute-start.5) | collective-permute-done | bytes 196640 | tf_op jit(solution)/shard_map/ppermute | solution.py:257
  34.0 0.0 collective-permute-done.7.refs_2_
  34.1 1.4 %shard_map.100 = (f32[16,64,128]{2,1,0:T(8,128)S(1)}, f32[16,64,128]{2,1,0:T(8,128)S(1)}, f32[8,64,128]{2,1,0:T(8,128)S(1)}, f32[8,64,128]{2,1,0:T(8,128)S(1)}, f32[4,64,128]{2,1,0:T(8,128)S(1)}) custom-call(s32[1,4,6]{2,1,0:T(4,128)S(1)} %bitcast.13, s32[1,6]{1,0:T(1,128)S(1)} %copy-done.8, s32[6]{0:T(128)S(1)} %stack.13.plan, s32[1]{0:T(128)} %bitcast.3.hour, ...), custom_call_target="tpu_custom_call" | custom-call | tf_op jit(solution)/shard_map/pallas_call | solution.py:22
  35.5 0.6 collective-permute-start.9
  36.1 2.6 %collective-permute-start.10 = (f32[8,64,128]{2,1,0:T(8,128)S(1)}, f32[8,64,128]{2,1,0:T(8,128)S(1)}, u32[]{:S(2)}, u32[]{:S(2)}) collective-permute-start(f32[8,64,128]{2,1,0:T(8,128)S(1)} %get-tuple-element.39), channel_id=1, source_target_pairs={{0,4},{4,8},{8,12},{12,0},{1,5},{5,9},{9,13},{13,1},{2,6},{6,10},{... | collective-permute-start | bytes 786440 | tf_op jit(solution)/shard_map/ppermute | solution.py:257
  38.7 0.0 collective-permute-start.8
  38.7 11.0 %collective-permute-done.8._.refs_2_ = f32[4,64,128]{2,1,0:T(8,128)S(1)} collective-permute-done((f32[4,64,128]{2,1,0:T(8,128)S(1)}, f32[4,64,128]{2,1,0:T(8,128)S(1)}, u32[]{:S(2)}, u32[]{:S(2)}) %collective-permute-start.8) | collective-permute-done | bytes 131104 | tf_op jit(solution)/shard_map/ppermute | solution.py:284
  49.8 0.0 collective-permute-done.9.refs_0_
  49.8 0.9 %shard_map.101 = (f32[16,64,128]{2,1,0:T(8,128)S(1)}, f32[8,64,128]{2,1,0:T(8,128)S(1)}, f32[8,64,128]{2,1,0:T(8,128)S(1)}, f32[4,64,128]{2,1,0:T(8,128)S(1)}) custom-call(s32[1,4,6]{2,1,0:T(4,128)S(1)} %bitcast.14, s32[6]{0:T(128)S(1)} %stack.13.plan, s32[1]{0:T(128)} %bitcast.3.hour, f32[16,64,128]{2,1,0:T(8,128)S(1)} %get-tuple-element.34.field.refs_0_, ...), custom_call_target="tpu_custom_call" | custom-call | tf_op jit(solution)/shard_map/pallas_call | solution.py:22
  50.7 1.2 %collective-permute-start.21 = (f32[8,64,128]{2,1,0:T(8,128)S(1)}, f32[8,64,128]{2,1,0:T(8,128)S(1)}, u32[]{:S(2)}, u32[]{:S(2)}) collective-permute-start(f32[8,64,128]{2,1,0:T(8,128)S(1)} %get-tuple-element.45), channel_id=1, source_target_pairs={{0,12},{4,0},{8,4},{12,8},{1,13},{5,1},{9,5},{13,9},{2,14},{6,2},{... | collective-permute-start | bytes 786440 | tf_op jit(solution)/shard_map/ppermute | solution.py:257
  51.8 0.0 collective-permute-start.12
  51.8 0.0 collective-permute-done.10.refs_0_
  51.9 0.6 collective-permute-start.11
  52.4 1.5 %collective-permute-start.19 = (f32[8,64,128]{2,1,0:T(8,128)S(1)}, f32[8,64,128]{2,1,0:T(8,128)S(1)}, u32[]{:S(2)}, u32[]{:S(2)}) collective-permute-start(f32[8,64,128]{2,1,0:T(8,128)S(1)} %get-tuple-element.43), channel_id=1, source_target_pairs={{0,2},{2,0},{1,3},{3,1},{4,6},{6,4},{5,7},{7,5},{8,10},{10,8},{9,1... | collective-permute-start | bytes 786440 | tf_op jit(solution)/shard_map/ppermute | solution.py:257
  53.9 2.6 %shard_map.102 = (f32[16,64,128]{2,1,0:T(8,128)S(1)}, f32[16,64,128]{2,1,0:T(8,128)S(1)}) custom-call(s32[6,16]{1,0:T(8,128)S(1)} %bitcast.18, f32[16,64]{1,0:T(8,128)S(1)} %copy-done.6, f32[16,64,384]{2,1,0:T(8,128)S(1)} %copy-done, f32[16,64,128]{2,1,0:T(8,128)S(1)} %get-tuple-element.34.field.refs_0_, f32[16,64,128]{2,1,0:T(8,128)S(1)} %get-tuple-element.37.refs_1_), custom_call_target="tpu_custom_call" | custom-call | tf_op jit(solution)/shard_map/pallas_call | solution.py:22
  56.5 0.0 copy-start.5
  56.6 0.6 collective-permute-done.12.refs_4_.refs_8_
  57.2 0.0 collective-permute-done.11.refs_1_
  57.2 0.9 %shard_map.103 = (f32[12,64,128]{2,1,0:T(8,128)S(1)}, f32[6,64,128]{2,1,0:T(8,128)S(1)}) custom-call(s32[6]{0:T(128)S(1)} %stack.13.plan, s32[1]{0:T(128)} %bitcast.3.hour, bf16[24,64,192]{2,1,0:T(8,128)(2,1)S(1)} %shard_map.95.stiffness, f32[8,64,128]{2,1,0:T(8,128)S(1)} %collective-permute-done.10.refs_0_, ...), custom_call_target="tpu_custom_call" | custom-call | tf_op jit(solution)/shard_map/pallas_call | solution.py:22
  58.1 0.0 copy-start.2
  58.2 0.8 %shard_map.104 = f32[8,128]{1,0:T(8,128)S(1)} custom-call(s32[1,4,6]{2,1,0:T(4,128)S(1)} %bitcast.15, s32[1,6]{1,0:T(1,128)S(1)} %copy-done.8, s32[6]{0:T(128)S(1)} %stack.13.plan, s32[1]{0:T(128)} %bitcast.3.hour, f32[16,64,128]{2,1,0:T(8,128)S(1)} %get-tuple-element.27.refs_0_.right, f32[16,64,128]{2,1,0:T(8,128)S(1)} %get-tuple-element.33.refs_1_.first, ...), custom_call_target="tpu_custom_call" | custom-call | tf_op jit(solution)/shard_map/pallas_call | solution.py:22
  59.0 2.4 %collective-permute-start.13 = (f32[8,128]{1,0:T(8,128)S(1)}, f32[8,128]{1,0:T(8,128)S(1)}, u32[]{:S(2)}, u32[]{:S(2)}) collective-permute-start(f32[8,128]{1,0:T(8,128)S(1)} %shard_map.104), channel_id=1, source_target_pairs={{0,1},{1,0},{2,3},{3,2},{4,5},{5,4},{6,7},{7,6},{8,9},{9,8},{10,11... | collective-permute-start | bytes 12296 | tf_op jit(solution)/shard_map/ppermute | solution.py:257
  61.4 1.5 %collective-permute-start.14 = (f32[8,128]{1,0:T(8,128)S(1)}, f32[8,128]{1,0:T(8,128)S(1)}, u32[]{:S(2)}, u32[]{:S(2)}) collective-permute-start(f32[8,128]{1,0:T(8,128)S(1)} %shard_map.104), channel_id=1, source_target_pairs={{0,2},{1,3},{2,0},{3,1},{4,6},{5,7},{6,4},{7,5},{8,10},{9,11},{10,... | collective-permute-start | bytes 12296 | tf_op jit(solution)/shard_map/ppermute | solution.py:257
  62.9 0.0 collective-permute-start.15
  62.9 0.0 collective-permute-done.21.refs_6_
  62.9 1.4 %collective-permute-start.20 = (f32[6,64,128]{2,1,0:T(8,128)S(1)}, f32[6,64,128]{2,1,0:T(8,128)S(1)}, u32[]{:S(2)}, u32[]{:S(2)}) collective-permute-start(f32[6,64,128]{2,1,0:T(8,128)S(1)} %get-tuple-element.44), channel_id=1, source_target_pairs={{0,2},{2,0},{1,3},{3,1},{4,6},{6,4},{5,7},{7,5},{8,10},{10,8},{9,1... | collective-permute-start | bytes 589832 | tf_op jit(solution)/shard_map/ppermute | solution.py:257
  64.3 0.0 collective-permute-done.13
  64.3 0.5 collective-permute-start.22
  64.8 0.2 collective-permute-done.14
  65.0 0.9 %collective-permute-done.15 = f32[8,128]{1,0:T(8,128)S(1)} collective-permute-done((f32[8,128]{1,0:T(8,128)S(1)}, f32[8,128]{1,0:T(8,128)S(1)}, u32[]{:S(2)}, u32[]{:S(2)}) %collective-permute-start.15) | collective-permute-done | bytes 4128 | tf_op jit(solution)/shard_map/ppermute | solution.py:257
  65.9 0.4 collective-permute-start.16
  66.3 2.7 %collective-permute-start.17 = (f32[8,128]{1,0:T(8,128)S(1)}, f32[8,128]{1,0:T(8,128)S(1)}, u32[]{:S(2)}, u32[]{:S(2)}) collective-permute-start(f32[8,128]{1,0:T(8,128)S(1)} %add_add_fusion.refs_0_), channel_id=1, source_target_pairs={{0,8},{4,12},{8,0},{12,4},{1,9},{5,13},{9,1},{13,5},{2,10},{6,14},... | collective-permute-start | bytes 12296 | tf_op jit(solution)/shard_map/ppermute | solution.py:257
  69.0 2.3 %collective-permute-done.16.refs_1_ = f32[8,128]{1,0:T(8,128)S(1)} collective-permute-done((f32[8,128]{1,0:T(8,128)S(1)}, f32[8,128]{1,0:T(8,128)S(1)}, u32[]{:S(2)}, u32[]{:S(2)}) %collective-permute-start.16) | collective-permute-done | bytes 4128 | tf_op jit(solution)/shard_map/ppermute | solution.py:257
  71.3 0.8 collective-permute-start.18
  72.1 0.0 collective-permute-done.17.refs_2_
  72.1 2.8 %collective-permute-done.18.refs_3_ = f32[8,128]{1,0:T(8,128)S(1)} collective-permute-done((f32[8,128]{1,0:T(8,128)S(1)}, f32[8,128]{1,0:T(8,128)S(1)}, u32[]{:S(2)}, u32[]{:S(2)}) %collective-permute-start.18) | collective-permute-done | bytes 4128 | tf_op jit(solution)/shard_map/ppermute | solution.py:257
  74.9 0.0 collective-permute-done.19.refs_4_
  74.9 0.0 collective-permute-done.20.refs_5_
  74.9 0.0 collective-permute-done.22.refs_7_
  75.0 2.1 %shard_map.105 = (f32[16,64,128]{2,1,0:T(8,128)}, f32[16,64,128]{2,1,0:T(8,128)}) custom-call(s32[1,4,6]{2,1,0:T(4,128)S(1)} %bitcast.16, s32[1,6]{1,0:T(1,128)S(1)} %copy-done.8, s32[6]{0:T(128)S(1)} %stack.13.plan, s32[1]{0:T(128)} %bitcast.3.hour, bf16[24,64,192]{2,1,0:T(8,128)(2,1)S(1)} %shard_map.95.stiffness, f32[16,64,128]{2,1,0:T(8,128)S(1)} %bitcast.10, ...), custom_call_target="tpu_custom_call" | custom-call | tf_op jit(solution)/shard_map/pallas_call | solution.py:22
  (17 shorter events, 0.1 us)
Async XLA Ops:
  0.6 22.3 %copy-start = (f32[16,64,384]{2,1,0:T(8,128)S(1)}, f32[16,64,384]{2,1,0:T(8,128)}, u32[]{:S(2)}) copy-start(f32[16,64,384]{2,1,0:T(8,128)} %stiffness.5) | copy-start | bytes 4718596
  0.7 1.1 %copy-start.1 = (f32[1,16,64,128]{3,2,1,0:T(8,128)S(1)}, f32[1,16,64,128]{3,2,1,0:T(8,128)}, u32[]{:S(2)}) copy-start(f32[1,16,64,128]{3,2,1,0:T(8,128)} %param.8) | copy-start | bytes 1572868
  1.9 0.7 copy-start.4
  2.6 20.4 %copy-start.6 = (f32[16,64]{1,0:T(8,128)S(1)}, f32[16,64]{1,0:T(8,128)}, u32[]{:S(2)}) copy-start(f32[16,64]{1,0:T(8,128)} %kappa.3) | copy-start | bytes 12292
  2.6 20.4 %copy-start.7 = (s32[16,6]{0,1:T(8,128)S(1)}, s32[16,6]{0,1:T(8,128)}, u32[]{:S(2)}) copy-start(s32[16,6]{0,1:T(8,128)} %param.13) | copy-start | bytes 1156
  3.3 15.4 %collective-permute-start.1 = (f32[8,64,128]{2,1,0:T(8,128)S(1)}, f32[8,64,128]{2,1,0:T(8,128)S(1)}, u32[]{:S(2)}, u32[]{:S(2)}) collective-permute-start(f32[8,64,128]{2,1,0:T(8,128)S(1)} %get-tuple-element.26), channel_id=1, source_target_pairs={{0,2},{2,0},{1,3},{3,1},{4,6},{6,4},{5,7},{7,5},{8,10},{10,8},{9,1... | collective-permute-start | bytes 786440 | tf_op jit(solution)/shard_map/ppermute | solution.py:257
  6.3 14.9 %collective-permute-start.2 = (f32[8,64,128]{2,1,0:T(8,128)S(1)}, f32[8,64,128]{2,1,0:T(8,128)S(1)}, u32[]{:S(2)}, u32[]{:S(2)}) collective-permute-start(f32[8,64,128]{2,1,0:T(8,128)S(1)} %get-tuple-element.28), channel_id=1, source_target_pairs={{0,4},{4,8},{8,12},{12,0},{1,5},{5,9},{9,13},{13,1},{2,6},{6,10},{... | collective-permute-start | bytes 786440 | tf_op jit(solution)/shard_map/ppermute | solution.py:257
  7.9 10.9 %collective-permute-start = (f32[4,64,128]{2,1,0:T(8,128)S(1)}, f32[4,64,128]{2,1,0:T(8,128)S(1)}, u32[]{:S(2)}, u32[]{:S(2)}) collective-permute-start(f32[4,64,128]{2,1,0:T(8,128)S(1)} %get-tuple-element.25), channel_id=1, source_target_pairs={{0,1},{1,8},{4,5},{5,12},{8,9},{9,0},{12,13},{13,4},{2,3},{3,10},{... | collective-permute-start | bytes 393224 | tf_op jit(solution)/shard_map/ppermute | solution.py:284
  19.6 8.5 %collective-permute-start.6 = (f32[8,64,128]{2,1,0:T(8,128)S(1)}, f32[8,64,128]{2,1,0:T(8,128)S(1)}, u32[]{:S(2)}, u32[]{:S(2)}) collective-permute-start(f32[8,64,128]{2,1,0:T(8,128)S(1)} %get-tuple-element.32), channel_id=1, source_target_pairs={{0,12},{4,0},{8,4},{12,8},{1,13},{5,1},{9,5},{13,9},{2,14},{6,2},{... | collective-permute-start | bytes 786440 | tf_op jit(solution)/shard_map/ppermute | solution.py:257
  21.2 5.3 %collective-permute-start.4 = (f32[4,64,128]{2,1,0:T(8,128)S(1)}, f32[4,64,128]{2,1,0:T(8,128)S(1)}, u32[]{:S(2)}, u32[]{:S(2)}) collective-permute-start(f32[4,64,128]{2,1,0:T(8,128)S(1)} %get-tuple-element.29), channel_id=1, source_target_pairs={{0,9},{1,0},{4,13},{5,4},{8,1},{9,8},{12,5},{13,12},{2,11},{3,2},{... | collective-permute-start | bytes 393224 | tf_op jit(solution)/shard_map/ppermute | solution.py:284
  21.2 5.3 %collective-permute-start.3 = (f32[4,64,128]{2,1,0:T(8,128)S(1)}, f32[4,64,128]{2,1,0:T(8,128)S(1)}, u32[]{:S(2)}, u32[]{:S(2)}) collective-permute-start(f32[4,64,128]{2,1,0:T(8,128)S(1)} %slice.16), channel_id=1, source_target_pairs={{0,1},{1,0},{2,3},{3,2},{4,5},{5,4},{6,7},{7,6},{8,9},{9,8},{10,11... | collective-permute-start | bytes 393224 | tf_op jit(solution)/shard_map/ppermute | solution.py:257
  21.8 1.0 %copy-start.3 = (f32[1,64,1536]{2,1,0:T(8,128)S(1)}, f32[1,64,1536]{2,1,0:T(8,128)}, u32[]{:S(2)}) copy-start(f32[1,64,1536]{2,1,0:T(8,128)} %stiffness.3) | copy-start | bytes 1179652
  24.6 9.4 %copy-start.8 = (s32[1,6]{1,0:T(1,128)S(1)}, s32[1,6]{1,0:T(1,128)}, u32[]{:S(2)}) copy-start(s32[1,6]{1,0:T(1,128)} %counts.5) | copy-start | bytes 76
  27.5 6.5 %collective-permute-start.5 = (f32[6,64,128]{2,1,0:T(8,128)S(1)}, f32[6,64,128]{2,1,0:T(8,128)S(1)}, u32[]{:S(2)}, u32[]{:S(2)}) collective-permute-start(f32[6,64,128]{2,1,0:T(8,128)S(1)} %get-tuple-element.31), channel_id=1, source_target_pairs={{0,2},{2,0},{1,3},{3,1},{4,6},{6,4},{5,7},{7,5},{8,10},{10,8},{9,1... | collective-permute-start | bytes 589832 | tf_op jit(solution)/shard_map/ppermute | solution.py:257
  28.1 5.9 %collective-permute-start.7 = (f32[4,64,128]{2,1,0:T(8,128)S(1)}, f32[4,64,128]{2,1,0:T(8,128)S(1)}, u32[]{:S(2)}, u32[]{:S(2)}) collective-permute-start(f32[4,64,128]{2,1,0:T(8,128)S(1)} %slice.17), channel_id=1, source_target_pairs={{0,1},{1,0},{2,3},{3,2},{4,5},{5,4},{6,7},{7,6},{8,9},{9,8},{10,11... | collective-permute-start | bytes 393224 | tf_op jit(solution)/shard_map/ppermute | solution.py:257
  35.5 14.3 %collective-permute-start.9 = (f32[8,64,128]{2,1,0:T(8,128)S(1)}, f32[8,64,128]{2,1,0:T(8,128)S(1)}, u32[]{:S(2)}, u32[]{:S(2)}) collective-permute-start(f32[8,64,128]{2,1,0:T(8,128)S(1)} %get-tuple-element.36), channel_id=1, source_target_pairs={{0,2},{2,0},{1,3},{3,1},{4,6},{6,4},{5,7},{7,5},{8,10},{10,8},{9,1... | collective-permute-start | bytes 786440 | tf_op jit(solution)/shard_map/ppermute | solution.py:257
  36.1 15.8 %collective-permute-start.10 = (f32[8,64,128]{2,1,0:T(8,128)S(1)}, f32[8,64,128]{2,1,0:T(8,128)S(1)}, u32[]{:S(2)}, u32[]{:S(2)}) collective-permute-start(f32[8,64,128]{2,1,0:T(8,128)S(1)} %get-tuple-element.39), channel_id=1, source_target_pairs={{0,4},{4,8},{8,12},{12,0},{1,5},{5,9},{9,13},{13,1},{2,6},{6,10},{... | collective-permute-start | bytes 786440 | tf_op jit(solution)/shard_map/ppermute | solution.py:257
  38.7 11.0 %collective-permute-start.8 = (f32[4,64,128]{2,1,0:T(8,128)S(1)}, f32[4,64,128]{2,1,0:T(8,128)S(1)}, u32[]{:S(2)}, u32[]{:S(2)}) collective-permute-start(f32[4,64,128]{2,1,0:T(8,128)S(1)} %get-tuple-element.35), channel_id=1, source_target_pairs={{0,1},{1,8},{4,5},{5,12},{8,9},{9,0},{12,13},{13,4},{2,3},{3,10},{... | collective-permute-start | bytes 393224 | tf_op jit(solution)/shard_map/ppermute | solution.py:284
  50.7 12.2 %collective-permute-start.21 = (f32[8,64,128]{2,1,0:T(8,128)S(1)}, f32[8,64,128]{2,1,0:T(8,128)S(1)}, u32[]{:S(2)}, u32[]{:S(2)}) collective-permute-start(f32[8,64,128]{2,1,0:T(8,128)S(1)} %get-tuple-element.45), channel_id=1, source_target_pairs={{0,12},{4,0},{8,4},{12,8},{1,13},{5,1},{9,5},{13,9},{2,14},{6,2},{... | collective-permute-start | bytes 786440 | tf_op jit(solution)/shard_map/ppermute | solution.py:257
  51.8 5.3 %collective-permute-start.12 = (f32[4,64,128]{2,1,0:T(8,128)S(1)}, f32[4,64,128]{2,1,0:T(8,128)S(1)}, u32[]{:S(2)}, u32[]{:S(2)}) collective-permute-start(f32[4,64,128]{2,1,0:T(8,128)S(1)} %get-tuple-element.40), channel_id=1, source_target_pairs={{0,9},{1,0},{4,13},{5,4},{8,1},{9,8},{12,5},{13,12},{2,11},{3,2},{... | collective-permute-start | bytes 393224 | tf_op jit(solution)/shard_map/ppermute | solution.py:284
  51.9 5.3 %collective-permute-start.11 = (f32[4,64,128]{2,1,0:T(8,128)S(1)}, f32[4,64,128]{2,1,0:T(8,128)S(1)}, u32[]{:S(2)}, u32[]{:S(2)}) collective-permute-start(f32[4,64,128]{2,1,0:T(8,128)S(1)} %slice.18), channel_id=1, source_target_pairs={{0,1},{1,0},{2,3},{3,2},{4,5},{5,4},{6,7},{7,6},{8,9},{9,8},{10,11... | collective-permute-start | bytes 393224 | tf_op jit(solution)/shard_map/ppermute | solution.py:257
  52.4 22.5 %collective-permute-start.19 = (f32[8,64,128]{2,1,0:T(8,128)S(1)}, f32[8,64,128]{2,1,0:T(8,128)S(1)}, u32[]{:S(2)}, u32[]{:S(2)}) collective-permute-start(f32[8,64,128]{2,1,0:T(8,128)S(1)} %get-tuple-element.43), channel_id=1, source_target_pairs={{0,2},{2,0},{1,3},{3,1},{4,6},{6,4},{5,7},{7,5},{8,10},{10,8},{9,1... | collective-permute-start | bytes 786440 | tf_op jit(solution)/shard_map/ppermute | solution.py:257
  56.5 1.6 %copy-start.5 = (s32[1,6,4]{1,2,0:T(4,128)S(1)}, s32[1,6,4]{1,2,0:T(4,128)}, u32[]{:S(2)}) copy-start(s32[1,6,4]{1,2,0:T(4,128)} %param.14) | copy-start | bytes 292
  58.1 16.8 %copy-start.2 = (f32[1,16,64,128]{3,2,1,0:T(8,128)S(1)}, f32[1,16,64,128]{3,2,1,0:T(8,128)}, u32[]{:S(2)}) copy-start(f32[1,16,64,128]{3,2,1,0:T(8,128)} %param.8) | copy-start | bytes 1572868
  59.0 5.3 %collective-permute-start.13 = (f32[8,128]{1,0:T(8,128)S(1)}, f32[8,128]{1,0:T(8,128)S(1)}, u32[]{:S(2)}, u32[]{:S(2)}) collective-permute-start(f32[8,128]{1,0:T(8,128)S(1)} %shard_map.104), channel_id=1, source_target_pairs={{0,1},{1,0},{2,3},{3,2},{4,5},{5,4},{6,7},{7,6},{8,9},{9,8},{10,11... | collective-permute-start | bytes 12296 | tf_op jit(solution)/shard_map/ppermute | solution.py:257
  61.4 3.6 %collective-permute-start.14 = (f32[8,128]{1,0:T(8,128)S(1)}, f32[8,128]{1,0:T(8,128)S(1)}, u32[]{:S(2)}, u32[]{:S(2)}) collective-permute-start(f32[8,128]{1,0:T(8,128)S(1)} %shard_map.104), channel_id=1, source_target_pairs={{0,2},{1,3},{2,0},{3,1},{4,6},{5,7},{6,4},{7,5},{8,10},{9,11},{10,... | collective-permute-start | bytes 12296 | tf_op jit(solution)/shard_map/ppermute | solution.py:257
  62.9 3.1 %collective-permute-start.15 = (f32[8,128]{1,0:T(8,128)S(1)}, f32[8,128]{1,0:T(8,128)S(1)}, u32[]{:S(2)}, u32[]{:S(2)}) collective-permute-start(f32[8,128]{1,0:T(8,128)S(1)} %shard_map.104), channel_id=1, source_target_pairs={{0,3},{1,2},{2,1},{3,0},{4,7},{5,6},{6,5},{7,4},{8,11},{9,10},{10,... | collective-permute-start | bytes 12296 | tf_op jit(solution)/shard_map/ppermute | solution.py:257
  62.9 12.1 %collective-permute-start.20 = (f32[6,64,128]{2,1,0:T(8,128)S(1)}, f32[6,64,128]{2,1,0:T(8,128)S(1)}, u32[]{:S(2)}, u32[]{:S(2)}) collective-permute-start(f32[6,64,128]{2,1,0:T(8,128)S(1)} %get-tuple-element.44), channel_id=1, source_target_pairs={{0,2},{2,0},{1,3},{3,1},{4,6},{6,4},{5,7},{7,5},{8,10},{10,8},{9,1... | collective-permute-start | bytes 589832 | tf_op jit(solution)/shard_map/ppermute | solution.py:257
  64.3 10.6 %collective-permute-start.22 = (f32[4,64,128]{2,1,0:T(8,128)S(1)}, f32[4,64,128]{2,1,0:T(8,128)S(1)}, u32[]{:S(2)}, u32[]{:S(2)}) collective-permute-start(f32[4,64,128]{2,1,0:T(8,128)S(1)} %slice.19), channel_id=1, source_target_pairs={{0,1},{1,0},{2,3},{3,2},{4,5},{5,4},{6,7},{7,6},{8,9},{9,8},{10,11... | collective-permute-start | bytes 393224 | tf_op jit(solution)/shard_map/ppermute | solution.py:257
  65.9 5.4 %collective-permute-start.16 = (f32[8,128]{1,0:T(8,128)S(1)}, f32[8,128]{1,0:T(8,128)S(1)}, u32[]{:S(2)}, u32[]{:S(2)}) collective-permute-start(f32[8,128]{1,0:T(8,128)S(1)} %add_add_fusion.refs_0_), channel_id=1, source_target_pairs={{0,4},{4,8},{8,12},{12,0},{1,5},{5,9},{9,13},{13,1},{2,6},{6,10},{... | collective-permute-start | bytes 12296 | tf_op jit(solution)/shard_map/ppermute | solution.py:257
  66.3 5.8 %collective-permute-start.17 = (f32[8,128]{1,0:T(8,128)S(1)}, f32[8,128]{1,0:T(8,128)S(1)}, u32[]{:S(2)}, u32[]{:S(2)}) collective-permute-start(f32[8,128]{1,0:T(8,128)S(1)} %add_add_fusion.refs_0_), channel_id=1, source_target_pairs={{0,8},{4,12},{8,0},{12,4},{1,9},{5,13},{9,1},{13,5},{2,10},{6,14},... | collective-permute-start | bytes 12296 | tf_op jit(solution)/shard_map/ppermute | solution.py:257
  71.3 3.6 %collective-permute-start.18 = (f32[8,128]{1,0:T(8,128)S(1)}, f32[8,128]{1,0:T(8,128)S(1)}, u32[]{:S(2)}, u32[]{:S(2)}) collective-permute-start(f32[8,128]{1,0:T(8,128)S(1)} %add_add_fusion.refs_0_), channel_id=1, source_target_pairs={{0,12},{4,0},{8,4},{12,8},{1,13},{5,1},{9,5},{13,9},{2,14},{6,2},{... | collective-permute-start | bytes 12296 | tf_op jit(solution)/shard_map/ppermute | solution.py:257

commit v4 on v3

--- a/solution.py
+++ b/solution.py
@@ -10,14 +10,16 @@
 SPACE = ("mesh", "rep")
 F32 = jnp.float32
 BF16 = jnp.bfloat16
-PLUS = 3
+EARLY = (4, 2, 0)
+PLUS = len(EARLY)
+ORDER = (0, 40, 0, 160)
 
 
 def struct(*shape, dtype=F32):
     return jax.ShapeDtypeStruct(shape, dtype)
 
 
-def call(body, outs, scalars, vectors, scratch=()):
+def call(body, outs, scalars, vectors, scratch=(), weight=0):
     spaces = [pltpu.SMEM] * len(scalars) + [pltpu.VMEM] * len(vectors)
     return pl.pallas_call(
         body,
@@ -25,6 +27,9 @@
         in_specs=[pl.BlockSpec(memory_space=space) for space in spaces],
         out_specs=jax.tree.map(lambda _: pl.BlockSpec(memory_space=pltpu.VMEM), outs),
         scratch_shapes=scratch,
+        cost_estimate=pl.CostEstimate(
+            flops=(weight << 30) + 1024, transcendentals=0, bytes_accessed=1024
+        ),
         compiler_params=pltpu.CompilerParams(vmem_limit_bytes=40 << 20),
     )(*scalars, *vectors)
 
@@ -101,19 +106,19 @@
     return jnp.where(f < counts[0, e], faces[0, f, e], spare)
 
 
-def open_body(hours, faces, plan, hour, field, *outs):
+def open_body(hours, faces, hour, field, *outs):
     pack_lanes(hours, hour[0], field, outs[: hours - 1])
-    pack_faces(faces, field, [plan[n] for n in range(PLUS)], outs[hours - 1 :])
-
-
-def turn_body(hours, extra, faces, plan, hour, field, _, *refs):
+    pack_faces(faces, field, EARLY, outs[hours - 1 :])
+
+
+def turn_body(hours, extra, faces, hour, field, *refs):
     packs, refs = refs[: hours - 1], refs[hours - 1 :]
     (out, *faces_out), others = refs[extra:], []
     if extra:
         others, faces_out = faces_out[: hours - 1], faces_out[hours - 1 :]
     for b in range(field.shape[0]):
         out[b] = merge_lanes(hours, hour[0], field[b], packs, b)
-    pack_faces(faces, out, [plan[PLUS + n] ^ 1 for n in range(PLUS)], faces_out)
+    pack_faces(faces, out, [e ^ 1 for e in EARLY], faces_out)
     if extra:
         pack_lanes(hours, hour[0], refs[0], others)
 
@@ -163,46 +168,54 @@
     )
 
 
-def early_body(hours, plan, hour, stiffness, *refs):
-    arrived, (out, *packs) = refs[:PLUS], refs[PLUS + 2 :]
+def early_body(hours, hour, stiffness, *refs):
+    arrived, (out, *packs) = refs[:PLUS], refs[PLUS:]
     slots = out.shape[0] // PLUS
     for n in range(PLUS):
         for f in range(slots):
-            q = (plan[PLUS + n] ^ 1) * slots + f
+            q = (EARLY[n] ^ 1) * slots + f
             out[n * slots + f] = far_product(stiffness, q, arrived[n][f])
     pack_lanes(hours, hour[0], out, packs)
 
 
-def gather_far(hours, faces, counts, plan, hour, stiffness, own, packs, arrived, near_part, field):
+def late_body(stiffness, *refs):
+    arrived, out = refs[:PLUS], refs[-1]
+    slots = out.shape[0] // PLUS
+    for n in range(PLUS):
+        for f in range(slots):
+            out[n * slots + f] = far_product(stiffness, EARLY[n] * slots + f, arrived[n][f])
+
+
+def gather_far(hours, faces, counts, hour, own, packs, late, near_part, field):
     blocks = near_part.shape[0]
     slots = own.shape[0] // PLUS
     for b in range(blocks):
         field[b] = near_part[b]
     for n in range(PLUS):
-        e = plan[n]
+        e = EARLY[n]
         for f in range(slots):
             q = n * slots + f
-            block = landing(faces, counts, plan[PLUS + n] ^ 1, f, blocks)
+            block = landing(faces, counts, e ^ 1, f, blocks)
             field[block] += merge_lanes(hours, hour[0], own[q], packs, q)
             block = landing(faces, counts, e, f, blocks)
-            field[block] += far_product(stiffness, e * slots + f, arrived[n][f])
-
-
-def middle_body(hours, faces, counts, plan, hour, coupling, stiffness, near_part, own, *refs):
+            field[block] += late[q]
+
+
+def middle_body(hours, faces, counts, hour, coupling, near_part, own, late, *refs):
     turns = hours - 1
-    packs, arrived = refs[:turns], refs[turns : turns + PLUS]
-    first, image, *rest, field = refs[turns + PLUS :]
+    packs = refs[:turns]
+    first, image, *rest, field = refs[turns:]
     image_packs, faces_out = rest[:turns], rest[turns:]
-    gather_far(hours, faces, counts, plan, hour, stiffness, own, packs, arrived, near_part, field)
+    gather_far(hours, faces, counts, hour, own, packs, late, near_part, field)
     for b in range(first.shape[0]):
         once = couple(hours, coupling[0], field[b])
         first[b] = once
         image[b] = couple(hours, coupling[0], once)
     pack_lanes(hours, hour[0], image, image_packs)
-    pack_faces(faces, image, [plan[n] for n in range(PLUS)], faces_out)
-
-
-def moments_body(hours, faces, counts, plan, hour, right, first, second, own, out):
+    pack_faces(faces, image, EARLY, faces_out)
+
+
+def moments_body(hours, faces, counts, hour, right, first, second, own, out):
     slots = own.shape[0] // PLUS
     sums = [jnp.zeros(right.shape[1:], F32) for _ in range(4)]
     for b in range(right.shape[0]):
@@ -212,7 +225,7 @@
         sums[2] += image * image
         sums[3] += image * second[b]
     for n in range(PLUS):
-        e = plan[PLUS + n] ^ 1
+        e = EARLY[n] ^ 1
         for f in range(slots):
             weight = jnp.where(f < counts[0, e], 2.0, 0.0)
             sums[3] += weight * (first[faces[0, f, e]] * own[n * slots + f])
@@ -223,12 +236,12 @@
 
 
 def close_body(
-    hours, parts, faces, counts, plan, hour, stiffness, right, first, near_part, own, *refs
+    hours, parts, faces, counts, hour, right, first, near_part, own, late, *refs
 ):
     turns = hours - 1
     sums, refs = refs[:parts], refs[parts:]
-    first_packs, packs, arrived = refs[:turns], refs[turns : 2 * turns], refs[2 * turns :][:PLUS]
-    solution, residual, field = refs[2 * turns + PLUS :]
+    first_packs, packs = refs[:turns], refs[turns : 2 * turns]
+    solution, residual, field = refs[2 * turns :]
     moment = total([s[...] for s in sums])
     m0, m1, m2, m3 = (moment[k : k + 1] for k in range(4))
     alpha = m0 / m1
@@ -237,7 +250,7 @@
     step = norm / (lift * lift * m1 - 2.0 * lift * alpha * m2 + alpha * alpha * m3)
     on_right = alpha + step * lift
     on_first = step * alpha
-    gather_far(hours, faces, counts, plan, hour, stiffness, own, packs, arrived, near_part, field)
+    gather_far(hours, faces, counts, hour, own, packs, late, near_part, field)
     for b in range(right.shape[0]):
         start = right[b]
         image = merge_lanes(hours, hour[0], first[b], first_packs, b)
@@ -257,33 +270,10 @@
     return lax.ppermute(value, axes, route)
 
 
-def paired(stride):
-    return stride == 3 and lax.axis_size("rep") == 2
-
-
-def face_plan(stride):
-    if not paired(stride):
-        return jnp.array([2, 0, 4, 2, 0, 4], jnp.int32)
-    odd = lax.axis_index("rep") == 1
-    near, long = jnp.where(odd, 0, 4), jnp.where(odd, 4, 0)
-    two = jnp.int32(2)
-    return jnp.stack([two, near, long, two, long, near]).astype(jnp.int32)
-
-
-def send_faces(outgoing, stride, sign):
-    mesh, rep = (lax.axis_size(axis) for axis in SPACE)
-    count = mesh * rep
-    if not paired(stride):
-        return [
-            shifted(v, SPACE, (count,), (sign * d,)) for v, d in zip(outgoing, (2, 1, stride))
-        ]
-    both, single = outgoing
-    slots = both.shape[0] // 2
-    hop = (1, 3) if sign > 0 else (-3, -1)
-    both = shifted(both, ("mesh",), (mesh,), (sign,))
-    single = lax.ppermute(single, SPACE, [(i, (i + hop[i % 2]) % count) for i in range(count)])
-    relayed = shifted(both[slots:], ("rep",), (rep,), (1,))
-    return [both, relayed, single]
+def send_faces(outgoing, offsets, opposite):
+    count = lax.axis_size(SPACE)
+    steps = [offsets[e ^ opposite] for e in EARLY]
+    return [shifted(v, SPACE, (count,), (d,)) for v, d in zip(outgoing, steps)]
 
 
 def send_lanes(packs):
@@ -321,10 +311,9 @@
     faces = jnp.swapaxes(face_blocks, 1, 2)
     columns = jnp.swapaxes(near_columns, 0, 1)
     counts = face_counts
-    plan = face_plan(stride)
+    offsets = (1, -1, 2, -2, stride, -stride)
     field = struct(*right.shape)
-    sent = [2 * slots, slots] if paired(stride) else [slots] * PLUS
-    face = [struct(n, width, lanes) for n in sent]
+    face = [struct(slots, width, lanes)] * PLUS
     pack = [struct(blocks // hours, width, lanes)] * (hours - 1)
     product = struct(PLUS * slots, width, lanes)
     product_pack = [struct(product.shape[0] // hours, width, lanes)] * (hours - 1)
@@ -334,55 +323,66 @@
     def body(function, *sizes):
         return functools.partial(function, hours, *sizes)
 
-    def early_products(early, after):
+    def early_products(early, weight):
         own, *packs = call(
-            body(early_body), [product] + product_pack, [plan, hour], [stiffness, *early, *after]
+            body(early_body),
+            [product] + product_pack,
+            [hour],
+            [stiffness, *early],
+            weight=weight,
         )
         return own, packs
 
-    outs = call(body(open_body), pack + face, [faces, plan, hour], [right])
+    def late_products(late, after, weight):
+        return call(late_body, product, [], [stiffness, *late, *after], weight=weight)
+
+    outs = call(body(open_body), pack + face, [faces, hour], [right])
     packs = send_lanes(outs[:turns])
-    early = send_faces(outs[turns:], stride, 1)
+    early = send_faces(outs[turns:], offsets, 0)
     probe_right, *outgoing = call(
-        body(turn_body, 0), [field] + face, [faces, plan, hour], [right, early[-1], *packs]
-    )
-    arrived = send_faces(outgoing, stride, -1)
+        body(turn_body, 0), [field] + face, [faces, hour], [right, *packs]
+    )
+    arrived = send_faces(outgoing, offsets, 1)
     stiffness = call(
         split_body, struct(headings * slots, width, 3 * width, dtype=BF16), [], [far_stiffness]
     )
     (near_part,) = near(columns, kappa_sq, near_stiffness, [probe_right])
-    own, packs = early_products(early, [near_part, arrived[-1]])
+    own, packs = early_products(early, ORDER[0])
     packs = send_lanes(packs)
+    late = late_products(arrived, [], ORDER[1])
     first, image, *outs = call(
         body(middle_body),
         [field, field] + pack + face,
-        [faces, counts, plan, hour, time_coupling],
-        [stiffness, near_part, own, *packs, *arrived],
+        [faces, counts, hour, time_coupling],
+        [near_part, own, late, *packs],
         spare,
     )
 
     packs = send_lanes(outs[:turns])
-    early = send_faces(outs[turns:], stride, 1)
+    early = send_faces(outs[turns:], offsets, 0)
     hour_image, *outs = call(
-        body(turn_body, 1), [field] + pack + face, [faces, plan, hour], [image, early[-1], *packs, first]
+        body(turn_body, 1), [field] + pack + face, [faces, hour], [image, *packs, first]
     )
     first_packs = send_lanes(outs[:turns])
-    arrived = send_faces(outs[turns:], stride, -1)
+    arrived = send_faces(outs[turns:], offsets, 1)
     near_probe, near_hour = near(columns, kappa_sq, near_stiffness, [image, hour_image])
-    own, packs = early_products(early, [near_hour, arrived[-1]])
+    own, packs = early_products(early, ORDER[2])
     sums = call(
         body(moments_body),
         struct(8, lanes),
-        [faces, counts, plan, hour],
+        [faces, counts, hour],
         [probe_right, first, near_probe, own],
     )
-    sums = everyone(total(everyone(sums, ("tm", "rep"))), ("mesh",))
+    for axis in ("rep", "tm"):
+        sums = total(everyone(sums, (axis,)))
+    sums = everyone(sums, ("mesh",))
     packs = send_lanes(packs)
+    late = late_products(arrived, first_packs, ORDER[3])
     solution_field, residual = call(
         body(close_body, len(sums)),
         [field, field],
-        [faces, counts, plan, hour],
-        [stiffness, right, first, near_hour, own, *sums, *first_packs, *packs, *arrived],
+        [faces, counts, hour],
+        [right, first, near_hour, own, late, *sums, *first_packs, *packs],
         spare,
     )
     return (solution_field[None], residual[None])

time: 77.3 us -> 69.7 us (0.902)
  waiting for transfers between devices: 33.9 us -> 18.4 us
  starting transfers between devices: 25.5 us -> 33.3 us
  local copies, waits for them, and re-layouts: 2.97 us -> 1.76 us
    ppermute x4 -> x0, waiting for transfers between devices: 24.4 us -> none  [send_faces(): lax.ppermute(single, SPACE, [(i, (i + hop[i % 2]) % count) for i in range...]
    ppermute x19 -> x22, waiting for transfers between devices: 9.51 us -> 18.4 us  [shifted(): return lax.ppermute(value, axes, route)]
    ppermute x19 -> x22, starting transfers between devices: 25.5 us -> 33.3 us  [shifted(): return lax.ppermute(value, axes, route)]
    unnamed x18 -> x24, local copies, waits for them, and re-layouts: 2.85 us -> 1.76 us
    pallas_call x11 -> x13, Pallas kernels: 13.2 us -> 13.9 us  [call(): pl.pallas_call(body, out_shape=outs, in_specs=[pl.BlockSpec(memory_space=...]
  transfers between devices with their start and end apart: 23 -> 22, of which waited for: 9 -> 11; matrix products, arithmetic and copies ran while one was open for 0% -> 1% of each run, Pallas kernels for 11% -> 13%
where the time goes in v4:
time: 69.7 us; the launch traced here: 69.5 us
  starting transfers between devices  33.3 us (48%)
  waiting for transfers between devices  18.4 us (26%)
  Pallas kernels  13.9 us (20%)
  local copies, waits for them, and re-layouts  1.76 us (3%)
  between operations  1.44 us (2%)
    ppermute x22, starting transfers between devices, shifted(): return lax.ppermute(value, axes, route)  33.3 us
    ppermute x22, waiting for transfers between devices, shifted(): return lax.ppermute(value, axes, route)  18.4 us
    pallas_call x13, Pallas kernels, call(): pl.pallas_call(body, out_shape=outs, in_specs=[pl.BlockSpec(memory_space=...  13.9 us
    unnamed x24, local copies, waits for them, and re-layouts  1.76 us
  transfers between devices with their start and end apart: 22, of which 11 were waited for; matrix products, arithmetic and copies ran while one was open for 1% of the time, Pallas kernels for 13%

profile of v4, /device:TPU:0, one launch (start us, length us, event | category | flops | bytes accessed | tf_op | source)
XLA Modules:
  0.0 69.5 jit_solution(7626383893936734954)
XLA Ops:
  0.6 0.0 copy-start.1
  0.6 1.0 %copy-done.1 = f32[1,16,64,128]{3,2,1,0:T(8,128)S(1)} copy-done((f32[1,16,64,128]{3,2,1,0:T(8,128)S(1)}, f32[1,16,64,128]{3,2,1,0:T(8,128)}, u32[]{:S(2)}) %copy-start.1) | copy-done | bytes 524312
  1.7 0.7 copy-done.6
  2.4 0.8 %shard_map.95 = (f32[8,64,128]{2,1,0:T(8,128)S(1)}, f32[4,64,128]{2,1,0:T(8,128)S(1)}, f32[4,64,128]{2,1,0:T(8,128)S(1)}, f32[4,64,128]{2,1,0:T(8,128)S(1)}) custom-call(s32[1,4,6]{2,1,0:T(4,128)S(1)} %bitcast.9, s32[1]{0:T(128)} %bitcast.1.hour, f32[16,64,128]{2,1,0:T(8,128)S(1)} %bitcast.6), custom_call_target="tpu_custom_call" | custom-call | flops 1024 | bytes 1024 | tf_op jit(solution)/shard_map/pallas_call | solution.py:24
  3.1 3.0 %collective-permute-start = (f32[8,64,128]{2,1,0:T(8,128)S(1)}, f32[8,64,128]{2,1,0:T(8,128)S(1)}, u32[]{:S(2)}, u32[]{:S(2)}) collective-permute-start(f32[8,64,128]{2,1,0:T(8,128)S(1)} %get-tuple-element.29), channel_id=1, source_target_pairs={{0,2},{2,0},{1,3},{3,1},{4,6},{6,4},{5,7},{7,5},{8,10},{10,8},{9,1... | collective-permute-start | bytes 786440 | tf_op jit(solution)/shard_map/ppermute | solution.py:270
  6.1 0.7 %collective-permute-start.1 = (f32[4,64,128]{2,1,0:T(8,128)S(1)}, f32[4,64,128]{2,1,0:T(8,128)S(1)}, u32[]{:S(2)}, u32[]{:S(2)}) collective-permute-start(f32[4,64,128]{2,1,0:T(8,128)S(1)} %get-tuple-element.31), channel_id=1, source_target_pairs={{0,5},{1,8},{4,9},{5,12},{8,13},{9,0},{12,1},{13,4},{2,7},{3,10},{... | collective-permute-start | bytes 393224 | tf_op jit(solution)/shard_map/ppermute | solution.py:270
  6.9 1.6 %collective-permute-start.2 = (f32[4,64,128]{2,1,0:T(8,128)S(1)}, f32[4,64,128]{2,1,0:T(8,128)S(1)}, u32[]{:S(2)}, u32[]{:S(2)}) collective-permute-start(f32[4,64,128]{2,1,0:T(8,128)S(1)} %get-tuple-element.32), channel_id=1, source_target_pairs={{0,4},{1,5},{4,8},{5,9},{8,12},{9,13},{12,0},{13,1},{2,6},{3,7},{6... | collective-permute-start | bytes 393224 | tf_op jit(solution)/shard_map/ppermute | solution.py:270
  8.5 1.7 %collective-permute-start.3 = (f32[4,64,128]{2,1,0:T(8,128)S(1)}, f32[4,64,128]{2,1,0:T(8,128)S(1)}, u32[]{:S(2)}, u32[]{:S(2)}) collective-permute-start(f32[4,64,128]{2,1,0:T(8,128)S(1)} %get-tuple-element.33), channel_id=1, source_target_pairs={{0,1},{1,4},{4,5},{5,8},{8,9},{9,12},{12,13},{13,0},{2,3},{3,6},{6... | collective-permute-start | bytes 393224 | tf_op jit(solution)/shard_map/ppermute | solution.py:270
  10.2 2.3 %collective-permute-done.refs_0_ = f32[8,64,128]{2,1,0:T(8,128)S(1)} collective-permute-done((f32[8,64,128]{2,1,0:T(8,128)S(1)}, f32[8,64,128]{2,1,0:T(8,128)S(1)}, u32[]{:S(2)}, u32[]{:S(2)}) %collective-permute-start) | collective-permute-done | bytes 262176 | tf_op jit(solution)/shard_map/ppermute | solution.py:270
  12.4 0.8 %shard_map.96 = (f32[16,64,128]{2,1,0:T(8,128)S(1)}, f32[4,64,128]{2,1,0:T(8,128)S(1)}, f32[4,64,128]{2,1,0:T(8,128)S(1)}, f32[4,64,128]{2,1,0:T(8,128)S(1)}) custom-call(s32[1,4,6]{2,1,0:T(4,128)S(1)} %bitcast.10, s32[1]{0:T(128)} %bitcast.1.hour, f32[16,64,128]{2,1,0:T(8,128)S(1)} %bitcast.7, f32[8,64,128]{2,1,0:T(8,128)S(1)} %collective-permute-done.refs_0_), custom_call_target="tpu_custom_call" | custom-call | flops 1024 | bytes 1024 | tf_op jit(solution)/shard_map/pallas_call | solution.py:24
  13.3 1.5 %collective-permute-start.4 = (f32[4,64,128]{2,1,0:T(8,128)S(1)}, f32[4,64,128]{2,1,0:T(8,128)S(1)}, u32[]{:S(2)}, u32[]{:S(2)}) collective-permute-start(f32[4,64,128]{2,1,0:T(8,128)S(1)} %get-tuple-element.35), channel_id=1, source_target_pairs={{0,9},{1,12},{4,13},{5,0},{8,1},{9,4},{12,5},{13,8},{2,11},{3,14},... | collective-permute-start | bytes 393224 | tf_op jit(solution)/shard_map/ppermute | solution.py:270
  14.7 2.5 %collective-permute-start.5 = (f32[4,64,128]{2,1,0:T(8,128)S(1)}, f32[4,64,128]{2,1,0:T(8,128)S(1)}, u32[]{:S(2)}, u32[]{:S(2)}) collective-permute-start(f32[4,64,128]{2,1,0:T(8,128)S(1)} %get-tuple-element.36), channel_id=1, source_target_pairs={{0,12},{1,13},{4,0},{5,1},{8,4},{9,5},{12,8},{13,9},{2,14},{3,15},... | collective-permute-start | bytes 393224 | tf_op jit(solution)/shard_map/ppermute | solution.py:270
  17.2 1.6 %collective-permute-done.1.refs_0_ = f32[4,64,128]{2,1,0:T(8,128)S(1)} collective-permute-done((f32[4,64,128]{2,1,0:T(8,128)S(1)}, f32[4,64,128]{2,1,0:T(8,128)S(1)}, u32[]{:S(2)}, u32[]{:S(2)}) %collective-permute-start.1) | collective-permute-done | bytes 131104 | tf_op jit(solution)/shard_map/ppermute | solution.py:270
  18.8 0.0 collective-permute-start.6
  18.8 0.0 copy-done.5
  18.8 0.2 shard_map.98.stiffness
  19.6 0.0 collective-permute-done.2.refs_1_
  19.6 0.0 collective-permute-done.3.refs_2_
  19.6 0.4 shard_map.99
  20.1 0.3 collective-permute-start.7
  20.3 1.6 %shard_map.97.near_part = f32[16,64,128]{2,1,0:T(8,128)S(1)} custom-call(s32[6,16]{1,0:T(8,128)S(1)} %bitcast.15, f32[16,64]{1,0:T(8,128)S(1)} %copy-done.8, f32[16,64,384]{2,1,0:T(8,128)S(1)} %copy-done, f32[16,64,128]{2,1,0:T(8,128)S(1)} %get-tuple-element.30.refs_0_.right), custom_call_target="tpu_custom_call" | custom-call | flops 1024 | bytes 1024 | tf_op jit(solution)/shard_map/pallas_call | solution.py:24
  22.0 0.0 copy-start.7
  22.0 0.0 copy-start.10
  22.0 0.6 collective-permute-done.4.refs_0_
  22.6 0.2 collective-permute-done.5.refs_1_
  22.8 0.5 collective-permute-done.6.refs_2_
  23.3 0.3 shard_map.100.late
  23.6 3.8 %collective-permute-done.7.refs_0_ = f32[6,64,128]{2,1,0:T(8,128)S(1)} collective-permute-done((f32[6,64,128]{2,1,0:T(8,128)S(1)}, f32[6,64,128]{2,1,0:T(8,128)S(1)}, u32[]{:S(2)}, u32[]{:S(2)}) %collective-permute-start.7) | collective-permute-done | bytes 196640 | tf_op jit(solution)/shard_map/ppermute | solution.py:270
  27.5 1.6 %shard_map.101 = (f32[16,64,128]{2,1,0:T(8,128)S(1)}, f32[16,64,128]{2,1,0:T(8,128)S(1)}, f32[8,64,128]{2,1,0:T(8,128)S(1)}, f32[4,64,128]{2,1,0:T(8,128)S(1)}, ...) custom-call(s32[1,4,6]{2,1,0:T(4,128)S(1)} %bitcast.11, s32[1,6]{1,0:T(1,128)S(1)} %copy-done.10, s32[1]{0:T(128)} %bitcast.1.hour, ...), custom_call_target="tpu_custom_call" | custom-call | flops 1024 | bytes 1024 | tf_op jit(solution)/shard_map/pallas_call | solution.py:24
  29.1 0.4 collective-permute-start.8
  29.4 2.6 %collective-permute-start.9 = (f32[4,64,128]{2,1,0:T(8,128)S(1)}, f32[4,64,128]{2,1,0:T(8,128)S(1)}, u32[]{:S(2)}, u32[]{:S(2)}) collective-permute-start(f32[4,64,128]{2,1,0:T(8,128)S(1)} %get-tuple-element.44), channel_id=1, source_target_pairs={{0,5},{1,8},{4,9},{5,12},{8,13},{9,0},{12,1},{13,4},{2,7},{3,10},{... | collective-permute-start | bytes 393224 | tf_op jit(solution)/shard_map/ppermute | solution.py:270
  32.0 0.0 collective-permute-start.10
  32.0 5.1 %collective-permute-done.8.refs_0_ = f32[8,64,128]{2,1,0:T(8,128)S(1)} collective-permute-done((f32[8,64,128]{2,1,0:T(8,128)S(1)}, f32[8,64,128]{2,1,0:T(8,128)S(1)}, u32[]{:S(2)}, u32[]{:S(2)}) %collective-permute-start.8) | collective-permute-done | bytes 262176 | tf_op jit(solution)/shard_map/ppermute | solution.py:270
  37.1 0.9 %shard_map.102 = (f32[16,64,128]{2,1,0:T(8,128)S(1)}, f32[8,64,128]{2,1,0:T(8,128)S(1)}, f32[4,64,128]{2,1,0:T(8,128)S(1)}, f32[4,64,128]{2,1,0:T(8,128)S(1)}, f32[4,64,128]{2,1,0:T(8,128)S(1)}) custom-call(s32[1,4,6]{2,1,0:T(4,128)S(1)} %bitcast.12, s32[1]{0:T(128)} %bitcast.1.hour, f32[16,64,128]{2,1,0:T(8,128)S(1)} %get-tuple-element.40.field.refs_0_, ...), custom_call_target="tpu_custom_call" | custom-call | flops 1024 | bytes 1024 | tf_op jit(solution)/shard_map/pallas_call | solution.py:24
  38.0 0.4 collective-permute-start.15
  38.5 1.7 %collective-permute-start.11 = (f32[4,64,128]{2,1,0:T(8,128)S(1)}, f32[4,64,128]{2,1,0:T(8,128)S(1)}, u32[]{:S(2)}, u32[]{:S(2)}) collective-permute-start(f32[4,64,128]{2,1,0:T(8,128)S(1)} %get-tuple-element.46), channel_id=1, source_target_pairs={{0,1},{1,4},{4,5},{5,8},{8,9},{9,12},{12,13},{13,0},{2,3},{3,6},{6... | collective-permute-start | bytes 393224 | tf_op jit(solution)/shard_map/ppermute | solution.py:270
  40.2 0.0 collective-permute-start.12
  40.2 0.0 collective-permute-done.9.refs_0_
  40.2 8.9 %collective-permute-start.13 = (f32[4,64,128]{2,1,0:T(8,128)S(1)}, f32[4,64,128]{2,1,0:T(8,128)S(1)}, u32[]{:S(2)}, u32[]{:S(2)}) collective-permute-start(f32[4,64,128]{2,1,0:T(8,128)S(1)} %get-tuple-element.49), channel_id=1, source_target_pairs={{0,12},{1,13},{4,0},{5,1},{8,4},{9,5},{12,8},{13,9},{2,14},{3,15},... | collective-permute-start | bytes 393224 | tf_op jit(solution)/shard_map/ppermute | solution.py:270
  49.1 0.0 collective-permute-done.10.refs_1_
  49.1 0.0 collective-permute-start.14
  49.1 0.0 collective-permute-done.11.refs_2_
  49.1 1.1 %shard_map.104 = (f32[12,64,128]{2,1,0:T(8,128)S(1)}, f32[6,64,128]{2,1,0:T(8,128)}) custom-call(s32[1]{0:T(128)} %bitcast.1.hour, bf16[24,64,192]{2,1,0:T(8,128)(2,1)S(1)} %shard_map.98.stiffness, f32[4,64,128]{2,1,0:T(8,128)S(1)} %collective-permute-done.9.refs_0_, f32[4,64,128]{2,1,0:T(8,128)S(1)} %collective-permute-done.10.refs_1_, ...), custom_call_target="tpu_custom_call" | custom-call | flops 1024 | bytes 1024 | tf_op jit(solution)/shard_map/pallas_call | solution.py:24
  50.2 2.7 %shard_map.103 = (f32[16,64,128]{2,1,0:T(8,128)S(1)}, f32[16,64,128]{2,1,0:T(8,128)S(1)}) custom-call(s32[6,16]{1,0:T(8,128)S(1)} %bitcast.16, f32[16,64]{1,0:T(8,128)S(1)} %copy-done.8, f32[16,64,384]{2,1,0:T(8,128)S(1)} %copy-done, f32[16,64,128]{2,1,0:T(8,128)S(1)} %get-tuple-element.40.field.refs_0_, f32[16,64,128]{2,1,0:T(8,128)S(1)} %get-tuple-element.42.refs_1_), custom_call_target="tpu_custom_call" | custom-call | flops 1024 | bytes 1024 | tf_op jit(solution)/shard_map/pallas_call | solution.py:24
  52.9 0.8 %shard_map.106 = f32[8,128]{1,0:T(8,128)S(1)} custom-call(s32[1,4,6]{2,1,0:T(4,128)S(1)} %bitcast.13, s32[1,6]{1,0:T(1,128)S(1)} %copy-done.10, s32[1]{0:T(128)} %bitcast.1.hour, f32[16,64,128]{2,1,0:T(8,128)S(1)} %get-tuple-element.30.refs_0_.right, f32[16,64,128]{2,1,0:T(8,128)S(1)} %get-tuple-element.39.refs_1_.first, ...), custom_call_target="tpu_custom_call" | custom-call | flops 1024 | bytes 1024 | tf_op jit(solution)/shard_map/pallas_call | solution.py:24
  53.7 0.5 collective-permute-start.16
  54.2 0.8 %collective-permute-done.16 = f32[8,128]{1,0:T(8,128)S(1)} collective-permute-done((f32[8,128]{1,0:T(8,128)S(1)}, f32[8,128]{1,0:T(8,128)S(1)}, u32[]{:S(2)}, u32[]{:S(2)}) %collective-permute-start.16) | collective-permute-done | bytes 4128 | tf_op jit(solution)/shard_map/ppermute | solution.py:270
  55.0 1.5 %collective-permute-start.17 = (f32[8,128]{1,0:T(8,128)S(1)}, f32[8,128]{1,0:T(8,128)S(1)}, u32[]{:S(2)}, u32[]{:S(2)}) collective-permute-start(f32[8,128]{1,0:T(8,128)S(1)} %add.6), channel_id=1, source_target_pairs={{0,2},{2,0},{1,3},{3,1},{4,6},{6,4},{5,7},{7,5},{8,10},{10,8},{9,1... | collective-permute-start | bytes 12296 | tf_op jit(solution)/shard_map/ppermute | solution.py:270
  56.6 2.1 %collective-permute-done.17 = f32[8,128]{1,0:T(8,128)S(1)} collective-permute-done((f32[8,128]{1,0:T(8,128)S(1)}, f32[8,128]{1,0:T(8,128)S(1)}, u32[]{:S(2)}, u32[]{:S(2)}) %collective-permute-start.17) | collective-permute-done | bytes 4128 | tf_op jit(solution)/shard_map/ppermute | solution.py:270
  58.6 1.5 %collective-permute-start.21 = (f32[6,64,128]{2,1,0:T(8,128)}, f32[6,64,128]{2,1,0:T(8,128)}, u32[]{:S(2)}, u32[]{:S(2)}) collective-permute-start(f32[6,64,128]{2,1,0:T(8,128)} %get-tuple-element.53), channel_id=1, source_target_pairs={{0,2},{2,0},{1,3},{3,1},{4,6},{6,4},{5,7},{7,5},{8,10},{10,8},{9,1... | collective-permute-start | bytes 589832 | tf_op jit(solution)/shard_map/ppermute | solution.py:270
  60.2 0.6 add.7.refs_0_
  60.8 0.0 collective-permute-done.12.refs_0_
  60.8 0.1 collective-permute-start.18
  60.9 0.0 collective-permute-done.13.refs_1_
  60.9 1.5 %collective-permute-start.19 = (f32[8,128]{1,0:T(8,128)}, f32[8,128]{1,0:T(8,128)}, u32[]{:S(2)}, u32[]{:S(2)}) collective-permute-start(f32[8,128]{1,0:T(8,128)} %add.7.refs_0_), channel_id=1, source_target_pairs={{0,8},{4,12},{8,0},{12,4},{1,9},{5,13},{9,1},{13,5},{2,10},{6,14},... | collective-permute-start | bytes 12296 | tf_op jit(solution)/shard_map/ppermute | solution.py:270
  62.4 0.0 collective-permute-done.14.refs_2_
  62.4 2.9 %collective-permute-start.20 = (f32[8,128]{1,0:T(8,128)}, f32[8,128]{1,0:T(8,128)}, u32[]{:S(2)}, u32[]{:S(2)}) collective-permute-start(f32[8,128]{1,0:T(8,128)} %add.7.refs_0_), channel_id=1, source_target_pairs={{0,12},{4,0},{8,4},{12,8},{1,13},{5,1},{9,5},{13,9},{2,14},{6,2},{... | collective-permute-start | bytes 12296 | tf_op jit(solution)/shard_map/ppermute | solution.py:270
  65.3 0.0 collective-permute-done.15.refs_3_.refs_4_
  65.3 0.3 shard_map.105.late
  65.6 0.9 %collective-permute-done.18.refs_1_ = f32[8,128]{1,0:T(8,128)} collective-permute-done((f32[8,128]{1,0:T(8,128)}, f32[8,128]{1,0:T(8,128)}, u32[]{:S(2)}, u32[]{:S(2)}) %collective-permute-start.18) | collective-permute-done | bytes 4128 | tf_op jit(solution)/shard_map/ppermute | solution.py:270
  66.5 0.0 collective-permute-done.19.refs_2_
  66.5 0.6 collective-permute-done.20.refs_3_
  67.1 0.0 collective-permute-done.21.refs_5_
  67.1 2.4 %shard_map.107 = (f32[16,64,128]{2,1,0:T(8,128)}, f32[16,64,128]{2,1,0:T(8,128)}) custom-call(s32[1,4,6]{2,1,0:T(4,128)S(1)} %bitcast.14, s32[1,6]{1,0:T(1,128)S(1)} %copy-done.11, s32[1]{0:T(128)} %bitcast.1.hour, f32[16,64,128]{2,1,0:T(8,128)S(1)} %bitcast.8, f32[16,64,128]{2,1,0:T(8,128)S(1)} %get-tuple-element.39.refs_1_.first, ...), custom_call_target="tpu_custom_call" | custom-call | flops 1024 | bytes 1024 | tf_op jit(solution)/shard_map/pallas_call | solution.py:24
  (19 shorter events, 0.0 us)
Async XLA Ops:
  0.6 1.0 %copy-start.1 = (f32[1,16,64,128]{3,2,1,0:T(8,128)S(1)}, f32[1,16,64,128]{3,2,1,0:T(8,128)}, u32[]{:S(2)}) copy-start(f32[1,16,64,128]{3,2,1,0:T(8,128)} %param.8) | copy-start | bytes 1572868
  1.7 0.7 copy-start.6
  2.4 16.4 %copy-start.5 = (f32[1,64,1536]{2,1,0:T(8,128)S(1)}, f32[1,64,1536]{2,1,0:T(8,128)}, u32[]{:S(2)}) copy-start(f32[1,64,1536]{2,1,0:T(8,128)} %stiffness.4) | copy-start | bytes 1179652
  3.1 9.3 %collective-permute-start = (f32[8,64,128]{2,1,0:T(8,128)S(1)}, f32[8,64,128]{2,1,0:T(8,128)S(1)}, u32[]{:S(2)}, u32[]{:S(2)}) collective-permute-start(f32[8,64,128]{2,1,0:T(8,128)S(1)} %get-tuple-element.29), channel_id=1, source_target_pairs={{0,2},{2,0},{1,3},{3,1},{4,6},{6,4},{5,7},{7,5},{8,10},{10,8},{9,1... | collective-permute-start | bytes 786440 | tf_op jit(solution)/shard_map/ppermute | solution.py:270
  6.1 12.6 %collective-permute-start.1 = (f32[4,64,128]{2,1,0:T(8,128)S(1)}, f32[4,64,128]{2,1,0:T(8,128)S(1)}, u32[]{:S(2)}, u32[]{:S(2)}) collective-permute-start(f32[4,64,128]{2,1,0:T(8,128)S(1)} %get-tuple-element.31), channel_id=1, source_target_pairs={{0,5},{1,8},{4,9},{5,12},{8,13},{9,0},{12,1},{13,4},{2,7},{3,10},{... | collective-permute-start | bytes 393224 | tf_op jit(solution)/shard_map/ppermute | solution.py:270
  6.9 12.7 %collective-permute-start.2 = (f32[4,64,128]{2,1,0:T(8,128)S(1)}, f32[4,64,128]{2,1,0:T(8,128)S(1)}, u32[]{:S(2)}, u32[]{:S(2)}) collective-permute-start(f32[4,64,128]{2,1,0:T(8,128)S(1)} %get-tuple-element.32), channel_id=1, source_target_pairs={{0,4},{1,5},{4,8},{5,9},{8,12},{9,13},{12,0},{13,1},{2,6},{3,7},{6... | collective-permute-start | bytes 393224 | tf_op jit(solution)/shard_map/ppermute | solution.py:270
  8.5 11.9 %copy-start = (f32[16,64,384]{2,1,0:T(8,128)S(1)}, f32[16,64,384]{2,1,0:T(8,128)}, u32[]{:S(2)}) copy-start(f32[16,64,384]{2,1,0:T(8,128)} %stiffness.5) | copy-start | bytes 4718596
  8.5 11.9 %copy-start.8 = (f32[16,64]{1,0:T(8,128)S(1)}, f32[16,64]{1,0:T(8,128)}, u32[]{:S(2)}) copy-start(f32[16,64]{1,0:T(8,128)} %kappa.3) | copy-start | bytes 12292
  8.5 11.9 %copy-start.9 = (s32[16,6]{0,1:T(8,128)S(1)}, s32[16,6]{0,1:T(8,128)}, u32[]{:S(2)}) copy-start(s32[16,6]{0,1:T(8,128)} %param.13) | copy-start | bytes 1156
  8.5 11.2 %collective-permute-start.3 = (f32[4,64,128]{2,1,0:T(8,128)S(1)}, f32[4,64,128]{2,1,0:T(8,128)S(1)}, u32[]{:S(2)}, u32[]{:S(2)}) collective-permute-start(f32[4,64,128]{2,1,0:T(8,128)S(1)} %get-tuple-element.33), channel_id=1, source_target_pairs={{0,1},{1,4},{4,5},{5,8},{8,9},{9,12},{12,13},{13,0},{2,3},{3,6},{6... | collective-permute-start | bytes 393224 | tf_op jit(solution)/shard_map/ppermute | solution.py:270
  13.3 9.3 %collective-permute-start.4 = (f32[4,64,128]{2,1,0:T(8,128)S(1)}, f32[4,64,128]{2,1,0:T(8,128)S(1)}, u32[]{:S(2)}, u32[]{:S(2)}) collective-permute-start(f32[4,64,128]{2,1,0:T(8,128)S(1)} %get-tuple-element.35), channel_id=1, source_target_pairs={{0,9},{1,12},{4,13},{5,0},{8,1},{9,4},{12,5},{13,8},{2,11},{3,14},... | collective-permute-start | bytes 393224 | tf_op jit(solution)/shard_map/ppermute | solution.py:270
  14.7 8.1 %collective-permute-start.5 = (f32[4,64,128]{2,1,0:T(8,128)S(1)}, f32[4,64,128]{2,1,0:T(8,128)S(1)}, u32[]{:S(2)}, u32[]{:S(2)}) collective-permute-start(f32[4,64,128]{2,1,0:T(8,128)S(1)} %get-tuple-element.36), channel_id=1, source_target_pairs={{0,12},{1,13},{4,0},{5,1},{8,4},{9,5},{12,8},{13,9},{2,14},{3,15},... | collective-permute-start | bytes 393224 | tf_op jit(solution)/shard_map/ppermute | solution.py:270
  18.8 4.5 %collective-permute-start.6 = (f32[4,64,128]{2,1,0:T(8,128)S(1)}, f32[4,64,128]{2,1,0:T(8,128)S(1)}, u32[]{:S(2)}, u32[]{:S(2)}) collective-permute-start(f32[4,64,128]{2,1,0:T(8,128)S(1)} %get-tuple-element.37), channel_id=1, source_target_pairs={{0,13},{1,0},{4,1},{5,4},{8,5},{9,8},{12,9},{13,12},{2,15},{3,2},{... | collective-permute-start | bytes 393224 | tf_op jit(solution)/shard_map/ppermute | solution.py:270
  20.1 7.4 %collective-permute-start.7 = (f32[6,64,128]{2,1,0:T(8,128)S(1)}, f32[6,64,128]{2,1,0:T(8,128)S(1)}, u32[]{:S(2)}, u32[]{:S(2)}) collective-permute-start(f32[6,64,128]{2,1,0:T(8,128)S(1)} %get-tuple-element.38), channel_id=1, source_target_pairs={{0,2},{2,0},{1,3},{3,1},{4,6},{6,4},{5,7},{7,5},{8,10},{10,8},{9,1... | collective-permute-start | bytes 589832 | tf_op jit(solution)/shard_map/ppermute | solution.py:270
  22.0 5.5 %copy-start.7 = (s32[1,6,4]{1,2,0:T(4,128)S(1)}, s32[1,6,4]{1,2,0:T(4,128)}, u32[]{:S(2)}) copy-start(s32[1,6,4]{1,2,0:T(4,128)} %param.14) | copy-start | bytes 292
  22.0 5.5 %copy-start.10 = (s32[1,6]{1,0:T(1,128)S(1)}, s32[1,6]{1,0:T(1,128)}, u32[]{:S(2)}) copy-start(s32[1,6]{1,0:T(1,128)} %counts.5) | copy-start | bytes 76
  29.1 8.0 %collective-permute-start.8 = (f32[8,64,128]{2,1,0:T(8,128)S(1)}, f32[8,64,128]{2,1,0:T(8,128)S(1)}, u32[]{:S(2)}, u32[]{:S(2)}) collective-permute-start(f32[8,64,128]{2,1,0:T(8,128)S(1)} %get-tuple-element.41), channel_id=1, source_target_pairs={{0,2},{2,0},{1,3},{3,1},{4,6},{6,4},{5,7},{7,5},{8,10},{10,8},{9,1... | collective-permute-start | bytes 786440 | tf_op jit(solution)/shard_map/ppermute | solution.py:270
  29.4 10.8 %collective-permute-start.9 = (f32[4,64,128]{2,1,0:T(8,128)S(1)}, f32[4,64,128]{2,1,0:T(8,128)S(1)}, u32[]{:S(2)}, u32[]{:S(2)}) collective-permute-start(f32[4,64,128]{2,1,0:T(8,128)S(1)} %get-tuple-element.44), channel_id=1, source_target_pairs={{0,5},{1,8},{4,9},{5,12},{8,13},{9,0},{12,1},{13,4},{2,7},{3,10},{... | collective-permute-start | bytes 393224 | tf_op jit(solution)/shard_map/ppermute | solution.py:270
  32.0 17.0 %collective-permute-start.10 = (f32[4,64,128]{2,1,0:T(8,128)S(1)}, f32[4,64,128]{2,1,0:T(8,128)S(1)}, u32[]{:S(2)}, u32[]{:S(2)}) collective-permute-start(f32[4,64,128]{2,1,0:T(8,128)S(1)} %get-tuple-element.45), channel_id=1, source_target_pairs={{0,4},{1,5},{4,8},{5,9},{8,12},{9,13},{12,0},{13,1},{2,6},{3,7},{6... | collective-permute-start | bytes 393224 | tf_op jit(solution)/shard_map/ppermute | solution.py:270
  38.0 27.3 %collective-permute-start.15 = (f32[8,64,128]{2,1,0:T(8,128)S(1)}, f32[8,64,128]{2,1,0:T(8,128)S(1)}, u32[]{:S(2)}, u32[]{:S(2)}) collective-permute-start(f32[8,64,128]{2,1,0:T(8,128)S(1)} %get-tuple-element.51), channel_id=1, source_target_pairs={{0,2},{2,0},{1,3},{3,1},{4,6},{6,4},{5,7},{7,5},{8,10},{10,8},{9,1... | collective-permute-start | bytes 786440 | tf_op jit(solution)/shard_map/ppermute | solution.py:270
  38.5 10.6 %collective-permute-start.11 = (f32[4,64,128]{2,1,0:T(8,128)S(1)}, f32[4,64,128]{2,1,0:T(8,128)S(1)}, u32[]{:S(2)}, u32[]{:S(2)}) collective-permute-start(f32[4,64,128]{2,1,0:T(8,128)S(1)} %get-tuple-element.46), channel_id=1, source_target_pairs={{0,1},{1,4},{4,5},{5,8},{8,9},{9,12},{12,13},{13,0},{2,3},{3,6},{6... | collective-permute-start | bytes 393224 | tf_op jit(solution)/shard_map/ppermute | solution.py:270
  40.2 20.6 %collective-permute-start.12 = (f32[4,64,128]{2,1,0:T(8,128)S(1)}, f32[4,64,128]{2,1,0:T(8,128)S(1)}, u32[]{:S(2)}, u32[]{:S(2)}) collective-permute-start(f32[4,64,128]{2,1,0:T(8,128)S(1)} %get-tuple-element.48), channel_id=1, source_target_pairs={{0,9},{1,12},{4,13},{5,0},{8,1},{9,4},{12,5},{13,8},{2,11},{3,14},... | collective-permute-start | bytes 393224 | tf_op jit(solution)/shard_map/ppermute | solution.py:270
  40.2 20.7 %collective-permute-start.13 = (f32[4,64,128]{2,1,0:T(8,128)S(1)}, f32[4,64,128]{2,1,0:T(8,128)S(1)}, u32[]{:S(2)}, u32[]{:S(2)}) collective-permute-start(f32[4,64,128]{2,1,0:T(8,128)S(1)} %get-tuple-element.49), channel_id=1, source_target_pairs={{0,12},{1,13},{4,0},{5,1},{8,4},{9,5},{12,8},{13,9},{2,14},{3,15},... | collective-permute-start | bytes 393224 | tf_op jit(solution)/shard_map/ppermute | solution.py:270
  49.1 13.3 %collective-permute-start.14 = (f32[4,64,128]{2,1,0:T(8,128)S(1)}, f32[4,64,128]{2,1,0:T(8,128)S(1)}, u32[]{:S(2)}, u32[]{:S(2)}) collective-permute-start(f32[4,64,128]{2,1,0:T(8,128)S(1)} %get-tuple-element.50), channel_id=1, source_target_pairs={{0,13},{1,0},{4,1},{5,4},{8,5},{9,8},{12,9},{13,12},{2,15},{3,2},{... | collective-permute-start | bytes 393224 | tf_op jit(solution)/shard_map/ppermute | solution.py:270
  50.2 3.5 %copy-start.3 = (f32[12,64,128]{2,1,0:T(8,128)}, f32[12,64,128]{2,1,0:T(8,128)S(1)}, u32[]{:S(2)}) copy-start(f32[12,64,128]{2,1,0:T(8,128)S(1)} %get-tuple-element.47.own) | copy-start | bytes 1179652
  53.7 1.3 %collective-permute-start.16 = (f32[8,128]{1,0:T(8,128)S(1)}, f32[8,128]{1,0:T(8,128)S(1)}, u32[]{:S(2)}, u32[]{:S(2)}) collective-permute-start(f32[8,128]{1,0:T(8,128)S(1)} %shard_map.106), channel_id=1, source_target_pairs={{0,1},{1,0},{2,3},{3,2},{4,5},{5,4},{6,7},{7,6},{8,9},{9,8},{10,11... | collective-permute-start | bytes 12296 | tf_op jit(solution)/shard_map/ppermute | solution.py:270
  55.0 3.6 %collective-permute-start.17 = (f32[8,128]{1,0:T(8,128)S(1)}, f32[8,128]{1,0:T(8,128)S(1)}, u32[]{:S(2)}, u32[]{:S(2)}) collective-permute-start(f32[8,128]{1,0:T(8,128)S(1)} %add.6), channel_id=1, source_target_pairs={{0,2},{2,0},{1,3},{3,1},{4,6},{6,4},{5,7},{7,5},{8,10},{10,8},{9,1... | collective-permute-start | bytes 12296 | tf_op jit(solution)/shard_map/ppermute | solution.py:270
  58.6 8.5 %collective-permute-start.21 = (f32[6,64,128]{2,1,0:T(8,128)}, f32[6,64,128]{2,1,0:T(8,128)}, u32[]{:S(2)}, u32[]{:S(2)}) collective-permute-start(f32[6,64,128]{2,1,0:T(8,128)} %get-tuple-element.53), channel_id=1, source_target_pairs={{0,2},{2,0},{1,3},{3,1},{4,6},{6,4},{5,7},{7,5},{8,10},{10,8},{9,1... | collective-permute-start | bytes 589832 | tf_op jit(solution)/shard_map/ppermute | solution.py:270
  60.8 5.7 %collective-permute-start.18 = (f32[8,128]{1,0:T(8,128)}, f32[8,128]{1,0:T(8,128)}, u32[]{:S(2)}, u32[]{:S(2)}) collective-permute-start(f32[8,128]{1,0:T(8,128)} %add.7.refs_0_), channel_id=1, source_target_pairs={{0,4},{4,8},{8,12},{12,0},{1,5},{5,9},{9,13},{13,1},{2,6},{6,10},{... | collective-permute-start | bytes 12296 | tf_op jit(solution)/shard_map/ppermute | solution.py:270
  60.9 5.6 %collective-permute-start.19 = (f32[8,128]{1,0:T(8,128)}, f32[8,128]{1,0:T(8,128)}, u32[]{:S(2)}, u32[]{:S(2)}) collective-permute-start(f32[8,128]{1,0:T(8,128)} %add.7.refs_0_), channel_id=1, source_target_pairs={{0,8},{4,12},{8,0},{12,4},{1,9},{5,13},{9,1},{13,5},{2,10},{6,14},... | collective-permute-start | bytes 12296 | tf_op jit(solution)/shard_map/ppermute | solution.py:270
  62.4 4.7 %collective-permute-start.20 = (f32[8,128]{1,0:T(8,128)}, f32[8,128]{1,0:T(8,128)}, u32[]{:S(2)}, u32[]{:S(2)}) collective-permute-start(f32[8,128]{1,0:T(8,128)} %add.7.refs_0_), channel_id=1, source_target_pairs={{0,12},{4,0},{8,4},{12,8},{1,13},{5,1},{9,5},{13,9},{2,14},{6,2},{... | collective-permute-start | bytes 12296 | tf_op jit(solution)/shard_map/ppermute | solution.py:270
  65.3 1.8 %copy-start.2 = (f32[1,16,64,128]{3,2,1,0:T(8,128)S(1)}, f32[1,16,64,128]{3,2,1,0:T(8,128)}, u32[]{:S(2)}) copy-start(f32[1,16,64,128]{3,2,1,0:T(8,128)} %param.8) | copy-start | bytes 1572868
  65.3 1.8 %copy-start.4 = (f32[12,64,128]{2,1,0:T(8,128)S(1)}, f32[12,64,128]{2,1,0:T(8,128)}, u32[]{:S(2)}) copy-start(f32[12,64,128]{2,1,0:T(8,128)} %copy-done.3) | copy-start | bytes 1179652
  65.3 1.8 %copy-start.11 = (s32[1,6]{1,0:T(1,128)S(1)}, s32[1,6]{1,0:T(1,128)}, u32[]{:S(2)}) copy-start(s32[1,6]{1,0:T(1,128)} %counts.5) | copy-start | bytes 76

commit v5 on v4

v5 whole, which is shorter than its diff:
```python
import functools

import jax
import jax.numpy as jnp
from jax import lax
from jax.experimental import pallas as pl
from jax.experimental.pallas import tpu as pltpu
from jax.sharding import PartitionSpec as P

SPACE = ("mesh", "rep")
F32 = jnp.float32
BF16 = jnp.bfloat16
PHASES = (((4, 2), (5, 3, 0, 1)), ((4, 2, 0), (5, 3, 1)))
STAGES = (("rep", (1,)), ("tm", (1,)), ("mesh", (1, 2, 3)))
SPLIT = 2
PIECES = 4
ORDER = (40, 160, 0, 0)


def struct(*shape, dtype=F32):
    return jax.ShapeDtypeStruct(shape, dtype)


def call(body, outs, scalars, vectors, scratch=(), weight=0, outs_in=pltpu.VMEM):
    spaces = [pltpu.SMEM] * len(scalars) + [pltpu.VMEM] * len(vectors)
    return pl.pallas_call(
        body,
        out_shape=outs,
        in_specs=[pl.BlockSpec(memory_space=space) for space in spaces],
        out_specs=jax.tree.map(lambda _: pl.BlockSpec(memory_space=outs_in), outs),
        scratch_shapes=scratch,
        cost_estimate=pl.CostEstimate(
            flops=(weight << 30) + 1024, transcendentals=0, bytes_accessed=1024
        ),
        compiler_params=pltpu.CompilerParams(vmem_limit_bytes=40 << 20),
    )(*scalars, *vectors)


def total(values):
    return functools.reduce(jnp.add, values)


def halves(value):
    high = value.astype(BF16)
    return high, (value - high.astype(F32)).astype(BF16)


def group_of(shape, hours):
    lanes = shape[-1]
    return lax.broadcasted_iota(jnp.int32, shape, len(shape) - 1) // (lanes // hours)


def turned(value, places, hours):
    width = value.shape[-1] // hours
    result = value
    for k in range(1, hours):
        result = jnp.where(places == k, pltpu.roll(value, k * width, value.ndim - 1), result)
    return result


def pack_lanes(hours, hour, field, outs):
    group = group_of(field.shape[1:], hours)
    for r, out in enumerate(outs):
        target = lax.rem(hour + r + 1, hours)
        for j in range(out.shape[0]):
            packed = None
            for i in range(hours):
                part = turned(field[j * hours + i], lax.rem(i - target + hours, hours), hours)
                packed = part if i == 0 else jnp.where(group == i, part, packed)
            out[j] = packed


def merge_lanes(hours, hour, own, packs, block):
    group = group_of(own.shape, hours)
    for r, pack in enumerate(packs):
        source = lax.rem(hour + hours - r - 1, hours)
        part = pack[block // hours]
        part = turned(part, lax.rem(source - block % hours + hours, hours), hours)
        own = jnp.where(group == source, part, own)
    return own


def couple(hours, coupling, value):
    lanes = value.shape[-1]
    width = lanes // hours
    before, after = (pltpu.roll(value, d, value.ndim - 1) for d in (width, lanes - width))
    if hours == 2:
        return value - coupling * before
    group = group_of(value.shape, hours)
    sides = jnp.where(group > 0, before, 0.0) + jnp.where(group < hours - 1, after, 0.0)
    return value - coupling * sides


def pack_faces(faces, field, headings, outs):
    slots = faces.shape[1]
    places = [out.at[k] for out in outs for k in range(out.shape[0])]
    for m, place in enumerate(places):
        place[...] = field[faces[0, m % slots, headings[m // slots]]]


def far_product(stiffness, q, block):
    high, low = halves(block)
    right = jnp.concatenate([high, high, low], axis=0)
    return jnp.dot(stiffness[q], right, preferred_element_type=F32)


def landing(faces, counts, e, f, spare):
    return jnp.where(f < counts[0, e], faces[0, f, e], spare)


def open_body(hours, heads, faces, hour, field, *outs):
    pack_lanes(hours, hour[0], field, outs[: hours - 1])
    pack_faces(faces, field, heads, outs[hours - 1 :])


def turn_body(hours, heads, faces, hour, field, *refs):
    packs, (out, *faces_out) = refs[: hours - 1], refs[-1 - len(heads) :]
    for b in range(field.shape[0]):
        out[b] = merge_lanes(hours, hour[0], field[b], packs, b)
    pack_faces(faces, out, heads, faces_out)


def split_body(stiffness, out):
    width = stiffness.shape[1]
    for q in range(out.shape[0]):
        high, low = halves(stiffness[0, :, q * width : (q + 1) * width])
        out[q] = jnp.concatenate([high, low, high], axis=1)


def near_body(count, columns, kappa, stiffness, *refs):
    fields, outs, (high, low, diagonal) = refs[:count], refs[-3 - count : -3], refs[-3:]
    blocks = stiffness.shape[0]
    slots = columns.shape[0]
    lanes = fields[0].shape[2]
    diagonal[...] = jnp.transpose(kappa[...])
    for n, field in enumerate(fields):
        part = slice(n * lanes, (n + 1) * lanes)
        for b in range(blocks):
            high[b, :, part], low[b, :, part] = halves(field[b])
    for b in range(blocks):
        index = [columns[k, b] for k in range(slots)]
        highs = jnp.concatenate([high[i] for i in index], axis=0)
        lows = jnp.concatenate([low[i] for i in index], axis=0)
        left_high, left_low = halves(stiffness[b])
        near = jnp.dot(left_high, highs, preferred_element_type=F32)
        near += jnp.dot(left_low, highs, preferred_element_type=F32)
        near += jnp.dot(left_high, lows, preferred_element_type=F32)
        weight = 3.0 + diagonal[:, b : b + 1]
        for n, (field, out) in enumerate(zip(fields, outs)):
            out[b] = near[:, n * lanes : (n + 1) * lanes] + weight * field[b]


def near(columns, kappa, stiffness, fields, after=()):
    blocks, width, lanes = fields[0].shape
    return call(
        functools.partial(near_body, len(fields)),
        [struct(*field.shape) for field in fields],
        [columns],
        [kappa, stiffness, *fields, *after],
        [
            pltpu.VMEM((blocks, width, lanes * len(fields)), BF16),
            pltpu.VMEM((blocks, width, lanes * len(fields)), BF16),
            pltpu.VMEM((width, blocks), F32),
        ],
    )


def products(heads, stiffness, arrived, out):
    slots = arrived[0].shape[0]
    for n, e in enumerate(heads):
        for f in range(slots):
            out[n * slots + f] = far_product(stiffness, (e ^ 1) * slots + f, arrived[n][f])


def early_body(hours, heads, hour, stiffness, *refs):
    arrived, (_, out, *packs) = refs[: len(heads)], refs[len(heads) :]
    products(heads, stiffness, arrived, out)
    pack_lanes(hours, hour[0], out, packs)


def repack_body(hours, heads, faces, hour, own, field, *refs):
    outs = refs[-(len(heads) + hours - 1) :]
    pack_faces(faces, field, heads, outs[: len(heads)])
    pack_lanes(hours, hour[0], own, outs[len(heads) :])


def sum_body(*refs):
    refs[-1][...] = total([ref[...] for ref in refs[:-1]])


def late_body(heads, stiffness, *refs):
    products(heads, stiffness, refs[:-1], refs[-1])


def gather_far(hours, phases, faces, counts, hour, own, packs, late, near_part, field):
    blocks = near_part.shape[0]
    slots = faces.shape[1]
    for b in range(blocks):
        field[b] = near_part[b]
    for part, heads in enumerate(phases):
        for n, e in enumerate(heads):
            for f in range(slots):
                q = n * slots + f
                value = late(q) if part else merge_lanes(hours, hour[0], own[q], packs, q)
                field[landing(faces, counts, e ^ 1, f, blocks)] += value


def middle_body(hours, phases, heads, faces, counts, hour, coupling, near_part, own, late, *refs):
    turns = hours - 1
    packs = refs[:turns]
    first, image, *rest, field = refs[turns:]
    image_packs, first_packs, faces_out = rest[:turns], rest[turns : 2 * turns], rest[2 * turns :]
    late = late.__getitem__
    gather_far(hours, phases, faces, counts, hour, own, packs, late, near_part, field)
    for b in range(first.shape[0]):
        once = couple(hours, coupling[0], field[b])
        first[b] = once
        image[b] = couple(hours, coupling[0], once)
    pack_lanes(hours, hour[0], image, image_packs)
    pack_faces(faces, image, heads, faces_out)
    pack_lanes(hours, hour[0], first, first_packs)


def moments_body(hours, heads, faces, counts, hour, right, first, second, stiffness, *refs):
    arrived, (own, out) = refs[: len(heads)], refs[-2:]
    products(heads, stiffness, arrived, own)
    slots = faces.shape[1]
    sums = [jnp.zeros(right.shape[1:], F32) for _ in range(4)]
    for b in range(right.shape[0]):
        start, image = right[b], first[b]
        sums[0] += start * start
        sums[1] += start * image
        sums[2] += image * image
        sums[3] += image * second[b]
    for n, e in enumerate(heads):
        for f in range(slots):
            weight = jnp.where(f < counts[0, e ^ 1], 2.0, 0.0)
            sums[3] += weight * (first[faces[0, f, e ^ 1]] * own[n * slots + f])
    rows = jnp.concatenate([jnp.sum(s, axis=0, keepdims=True) for s in sums] * 2, axis=0)
    width = rows.shape[1] // hours
    rows = total([rows] + [pltpu.roll(rows, k * width, 1) for k in range(1, hours)])
    out[...] = jnp.where(group_of(rows.shape, hours) == hour[0], rows, 0.0)


def settle_body(
    hours, phases, faces, counts, hour, near_part, own, first, done, stiffness, *refs
):
    turns = hours - 1
    packs, first_packs, arrived = refs[:turns], refs[turns : 2 * turns], refs[2 * turns :]
    arrived, (image, out, rest, field) = arrived[:-4], arrived[-4:]
    count = done.shape[0]
    products(phases[1][len(phases[1]) - len(arrived) :], stiffness, arrived, rest)

    def late(q):
        return done[q] if q < count else rest[q - count]

    gather_far(hours, phases, faces, counts, hour, own, packs, late, near_part, field)
    for b in range(first.shape[0]):
        image[b] = merge_lanes(hours, hour[0], first[b], first_packs, b)
        out[b] = field[b]


def close_body(parts, right, first, second, *refs):
    sums, (solution, residual, solved, left, sems) = refs[:parts], refs[parts:]
    moment = total([s[...] for s in sums])
    m0, m1, m2, m3 = (moment[k : k + 1] for k in range(4))
    alpha = m0 / m1
    norm = alpha * alpha * m2 - m0
    lift = 1.0 + norm / m0
    step = norm / (lift * lift * m1 - 2.0 * lift * alpha * m2 + alpha * alpha * m3)
    on_right = alpha + step * lift
    on_first = step * alpha
    pieces = sems.shape[1]
    size = right.shape[0] // pieces
    copies = []
    for p in range(pieces):
        part = pl.ds(p * size, size)
        for b in range(p * size, (p + 1) * size):
            start, image = right[b], first[b]
            solved[b] = on_right * start - on_first * image
            left[b] = start - on_right * image + on_first * second[b]
        for n, (source, target) in enumerate(((solved, solution), (left, residual))):
            copies.append(pltpu.make_async_copy(source.at[part], target.at[part], sems.at[n, p]))
            copies[-1].start()
    for copy in copies:
        copy.wait()


def shifted(value, axes, sizes, steps):
    route = []
    for source in range(functools.reduce(lambda a, b: a * b, sizes)):
        rest, target, scale = source, 0, 1
        for size, step in reversed(list(zip(sizes, steps))):
            rest, place = divmod(rest, size)
            target += (place + step) % size * scale
            scale *= size
        route.append((source, target))
    return lax.ppermute(value, axes, route)


def send_faces(outgoing, heads, offsets):
    count = lax.axis_size(SPACE)
    return [shifted(v, SPACE, (count,), (offsets[e],)) for v, e in zip(outgoing, heads)]


def send_lanes(packs):
    hours = lax.axis_size("tm")
    return [shifted(v, ("tm",), (hours,), (r + 1,)) for r, v in enumerate(packs)]


def everywhere_sum(value):
    terms, summed, marks = [value], [], []
    for axis, partners in STAGES:
        if axis in summed:
            continue
        if len(terms) > 1:
            weight = ORDER[2 + len(marks)]
            terms = [call(sum_body, struct(*value.shape), [], terms, weight=weight)]
            marks += terms
        count = lax.axis_size(axis)
        if count in (2, 4):
            routes = [[(i, i ^ k) for i in range(count)] for k in partners]
            terms += [lax.ppermute(terms[0], axis, route) for route in routes]
        else:
            terms = [lax.psum(terms[0], axis)]
            summed.append(axis)
    return terms, marks


def shards(
    right_side,
    kappa_sq,
    time_coupling,
    near_stiffness,
    far_stiffness,
    near_columns,
    face_blocks,
    face_counts,
):
    right = right_side.reshape(right_side.shape[1:])
    blocks, width, lanes = right.shape
    hours = lax.axis_size("tm")
    hour = lax.axis_index("tm").reshape(1)
    headings, slots = face_blocks.shape[1:]
    stride = lax.axis_size(SPACE) // 4 + 1
    faces = jnp.swapaxes(face_blocks, 1, 2)
    columns = jnp.swapaxes(near_columns, 0, 1)
    counts = face_counts
    offsets = (1, -1, 2, -2, stride, -stride)
    field = struct(*right.shape)
    turns = hours - 1
    spare = [pltpu.VMEM((blocks + 1, width, lanes), F32)]

    def packs_of(count):
        return [struct(count // hours, width, lanes)] * turns

    def faces_of(heads):
        return [struct(slots, width, lanes)] * len(heads)

    def products_of(heads):
        return struct(len(heads) * slots, width, lanes)

    def body(function, *sizes):
        return functools.partial(function, hours, *sizes)

    def turn(heads, field_in, packs, after):
        out, *outgoing = call(
            body(turn_body, heads),
            [field] + faces_of(heads),
            [faces, hour],
            [field_in, *packs, *after],
        )
        return out, send_faces(outgoing, heads, offsets)

    def late_products(heads, arrived, weight):
        return call(
            functools.partial(late_body, heads),
            products_of(heads),
            [],
            [stiffness, *arrived],
            weight=weight,
        )

    phases, (heads, _) = PHASES
    outs = call(
        body(open_body, phases[0]),
        packs_of(blocks) + faces_of(phases[0]),
        [faces, hour],
        [right],
    )
    packs = send_lanes(outs[:turns])
    early = send_faces(outs[turns:], phases[0], offsets)
    probe_right, late = turn(phases[1], right, packs, [])
    stiffness = call(
        split_body, struct(headings * slots, width, 3 * width, dtype=BF16), [], [far_stiffness]
    )
    (near_part,) = near(columns, kappa_sq, near_stiffness, [probe_right])
    out = products_of(phases[0])
    own, *packs = call(
        body(early_body, phases[0]),
        [out] + packs_of(out.shape[0]),
        [hour],
        [stiffness, *early, probe_right],
    )
    packs = send_lanes(packs)
    late = late_products(phases[1], late, ORDER[0])
    first, image, *outs = call(
        body(middle_body, phases, heads),
        [field, field] + packs_of(blocks) * 2 + faces_of(heads),
        [faces, counts, hour, time_coupling],
        [near_part, own, late, *packs],
        spare,
    )

    phases = PHASES[1]
    packs, first_packs = send_lanes(outs[:turns]), send_lanes(outs[turns : 2 * turns])
    early = send_faces(outs[2 * turns :], phases[0], offsets)
    (near_probe,) = near(columns, kappa_sq, near_stiffness, [image])
    hour_image, late = turn(phases[1][:SPLIT], image, packs, [near_probe])
    own, sums = call(
        body(moments_body, phases[0]),
        [products_of(phases[0]), struct(8, lanes)],
        [faces, counts, hour],
        [probe_right, first, near_probe, stiffness, *early, *first_packs, hour_image],
    )
    sums, marks = everywhere_sum(sums)
    heads = phases[1][SPLIT:]
    outs = call(
        body(repack_body, heads),
        faces_of(heads) + packs_of(own.shape[0]),
        [faces, hour],
        [own, hour_image, *marks[:1]],
    )
    late += send_faces(outs[: len(heads)], heads, offsets)
    packs = send_lanes(outs[len(heads) :])
    (near_hour,) = near(columns, kappa_sq, near_stiffness, [hour_image], marks[-1:])
    done = late_products(phases[1][:SPLIT], late[:SPLIT], ORDER[1])
    hour_first, second = call(
        body(settle_body, phases),
        [field, field],
        [faces, counts, hour],
        [near_hour, own, first, done, stiffness, *packs, *first_packs, *late[SPLIT:]],
        [pltpu.VMEM((len(heads) * slots, width, lanes), F32)] + spare,
    )
    solution_field, residual = call(
        functools.partial(close_body, len(sums)),
        [field, field],
        [],
        [right, hour_first, second, *sums],
        [pltpu.VMEM(right.shape, F32)] * 2 + [pltpu.SemaphoreType.DMA((2, PIECES))],
        outs_in=pl.ANY,
    )
    return (solution_field[None], residual[None])


def solution(mesh):
    placed = (
        P(("grp", "tm"), SPACE, None, None),
        P(("grp", "mesh", "rep"), None),
        P("grp"),
        P(SPACE, None, None),
        P(SPACE, None, None),
        P(SPACE, None),
        P(SPACE, None, None),
        P(SPACE, None),
    )
    return jax.shard_map(
        shards,
        mesh=mesh,
        in_specs=placed,
        out_specs=(
            P(("grp", "tm"), SPACE, None, None),
            P(("grp", "tm"), SPACE, None, None),
        ),
        check_vma=False,
    )
```

time: 69.7 us -> 61.9 us (0.89)
  starting transfers between devices: 33.3 us -> 26 us
  waiting for transfers between devices: 18.4 us -> 15.2 us
  Pallas kernels: 13.9 us -> 16.4 us
  local copies, waits for them, and re-layouts: 1.76 us -> 2.46 us
    ppermute x22 -> x17, starting transfers between devices: 33.3 us -> 20.1 us  [shifted(): return lax.ppermute(value, axes, route)]
    ppermute x0 -> x5, starting transfers between devices: none -> 5.94 us  [everywhere_sum(): terms += [lax.ppermute(terms[0], axis, route) for route in routes]]
    ppermute x22 -> x17, waiting for transfers between devices: 18.4 us -> 13.9 us  [shifted(): return lax.ppermute(value, axes, route)]
    pallas_call x13 -> x17, Pallas kernels: 13.9 us -> 16.4 us  [call(): pl.pallas_call(body, out_shape=outs, in_specs=[pl.BlockSpec(memory_space=...]
    ppermute x0 -> x5, waiting for transfers between devices: none -> 1.28 us  [everywhere_sum(): terms += [lax.ppermute(terms[0], axis, route) for route in routes]]
    unnamed x24, local copies, waits for them, and re-layouts: 1.76 us -> 2.46 us
  transfers between devices with their start and end apart: 22 -> 22, of which waited for: 11 -> 6; matrix products, arithmetic and copies ran while one was open for 1% -> 0% of each run, Pallas kernels for 13% -> 20%
where the time goes in v5:
time: 61.9 us; the launch traced here: 61.6 us
  starting transfers between devices  26 us (42%)
  Pallas kernels  16.4 us (26%)
  waiting for transfers between devices  15.2 us (25%)
  local copies, waits for them, and re-layouts  2.46 us (4%)
  between operations  1.57 us (3%)
    ppermute x17, starting transfers between devices, shifted(): return lax.ppermute(value, axes, route)  20.1 us
    pallas_call x17, Pallas kernels, call(): pl.pallas_call(body, out_shape=outs, in_specs=[pl.BlockSpec(memory_space=...  16.4 us
    ppermute x17, waiting for transfers between devices, shifted(): return lax.ppermute(value, axes, route)  13.9 us
    ppermute x5, starting transfers between devices, everywhere_sum(): terms += [lax.ppermute(terms[0], axis, route) for route in routes]  5.94 us
    unnamed x24, local copies, waits for them, and re-layouts  2.46 us
    ppermute x5, waiting for transfers between devices, everywhere_sum(): terms += [lax.ppermute(terms[0], axis, route) for route in routes]  1.28 us
  transfers between devices with their start and end apart: 22, of which 6 were waited for; matrix products, arithmetic and copies ran while one was open for 0% of the time, Pallas kernels for 20%

profile of v5, /device:TPU:0, one launch (start us, length us, event | category | flops | bytes accessed | tf_op | source)
XLA Modules:
  0.0 61.6 jit_solution(11141090934355679107)
XLA Ops:
  0.6 0.0 copy-start.1
  0.6 1.0 %copy-done.1 = f32[1,16,64,128]{3,2,1,0:T(8,128)S(1)} copy-done((f32[1,16,64,128]{3,2,1,0:T(8,128)S(1)}, f32[1,16,64,128]{3,2,1,0:T(8,128)}, u32[]{:S(2)}) %copy-start.1) | copy-done | bytes 524312
  1.7 0.7 %copy-done.6 = s32[1,6,4]{1,2,0:T(4,128)S(1)} copy-done((s32[1,6,4]{1,2,0:T(4,128)S(1)}, s32[1,6,4]{1,2,0:T(4,128)}, u32[]{:S(2)}) %copy-start.6) | copy-done | bytes 120
  2.4 0.8 %shard_map.95 = (f32[8,64,128]{2,1,0:T(8,128)S(1)}, f32[4,64,128]{2,1,0:T(8,128)S(1)}, f32[4,64,128]{2,1,0:T(8,128)S(1)}) custom-call(s32[1,4,6]{2,1,0:T(4,128)S(1)} %bitcast.9, s32[1]{0:T(128)} %bitcast.2.hour, f32[16,64,128]{2,1,0:T(8,128)S(1)} %bitcast.6), custom_call_target="tpu_custom_call" | custom-call | flops 1024 | bytes 1024 | tf_op jit(solution)/shard_map/pallas_call | solution.py:26
  3.1 3.0 %collective-permute-start = (f32[8,64,128]{2,1,0:T(8,128)S(1)}, f32[8,64,128]{2,1,0:T(8,128)S(1)}, u32[]{:S(2)}, u32[]{:S(2)}) collective-permute-start(f32[8,64,128]{2,1,0:T(8,128)S(1)} %get-tuple-element.30), channel_id=1, source_target_pairs={{0,2},{2,0},{1,3},{3,1},{4,6},{6,4},{5,7},{7,5},{8,10},{10,8},{9,1... | collective-permute-start | bytes 786440 | tf_op jit(solution)/shard_map/ppermute | solution.py:298
  6.1 0.7 %collective-permute-start.1 = (f32[4,64,128]{2,1,0:T(8,128)S(1)}, f32[4,64,128]{2,1,0:T(8,128)S(1)}, u32[]{:S(2)}, u32[]{:S(2)}) collective-permute-start(f32[4,64,128]{2,1,0:T(8,128)S(1)} %get-tuple-element.32), channel_id=1, source_target_pairs={{0,5},{1,8},{4,9},{5,12},{8,13},{9,0},{12,1},{13,4},{2,7},{3,10},{... | collective-permute-start | bytes 393224 | tf_op jit(solution)/shard_map/ppermute | solution.py:298
  6.9 1.6 %collective-permute-start.2 = (f32[4,64,128]{2,1,0:T(8,128)S(1)}, f32[4,64,128]{2,1,0:T(8,128)S(1)}, u32[]{:S(2)}, u32[]{:S(2)}) collective-permute-start(f32[4,64,128]{2,1,0:T(8,128)S(1)} %get-tuple-element.33), channel_id=1, source_target_pairs={{0,4},{1,5},{4,8},{5,9},{8,12},{9,13},{12,0},{13,1},{2,6},{3,7},{6... | collective-permute-start | bytes 393224 | tf_op jit(solution)/shard_map/ppermute | solution.py:298
  8.5 4.0 %collective-permute-done.refs_0_ = f32[8,64,128]{2,1,0:T(8,128)S(1)} collective-permute-done((f32[8,64,128]{2,1,0:T(8,128)S(1)}, f32[8,64,128]{2,1,0:T(8,128)S(1)}, u32[]{:S(2)}, u32[]{:S(2)}) %collective-permute-start) | collective-permute-done | bytes 262176 | tf_op jit(solution)/shard_map/ppermute | solution.py:298
  12.4 0.8 %shard_map.96 = (f32[16,64,128]{2,1,0:T(8,128)S(1)}, f32[4,64,128]{2,1,0:T(8,128)S(1)}, f32[4,64,128]{2,1,0:T(8,128)S(1)}, f32[4,64,128]{2,1,0:T(8,128)S(1)}, f32[4,64,128]{2,1,0:T(8,128)S(1)}) custom-call(s32[1,4,6]{2,1,0:T(4,128)S(1)} %bitcast.10, s32[1]{0:T(128)} %bitcast.2.hour, f32[16,64,128]{2,1,0:T(8,128)S(1)} %bitcast.7, ...), custom_call_target="tpu_custom_call" | custom-call | flops 1024 | bytes 1024 | tf_op jit(solution)/shard_map/pallas_call | solution.py:26
  13.3 0.0 copy-start
  13.3 0.0 copy-start.8
  13.3 0.0 copy-start.9
  13.3 1.5 %collective-permute-start.3 = (f32[4,64,128]{2,1,0:T(8,128)S(1)}, f32[4,64,128]{2,1,0:T(8,128)S(1)}, u32[]{:S(2)}, u32[]{:S(2)}) collective-permute-start(f32[4,64,128]{2,1,0:T(8,128)S(1)} %get-tuple-element.35), channel_id=1, source_target_pairs={{0,9},{1,12},{4,13},{5,0},{8,1},{9,4},{12,5},{13,8},{2,11},{3,14},... | collective-permute-start | bytes 393224 | tf_op jit(solution)/shard_map/ppermute | solution.py:298
  14.7 2.5 %collective-permute-start.4 = (f32[4,64,128]{2,1,0:T(8,128)S(1)}, f32[4,64,128]{2,1,0:T(8,128)S(1)}, u32[]{:S(2)}, u32[]{:S(2)}) collective-permute-start(f32[4,64,128]{2,1,0:T(8,128)S(1)} %get-tuple-element.36), channel_id=1, source_target_pairs={{0,12},{1,13},{4,0},{5,1},{8,4},{9,5},{12,8},{13,9},{2,14},{3,15},... | collective-permute-start | bytes 393224 | tf_op jit(solution)/shard_map/ppermute | solution.py:298
  17.3 0.2 collective-permute-start.5
  17.5 0.0 collective-permute-done.1.refs_0_
  17.5 3.3 %collective-permute-start.6 = (f32[4,64,128]{2,1,0:T(8,128)S(1)}, f32[4,64,128]{2,1,0:T(8,128)S(1)}, u32[]{:S(2)}, u32[]{:S(2)}) collective-permute-start(f32[4,64,128]{2,1,0:T(8,128)S(1)} %get-tuple-element.38), channel_id=1, source_target_pairs={{0,13},{1,0},{4,1},{5,4},{8,5},{9,8},{12,9},{13,12},{2,15},{3,2},{... | collective-permute-start | bytes 393224 | tf_op jit(solution)/shard_map/ppermute | solution.py:298
  20.8 0.2 shard_map.98.stiffness
  21.6 0.0 collective-permute-done.2.refs_1_
  21.6 0.3 shard_map.99
  22.0 1.6 %collective-permute-start.7 = (f32[4,64,128]{2,1,0:T(8,128)S(1)}, f32[4,64,128]{2,1,0:T(8,128)S(1)}, u32[]{:S(2)}, u32[]{:S(2)}) collective-permute-start(f32[4,64,128]{2,1,0:T(8,128)S(1)} %get-tuple-element.39), channel_id=1, source_target_pairs={{0,2},{2,0},{1,3},{3,1},{4,6},{6,4},{5,7},{7,5},{8,10},{10,8},{9,1... | collective-permute-start | bytes 393224 | tf_op jit(solution)/shard_map/ppermute | solution.py:298
  23.6 1.6 %shard_map.97.near_part = f32[16,64,128]{2,1,0:T(8,128)S(1)} custom-call(s32[6,16]{1,0:T(8,128)S(1)} %bitcast.16, f32[16,64]{1,0:T(8,128)S(1)} %copy-done.8, f32[16,64,384]{2,1,0:T(8,128)S(1)} %copy-done, f32[16,64,128]{2,1,0:T(8,128)S(1)} %get-tuple-element.31.refs_0_.refs_2_.right), custom_call_target="tpu_custom_call" | custom-call | flops 1024 | bytes 1024 | tf_op jit(solution)/shard_map/pallas_call | solution.py:26
  25.2 0.0 copy-start.7
  25.2 0.0 copy-start.10
  25.2 0.0 collective-permute-done.3.refs_0_
  25.2 0.0 collective-permute-done.4.refs_1_
  25.2 1.7 %collective-permute-done.5.refs_2_ = f32[4,64,128]{2,1,0:T(8,128)S(1)} collective-permute-done((f32[4,64,128]{2,1,0:T(8,128)S(1)}, f32[4,64,128]{2,1,0:T(8,128)S(1)}, u32[]{:S(2)}, u32[]{:S(2)}) %collective-permute-start.5) | collective-permute-done | bytes 131104 | tf_op jit(solution)/shard_map/ppermute | solution.py:298
  26.9 0.4 shard_map.100.late
  27.3 0.0 collective-permute-done.7.refs_0_
  27.4 1.7 %shard_map.101 = (f32[16,64,128]{2,1,0:T(8,128)S(1)}, f32[16,64,128]{2,1,0:T(8,128)S(1)}, f32[8,64,128]{2,1,0:T(8,128)S(1)}, f32[8,64,128]{2,1,0:T(8,128)S(1)}, ...) custom-call(s32[1,4,6]{2,1,0:T(4,128)S(1)} %bitcast.11, s32[1,6]{1,0:T(1,128)S(1)} %copy-done.10, ...), custom_call_target="tpu_custom_call" | custom-call | flops 1024 | bytes 1024 | tf_op jit(solution)/shard_map/pallas_call | solution.py:26
  29.0 1.6 %collective-permute-start.8 = (f32[8,64,128]{2,1,0:T(8,128)S(1)}, f32[8,64,128]{2,1,0:T(8,128)S(1)}, u32[]{:S(2)}, u32[]{:S(2)}) collective-permute-start(f32[8,64,128]{2,1,0:T(8,128)S(1)} %get-tuple-element.41), channel_id=1, source_target_pairs={{0,2},{2,0},{1,3},{3,1},{4,6},{6,4},{5,7},{7,5},{8,10},{10,8},{9,1... | collective-permute-start | bytes 786440 | tf_op jit(solution)/shard_map/ppermute | solution.py:298
  30.6 0.5 collective-permute-start.12
  31.1 0.0 collective-permute-start.9
  31.1 0.4 collective-permute-start.10
  31.5 1.9 %collective-permute-start.11 = (f32[4,64,128]{2,1,0:T(8,128)S(1)}, f32[4,64,128]{2,1,0:T(8,128)S(1)}, u32[]{:S(2)}, u32[]{:S(2)}) collective-permute-start(f32[4,64,128]{2,1,0:T(8,128)S(1)} %get-tuple-element.46), channel_id=1, source_target_pairs={{0,1},{1,4},{4,5},{5,8},{8,9},{9,12},{12,13},{13,0},{2,3},{3,6},{6... | collective-permute-start | bytes 393224 | tf_op jit(solution)/shard_map/ppermute | solution.py:298
  33.4 1.6 %shard_map.102.refs_1_.second = f32[16,64,128]{2,1,0:T(8,128)S(1)} custom-call(s32[6,16]{1,0:T(8,128)S(1)} %bitcast.17, f32[16,64]{1,0:T(8,128)S(1)} %copy-done.8, f32[16,64,384]{2,1,0:T(8,128)S(1)} %copy-done, f32[16,64,128]{2,1,0:T(8,128)S(1)} %get-tuple-element.40.refs_0_.field), custom_call_target="tpu_custom_call" | custom-call | flops 1024 | bytes 1024 | tf_op jit(solution)/shard_map/pallas_call | solution.py:26
  35.0 3.0 %collective-permute-done.8.refs_0_ = f32[8,64,128]{2,1,0:T(8,128)S(1)} collective-permute-done((f32[8,64,128]{2,1,0:T(8,128)S(1)}, f32[8,64,128]{2,1,0:T(8,128)S(1)}, u32[]{:S(2)}, u32[]{:S(2)}) %collective-permute-start.8) | collective-permute-done | bytes 262176 | tf_op jit(solution)/shard_map/ppermute | solution.py:298
  38.0 0.8 %shard_map.103 = (f32[16,64,128]{2,1,0:T(8,128)S(1)}, f32[4,64,128]{2,1,0:T(8,128)S(1)}, f32[4,64,128]{2,1,0:T(8,128)S(1)}) custom-call(s32[1,4,6]{2,1,0:T(4,128)S(1)} %bitcast.12, s32[1]{0:T(128)} %bitcast.2.hour, f32[16,64,128]{2,1,0:T(8,128)S(1)} %get-tuple-element.40.refs_0_.field, f32[8,64,128]{2,1,0:T(8,128)S(1)} %collective-permute-done.8.refs_0_, ...), custom_call_target="tpu_custom_call" | custom-call | flops 1024 | bytes 1024 | tf_op jit(solution)/shard_map/pallas_call | solution.py:26
  38.8 0.1 collective-permute-start.15
  38.9 5.2 %collective-permute-done.9.refs_0_ = f32[4,64,128]{2,1,0:T(8,128)S(1)} collective-permute-done((f32[4,64,128]{2,1,0:T(8,128)S(1)}, f32[4,64,128]{2,1,0:T(8,128)S(1)}, u32[]{:S(2)}, u32[]{:S(2)}) %collective-permute-start.9) | collective-permute-done | bytes 131104 | tf_op jit(solution)/shard_map/ppermute | solution.py:298
  44.1 0.0 collective-permute-start.16
  44.1 0.0 collective-permute-done.10.refs_1_
  44.1 0.0 collective-permute-done.11.refs_2_
  44.1 1.1 %shard_map.104 = (f32[12,64,128]{2,1,0:T(8,128)S(1)}, f32[8,128]{1,0:T(8,128)S(1)}) custom-call(s32[1,4,6]{2,1,0:T(4,128)S(1)} %bitcast.13, s32[1,6]{1,0:T(1,128)S(1)} %copy-done.10, s32[1]{0:T(128)} %bitcast.2.hour, f32[16,64,128]{2,1,0:T(8,128)S(1)} %get-tuple-element.31.refs_0_.refs_2_.right, f32[16,64,128]{2,1,0:T(8,128)S(1)} %get-tuple-element.43.first, ...), custom_call_target="tpu_custom_call" | custom-call | flops 1024 | bytes 1024 | tf_op jit(solution)/shard_map/pallas_call | solution.py:26
  45.2 0.0 collective-permute-start.13
  45.2 1.2 %collective-permute-done.13.refs_1_ = f32[8,128]{1,0:T(8,128)S(1)} collective-permute-done((f32[8,128]{1,0:T(8,128)S(1)}, f32[8,128]{1,0:T(8,128)S(1)}, u32[]{:S(2)}, u32[]{:S(2)}) %collective-permute-start.13) | collective-permute-done | bytes 4128 | tf_op jit(solution)/shard_map/ppermute | solution.py:323
  46.4 1.5 %collective-permute-start.14 = (f32[8,128]{1,0:T(8,128)S(1)}, f32[8,128]{1,0:T(8,128)S(1)}, u32[]{:S(2)}, u32[]{:S(2)}) collective-permute-start(f32[8,128]{1,0:T(8,128)S(1)} %shard_map.105.refs_0_), channel_id=1, source_target_pairs={{0,2},{2,0},{1,3},{3,1},{4,6},{6,4},{5,7},{7,5},{8,10},{10,8},{9,1... | collective-permute-start | bytes 12296 | tf_op jit(solution)/shard_map/ppermute | solution.py:323
  47.8 1.4 %shard_map.109 = (f32[4,64,128]{2,1,0:T(8,128)}, f32[6,64,128]{2,1,0:T(8,128)}) custom-call(s32[1,4,6]{2,1,0:T(4,128)S(1)} %bitcast.14, s32[1]{0:T(128)} %bitcast.2.hour, f32[12,64,128]{2,1,0:T(8,128)S(1)} %get-tuple-element.49.own, f32[16,64,128]{2,1,0:T(8,128)S(1)} %get-tuple-element.42.refs_4_.refs_0_.field, f32[8,128]{1,0:T(8,128)S(1)} %shard_map.105.refs_0_), custom_call_target="tpu_custom_call" | custom-call | flops 1024 | bytes 1024 | tf_op jit(solution)/shard_map/pallas_call | solution.py:26
  49.2 0.7 %collective-permute-start.18 = (f32[4,64,128]{2,1,0:T(8,128)}, f32[4,64,128]{2,1,0:T(8,128)}, u32[]{:S(2)}, u32[]{:S(2)}) collective-permute-start(f32[4,64,128]{2,1,0:T(8,128)} %get-tuple-element.53), channel_id=1, source_target_pairs={{0,13},{1,0},{4,1},{5,4},{8,5},{9,8},{12,9},{13,12},{2,15},{3,2},{... | collective-permute-start | bytes 393224 | tf_op jit(solution)/shard_map/ppermute | solution.py:298
  49.9 0.5 collective-permute-start.17
  50.5 0.6 shard_map.106.refs_1_.refs_0_
  51.1 0.7 %collective-permute-start.21 = (f32[8,128]{1,0:T(8,128)}, f32[8,128]{1,0:T(8,128)}, u32[]{:S(2)}, u32[]{:S(2)}) collective-permute-start(f32[8,128]{1,0:T(8,128)} %shard_map.106.refs_1_.refs_0_), channel_id=1, source_target_pairs={{0,12},{4,8},{8,4},{12,0},{1,13},{5,9},{9,5},{13,1},{2,14},{6,10},... | collective-permute-start | bytes 12296 | tf_op jit(solution)/shard_map/ppermute | solution.py:323
  51.7 1.7 %shard_map.107.near_part = f32[16,64,128]{2,1,0:T(8,128)S(1)} custom-call(s32[6,16]{1,0:T(8,128)S(1)} %bitcast.18, f32[16,64]{1,0:T(8,128)S(1)} %copy-done.8, f32[16,64,384]{2,1,0:T(8,128)S(1)} %copy-done, f32[16,64,128]{2,1,0:T(8,128)S(1)} %get-tuple-element.42.refs_4_.refs_0_.field, f32[8,128]{1,0:T(8,128)} %shard_map.106.refs_1_.refs_0_), custom_call_target="tpu_custom_call" | custom-call | flops 1024 | bytes 1024 | tf_op jit(solution)/shard_map/pallas_call | solution.py:26
  53.5 2.4 %collective-permute-start.20 = (f32[8,128]{1,0:T(8,128)}, f32[8,128]{1,0:T(8,128)}, u32[]{:S(2)}, u32[]{:S(2)}) collective-permute-start(f32[8,128]{1,0:T(8,128)} %shard_map.106.refs_1_.refs_0_), channel_id=1, source_target_pairs={{0,8},{4,12},{8,0},{12,4},{1,9},{5,13},{9,1},{13,5},{2,10},{6,14},... | collective-permute-start | bytes 12296 | tf_op jit(solution)/shard_map/ppermute | solution.py:323
  55.9 0.0 collective-permute-done.16.refs_1_
  55.9 1.4 %collective-permute-start.19 = (f32[8,128]{1,0:T(8,128)}, f32[8,128]{1,0:T(8,128)}, u32[]{:S(2)}, u32[]{:S(2)}) collective-permute-start(f32[8,128]{1,0:T(8,128)} %shard_map.106.refs_1_.refs_0_), channel_id=1, source_target_pairs={{0,4},{4,0},{8,12},{12,8},{1,5},{5,1},{9,13},{13,9},{2,6},{6,2},{1... | collective-permute-start | bytes 12296 | tf_op jit(solution)/shard_map/ppermute | solution.py:323
  57.3 0.3 shard_map.108.done
  57.6 0.0 copy-start.2
  57.6 0.0 collective-permute-done.18.refs_2_
  57.6 0.7 %copy-done.4 = f32[12,64,128]{2,1,0:T(8,128)S(1)} copy-done((f32[12,64,128]{2,1,0:T(8,128)S(1)}, f32[12,64,128]{2,1,0:T(8,128)}, u32[]{:S(2)}) %copy-start.4) | copy-done | bytes 393240
  58.3 1.4 %shard_map.110 = (f32[16,64,128]{2,1,0:T(8,128)S(1)}, f32[16,64,128]{2,1,0:T(8,128)S(1)}) custom-call(s32[1,4,6]{2,1,0:T(4,128)S(1)} %bitcast.15, s32[1,6]{1,0:T(1,128)S(1)} %copy-done.11, s32[1]{0:T(128)} %bitcast.2.hour, f32[16,64,128]{2,1,0:T(8,128)S(1)} %shard_map.107.near_part, f32[12,64,128]{2,1,0:T(8,128)S(1)} %copy-done.4, ...), custom_call_target="tpu_custom_call" | custom-call | flops 1024 | bytes 1024 | tf_op jit(solution)/shard_map/pallas_call | solution.py:26
  59.7 0.0 collective-permute-done.21.refs_3_
  59.7 0.1 collective-permute-done.19.refs_1_
  59.8 1.8 %shard_map.111 = (f32[16,64,128]{2,1,0:T(8,128)}, f32[16,64,128]{2,1,0:T(8,128)}) custom-call(f32[16,64,128]{2,1,0:T(8,128)S(1)} %bitcast.8, f32[16,64,128]{2,1,0:T(8,128)S(1)} %get-tuple-element.54.first, f32[16,64,128]{2,1,0:T(8,128)S(1)} %get-tuple-element.55.second, f32[8,128]{1,0:T(8,128)} %shard_map.106.refs_1_.refs_0_, ...), custom_call_target="tpu_custom_call" | custom-call | flops 1024 | bytes 1024 | tf_op jit(solution)/shard_map/pallas_call | solution.py:26
  (21 shorter events, 0.0 us)
Async XLA Ops:
  0.6 1.0 %copy-start.1 = (f32[1,16,64,128]{3,2,1,0:T(8,128)S(1)}, f32[1,16,64,128]{3,2,1,0:T(8,128)}, u32[]{:S(2)}) copy-start(f32[1,16,64,128]{3,2,1,0:T(8,128)} %param.8) | copy-start | bytes 1572868
  1.7 0.7 %copy-start.6 = (s32[1,6,4]{1,2,0:T(4,128)S(1)}, s32[1,6,4]{1,2,0:T(4,128)}, u32[]{:S(2)}) copy-start(s32[1,6,4]{1,2,0:T(4,128)} %param.14) | copy-start | bytes 292
  2.4 18.4 %copy-start.5 = (f32[1,64,1536]{2,1,0:T(8,128)S(1)}, f32[1,64,1536]{2,1,0:T(8,128)}, u32[]{:S(2)}) copy-start(f32[1,64,1536]{2,1,0:T(8,128)} %stiffness.5) | copy-start | bytes 1179652
  3.1 9.3 %collective-permute-start = (f32[8,64,128]{2,1,0:T(8,128)S(1)}, f32[8,64,128]{2,1,0:T(8,128)S(1)}, u32[]{:S(2)}, u32[]{:S(2)}) collective-permute-start(f32[8,64,128]{2,1,0:T(8,128)S(1)} %get-tuple-element.30), channel_id=1, source_target_pairs={{0,2},{2,0},{1,3},{3,1},{4,6},{6,4},{5,7},{7,5},{8,10},{10,8},{9,1... | collective-permute-start | bytes 786440 | tf_op jit(solution)/shard_map/ppermute | solution.py:298
  6.1 11.3 %collective-permute-start.1 = (f32[4,64,128]{2,1,0:T(8,128)S(1)}, f32[4,64,128]{2,1,0:T(8,128)S(1)}, u32[]{:S(2)}, u32[]{:S(2)}) collective-permute-start(f32[4,64,128]{2,1,0:T(8,128)S(1)} %get-tuple-element.32), channel_id=1, source_target_pairs={{0,5},{1,8},{4,9},{5,12},{8,13},{9,0},{12,1},{13,4},{2,7},{3,10},{... | collective-permute-start | bytes 393224 | tf_op jit(solution)/shard_map/ppermute | solution.py:298
  6.9 14.8 %collective-permute-start.2 = (f32[4,64,128]{2,1,0:T(8,128)S(1)}, f32[4,64,128]{2,1,0:T(8,128)S(1)}, u32[]{:S(2)}, u32[]{:S(2)}) collective-permute-start(f32[4,64,128]{2,1,0:T(8,128)S(1)} %get-tuple-element.33), channel_id=1, source_target_pairs={{0,4},{1,5},{4,8},{5,9},{8,12},{9,13},{12,0},{13,1},{2,6},{3,7},{6... | collective-permute-start | bytes 393224 | tf_op jit(solution)/shard_map/ppermute | solution.py:298
  13.3 10.3 %copy-start = (f32[16,64,384]{2,1,0:T(8,128)S(1)}, f32[16,64,384]{2,1,0:T(8,128)}, u32[]{:S(2)}) copy-start(f32[16,64,384]{2,1,0:T(8,128)} %stiffness.7) | copy-start | bytes 4718596
  13.3 10.3 %copy-start.8 = (f32[16,64]{1,0:T(8,128)S(1)}, f32[16,64]{1,0:T(8,128)}, u32[]{:S(2)}) copy-start(f32[16,64]{1,0:T(8,128)} %kappa.5) | copy-start | bytes 12292
  13.3 10.3 %copy-start.9 = (s32[16,6]{0,1:T(8,128)S(1)}, s32[16,6]{0,1:T(8,128)}, u32[]{:S(2)}) copy-start(s32[16,6]{0,1:T(8,128)} %param.13) | copy-start | bytes 1156
  13.3 11.9 %collective-permute-start.3 = (f32[4,64,128]{2,1,0:T(8,128)S(1)}, f32[4,64,128]{2,1,0:T(8,128)S(1)}, u32[]{:S(2)}, u32[]{:S(2)}) collective-permute-start(f32[4,64,128]{2,1,0:T(8,128)S(1)} %get-tuple-element.35), channel_id=1, source_target_pairs={{0,9},{1,12},{4,13},{5,0},{8,1},{9,4},{12,5},{13,8},{2,11},{3,14},... | collective-permute-start | bytes 393224 | tf_op jit(solution)/shard_map/ppermute | solution.py:298
  14.7 10.5 %collective-permute-start.4 = (f32[4,64,128]{2,1,0:T(8,128)S(1)}, f32[4,64,128]{2,1,0:T(8,128)S(1)}, u32[]{:S(2)}, u32[]{:S(2)}) collective-permute-start(f32[4,64,128]{2,1,0:T(8,128)S(1)} %get-tuple-element.36), channel_id=1, source_target_pairs={{0,12},{1,13},{4,0},{5,1},{8,4},{9,5},{12,8},{13,9},{2,14},{3,15},... | collective-permute-start | bytes 393224 | tf_op jit(solution)/shard_map/ppermute | solution.py:298
  17.3 9.6 %collective-permute-start.5 = (f32[4,64,128]{2,1,0:T(8,128)S(1)}, f32[4,64,128]{2,1,0:T(8,128)S(1)}, u32[]{:S(2)}, u32[]{:S(2)}) collective-permute-start(f32[4,64,128]{2,1,0:T(8,128)S(1)} %get-tuple-element.37), channel_id=1, source_target_pairs={{0,1},{1,4},{4,5},{5,8},{8,9},{9,12},{12,13},{13,0},{2,3},{3,6},{6... | collective-permute-start | bytes 393224 | tf_op jit(solution)/shard_map/ppermute | solution.py:298
  17.5 9.4 %collective-permute-start.6 = (f32[4,64,128]{2,1,0:T(8,128)S(1)}, f32[4,64,128]{2,1,0:T(8,128)S(1)}, u32[]{:S(2)}, u32[]{:S(2)}) collective-permute-start(f32[4,64,128]{2,1,0:T(8,128)S(1)} %get-tuple-element.38), channel_id=1, source_target_pairs={{0,13},{1,0},{4,1},{5,4},{8,5},{9,8},{12,9},{13,12},{2,15},{3,2},{... | collective-permute-start | bytes 393224 | tf_op jit(solution)/shard_map/ppermute | solution.py:298
  22.0 5.3 %collective-permute-start.7 = (f32[4,64,128]{2,1,0:T(8,128)S(1)}, f32[4,64,128]{2,1,0:T(8,128)S(1)}, u32[]{:S(2)}, u32[]{:S(2)}) collective-permute-start(f32[4,64,128]{2,1,0:T(8,128)S(1)} %get-tuple-element.39), channel_id=1, source_target_pairs={{0,2},{2,0},{1,3},{3,1},{4,6},{6,4},{5,7},{7,5},{8,10},{10,8},{9,1... | collective-permute-start | bytes 393224 | tf_op jit(solution)/shard_map/ppermute | solution.py:298
  25.2 2.2 %copy-start.7 = (s32[1,6,4]{1,2,0:T(4,128)S(1)}, s32[1,6,4]{1,2,0:T(4,128)}, u32[]{:S(2)}) copy-start(s32[1,6,4]{1,2,0:T(4,128)} %param.14) | copy-start | bytes 292
  25.2 2.1 %copy-start.10 = (s32[1,6]{1,0:T(1,128)S(1)}, s32[1,6]{1,0:T(1,128)}, u32[]{:S(2)}) copy-start(s32[1,6]{1,0:T(1,128)} %counts.5) | copy-start | bytes 76
  29.0 9.0 %collective-permute-start.8 = (f32[8,64,128]{2,1,0:T(8,128)S(1)}, f32[8,64,128]{2,1,0:T(8,128)S(1)}, u32[]{:S(2)}, u32[]{:S(2)}) collective-permute-start(f32[8,64,128]{2,1,0:T(8,128)S(1)} %get-tuple-element.41), channel_id=1, source_target_pairs={{0,2},{2,0},{1,3},{3,1},{4,6},{6,4},{5,7},{7,5},{8,10},{10,8},{9,1... | collective-permute-start | bytes 786440 | tf_op jit(solution)/shard_map/ppermute | solution.py:298
  30.6 13.5 %collective-permute-start.12 = (f32[8,64,128]{2,1,0:T(8,128)S(1)}, f32[8,64,128]{2,1,0:T(8,128)S(1)}, u32[]{:S(2)}, u32[]{:S(2)}) collective-permute-start(f32[8,64,128]{2,1,0:T(8,128)S(1)} %get-tuple-element.47), channel_id=1, source_target_pairs={{0,2},{2,0},{1,3},{3,1},{4,6},{6,4},{5,7},{7,5},{8,10},{10,8},{9,1... | collective-permute-start | bytes 786440 | tf_op jit(solution)/shard_map/ppermute | solution.py:298
  31.1 13.0 %collective-permute-start.9 = (f32[4,64,128]{2,1,0:T(8,128)S(1)}, f32[4,64,128]{2,1,0:T(8,128)S(1)}, u32[]{:S(2)}, u32[]{:S(2)}) collective-permute-start(f32[4,64,128]{2,1,0:T(8,128)S(1)} %get-tuple-element.44), channel_id=1, source_target_pairs={{0,5},{1,8},{4,9},{5,12},{8,13},{9,0},{12,1},{13,4},{2,7},{3,10},{... | collective-permute-start | bytes 393224 | tf_op jit(solution)/shard_map/ppermute | solution.py:298
  31.1 13.0 %collective-permute-start.10 = (f32[4,64,128]{2,1,0:T(8,128)S(1)}, f32[4,64,128]{2,1,0:T(8,128)S(1)}, u32[]{:S(2)}, u32[]{:S(2)}) collective-permute-start(f32[4,64,128]{2,1,0:T(8,128)S(1)} %get-tuple-element.45), channel_id=1, source_target_pairs={{0,4},{1,5},{4,8},{5,9},{8,12},{9,13},{12,0},{13,1},{2,6},{3,7},{6... | collective-permute-start | bytes 393224 | tf_op jit(solution)/shard_map/ppermute | solution.py:298
  31.5 12.6 %collective-permute-start.11 = (f32[4,64,128]{2,1,0:T(8,128)S(1)}, f32[4,64,128]{2,1,0:T(8,128)S(1)}, u32[]{:S(2)}, u32[]{:S(2)}) collective-permute-start(f32[4,64,128]{2,1,0:T(8,128)S(1)} %get-tuple-element.46), channel_id=1, source_target_pairs={{0,1},{1,4},{4,5},{5,8},{8,9},{9,12},{12,13},{13,0},{2,3},{3,6},{6... | collective-permute-start | bytes 393224 | tf_op jit(solution)/shard_map/ppermute | solution.py:298
  38.8 14.7 %collective-permute-start.15 = (f32[4,64,128]{2,1,0:T(8,128)S(1)}, f32[4,64,128]{2,1,0:T(8,128)S(1)}, u32[]{:S(2)}, u32[]{:S(2)}) collective-permute-start(f32[4,64,128]{2,1,0:T(8,128)S(1)} %get-tuple-element.50), channel_id=1, source_target_pairs={{0,9},{1,12},{4,13},{5,0},{8,1},{9,4},{12,5},{13,8},{2,11},{3,14},... | collective-permute-start | bytes 393224 | tf_op jit(solution)/shard_map/ppermute | solution.py:298
  44.1 11.8 %collective-permute-start.16 = (f32[4,64,128]{2,1,0:T(8,128)S(1)}, f32[4,64,128]{2,1,0:T(8,128)S(1)}, u32[]{:S(2)}, u32[]{:S(2)}) collective-permute-start(f32[4,64,128]{2,1,0:T(8,128)S(1)} %get-tuple-element.51), channel_id=1, source_target_pairs={{0,12},{1,13},{4,0},{5,1},{8,4},{9,5},{12,8},{13,9},{2,14},{3,15},... | collective-permute-start | bytes 393224 | tf_op jit(solution)/shard_map/ppermute | solution.py:298
  45.2 8.3 %copy-start.3 = (f32[12,64,128]{2,1,0:T(8,128)}, f32[12,64,128]{2,1,0:T(8,128)S(1)}, u32[]{:S(2)}) copy-start(f32[12,64,128]{2,1,0:T(8,128)S(1)} %get-tuple-element.49.own) | copy-start | bytes 1179652
  45.2 1.2 %collective-permute-start.13 = (f32[8,128]{1,0:T(8,128)S(1)}, f32[8,128]{1,0:T(8,128)S(1)}, u32[]{:S(2)}, u32[]{:S(2)}) collective-permute-start(f32[8,128]{1,0:T(8,128)S(1)} %get-tuple-element.48.refs_0_), channel_id=1, source_target_pairs={{0,1},{1,0},{2,3},{3,2},{4,5},{5,4},{6,7},{7,6},{8,9},{9,8},{10,11... | collective-permute-start | bytes 12296 | tf_op jit(solution)/shard_map/ppermute | solution.py:323
  46.4 4.1 %collective-permute-start.14 = (f32[8,128]{1,0:T(8,128)S(1)}, f32[8,128]{1,0:T(8,128)S(1)}, u32[]{:S(2)}, u32[]{:S(2)}) collective-permute-start(f32[8,128]{1,0:T(8,128)S(1)} %shard_map.105.refs_0_), channel_id=1, source_target_pairs={{0,2},{2,0},{1,3},{3,1},{4,6},{6,4},{5,7},{7,5},{8,10},{10,8},{9,1... | collective-permute-start | bytes 12296 | tf_op jit(solution)/shard_map/ppermute | solution.py:323
  49.2 8.3 %collective-permute-start.18 = (f32[4,64,128]{2,1,0:T(8,128)}, f32[4,64,128]{2,1,0:T(8,128)}, u32[]{:S(2)}, u32[]{:S(2)}) collective-permute-start(f32[4,64,128]{2,1,0:T(8,128)} %get-tuple-element.53), channel_id=1, source_target_pairs={{0,13},{1,0},{4,1},{5,4},{8,5},{9,8},{12,9},{13,12},{2,15},{3,2},{... | collective-permute-start | bytes 393224 | tf_op jit(solution)/shard_map/ppermute | solution.py:298
  49.9 7.7 %collective-permute-start.17 = (f32[6,64,128]{2,1,0:T(8,128)}, f32[6,64,128]{2,1,0:T(8,128)}, u32[]{:S(2)}, u32[]{:S(2)}) collective-permute-start(f32[6,64,128]{2,1,0:T(8,128)} %get-tuple-element.52), channel_id=1, source_target_pairs={{0,2},{2,0},{1,3},{3,1},{4,6},{6,4},{5,7},{7,5},{8,10},{10,8},{9,1... | collective-permute-start | bytes 589832 | tf_op jit(solution)/shard_map/ppermute | solution.py:298
  51.1 8.6 %collective-permute-start.21 = (f32[8,128]{1,0:T(8,128)}, f32[8,128]{1,0:T(8,128)}, u32[]{:S(2)}, u32[]{:S(2)}) collective-permute-start(f32[8,128]{1,0:T(8,128)} %shard_map.106.refs_1_.refs_0_), channel_id=1, source_target_pairs={{0,12},{4,8},{8,4},{12,0},{1,13},{5,9},{9,5},{13,1},{2,14},{6,10},... | collective-permute-start | bytes 12296 | tf_op jit(solution)/shard_map/ppermute | solution.py:323
  53.5 6.2 %collective-permute-start.20 = (f32[8,128]{1,0:T(8,128)}, f32[8,128]{1,0:T(8,128)}, u32[]{:S(2)}, u32[]{:S(2)}) collective-permute-start(f32[8,128]{1,0:T(8,128)} %shard_map.106.refs_1_.refs_0_), channel_id=1, source_target_pairs={{0,8},{4,12},{8,0},{12,4},{1,9},{5,13},{9,1},{13,5},{2,10},{6,14},... | collective-permute-start | bytes 12296 | tf_op jit(solution)/shard_map/ppermute | solution.py:323
  55.9 3.9 %collective-permute-start.19 = (f32[8,128]{1,0:T(8,128)}, f32[8,128]{1,0:T(8,128)}, u32[]{:S(2)}, u32[]{:S(2)}) collective-permute-start(f32[8,128]{1,0:T(8,128)} %shard_map.106.refs_1_.refs_0_), channel_id=1, source_target_pairs={{0,4},{4,0},{8,12},{12,8},{1,5},{5,1},{9,13},{13,9},{2,6},{6,2},{1... | collective-permute-start | bytes 12296 | tf_op jit(solution)/shard_map/ppermute | solution.py:323
  57.3 1.0 %copy-start.4 = (f32[12,64,128]{2,1,0:T(8,128)S(1)}, f32[12,64,128]{2,1,0:T(8,128)}, u32[]{:S(2)}) copy-start(f32[12,64,128]{2,1,0:T(8,128)} %copy-done.3) | copy-start | bytes 1179652
  57.3 1.0 %copy-start.11 = (s32[1,6]{1,0:T(1,128)S(1)}, s32[1,6]{1,0:T(1,128)}, u32[]{:S(2)}) copy-start(s32[1,6]{1,0:T(1,128)} %counts.5) | copy-start | bytes 76
  57.6 2.3 %copy-start.2 = (f32[1,16,64,128]{3,2,1,0:T(8,128)S(1)}, f32[1,16,64,128]{3,2,1,0:T(8,128)}, u32[]{:S(2)}) copy-start(f32[1,16,64,128]{3,2,1,0:T(8,128)} %param.8) | copy-start | bytes 1572868

commit v6 on v5

--- a/solution.py
+++ b/solution.py
@@ -10,9 +10,9 @@
 SPACE = ("mesh", "rep")
 F32 = jnp.float32
 BF16 = jnp.bfloat16
-PHASES = (((4, 2), (5, 3, 0, 1)), ((4, 2, 0), (5, 3, 1)))
+PHASES = (((4, 2), (3, 5, 1, 0)), ((4, 2, 0), (5, 3, 1)))
 STAGES = (("rep", (1,)), ("tm", (1,)), ("mesh", (1, 2, 3)))
-SPLIT = 2
+SPLIT = (3, 2)
 PIECES = 4
 ORDER = (40, 160, 0, 0)
 
@@ -32,7 +32,7 @@
         cost_estimate=pl.CostEstimate(
             flops=(weight << 30) + 1024, transcendentals=0, bytes_accessed=1024
         ),
-        compiler_params=pltpu.CompilerParams(vmem_limit_bytes=40 << 20),
+        compiler_params=pltpu.CompilerParams(vmem_limit_bytes=16 << 20),
     )(*scalars, *vectors)
 
 
@@ -114,10 +114,17 @@
 
 
 def turn_body(hours, heads, faces, hour, field, *refs):
-    packs, (out, *faces_out) = refs[: hours - 1], refs[-1 - len(heads) :]
+    packs, (out, *faces_out) = refs[: hours - 1], refs[hours - 1 :]
     for b in range(field.shape[0]):
         out[b] = merge_lanes(hours, hour[0], field[b], packs, b)
     pack_faces(faces, out, heads, faces_out)
+
+
+def turn_near_body(hours, heads, faces, hour, columns, field, kappa, stiffness, _, *refs):
+    packs, (near_out, *outs) = refs[: hours - 1], refs[hours - 1 :]
+    outs, scratch = outs[: 1 + len(heads)], outs[1 + len(heads) :]
+    turn_body(hours, heads, faces, hour, field, *packs, *outs)
+    near_body(columns, kappa, stiffness, outs[0], near_out, *scratch)
 
 
 def split_body(stiffness, out):
@@ -127,47 +134,41 @@
         out[q] = jnp.concatenate([high, low, high], axis=1)
 
 
-def near_body(count, columns, kappa, stiffness, *refs):
-    fields, outs, (high, low, diagonal) = refs[:count], refs[-3 - count : -3], refs[-3:]
-    blocks = stiffness.shape[0]
+def near_body(columns, kappa, stiffness, field, out, high, low, diagonal):
+    blocks = field.shape[0]
     slots = columns.shape[0]
-    lanes = fields[0].shape[2]
     diagonal[...] = jnp.transpose(kappa[...])
-    for n, field in enumerate(fields):
-        part = slice(n * lanes, (n + 1) * lanes)
-        for b in range(blocks):
-            high[b, :, part], low[b, :, part] = halves(field[b])
+    for b in range(blocks):
+        high[b], low[b] = halves(field[b])
     for b in range(blocks):
         index = [columns[k, b] for k in range(slots)]
         highs = jnp.concatenate([high[i] for i in index], axis=0)
         lows = jnp.concatenate([low[i] for i in index], axis=0)
         left_high, left_low = halves(stiffness[b])
-        near = jnp.dot(left_high, highs, preferred_element_type=F32)
-        near += jnp.dot(left_low, highs, preferred_element_type=F32)
-        near += jnp.dot(left_high, lows, preferred_element_type=F32)
-        weight = 3.0 + diagonal[:, b : b + 1]
-        for n, (field, out) in enumerate(zip(fields, outs)):
-            out[b] = near[:, n * lanes : (n + 1) * lanes] + weight * field[b]
-
-
-def near(columns, kappa, stiffness, fields, after=()):
-    blocks, width, lanes = fields[0].shape
+        value = jnp.dot(left_high, highs, preferred_element_type=F32)
+        value += jnp.dot(left_low, highs, preferred_element_type=F32)
+        value += jnp.dot(left_high, lows, preferred_element_type=F32)
+        out[b] = value + (3.0 + diagonal[:, b : b + 1]) * field[b]
+
+
+def near_scratch(field):
+    blocks, width, lanes = field.shape
+    return [pltpu.VMEM(field.shape, BF16)] * 2 + [pltpu.VMEM((width, blocks), F32)]
+
+
+def near(columns, kappa, stiffness, field):
     return call(
-        functools.partial(near_body, len(fields)),
-        [struct(*field.shape) for field in fields],
+        near_body,
+        struct(*field.shape),
         [columns],
-        [kappa, stiffness, *fields, *after],
-        [
-            pltpu.VMEM((blocks, width, lanes * len(fields)), BF16),
-            pltpu.VMEM((blocks, width, lanes * len(fields)), BF16),
-            pltpu.VMEM((width, blocks), F32),
-        ],
+        [kappa, stiffness, field],
+        near_scratch(field),
     )
 
 
 def products(heads, stiffness, arrived, out):
-    slots = arrived[0].shape[0]
     for n, e in enumerate(heads):
+        slots = arrived[n].shape[0]
         for f in range(slots):
             out[n * slots + f] = far_product(stiffness, (e ^ 1) * slots + f, arrived[n][f])
 
@@ -178,10 +179,8 @@
     pack_lanes(hours, hour[0], out, packs)
 
 
-def repack_body(hours, heads, faces, hour, own, field, *refs):
-    outs = refs[-(len(heads) + hours - 1) :]
-    pack_faces(faces, field, heads, outs[: len(heads)])
-    pack_lanes(hours, hour[0], own, outs[len(heads) :])
+def repack_body(hours, hour, own, *refs):
+    pack_lanes(hours, hour[0], own, refs[1 - hours :])
 
 
 def sum_body(*refs):
@@ -205,12 +204,21 @@
                 field[landing(faces, counts, e ^ 1, f, blocks)] += value
 
 
-def middle_body(hours, phases, heads, faces, counts, hour, coupling, near_part, own, late, *refs):
+def late_values(phases, done, stiffness, arrived, rest):
+    count = done.shape[0]
+    products(phases[1][len(phases[1]) - len(arrived) :], stiffness, arrived, rest)
+    return lambda q: done[q] if q < count else rest[q - count]
+
+
+def middle_body(
+    hours, phases, heads, split, faces, counts, hour, coupling, near_part, own, done, stiffness, *refs
+):
     turns = hours - 1
-    packs = refs[:turns]
-    first, image, *rest, field = refs[turns:]
-    image_packs, first_packs, faces_out = rest[:turns], rest[turns : 2 * turns], rest[2 * turns :]
-    late = late.__getitem__
+    packs, refs = refs[:turns], refs[turns:]
+    left = len(phases[1]) - split
+    arrived, (first, image, *outs, rest, field) = refs[:left], refs[left:]
+    image_packs, first_packs, faces_out = outs[:turns], outs[turns : 2 * turns], outs[2 * turns :]
+    late = late_values(phases, done, stiffness, arrived, rest)
     gather_far(hours, phases, faces, counts, hour, own, packs, late, near_part, field)
     for b in range(first.shape[0]):
         once = couple(hours, coupling[0], field[b])
@@ -242,21 +250,48 @@
     out[...] = jnp.where(group_of(rows.shape, hours) == hour[0], rows, 0.0)
 
 
-def settle_body(
-    hours, phases, faces, counts, hour, near_part, own, first, done, stiffness, *refs
+def gather_body(
+    hours, phases, split, faces, counts, hour, near_part, own, first, stiffness, *refs
 ):
     turns = hours - 1
-    packs, first_packs, arrived = refs[:turns], refs[turns : 2 * turns], refs[2 * turns :]
-    arrived, (image, out, rest, field) = arrived[:-4], arrived[-4:]
-    count = done.shape[0]
-    products(phases[1][len(phases[1]) - len(arrived) :], stiffness, arrived, rest)
-
-    def late(q):
-        return done[q] if q < count else rest[q - count]
-
-    gather_far(hours, phases, faces, counts, hour, own, packs, late, near_part, field)
-    for b in range(first.shape[0]):
+    first_packs, refs = refs[:turns], refs[turns:]
+    arrived, (image, out, made, field) = refs[:split], refs[split:]
+    blocks, slots = first.shape[0], faces.shape[1]
+    heads = phases[1][:split]
+    products(heads, stiffness, arrived, made)
+    for b in range(blocks):
         image[b] = merge_lanes(hours, hour[0], first[b], first_packs, b)
+        field[b] = near_part[b]
+    mine = group_of(own.shape[1:], hours) == hour[0]
+    for n, e in enumerate(phases[0]):
+        for f in range(slots):
+            block = landing(faces, counts, e ^ 1, f, blocks)
+            field[block] += jnp.where(mine, own[n * slots + f], 0.0)
+    for n, e in enumerate(heads):
+        for f in range(slots):
+            field[landing(faces, counts, e ^ 1, f, blocks)] += made[n * slots + f]
+    for b in range(blocks):
+        out[b] = field[b]
+
+
+def settle_body(hours, phases, split, faces, counts, hour, start, stiffness, *refs):
+    turns = hours - 1
+    packs, refs = refs[:turns], refs[turns:]
+    arrived, (out, made, field) = refs[:-3], refs[-3:]
+    blocks, slots = start.shape[0], faces.shape[1]
+    heads = phases[1][split:]
+    products(heads, stiffness, arrived, made)
+    for b in range(blocks):
+        field[b] = start[b]
+    zero = jnp.zeros(start.shape[1:], F32)
+    for n, e in enumerate(phases[0]):
+        for f in range(slots):
+            value = merge_lanes(hours, hour[0], zero, packs, n * slots + f)
+            field[landing(faces, counts, e ^ 1, f, blocks)] += value
+    for n, e in enumerate(heads):
+        for f in range(slots):
+            field[landing(faces, counts, e ^ 1, f, blocks)] += made[n * slots + f]
+    for b in range(blocks):
         out[b] = field[b]
 
 
@@ -360,15 +395,15 @@
     def products_of(heads):
         return struct(len(heads) * slots, width, lanes)
 
+    def products_in(heads):
+        return pltpu.VMEM((max(len(heads), 1) * slots, width, lanes), F32)
+
     def body(function, *sizes):
         return functools.partial(function, hours, *sizes)
 
-    def turn(heads, field_in, packs, after):
+    def turn(heads, field_in, packs):
         out, *outgoing = call(
-            body(turn_body, heads),
-            [field] + faces_of(heads),
-            [faces, hour],
-            [field_in, *packs, *after],
+            body(turn_body, heads), [field] + faces_of(heads), [faces, hour], [field_in, *packs]
         )
         return out, send_faces(outgoing, heads, offsets)
 
@@ -390,11 +425,11 @@
     )
     packs = send_lanes(outs[:turns])
     early = send_faces(outs[turns:], phases[0], offsets)
-    probe_right, late = turn(phases[1], right, packs, [])
+    probe_right, late = turn(phases[1], right, packs)
     stiffness = call(
         split_body, struct(headings * slots, width, 3 * width, dtype=BF16), [], [far_stiffness]
     )
-    (near_part,) = near(columns, kappa_sq, near_stiffness, [probe_right])
+    near_part = near(columns, kappa_sq, near_stiffness, probe_right)
     out = products_of(phases[0])
     own, *packs = call(
         body(early_body, phases[0]),
@@ -403,20 +438,28 @@
         [stiffness, *early, probe_right],
     )
     packs = send_lanes(packs)
-    late = late_products(phases[1], late, ORDER[0])
+    split = SPLIT[0]
+    done = late_products(phases[1][:split], late[:split], ORDER[0])
     first, image, *outs = call(
-        body(middle_body, phases, heads),
+        body(middle_body, phases, heads, split),
         [field, field] + packs_of(blocks) * 2 + faces_of(heads),
         [faces, counts, hour, time_coupling],
-        [near_part, own, late, *packs],
-        spare,
+        [near_part, own, done, stiffness, *packs, *late[split:]],
+        [products_in(phases[1][split:])] + spare,
     )
 
     phases = PHASES[1]
     packs, first_packs = send_lanes(outs[:turns]), send_lanes(outs[turns : 2 * turns])
     early = send_faces(outs[2 * turns :], phases[0], offsets)
-    (near_probe,) = near(columns, kappa_sq, near_stiffness, [image])
-    hour_image, late = turn(phases[1][:SPLIT], image, packs, [near_probe])
+    near_probe = near(columns, kappa_sq, near_stiffness, image)
+    near_hour, hour_image, *outgoing = call(
+        body(turn_near_body, phases[1]),
+        [field, field] + faces_of(phases[1]),
+        [faces, hour, columns],
+        [image, kappa_sq, near_stiffness, near_probe, *packs],
+        near_scratch(right),
+    )
+    late = send_faces(outgoing, phases[1], offsets)
     own, sums = call(
         body(moments_body, phases[0]),
         [products_of(phases[0]), struct(8, lanes)],
@@ -424,23 +467,29 @@
         [probe_right, first, near_probe, stiffness, *early, *first_packs, hour_image],
     )
     sums, marks = everywhere_sum(sums)
-    heads = phases[1][SPLIT:]
-    outs = call(
-        body(repack_body, heads),
-        faces_of(heads) + packs_of(own.shape[0]),
-        [faces, hour],
-        [own, hour_image, *marks[:1]],
-    )
-    late += send_faces(outs[: len(heads)], heads, offsets)
-    packs = send_lanes(outs[len(heads) :])
-    (near_hour,) = near(columns, kappa_sq, near_stiffness, [hour_image], marks[-1:])
-    done = late_products(phases[1][:SPLIT], late[:SPLIT], ORDER[1])
-    hour_first, second = call(
-        body(settle_body, phases),
+    packs = send_lanes(
+        call(
+            body(repack_body),
+            packs_of(own.shape[0]),
+            [hour],
+            [own, *marks[:1]],
+        )
+    )
+    split = SPLIT[1]
+    hour_first, partial = call(
+        body(gather_body, phases, split),
         [field, field],
         [faces, counts, hour],
-        [near_hour, own, first, done, stiffness, *packs, *first_packs, *late[SPLIT:]],
-        [pltpu.VMEM((len(heads) * slots, width, lanes), F32)] + spare,
+        [near_hour, own, first, stiffness, *first_packs, *late[:split]],
+        [products_in(phases[1][:split])] + spare,
+        weight=ORDER[1],
+    )
+    second = call(
+        body(settle_body, phases, split),
+        field,
+        [faces, counts, hour],
+        [partial, stiffness, *packs, *late[split:]],
+        [products_in(phases[1][split:])] + spare,
     )
     solution_field, residual = call(
         functools.partial(close_body, len(sums)),

time: 61.9 us -> 58.2 us (0.940)
  starting transfers between devices: 26 us -> 23.9 us
  local copies, waits for them, and re-layouts: 2.46 us -> 1.76 us
    ppermute x17, starting transfers between devices: 20.1 us -> 16.9 us  [shifted(): return lax.ppermute(value, axes, route)]
    ppermute x5, starting transfers between devices: 5.94 us -> 6.96 us  [everywhere_sum(): terms += [lax.ppermute(terms[0], axis, route) for route in routes]]
    unnamed x24 -> x18, local copies, waits for them, and re-layouts: 2.46 us -> 1.76 us
    pallas_call x17 -> x16, Pallas kernels: 16.4 us -> 16.2 us  [call(): pl.pallas_call(body, out_shape=outs, in_specs=[pl.BlockSpec(memory_space=...]
  transfers between devices with their start and end apart: 22 -> 22, of which waited for: 6 -> 9; matrix products, arithmetic and copies ran while one was open for 0% -> 0% of each run, Pallas kernels for 20% -> 21%
where the time goes in v6:
time: 58.2 us; the launch traced here: 58 us
  starting transfers between devices  23.9 us (41%)
  Pallas kernels  16.2 us (28%)
  waiting for transfers between devices  14.6 us (25%)
  local copies, waits for them, and re-layouts  1.76 us (3%)
  between operations  1.53 us (3%)
    ppermute x17, starting transfers between devices, shifted(): return lax.ppermute(value, axes, route)  16.9 us
    pallas_call x16, Pallas kernels, call(): pl.pallas_call(body, out_shape=outs, in_specs=[pl.BlockSpec(memory_space=...  16.2 us
    ppermute x17, waiting for transfers between devices, shifted(): return lax.ppermute(value, axes, route)  13.6 us
    ppermute x5, starting transfers between devices, everywhere_sum(): terms += [lax.ppermute(terms[0], axis, route) for route in routes]  6.96 us
    unnamed x18, local copies, waits for them, and re-layouts  1.76 us
  transfers between devices with their start and end apart: 22, of which 9 were waited for; matrix products, arithmetic and copies ran while one was open for 0% of the time, Pallas kernels for 21%

profile of v6, /device:TPU:0, one launch (start us, length us, event | category | flops | bytes accessed | tf_op | source)
XLA Modules:
  0.0 58.0 jit_solution(17564591317869934465)
XLA Ops:
  0.6 0.0 copy-start.1
  0.6 1.0 %copy-done.1 = f32[1,16,64,128]{3,2,1,0:T(8,128)S(1)} copy-done((f32[1,16,64,128]{3,2,1,0:T(8,128)S(1)}, f32[1,16,64,128]{3,2,1,0:T(8,128)}, u32[]{:S(2)}) %copy-start.1) | copy-done | bytes 524312
  1.7 0.7 %copy-done.5 = s32[1,6,4]{1,2,0:T(4,128)S(1)} copy-done((s32[1,6,4]{1,2,0:T(4,128)S(1)}, s32[1,6,4]{1,2,0:T(4,128)}, u32[]{:S(2)}) %copy-start.5) | copy-done | bytes 120
  2.4 0.8 %shard_map.95 = (f32[8,64,128]{2,1,0:T(8,128)S(1)}, f32[4,64,128]{2,1,0:T(8,128)S(1)}, f32[4,64,128]{2,1,0:T(8,128)S(1)}) custom-call(s32[1,4,6]{2,1,0:T(4,128)S(1)} %bitcast.9, s32[1]{0:T(128)} %bitcast.2.hour, f32[16,64,128]{2,1,0:T(8,128)S(1)} %bitcast.6), custom_call_target="tpu_custom_call" | custom-call | flops 1024 | bytes 1024 | tf_op jit(solution)/shard_map/pallas_call | solution.py:26
  3.1 3.0 %collective-permute-start = (f32[8,64,128]{2,1,0:T(8,128)S(1)}, f32[8,64,128]{2,1,0:T(8,128)S(1)}, u32[]{:S(2)}, u32[]{:S(2)}) collective-permute-start(f32[8,64,128]{2,1,0:T(8,128)S(1)} %get-tuple-element.30), channel_id=1, source_target_pairs={{0,2},{2,0},{1,3},{3,1},{4,6},{6,4},{5,7},{7,5},{8,10},{10,8},{9,1... | collective-permute-start | bytes 786440 | tf_op jit(solution)/shard_map/ppermute | solution.py:333
  6.1 0.7 %collective-permute-start.1 = (f32[4,64,128]{2,1,0:T(8,128)S(1)}, f32[4,64,128]{2,1,0:T(8,128)S(1)}, u32[]{:S(2)}, u32[]{:S(2)}) collective-permute-start(f32[4,64,128]{2,1,0:T(8,128)S(1)} %get-tuple-element.32), channel_id=1, source_target_pairs={{0,5},{1,8},{4,9},{5,12},{8,13},{9,0},{12,1},{13,4},{2,7},{3,10},{... | collective-permute-start | bytes 393224 | tf_op jit(solution)/shard_map/ppermute | solution.py:333
  6.9 1.6 %collective-permute-start.2 = (f32[4,64,128]{2,1,0:T(8,128)S(1)}, f32[4,64,128]{2,1,0:T(8,128)S(1)}, u32[]{:S(2)}, u32[]{:S(2)}) collective-permute-start(f32[4,64,128]{2,1,0:T(8,128)S(1)} %get-tuple-element.33), channel_id=1, source_target_pairs={{0,4},{1,5},{4,8},{5,9},{8,12},{9,13},{12,0},{13,1},{2,6},{3,7},{6... | collective-permute-start | bytes 393224 | tf_op jit(solution)/shard_map/ppermute | solution.py:333
  8.5 4.0 %collective-permute-done.refs_0_ = f32[8,64,128]{2,1,0:T(8,128)S(1)} collective-permute-done((f32[8,64,128]{2,1,0:T(8,128)S(1)}, f32[8,64,128]{2,1,0:T(8,128)S(1)}, u32[]{:S(2)}, u32[]{:S(2)}) %collective-permute-start) | collective-permute-done | bytes 262176 | tf_op jit(solution)/shard_map/ppermute | solution.py:333
  12.4 0.8 %shard_map.96 = (f32[16,64,128]{2,1,0:T(8,128)S(1)}, f32[4,64,128]{2,1,0:T(8,128)S(1)}, f32[4,64,128]{2,1,0:T(8,128)S(1)}, f32[4,64,128]{2,1,0:T(8,128)S(1)}, f32[4,64,128]{2,1,0:T(8,128)S(1)}) custom-call(s32[1,4,6]{2,1,0:T(4,128)S(1)} %bitcast.10, s32[1]{0:T(128)} %bitcast.2.hour, f32[16,64,128]{2,1,0:T(8,128)S(1)} %bitcast.7, ...), custom_call_target="tpu_custom_call" | custom-call | flops 1024 | bytes 1024 | tf_op jit(solution)/shard_map/pallas_call | solution.py:26
  13.3 0.0 copy-start
  13.3 0.0 copy-start.4
  13.3 0.0 copy-start.7
  13.3 3.9 %collective-permute-start.3 = (f32[4,64,128]{2,1,0:T(8,128)S(1)}, f32[4,64,128]{2,1,0:T(8,128)S(1)}, u32[]{:S(2)}, u32[]{:S(2)}) collective-permute-start(f32[4,64,128]{2,1,0:T(8,128)S(1)} %get-tuple-element.35), channel_id=1, source_target_pairs={{0,12},{1,13},{4,0},{5,1},{8,4},{9,5},{12,8},{13,9},{2,14},{3,15},... | collective-permute-start | bytes 393224 | tf_op jit(solution)/shard_map/ppermute | solution.py:333
  17.2 0.0 collective-permute-start.4
  17.2 0.6 %collective-permute-start.5 = (f32[4,64,128]{2,1,0:T(8,128)S(1)}, f32[4,64,128]{2,1,0:T(8,128)S(1)}, u32[]{:S(2)}, u32[]{:S(2)}) collective-permute-start(f32[4,64,128]{2,1,0:T(8,128)S(1)} %get-tuple-element.37), channel_id=1, source_target_pairs={{0,13},{1,0},{4,1},{5,4},{8,5},{9,8},{12,9},{13,12},{2,15},{3,2},{... | collective-permute-start | bytes 393224 | tf_op jit(solution)/shard_map/ppermute | solution.py:333
  17.8 0.2 shard_map.98.stiffness
  18.6 0.0 collective-permute-done.1.refs_0_
  18.7 0.0 collective-permute-done.2.refs_1_
  18.7 0.3 shard_map.99
  19.0 1.6 %collective-permute-start.6 = (f32[4,64,128]{2,1,0:T(8,128)S(1)}, f32[4,64,128]{2,1,0:T(8,128)S(1)}, u32[]{:S(2)}, u32[]{:S(2)}) collective-permute-start(f32[4,64,128]{2,1,0:T(8,128)S(1)} %get-tuple-element.38), channel_id=1, source_target_pairs={{0,2},{2,0},{1,3},{3,1},{4,6},{6,4},{5,7},{7,5},{8,10},{10,8},{9,1... | collective-permute-start | bytes 393224 | tf_op jit(solution)/shard_map/ppermute | solution.py:333
  20.6 0.0 collective-permute-start.7
  20.6 1.6 %shard_map.97.near_part = f32[16,64,128]{2,1,0:T(8,128)S(1)} custom-call(s32[6,16]{1,0:T(8,128)S(1)} %bitcast.16, f32[16,64]{1,0:T(8,128)S(1)} %copy-done.4, f32[16,64,384]{2,1,0:T(8,128)S(1)} %copy-done, f32[16,64,128]{2,1,0:T(8,128)S(1)} %get-tuple-element.31.field.refs_2_.right), custom_call_target="tpu_custom_call" | custom-call | flops 1024 | bytes 1024 | tf_op jit(solution)/shard_map/pallas_call | solution.py:26
  22.2 0.0 copy-start.6
  22.2 0.0 copy-start.8
  22.3 0.0 collective-permute-done.3.refs_0_
  22.3 0.7 %collective-permute-done.4.refs_1_ = f32[4,64,128]{2,1,0:T(8,128)S(1)} collective-permute-done((f32[4,64,128]{2,1,0:T(8,128)S(1)}, f32[4,64,128]{2,1,0:T(8,128)S(1)}, u32[]{:S(2)}, u32[]{:S(2)}) %collective-permute-start.4) | collective-permute-done | bytes 131104 | tf_op jit(solution)/shard_map/ppermute | solution.py:333
  22.9 1.9 %collective-permute-done.5.refs_2_ = f32[4,64,128]{2,1,0:T(8,128)S(1)} collective-permute-done((f32[4,64,128]{2,1,0:T(8,128)S(1)}, f32[4,64,128]{2,1,0:T(8,128)S(1)}, u32[]{:S(2)}, u32[]{:S(2)}) %collective-permute-start.5) | collective-permute-done | bytes 131104 | tf_op jit(solution)/shard_map/ppermute | solution.py:333
  24.8 0.3 shard_map.100.done
  25.2 0.0 collective-permute-done.6.refs_0_
  25.2 1.7 %collective-permute-done.7.refs_1_ = f32[4,64,128]{2,1,0:T(8,128)S(1)} collective-permute-done((f32[4,64,128]{2,1,0:T(8,128)S(1)}, f32[4,64,128]{2,1,0:T(8,128)S(1)}, u32[]{:S(2)}, u32[]{:S(2)}) %collective-permute-start.7) | collective-permute-done | bytes 131104 | tf_op jit(solution)/shard_map/ppermute | solution.py:333
  26.9 1.7 %shard_map.101 = (f32[16,64,128]{2,1,0:T(8,128)S(1)}, f32[16,64,128]{2,1,0:T(8,128)S(1)}, f32[8,64,128]{2,1,0:T(8,128)S(1)}, f32[8,64,128]{2,1,0:T(8,128)S(1)}, ...) custom-call(s32[1,4,6]{2,1,0:T(4,128)S(1)} %bitcast.11, s32[1,6]{1,0:T(1,128)S(1)} %copy-done.8, ...), custom_call_target="tpu_custom_call" | custom-call | flops 1024 | bytes 1024 | tf_op jit(solution)/shard_map/pallas_call | solution.py:26
  28.6 0.9 %collective-permute-start.8 = (f32[8,64,128]{2,1,0:T(8,128)S(1)}, f32[8,64,128]{2,1,0:T(8,128)S(1)}, u32[]{:S(2)}, u32[]{:S(2)}) collective-permute-start(f32[8,64,128]{2,1,0:T(8,128)S(1)} %get-tuple-element.41), channel_id=1, source_target_pairs={{0,2},{2,0},{1,3},{3,1},{4,6},{6,4},{5,7},{7,5},{8,10},{10,8},{9,1... | collective-permute-start | bytes 786440 | tf_op jit(solution)/shard_map/ppermute | solution.py:333
  29.5 1.2 %collective-permute-start.12 = (f32[8,64,128]{2,1,0:T(8,128)S(1)}, f32[8,64,128]{2,1,0:T(8,128)S(1)}, u32[]{:S(2)}, u32[]{:S(2)}) collective-permute-start(f32[8,64,128]{2,1,0:T(8,128)S(1)} %get-tuple-element.47), channel_id=1, source_target_pairs={{0,2},{2,0},{1,3},{3,1},{4,6},{6,4},{5,7},{7,5},{8,10},{10,8},{9,1... | collective-permute-start | bytes 786440 | tf_op jit(solution)/shard_map/ppermute | solution.py:333
  30.7 0.2 collective-permute-start.9
  30.8 0.6 %collective-permute-start.10 = (f32[4,64,128]{2,1,0:T(8,128)S(1)}, f32[4,64,128]{2,1,0:T(8,128)S(1)}, u32[]{:S(2)}, u32[]{:S(2)}) collective-permute-start(f32[4,64,128]{2,1,0:T(8,128)S(1)} %get-tuple-element.45), channel_id=1, source_target_pairs={{0,4},{1,5},{4,8},{5,9},{8,12},{9,13},{12,0},{13,1},{2,6},{3,7},{6... | collective-permute-start | bytes 393224 | tf_op jit(solution)/shard_map/ppermute | solution.py:333
  31.4 1.8 %collective-permute-start.11 = (f32[4,64,128]{2,1,0:T(8,128)S(1)}, f32[4,64,128]{2,1,0:T(8,128)S(1)}, u32[]{:S(2)}, u32[]{:S(2)}) collective-permute-start(f32[4,64,128]{2,1,0:T(8,128)S(1)} %get-tuple-element.46), channel_id=1, source_target_pairs={{0,1},{1,4},{4,5},{5,8},{8,9},{9,12},{12,13},{13,0},{2,3},{3,6},{6... | collective-permute-start | bytes 393224 | tf_op jit(solution)/shard_map/ppermute | solution.py:333
  33.2 1.6 %shard_map.102._.second = f32[16,64,128]{2,1,0:T(8,128)S(1)} custom-call(s32[6,16]{1,0:T(8,128)S(1)} %bitcast.17, f32[16,64]{1,0:T(8,128)S(1)} %copy-done.4, f32[16,64,384]{2,1,0:T(8,128)S(1)} %copy-done, f32[16,64,128]{2,1,0:T(8,128)S(1)} %get-tuple-element.40.field), custom_call_target="tpu_custom_call" | custom-call | flops 1024 | bytes 1024 | tf_op jit(solution)/shard_map/pallas_call | solution.py:26
  34.9 3.0 %collective-permute-done.8.refs_0_ = f32[8,64,128]{2,1,0:T(8,128)S(1)} collective-permute-done((f32[8,64,128]{2,1,0:T(8,128)S(1)}, f32[8,64,128]{2,1,0:T(8,128)S(1)}, u32[]{:S(2)}, u32[]{:S(2)}) %collective-permute-start.8) | collective-permute-done | bytes 262176 | tf_op jit(solution)/shard_map/ppermute | solution.py:333
  37.9 2.4 %shard_map.103 = (f32[16,64,128]{2,1,0:T(8,128)S(1)}, f32[16,64,128]{2,1,0:T(8,128)S(1)}, f32[4,64,128]{2,1,0:T(8,128)S(1)}, f32[4,64,128]{2,1,0:T(8,128)S(1)}, f32[4,64,128]{2,1,0:T(8,128)}) custom-call(s32[1,4,6]{2,1,0:T(4,128)S(1)} %bitcast.12, s32[1]{0:T(128)} %bitcast.2.hour, s32[6,16]{1,0:T(8,128)S(1)} %bitcast.18, ...), custom_call_target="tpu_custom_call" | custom-call | flops 1024 | bytes 1024 | tf_op jit(solution)/shard_map/pallas_call | solution.py:26
  40.3 0.0 collective-permute-start.13
  40.3 1.7 %collective-permute-done.9.refs_0_ = f32[4,64,128]{2,1,0:T(8,128)S(1)} collective-permute-done((f32[4,64,128]{2,1,0:T(8,128)S(1)}, f32[4,64,128]{2,1,0:T(8,128)S(1)}, u32[]{:S(2)}, u32[]{:S(2)}) %collective-permute-start.9) | collective-permute-done | bytes 131104 | tf_op jit(solution)/shard_map/ppermute | solution.py:333
  41.9 0.0 collective-permute-start.14
  41.9 0.0 collective-permute-done.12.refs_3_.refs_0_
  41.9 1.1 %shard_map.104 = (f32[12,64,128]{2,1,0:T(8,128)S(1)}, f32[8,128]{1,0:T(8,128)S(1)}) custom-call(s32[1,4,6]{2,1,0:T(4,128)S(1)} %bitcast.13, s32[1,6]{1,0:T(1,128)S(1)} %copy-done.8, s32[1]{0:T(128)} %bitcast.2.hour, f32[16,64,128]{2,1,0:T(8,128)S(1)} %get-tuple-element.31.field.refs_2_.right, f32[16,64,128]{2,1,0:T(8,128)S(1)} %get-tuple-element.43.first, ...), custom_call_target="tpu_custom_call" | custom-call | flops 1024 | bytes 1024 | tf_op jit(solution)/shard_map/pallas_call | solution.py:26
  43.0 0.8 %collective-permute-start.15 = (f32[8,128]{1,0:T(8,128)S(1)}, f32[8,128]{1,0:T(8,128)S(1)}, u32[]{:S(2)}, u32[]{:S(2)}) collective-permute-start(f32[8,128]{1,0:T(8,128)S(1)} %get-tuple-element.54.refs_0_), channel_id=1, source_target_pairs={{0,1},{1,0},{2,3},{3,2},{4,5},{5,4},{6,7},{7,6},{8,9},{9,8},{10,11... | collective-permute-start | bytes 12296 | tf_op jit(solution)/shard_map/ppermute | solution.py:358
  43.8 0.8 %collective-permute-done.15.refs_1_ = f32[8,128]{1,0:T(8,128)S(1)} collective-permute-done((f32[8,128]{1,0:T(8,128)S(1)}, f32[8,128]{1,0:T(8,128)S(1)}, u32[]{:S(2)}, u32[]{:S(2)}) %collective-permute-start.15) | collective-permute-done | bytes 4128 | tf_op jit(solution)/shard_map/ppermute | solution.py:358
  44.7 1.7 %collective-permute-start.18 = (f32[8,128]{1,0:T(8,128)S(1)}, f32[8,128]{1,0:T(8,128)S(1)}, u32[]{:S(2)}, u32[]{:S(2)}) collective-permute-start(f32[8,128]{1,0:T(8,128)S(1)} %shard_map.106.refs_0_), channel_id=1, source_target_pairs={{0,2},{2,0},{1,3},{3,1},{4,6},{6,4},{5,7},{7,5},{8,10},{10,8},{9,1... | collective-permute-start | bytes 12296 | tf_op jit(solution)/shard_map/ppermute | solution.py:358
  46.4 0.0 collective-permute-start.17
  46.4 0.8 %shard_map.107 = f32[6,64,128]{2,1,0:T(8,128)} custom-call(s32[1]{0:T(128)} %bitcast.2.hour, f32[12,64,128]{2,1,0:T(8,128)S(1)} %get-tuple-element.49.own, f32[8,128]{1,0:T(8,128)S(1)} %shard_map.106.refs_0_), custom_call_target="tpu_custom_call" | custom-call | flops 1024 | bytes 1024 | tf_op jit(solution)/shard_map/pallas_call | solution.py:26
  47.3 0.9 %collective-permute-start.16 = (f32[6,64,128]{2,1,0:T(8,128)}, f32[6,64,128]{2,1,0:T(8,128)}, u32[]{:S(2)}, u32[]{:S(2)}) collective-permute-start(f32[6,64,128]{2,1,0:T(8,128)} %shard_map.107), channel_id=1, source_target_pairs={{0,2},{2,0},{1,3},{3,1},{4,6},{6,4},{5,7},{7,5},{8,10},{10,8},{9,1... | collective-permute-start | bytes 589832 | tf_op jit(solution)/shard_map/ppermute | solution.py:333
  48.1 0.1 collective-permute-done.18.refs_1_
  48.3 0.6 %shard_map.109.refs_0_ = f32[8,128]{1,0:T(8,128)} custom-call(f32[8,128]{1,0:T(8,128)S(1)} %shard_map.106.refs_0_, f32[8,128]{1,0:T(8,128)S(1)} %collective-permute-done.18.refs_1_), custom_call_target="tpu_custom_call" | custom-call | flops 1024 | bytes 1024 | tf_op jit(solution)/shard_map/pallas_call | solution.py:26
  48.9 1.7 %collective-permute-start.21 = (f32[8,128]{1,0:T(8,128)}, f32[8,128]{1,0:T(8,128)}, u32[]{:S(2)}, u32[]{:S(2)}) collective-permute-start(f32[8,128]{1,0:T(8,128)} %shard_map.109.refs_0_), channel_id=1, source_target_pairs={{0,12},{4,8},{8,4},{12,0},{1,13},{5,9},{9,5},{13,1},{2,14},{6,10},... | collective-permute-start | bytes 12296 | tf_op jit(solution)/shard_map/ppermute | solution.py:358
  50.5 0.0 collective-permute-done.13.refs_1_
  50.5 1.3 %collective-permute-start.20 = (f32[8,128]{1,0:T(8,128)}, f32[8,128]{1,0:T(8,128)}, u32[]{:S(2)}, u32[]{:S(2)}) collective-permute-start(f32[8,128]{1,0:T(8,128)} %shard_map.109.refs_0_), channel_id=1, source_target_pairs={{0,8},{4,12},{8,0},{12,4},{1,9},{5,13},{9,1},{13,5},{2,10},{6,14},... | collective-permute-start | bytes 12296 | tf_op jit(solution)/shard_map/ppermute | solution.py:358
  51.9 0.0 collective-permute-done.14.refs_2_
  51.9 1.4 %collective-permute-start.19 = (f32[8,128]{1,0:T(8,128)}, f32[8,128]{1,0:T(8,128)}, u32[]{:S(2)}, u32[]{:S(2)}) collective-permute-start(f32[8,128]{1,0:T(8,128)} %shard_map.109.refs_0_), channel_id=1, source_target_pairs={{0,4},{4,0},{8,12},{12,8},{1,5},{5,1},{9,13},{13,9},{2,6},{6,2},{1... | collective-permute-start | bytes 12296 | tf_op jit(solution)/shard_map/ppermute | solution.py:358
  53.3 0.9 %shard_map.105 = (f32[16,64,128]{2,1,0:T(8,128)S(1)}, f32[16,64,128]{2,1,0:T(8,128)S(1)}) custom-call(s32[1,4,6]{2,1,0:T(4,128)S(1)} %bitcast.14, s32[1,6]{1,0:T(1,128)S(1)} %copy-done.8, s32[1]{0:T(128)} %bitcast.2.hour, f32[16,64,128]{2,1,0:T(8,128)S(1)} %get-tuple-element.42.near_part, f32[12,64,128]{2,1,0:T(8,128)S(1)} %get-tuple-element.49.own, ...), custom_call_target="tpu_custom_call" | custom-call | flops 171798691840 | bytes 1024 | tf_op jit(solution)/shard_map/pallas_call | solution.py:26
  54.2 0.0 copy-start.2
  54.2 0.7 %collective-permute-done.16.refs_0_ = f32[6,64,128]{2,1,0:T(8,128)} collective-permute-done((f32[6,64,128]{2,1,0:T(8,128)}, f32[6,64,128]{2,1,0:T(8,128)}, u32[]{:S(2)}, u32[]{:S(2)}) %collective-permute-start.16) | collective-permute-done | bytes 196640 | tf_op jit(solution)/shard_map/ppermute | solution.py:333
  54.9 1.3 %shard_map.108.second = f32[16,64,128]{2,1,0:T(8,128)S(1)} custom-call(s32[1,4,6]{2,1,0:T(4,128)S(1)} %bitcast.15, s32[1,6]{1,0:T(1,128)S(1)} %copy-done.8, s32[1]{0:T(128)} %bitcast.2.hour, f32[16,64,128]{2,1,0:T(8,128)S(1)} %get-tuple-element.53.start, bf16[24,64,192]{2,1,0:T(8,128)(2,1)S(1)} %shard_map.98.stiffness, ...), custom_call_target="tpu_custom_call" | custom-call | flops 1024 | bytes 1024 | tf_op jit(solution)/shard_map/pallas_call | solution.py:26
  56.2 0.0 collective-permute-done.21.refs_3_
  56.2 0.0 collective-permute-done.20.refs_2_
  56.2 1.8 %shard_map.110 = (f32[16,64,128]{2,1,0:T(8,128)}, f32[16,64,128]{2,1,0:T(8,128)}) custom-call(f32[16,64,128]{2,1,0:T(8,128)S(1)} %bitcast.8, f32[16,64,128]{2,1,0:T(8,128)S(1)} %get-tuple-element.52.first, f32[16,64,128]{2,1,0:T(8,128)S(1)} %shard_map.108.second, f32[8,128]{1,0:T(8,128)} %shard_map.109.refs_0_, f32[8,128]{1,0:T(8,128)} %collective-permute-done.19.refs_1_, ...), custom_call_target="tpu_custom_call" | custom-call | flops 1024 | bytes 1024 | tf_op jit(solution)/shard_map/pallas_call | solution.py:26
  (14 shorter events, 0.0 us)
Async XLA Ops:
  0.6 1.0 %copy-start.1 = (f32[1,16,64,128]{3,2,1,0:T(8,128)S(1)}, f32[1,16,64,128]{3,2,1,0:T(8,128)}, u32[]{:S(2)}) copy-start(f32[1,16,64,128]{3,2,1,0:T(8,128)} %param.8) | copy-start | bytes 1572868
  1.7 0.7 %copy-start.5 = (s32[1,6,4]{1,2,0:T(4,128)S(1)}, s32[1,6,4]{1,2,0:T(4,128)}, u32[]{:S(2)}) copy-start(s32[1,6,4]{1,2,0:T(4,128)} %param.14) | copy-start | bytes 292
  2.4 15.5 %copy-start.3 = (f32[1,64,1536]{2,1,0:T(8,128)S(1)}, f32[1,64,1536]{2,1,0:T(8,128)}, u32[]{:S(2)}) copy-start(f32[1,64,1536]{2,1,0:T(8,128)} %stiffness.5) | copy-start | bytes 1179652
  3.1 9.3 %collective-permute-start = (f32[8,64,128]{2,1,0:T(8,128)S(1)}, f32[8,64,128]{2,1,0:T(8,128)S(1)}, u32[]{:S(2)}, u32[]{:S(2)}) collective-permute-start(f32[8,64,128]{2,1,0:T(8,128)S(1)} %get-tuple-element.30), channel_id=1, source_target_pairs={{0,2},{2,0},{1,3},{3,1},{4,6},{6,4},{5,7},{7,5},{8,10},{10,8},{9,1... | collective-permute-start | bytes 786440 | tf_op jit(solution)/shard_map/ppermute | solution.py:333
  6.1 12.5 %collective-permute-start.1 = (f32[4,64,128]{2,1,0:T(8,128)S(1)}, f32[4,64,128]{2,1,0:T(8,128)S(1)}, u32[]{:S(2)}, u32[]{:S(2)}) collective-permute-start(f32[4,64,128]{2,1,0:T(8,128)S(1)} %get-tuple-element.32), channel_id=1, source_target_pairs={{0,5},{1,8},{4,9},{5,12},{8,13},{9,0},{12,1},{13,4},{2,7},{3,10},{... | collective-permute-start | bytes 393224 | tf_op jit(solution)/shard_map/ppermute | solution.py:333
  6.9 11.8 %collective-permute-start.2 = (f32[4,64,128]{2,1,0:T(8,128)S(1)}, f32[4,64,128]{2,1,0:T(8,128)S(1)}, u32[]{:S(2)}, u32[]{:S(2)}) collective-permute-start(f32[4,64,128]{2,1,0:T(8,128)S(1)} %get-tuple-element.33), channel_id=1, source_target_pairs={{0,4},{1,5},{4,8},{5,9},{8,12},{9,13},{12,0},{13,1},{2,6},{3,7},{6... | collective-permute-start | bytes 393224 | tf_op jit(solution)/shard_map/ppermute | solution.py:333
  13.3 7.3 %copy-start = (f32[16,64,384]{2,1,0:T(8,128)S(1)}, f32[16,64,384]{2,1,0:T(8,128)}, u32[]{:S(2)}) copy-start(f32[16,64,384]{2,1,0:T(8,128)} %stiffness.7) | copy-start | bytes 4718596
  13.3 7.3 %copy-start.4 = (f32[16,64]{1,0:T(8,128)S(1)}, f32[16,64]{1,0:T(8,128)}, u32[]{:S(2)}) copy-start(f32[16,64]{1,0:T(8,128)} %kappa.5) | copy-start | bytes 12292
  13.3 7.3 %copy-start.7 = (s32[16,6]{0,1:T(8,128)S(1)}, s32[16,6]{0,1:T(8,128)}, u32[]{:S(2)}) copy-start(s32[16,6]{0,1:T(8,128)} %param.13) | copy-start | bytes 1156
  13.3 9.0 %collective-permute-start.3 = (f32[4,64,128]{2,1,0:T(8,128)S(1)}, f32[4,64,128]{2,1,0:T(8,128)S(1)}, u32[]{:S(2)}, u32[]{:S(2)}) collective-permute-start(f32[4,64,128]{2,1,0:T(8,128)S(1)} %get-tuple-element.35), channel_id=1, source_target_pairs={{0,12},{1,13},{4,0},{5,1},{8,4},{9,5},{12,8},{13,9},{2,14},{3,15},... | collective-permute-start | bytes 393224 | tf_op jit(solution)/shard_map/ppermute | solution.py:333
  17.2 5.8 %collective-permute-start.4 = (f32[4,64,128]{2,1,0:T(8,128)S(1)}, f32[4,64,128]{2,1,0:T(8,128)S(1)}, u32[]{:S(2)}, u32[]{:S(2)}) collective-permute-start(f32[4,64,128]{2,1,0:T(8,128)S(1)} %get-tuple-element.36), channel_id=1, source_target_pairs={{0,9},{1,12},{4,13},{5,0},{8,1},{9,4},{12,5},{13,8},{2,11},{3,14},... | collective-permute-start | bytes 393224 | tf_op jit(solution)/shard_map/ppermute | solution.py:333
  17.2 7.6 %collective-permute-start.5 = (f32[4,64,128]{2,1,0:T(8,128)S(1)}, f32[4,64,128]{2,1,0:T(8,128)S(1)}, u32[]{:S(2)}, u32[]{:S(2)}) collective-permute-start(f32[4,64,128]{2,1,0:T(8,128)S(1)} %get-tuple-element.37), channel_id=1, source_target_pairs={{0,13},{1,0},{4,1},{5,4},{8,5},{9,8},{12,9},{13,12},{2,15},{3,2},{... | collective-permute-start | bytes 393224 | tf_op jit(solution)/shard_map/ppermute | solution.py:333
  19.0 6.2 %collective-permute-start.6 = (f32[4,64,128]{2,1,0:T(8,128)S(1)}, f32[4,64,128]{2,1,0:T(8,128)S(1)}, u32[]{:S(2)}, u32[]{:S(2)}) collective-permute-start(f32[4,64,128]{2,1,0:T(8,128)S(1)} %get-tuple-element.38), channel_id=1, source_target_pairs={{0,2},{2,0},{1,3},{3,1},{4,6},{6,4},{5,7},{7,5},{8,10},{10,8},{9,1... | collective-permute-start | bytes 393224 | tf_op jit(solution)/shard_map/ppermute | solution.py:333
  20.6 6.3 %collective-permute-start.7 = (f32[4,64,128]{2,1,0:T(8,128)S(1)}, f32[4,64,128]{2,1,0:T(8,128)S(1)}, u32[]{:S(2)}, u32[]{:S(2)}) collective-permute-start(f32[4,64,128]{2,1,0:T(8,128)S(1)} %get-tuple-element.39), channel_id=1, source_target_pairs={{0,1},{1,4},{4,5},{5,8},{8,9},{9,12},{12,13},{13,0},{2,3},{3,6},{6... | collective-permute-start | bytes 393224 | tf_op jit(solution)/shard_map/ppermute | solution.py:333
  22.2 4.6 %copy-start.6 = (s32[1,6,4]{1,2,0:T(4,128)S(1)}, s32[1,6,4]{1,2,0:T(4,128)}, u32[]{:S(2)}) copy-start(s32[1,6,4]{1,2,0:T(4,128)} %param.14) | copy-start | bytes 292
  22.2 4.6 %copy-start.8 = (s32[1,6]{1,0:T(1,128)S(1)}, s32[1,6]{1,0:T(1,128)}, u32[]{:S(2)}) copy-start(s32[1,6]{1,0:T(1,128)} %counts.7) | copy-start | bytes 76
  28.6 9.3 %collective-permute-start.8 = (f32[8,64,128]{2,1,0:T(8,128)S(1)}, f32[8,64,128]{2,1,0:T(8,128)S(1)}, u32[]{:S(2)}, u32[]{:S(2)}) collective-permute-start(f32[8,64,128]{2,1,0:T(8,128)S(1)} %get-tuple-element.41), channel_id=1, source_target_pairs={{0,2},{2,0},{1,3},{3,1},{4,6},{6,4},{5,7},{7,5},{8,10},{10,8},{9,1... | collective-permute-start | bytes 786440 | tf_op jit(solution)/shard_map/ppermute | solution.py:333
  29.5 12.5 %collective-permute-start.12 = (f32[8,64,128]{2,1,0:T(8,128)S(1)}, f32[8,64,128]{2,1,0:T(8,128)S(1)}, u32[]{:S(2)}, u32[]{:S(2)}) collective-permute-start(f32[8,64,128]{2,1,0:T(8,128)S(1)} %get-tuple-element.47), channel_id=1, source_target_pairs={{0,2},{2,0},{1,3},{3,1},{4,6},{6,4},{5,7},{7,5},{8,10},{10,8},{9,1... | collective-permute-start | bytes 786440 | tf_op jit(solution)/shard_map/ppermute | solution.py:333
  30.7 11.3 %collective-permute-start.9 = (f32[4,64,128]{2,1,0:T(8,128)S(1)}, f32[4,64,128]{2,1,0:T(8,128)S(1)}, u32[]{:S(2)}, u32[]{:S(2)}) collective-permute-start(f32[4,64,128]{2,1,0:T(8,128)S(1)} %get-tuple-element.44), channel_id=1, source_target_pairs={{0,5},{1,8},{4,9},{5,12},{8,13},{9,0},{12,1},{13,4},{2,7},{3,10},{... | collective-permute-start | bytes 393224 | tf_op jit(solution)/shard_map/ppermute | solution.py:333
  30.8 11.1 %collective-permute-start.10 = (f32[4,64,128]{2,1,0:T(8,128)S(1)}, f32[4,64,128]{2,1,0:T(8,128)S(1)}, u32[]{:S(2)}, u32[]{:S(2)}) collective-permute-start(f32[4,64,128]{2,1,0:T(8,128)S(1)} %get-tuple-element.45), channel_id=1, source_target_pairs={{0,4},{1,5},{4,8},{5,9},{8,12},{9,13},{12,0},{13,1},{2,6},{3,7},{6... | collective-permute-start | bytes 393224 | tf_op jit(solution)/shard_map/ppermute | solution.py:333
  31.4 10.5 %collective-permute-start.11 = (f32[4,64,128]{2,1,0:T(8,128)S(1)}, f32[4,64,128]{2,1,0:T(8,128)S(1)}, u32[]{:S(2)}, u32[]{:S(2)}) collective-permute-start(f32[4,64,128]{2,1,0:T(8,128)S(1)} %get-tuple-element.46), channel_id=1, source_target_pairs={{0,1},{1,4},{4,5},{5,8},{8,9},{9,12},{12,13},{13,0},{2,3},{3,6},{6... | collective-permute-start | bytes 393224 | tf_op jit(solution)/shard_map/ppermute | solution.py:333
  40.3 10.3 %collective-permute-start.13 = (f32[4,64,128]{2,1,0:T(8,128)S(1)}, f32[4,64,128]{2,1,0:T(8,128)S(1)}, u32[]{:S(2)}, u32[]{:S(2)}) collective-permute-start(f32[4,64,128]{2,1,0:T(8,128)S(1)} %get-tuple-element.50), channel_id=1, source_target_pairs={{0,9},{1,12},{4,13},{5,0},{8,1},{9,4},{12,5},{13,8},{2,11},{3,14},... | collective-permute-start | bytes 393224 | tf_op jit(solution)/shard_map/ppermute | solution.py:333
  41.9 9.9 %collective-permute-start.14 = (f32[4,64,128]{2,1,0:T(8,128)S(1)}, f32[4,64,128]{2,1,0:T(8,128)S(1)}, u32[]{:S(2)}, u32[]{:S(2)}) collective-permute-start(f32[4,64,128]{2,1,0:T(8,128)S(1)} %get-tuple-element.51), channel_id=1, source_target_pairs={{0,12},{1,13},{4,0},{5,1},{8,4},{9,5},{12,8},{13,9},{2,14},{3,15},... | collective-permute-start | bytes 393224 | tf_op jit(solution)/shard_map/ppermute | solution.py:333
  43.0 1.7 %collective-permute-start.15 = (f32[8,128]{1,0:T(8,128)S(1)}, f32[8,128]{1,0:T(8,128)S(1)}, u32[]{:S(2)}, u32[]{:S(2)}) collective-permute-start(f32[8,128]{1,0:T(8,128)S(1)} %get-tuple-element.54.refs_0_), channel_id=1, source_target_pairs={{0,1},{1,0},{2,3},{3,2},{4,5},{5,4},{6,7},{7,6},{8,9},{9,8},{10,11... | collective-permute-start | bytes 12296 | tf_op jit(solution)/shard_map/ppermute | solution.py:358
  44.7 3.6 %collective-permute-start.18 = (f32[8,128]{1,0:T(8,128)S(1)}, f32[8,128]{1,0:T(8,128)S(1)}, u32[]{:S(2)}, u32[]{:S(2)}) collective-permute-start(f32[8,128]{1,0:T(8,128)S(1)} %shard_map.106.refs_0_), channel_id=1, source_target_pairs={{0,2},{2,0},{1,3},{3,1},{4,6},{6,4},{5,7},{7,5},{8,10},{10,8},{9,1... | collective-permute-start | bytes 12296 | tf_op jit(solution)/shard_map/ppermute | solution.py:358
  46.4 7.8 %collective-permute-start.17 = (f32[4,64,128]{2,1,0:T(8,128)}, f32[4,64,128]{2,1,0:T(8,128)}, u32[]{:S(2)}, u32[]{:S(2)}) collective-permute-start(f32[4,64,128]{2,1,0:T(8,128)} %get-tuple-element.55), channel_id=1, source_target_pairs={{0,13},{1,0},{4,1},{5,4},{8,5},{9,8},{12,9},{13,12},{2,15},{3,2},{... | collective-permute-start | bytes 393224 | tf_op jit(solution)/shard_map/ppermute | solution.py:333
  47.3 7.6 %collective-permute-start.16 = (f32[6,64,128]{2,1,0:T(8,128)}, f32[6,64,128]{2,1,0:T(8,128)}, u32[]{:S(2)}, u32[]{:S(2)}) collective-permute-start(f32[6,64,128]{2,1,0:T(8,128)} %shard_map.107), channel_id=1, source_target_pairs={{0,2},{2,0},{1,3},{3,1},{4,6},{6,4},{5,7},{7,5},{8,10},{10,8},{9,1... | collective-permute-start | bytes 589832 | tf_op jit(solution)/shard_map/ppermute | solution.py:333
  48.9 7.3 %collective-permute-start.21 = (f32[8,128]{1,0:T(8,128)}, f32[8,128]{1,0:T(8,128)}, u32[]{:S(2)}, u32[]{:S(2)}) collective-permute-start(f32[8,128]{1,0:T(8,128)} %shard_map.109.refs_0_), channel_id=1, source_target_pairs={{0,12},{4,8},{8,4},{12,0},{1,13},{5,9},{9,5},{13,1},{2,14},{6,10},... | collective-permute-start | bytes 12296 | tf_op jit(solution)/shard_map/ppermute | solution.py:358
  50.5 5.6 %collective-permute-start.20 = (f32[8,128]{1,0:T(8,128)}, f32[8,128]{1,0:T(8,128)}, u32[]{:S(2)}, u32[]{:S(2)}) collective-permute-start(f32[8,128]{1,0:T(8,128)} %shard_map.109.refs_0_), channel_id=1, source_target_pairs={{0,8},{4,12},{8,0},{12,4},{1,9},{5,13},{9,1},{13,5},{2,10},{6,14},... | collective-permute-start | bytes 12296 | tf_op jit(solution)/shard_map/ppermute | solution.py:358
  51.9 4.3 %collective-permute-start.19 = (f32[8,128]{1,0:T(8,128)}, f32[8,128]{1,0:T(8,128)}, u32[]{:S(2)}, u32[]{:S(2)}) collective-permute-start(f32[8,128]{1,0:T(8,128)} %shard_map.109.refs_0_), channel_id=1, source_target_pairs={{0,4},{4,0},{8,12},{12,8},{1,5},{5,1},{9,13},{13,9},{2,6},{6,2},{1... | collective-permute-start | bytes 12296 | tf_op jit(solution)/shard_map/ppermute | solution.py:358
  54.2 2.0 %copy-start.2 = (f32[1,16,64,128]{3,2,1,0:T(8,128)S(1)}, f32[1,16,64,128]{3,2,1,0:T(8,128)}, u32[]{:S(2)}) copy-start(f32[1,16,64,128]{3,2,1,0:T(8,128)} %param.8) | copy-start | bytes 1572868

commit v7 on v6

--- a/solution.py
+++ b/solution.py
@@ -21,8 +21,10 @@
     return jax.ShapeDtypeStruct(shape, dtype)
 
 
-def call(body, outs, scalars, vectors, scratch=(), weight=0, outs_in=pltpu.VMEM):
-    spaces = [pltpu.SMEM] * len(scalars) + [pltpu.VMEM] * len(vectors)
+def call(
+    body, outs, scalars, vectors, scratch=(), weight=0, vectors_in=pltpu.VMEM, outs_in=pltpu.VMEM
+):
+    spaces = [pltpu.SMEM] * len(scalars) + [vectors_in] * len(vectors)
     return pl.pallas_call(
         body,
         out_shape=outs,
@@ -108,9 +110,20 @@
     return jnp.where(f < counts[0, e], faces[0, f, e], spare)
 
 
-def open_body(hours, heads, faces, hour, field, *outs):
+def open_body(hours, heads, hour, faces_in, field_in, *refs):
+    (field, table, *outs), (faces, sems) = refs[:-2], refs[-2:]
+    copies = [
+        pltpu.make_async_copy(field_in, field, sems.at[0]),
+        pltpu.make_async_copy(faces_in, faces, sems.at[1]),
+        pltpu.make_async_copy(faces_in, table, sems.at[2]),
+    ]
+    for copy in copies:
+        copy.start()
+    copies[0].wait()
     pack_lanes(hours, hour[0], field, outs[: hours - 1])
+    copies[1].wait()
     pack_faces(faces, field, heads, outs[hours - 1 :])
+    copies[2].wait()
 
 
 def turn_body(hours, heads, faces, hour, field, *refs):
@@ -184,7 +197,7 @@
 
 
 def sum_body(*refs):
-    refs[-1][...] = total([ref[...] for ref in refs[:-1]])
+    refs[-1][...] = refs[-2][...] = total([ref[...] for ref in refs[:-2]])
 
 
 def late_body(heads, stiffness, *refs):
@@ -350,14 +363,17 @@
             continue
         if len(terms) > 1:
             weight = ORDER[2 + len(marks)]
-            terms = [call(sum_body, struct(*value.shape), [], terms, weight=weight)]
+            sent, kept = call(sum_body, [struct(*value.shape)] * 2, [], terms, weight=weight)
+            terms = [kept]
             marks += terms
+        else:
+            sent = value
         count = lax.axis_size(axis)
         if count in (2, 4):
             routes = [[(i, i ^ k) for i in range(count)] for k in partners]
-            terms += [lax.ppermute(terms[0], axis, route) for route in routes]
+            terms += [lax.ppermute(sent, axis, route) for route in routes]
         else:
-            terms = [lax.psum(terms[0], axis)]
+            terms = [lax.psum(sent, axis)]
             summed.append(axis)
     return terms, marks
 
@@ -417,15 +433,21 @@
         )
 
     phases, (heads, _) = PHASES
-    outs = call(
+    kept, table, *outs = call(
         body(open_body, phases[0]),
-        packs_of(blocks) + faces_of(phases[0]),
-        [faces, hour],
-        [right],
-    )
+        [field, struct(*faces.shape, dtype=jnp.int32)] + packs_of(blocks) + faces_of(phases[0]),
+        [hour],
+        [pltpu.with_memory_space_constraint(v, pltpu.HBM) for v in (faces, right)],
+        [
+            pltpu.SMEM(faces.shape, jnp.int32),
+            pltpu.SemaphoreType.DMA((3,)),
+        ],
+        vectors_in=pltpu.HBM,
+    )
+    faces = table
     packs = send_lanes(outs[:turns])
     early = send_faces(outs[turns:], phases[0], offsets)
-    probe_right, late = turn(phases[1], right, packs)
+    probe_right, late = turn(phases[1], kept, packs)
     stiffness = call(
         split_body, struct(headings * slots, width, 3 * width, dtype=BF16), [], [far_stiffness]
     )

time: 58.2 us -> 57 us (0.979)
  local copies, waits for them, and re-layouts: 1.76 us -> 0.04 us
    unnamed x18 -> x12, local copies, waits for them, and re-layouts: 1.76 us -> 0.04 us
where the time goes in v7:
time: 57 us; the launch traced here: 56.8 us
  starting transfers between devices  23.9 us (42%)
  Pallas kernels  16.7 us (29%)
  waiting for transfers between devices  14.6 us (26%)
  between operations  1.52 us (3%)
    ppermute x17, starting transfers between devices, shifted(): return lax.ppermute(value, axes, route)  17 us
    pallas_call x16, Pallas kernels, call(): pl.pallas_call(body, out_shape=outs, in_specs=[pl.BlockSpec(memory_space=...  16.7 us
    ppermute x17, waiting for transfers between devices, shifted(): return lax.ppermute(value, axes, route)  13.6 us
    ppermute x5, starting transfers between devices, everywhere_sum(): terms += [lax.ppermute(sent, axis, route) for route in routes]  6.97 us
  transfers between devices with their start and end apart: 22, of which 9 were waited for; matrix products, arithmetic and copies ran while one was open for 0% of the time, Pallas kernels for 21%

profile of v7, /device:TPU:0, one launch (start us, length us, event | category | flops | bytes accessed | tf_op | source)
XLA Modules:
  0.0 56.8 jit_solution(5773493084686344118)
XLA Ops:
  0.6 1.4 %shard_map.95 = (f32[16,64,128]{2,1,0:T(8,128)S(1)}, s32[1,4,6]{2,1,0:T(4,128)S(1)}, f32[8,64,128]{2,1,0:T(8,128)S(1)}, f32[4,64,128]{2,1,0:T(8,128)S(1)}, f32[4,64,128]{2,1,0:T(8,128)S(1)}) custom-call(s32[1]{0:T(128)} %bitcast.1.hour, s32[1,4,6]{2,1,0:T(4,128)} %bitcast.11, f32[16,64,128]{2,1,0:T(8,128)} %bitcast.6), custom_call_target="tpu_custom_call" | custom-call | flops 1024 | bytes 1024 | tf_op jit(solution)/shard_map/pallas_call | solution.py:28
  2.0 3.0 %collective-permute-start = (f32[8,64,128]{2,1,0:T(8,128)S(1)}, f32[8,64,128]{2,1,0:T(8,128)S(1)}, u32[]{:S(2)}, u32[]{:S(2)}) collective-permute-start(f32[8,64,128]{2,1,0:T(8,128)S(1)} %get-tuple-element.38), channel_id=1, source_target_pairs={{0,2},{2,0},{1,3},{3,1},{4,6},{6,4},{5,7},{7,5},{8,10},{10,8},{9,1... | collective-permute-start | bytes 786440 | tf_op jit(solution)/shard_map/ppermute | solution.py:346
  5.0 0.7 %collective-permute-start.1 = (f32[4,64,128]{2,1,0:T(8,128)S(1)}, f32[4,64,128]{2,1,0:T(8,128)S(1)}, u32[]{:S(2)}, u32[]{:S(2)}) collective-permute-start(f32[4,64,128]{2,1,0:T(8,128)S(1)} %get-tuple-element.40), channel_id=1, source_target_pairs={{0,5},{1,8},{4,9},{5,12},{8,13},{9,0},{12,1},{13,4},{2,7},{3,10},{... | collective-permute-start | bytes 393224 | tf_op jit(solution)/shard_map/ppermute | solution.py:346
  5.7 1.6 %collective-permute-start.2 = (f32[4,64,128]{2,1,0:T(8,128)S(1)}, f32[4,64,128]{2,1,0:T(8,128)S(1)}, u32[]{:S(2)}, u32[]{:S(2)}) collective-permute-start(f32[4,64,128]{2,1,0:T(8,128)S(1)} %get-tuple-element.41), channel_id=1, source_target_pairs={{0,4},{1,5},{4,8},{5,9},{8,12},{9,13},{12,0},{13,1},{2,6},{3,7},{6... | collective-permute-start | bytes 393224 | tf_op jit(solution)/shard_map/ppermute | solution.py:346
  7.3 4.0 %collective-permute-done.refs_0_ = f32[8,64,128]{2,1,0:T(8,128)S(1)} collective-permute-done((f32[8,64,128]{2,1,0:T(8,128)S(1)}, f32[8,64,128]{2,1,0:T(8,128)S(1)}, u32[]{:S(2)}, u32[]{:S(2)}) %collective-permute-start) | collective-permute-done | bytes 262176 | tf_op jit(solution)/shard_map/ppermute | solution.py:346
  11.3 0.8 %shard_map.96 = (f32[16,64,128]{2,1,0:T(8,128)S(1)}, f32[4,64,128]{2,1,0:T(8,128)S(1)}, f32[4,64,128]{2,1,0:T(8,128)S(1)}, f32[4,64,128]{2,1,0:T(8,128)S(1)}, f32[4,64,128]{2,1,0:T(8,128)S(1)}) custom-call(s32[1,4,6]{2,1,0:T(4,128)S(1)} %get-tuple-element.36.faces, s32[1]{0:T(128)} %bitcast.1.hour, f32[16,64,128]{2,1,0:T(8,128)S(1)} %get-tuple-element.37.field, ...), custom_call_target="tpu_custom_call" | custom-call | flops 1024 | bytes 1024 | tf_op jit(solution)/shard_map/pallas_call | solution.py:28
  12.1 0.0 copy-start
  12.1 0.0 copy-start.3
  12.2 0.0 copy-start.4
  12.2 3.9 %collective-permute-start.3 = (f32[4,64,128]{2,1,0:T(8,128)S(1)}, f32[4,64,128]{2,1,0:T(8,128)S(1)}, u32[]{:S(2)}, u32[]{:S(2)}) collective-permute-start(f32[4,64,128]{2,1,0:T(8,128)S(1)} %get-tuple-element.43), channel_id=1, source_target_pairs={{0,12},{1,13},{4,0},{5,1},{8,4},{9,5},{12,8},{13,9},{2,14},{3,15},... | collective-permute-start | bytes 393224 | tf_op jit(solution)/shard_map/ppermute | solution.py:346
  16.1 0.0 collective-permute-start.4
  16.1 0.6 %collective-permute-start.5 = (f32[4,64,128]{2,1,0:T(8,128)S(1)}, f32[4,64,128]{2,1,0:T(8,128)S(1)}, u32[]{:S(2)}, u32[]{:S(2)}) collective-permute-start(f32[4,64,128]{2,1,0:T(8,128)S(1)} %get-tuple-element.45), channel_id=1, source_target_pairs={{0,13},{1,0},{4,1},{5,4},{8,5},{9,8},{12,9},{13,12},{2,15},{3,2},{... | collective-permute-start | bytes 393224 | tf_op jit(solution)/shard_map/ppermute | solution.py:346
  16.7 0.2 shard_map.98.stiffness
  17.5 0.0 collective-permute-done.1.refs_0_
  17.5 0.0 collective-permute-done.2.refs_1_
  17.5 0.3 shard_map.99
  17.9 1.6 %collective-permute-start.6 = (f32[4,64,128]{2,1,0:T(8,128)S(1)}, f32[4,64,128]{2,1,0:T(8,128)S(1)}, u32[]{:S(2)}, u32[]{:S(2)}) collective-permute-start(f32[4,64,128]{2,1,0:T(8,128)S(1)} %get-tuple-element.46), channel_id=1, source_target_pairs={{0,2},{2,0},{1,3},{3,1},{4,6},{6,4},{5,7},{7,5},{8,10},{10,8},{9,1... | collective-permute-start | bytes 393224 | tf_op jit(solution)/shard_map/ppermute | solution.py:346
  19.4 0.0 collective-permute-start.7
  19.5 1.6 %shard_map.97.near_part = f32[16,64,128]{2,1,0:T(8,128)S(1)} custom-call(s32[6,16]{1,0:T(8,128)S(1)} %bitcast.8, f32[16,64]{1,0:T(8,128)S(1)} %copy-done.3, f32[16,64,384]{2,1,0:T(8,128)S(1)} %copy-done, f32[16,64,128]{2,1,0:T(8,128)S(1)} %get-tuple-element.39.field.refs_2_.right), custom_call_target="tpu_custom_call" | custom-call | flops 1024 | bytes 1024 | tf_op jit(solution)/shard_map/pallas_call | solution.py:28
  21.1 0.0 copy-start.5
  21.1 0.0 collective-permute-done.3.refs_0_
  21.1 0.7 %collective-permute-done.4.refs_1_ = f32[4,64,128]{2,1,0:T(8,128)S(1)} collective-permute-done((f32[4,64,128]{2,1,0:T(8,128)S(1)}, f32[4,64,128]{2,1,0:T(8,128)S(1)}, u32[]{:S(2)}, u32[]{:S(2)}) %collective-permute-start.4) | collective-permute-done | bytes 131104 | tf_op jit(solution)/shard_map/ppermute | solution.py:346
  21.8 1.9 %collective-permute-done.5.refs_2_ = f32[4,64,128]{2,1,0:T(8,128)S(1)} collective-permute-done((f32[4,64,128]{2,1,0:T(8,128)S(1)}, f32[4,64,128]{2,1,0:T(8,128)S(1)}, u32[]{:S(2)}, u32[]{:S(2)}) %collective-permute-start.5) | collective-permute-done | bytes 131104 | tf_op jit(solution)/shard_map/ppermute | solution.py:346
  23.7 0.3 shard_map.100.done
  24.0 0.0 collective-permute-done.6.refs_0_
  24.0 1.7 %collective-permute-done.7.refs_1_ = f32[4,64,128]{2,1,0:T(8,128)S(1)} collective-permute-done((f32[4,64,128]{2,1,0:T(8,128)S(1)}, f32[4,64,128]{2,1,0:T(8,128)S(1)}, u32[]{:S(2)}, u32[]{:S(2)}) %collective-permute-start.7) | collective-permute-done | bytes 131104 | tf_op jit(solution)/shard_map/ppermute | solution.py:346
  25.7 1.7 %shard_map.101 = (f32[16,64,128]{2,1,0:T(8,128)S(1)}, f32[16,64,128]{2,1,0:T(8,128)S(1)}, f32[8,64,128]{2,1,0:T(8,128)S(1)}, f32[8,64,128]{2,1,0:T(8,128)S(1)}, ...) custom-call(s32[1,4,6]{2,1,0:T(4,128)S(1)} %get-tuple-element.36.faces, ...), custom_call_target="tpu_custom_call" | custom-call | flops 1024 | bytes 1024 | tf_op jit(solution)/shard_map/pallas_call | solution.py:28
  27.4 0.9 %collective-permute-start.8 = (f32[8,64,128]{2,1,0:T(8,128)S(1)}, f32[8,64,128]{2,1,0:T(8,128)S(1)}, u32[]{:S(2)}, u32[]{:S(2)}) collective-permute-start(f32[8,64,128]{2,1,0:T(8,128)S(1)} %get-tuple-element.49), channel_id=1, source_target_pairs={{0,2},{2,0},{1,3},{3,1},{4,6},{6,4},{5,7},{7,5},{8,10},{10,8},{9,1... | collective-permute-start | bytes 786440 | tf_op jit(solution)/shard_map/ppermute | solution.py:346
  28.3 1.2 %collective-permute-start.12 = (f32[8,64,128]{2,1,0:T(8,128)S(1)}, f32[8,64,128]{2,1,0:T(8,128)S(1)}, u32[]{:S(2)}, u32[]{:S(2)}) collective-permute-start(f32[8,64,128]{2,1,0:T(8,128)S(1)} %get-tuple-element.55), channel_id=1, source_target_pairs={{0,2},{2,0},{1,3},{3,1},{4,6},{6,4},{5,7},{7,5},{8,10},{10,8},{9,1... | collective-permute-start | bytes 786440 | tf_op jit(solution)/shard_map/ppermute | solution.py:346
  29.5 0.2 collective-permute-start.9
  29.7 0.7 %collective-permute-start.10 = (f32[4,64,128]{2,1,0:T(8,128)S(1)}, f32[4,64,128]{2,1,0:T(8,128)S(1)}, u32[]{:S(2)}, u32[]{:S(2)}) collective-permute-start(f32[4,64,128]{2,1,0:T(8,128)S(1)} %get-tuple-element.53), channel_id=1, source_target_pairs={{0,4},{1,5},{4,8},{5,9},{8,12},{9,13},{12,0},{13,1},{2,6},{3,7},{6... | collective-permute-start | bytes 393224 | tf_op jit(solution)/shard_map/ppermute | solution.py:346
  30.3 1.8 %collective-permute-start.11 = (f32[4,64,128]{2,1,0:T(8,128)S(1)}, f32[4,64,128]{2,1,0:T(8,128)S(1)}, u32[]{:S(2)}, u32[]{:S(2)}) collective-permute-start(f32[4,64,128]{2,1,0:T(8,128)S(1)} %get-tuple-element.54), channel_id=1, source_target_pairs={{0,1},{1,4},{4,5},{5,8},{8,9},{9,12},{12,13},{13,0},{2,3},{3,6},{6... | collective-permute-start | bytes 393224 | tf_op jit(solution)/shard_map/ppermute | solution.py:346
  32.1 1.6 %shard_map.102._.second = f32[16,64,128]{2,1,0:T(8,128)S(1)} custom-call(s32[6,16]{1,0:T(8,128)S(1)} %bitcast.9, f32[16,64]{1,0:T(8,128)S(1)} %copy-done.3, f32[16,64,384]{2,1,0:T(8,128)S(1)} %copy-done, f32[16,64,128]{2,1,0:T(8,128)S(1)} %get-tuple-element.48.field), custom_call_target="tpu_custom_call" | custom-call | flops 1024 | bytes 1024 | tf_op jit(solution)/shard_map/pallas_call | solution.py:28
  33.7 3.0 %collective-permute-done.8.refs_0_ = f32[8,64,128]{2,1,0:T(8,128)S(1)} collective-permute-done((f32[8,64,128]{2,1,0:T(8,128)S(1)}, f32[8,64,128]{2,1,0:T(8,128)S(1)}, u32[]{:S(2)}, u32[]{:S(2)}) %collective-permute-start.8) | collective-permute-done | bytes 262176 | tf_op jit(solution)/shard_map/ppermute | solution.py:346
  36.7 2.4 %shard_map.103 = (f32[16,64,128]{2,1,0:T(8,128)S(1)}, f32[16,64,128]{2,1,0:T(8,128)S(1)}, f32[4,64,128]{2,1,0:T(8,128)S(1)}, f32[4,64,128]{2,1,0:T(8,128)S(1)}, f32[4,64,128]{2,1,0:T(8,128)}) custom-call(s32[1,4,6]{2,1,0:T(4,128)S(1)} %get-tuple-element.36.faces, s32[1]{0:T(128)} %bitcast.1.hour, s32[6,16]{1,0:T(8,128)S(1)} %bitcast.10, ...), custom_call_target="tpu_custom_call" | custom-call | flops 1024 | bytes 1024 | tf_op jit(solution)/shard_map/pallas_call | solution.py:28
  39.1 0.0 collective-permute-start.13
  39.1 1.7 %collective-permute-done.9.refs_0_ = f32[4,64,128]{2,1,0:T(8,128)S(1)} collective-permute-done((f32[4,64,128]{2,1,0:T(8,128)S(1)}, f32[4,64,128]{2,1,0:T(8,128)S(1)}, u32[]{:S(2)}, u32[]{:S(2)}) %collective-permute-start.9) | collective-permute-done | bytes 131104 | tf_op jit(solution)/shard_map/ppermute | solution.py:346
  40.8 0.0 collective-permute-start.14
  40.8 0.0 collective-permute-done.10.refs_1_
  40.8 0.0 collective-permute-done.11.refs_2_
  40.8 0.0 collective-permute-done.12.refs_3_.refs_0_
  40.8 1.1 %shard_map.104 = (f32[12,64,128]{2,1,0:T(8,128)S(1)}, f32[8,128]{1,0:T(8,128)S(1)}) custom-call(s32[1,4,6]{2,1,0:T(4,128)S(1)} %get-tuple-element.36.faces, s32[1,6]{1,0:T(1,128)S(1)} %copy-done.5, s32[1]{0:T(128)} %bitcast.1.hour, f32[16,64,128]{2,1,0:T(8,128)S(1)} %get-tuple-element.39.field.refs_2_.right, f32[16,64,128]{2,1,0:T(8,128)S(1)} %get-tuple-element.51.first, ...), custom_call_target="tpu_custom_call" | custom-call | flops 1024 | bytes 1024 | tf_op jit(solution)/shard_map/pallas_call | solution.py:28
  41.9 0.8 %collective-permute-start.15 = (f32[8,128]{1,0:T(8,128)S(1)}, f32[8,128]{1,0:T(8,128)S(1)}, u32[]{:S(2)}, u32[]{:S(2)}) collective-permute-start(f32[8,128]{1,0:T(8,128)S(1)} %get-tuple-element.62.refs_0_), channel_id=1, source_target_pairs={{0,1},{1,0},{2,3},{3,2},{4,5},{5,4},{6,7},{7,6},{8,9},{9,8},{10,11... | collective-permute-start | bytes 12296 | tf_op jit(solution)/shard_map/ppermute | solution.py:374
  42.7 0.8 %collective-permute-done.15.refs_1_ = f32[8,128]{1,0:T(8,128)S(1)} collective-permute-done((f32[8,128]{1,0:T(8,128)S(1)}, f32[8,128]{1,0:T(8,128)S(1)}, u32[]{:S(2)}, u32[]{:S(2)}) %collective-permute-start.15) | collective-permute-done | bytes 4128 | tf_op jit(solution)/shard_map/ppermute | solution.py:374
  43.5 1.7 %collective-permute-start.18 = (f32[8,128]{1,0:T(8,128)S(1)}, f32[8,128]{1,0:T(8,128)S(1)}, u32[]{:S(2)}, u32[]{:S(2)}) collective-permute-start(f32[8,128]{1,0:T(8,128)S(1)} %get-tuple-element.65), channel_id=1, source_target_pairs={{0,2},{2,0},{1,3},{3,1},{4,6},{6,4},{5,7},{7,5},{8,10},{10,8},{9,1... | collective-permute-start | bytes 12296 | tf_op jit(solution)/shard_map/ppermute | solution.py:374
  45.3 0.0 collective-permute-start.17
  45.3 0.8 %shard_map.107 = f32[6,64,128]{2,1,0:T(8,128)} custom-call(s32[1]{0:T(128)} %bitcast.1.hour, f32[12,64,128]{2,1,0:T(8,128)S(1)} %get-tuple-element.57.own, f32[8,128]{1,0:T(8,128)S(1)} %get-tuple-element.63.refs_0_), custom_call_target="tpu_custom_call" | custom-call | flops 1024 | bytes 1024 | tf_op jit(solution)/shard_map/pallas_call | solution.py:28
  46.1 0.9 %collective-permute-start.16 = (f32[6,64,128]{2,1,0:T(8,128)}, f32[6,64,128]{2,1,0:T(8,128)}, u32[]{:S(2)}, u32[]{:S(2)}) collective-permute-start(f32[6,64,128]{2,1,0:T(8,128)} %shard_map.107), channel_id=1, source_target_pairs={{0,2},{2,0},{1,3},{3,1},{4,6},{6,4},{5,7},{7,5},{8,10},{10,8},{9,1... | collective-permute-start | bytes 589832 | tf_op jit(solution)/shard_map/ppermute | solution.py:346
  47.0 0.1 collective-permute-done.18.refs_1_
  47.1 0.6 %shard_map.109 = (f32[8,128]{1,0:T(8,128)}, f32[8,128]{1,0:T(8,128)S(1)}) custom-call(f32[8,128]{1,0:T(8,128)S(1)} %get-tuple-element.63.refs_0_, f32[8,128]{1,0:T(8,128)S(1)} %collective-permute-done.18.refs_1_), custom_call_target="tpu_custom_call" | custom-call | flops 1024 | bytes 1024 | tf_op jit(solution)/shard_map/pallas_call | solution.py:28
  47.7 1.7 %collective-permute-start.21 = (f32[8,128]{1,0:T(8,128)}, f32[8,128]{1,0:T(8,128)}, u32[]{:S(2)}, u32[]{:S(2)}) collective-permute-start(f32[8,128]{1,0:T(8,128)} %get-tuple-element.67), channel_id=1, source_target_pairs={{0,12},{4,8},{8,4},{12,0},{1,13},{5,9},{9,5},{13,1},{2,14},{6,10},... | collective-permute-start | bytes 12296 | tf_op jit(solution)/shard_map/ppermute | solution.py:374
  49.4 0.0 collective-permute-done.13.refs_1_
  49.4 1.3 %collective-permute-start.20 = (f32[8,128]{1,0:T(8,128)}, f32[8,128]{1,0:T(8,128)}, u32[]{:S(2)}, u32[]{:S(2)}) collective-permute-start(f32[8,128]{1,0:T(8,128)} %get-tuple-element.67), channel_id=1, source_target_pairs={{0,8},{4,12},{8,0},{12,4},{1,9},{5,13},{9,1},{13,5},{2,10},{6,14},... | collective-permute-start | bytes 12296 | tf_op jit(solution)/shard_map/ppermute | solution.py:374
  50.7 0.0 collective-permute-done.14.refs_2_
  50.7 1.4 %collective-permute-start.19 = (f32[8,128]{1,0:T(8,128)}, f32[8,128]{1,0:T(8,128)}, u32[]{:S(2)}, u32[]{:S(2)}) collective-permute-start(f32[8,128]{1,0:T(8,128)} %get-tuple-element.67), channel_id=1, source_target_pairs={{0,4},{4,0},{8,12},{12,8},{1,5},{5,1},{9,13},{13,9},{2,6},{6,2},{1... | collective-permute-start | bytes 12296 | tf_op jit(solution)/shard_map/ppermute | solution.py:374
  52.1 0.9 %shard_map.105 = (f32[16,64,128]{2,1,0:T(8,128)S(1)}, f32[16,64,128]{2,1,0:T(8,128)S(1)}) custom-call(s32[1,4,6]{2,1,0:T(4,128)S(1)} %get-tuple-element.36.faces, s32[1,6]{1,0:T(1,128)S(1)} %copy-done.5, s32[1]{0:T(128)} %bitcast.1.hour, f32[16,64,128]{2,1,0:T(8,128)S(1)} %get-tuple-element.50.near_part, f32[12,64,128]{2,1,0:T(8,128)S(1)} %get-tuple-element.57.own, ...), custom_call_target="tpu_custom_call" | custom-call | flops 171798691840 | bytes 1024 | tf_op jit(solution)/shard_map/pallas_call | solution.py:28
  53.0 0.0 copy-start.1
  53.1 0.0 collective-permute-done.17.refs_1_
  53.1 0.7 %collective-permute-done.16.refs_0_ = f32[6,64,128]{2,1,0:T(8,128)} collective-permute-done((f32[6,64,128]{2,1,0:T(8,128)}, f32[6,64,128]{2,1,0:T(8,128)}, u32[]{:S(2)}, u32[]{:S(2)}) %collective-permute-start.16) | collective-permute-done | bytes 196640 | tf_op jit(solution)/shard_map/ppermute | solution.py:346
  53.7 1.3 %shard_map.108.second = f32[16,64,128]{2,1,0:T(8,128)S(1)} custom-call(s32[1,4,6]{2,1,0:T(4,128)S(1)} %get-tuple-element.36.faces, s32[1,6]{1,0:T(1,128)S(1)} %copy-done.5, s32[1]{0:T(128)} %bitcast.1.hour, f32[16,64,128]{2,1,0:T(8,128)S(1)} %get-tuple-element.61.start, bf16[24,64,192]{2,1,0:T(8,128)(2,1)S(1)} %shard_map.98.stiffness, ...), custom_call_target="tpu_custom_call" | custom-call | flops 1024 | bytes 1024 | tf_op jit(solution)/shard_map/pallas_call | solution.py:28
  55.0 0.0 collective-permute-done.21.refs_3_
  55.0 0.0 collective-permute-done.20.refs_2_
  55.0 0.0 collective-permute-done.19.refs_1_
  55.1 1.8 %shard_map.110 = (f32[16,64,128]{2,1,0:T(8,128)}, f32[16,64,128]{2,1,0:T(8,128)}) custom-call(f32[16,64,128]{2,1,0:T(8,128)S(1)} %bitcast.7, f32[16,64,128]{2,1,0:T(8,128)S(1)} %get-tuple-element.60.first, f32[16,64,128]{2,1,0:T(8,128)S(1)} %shard_map.108.second, f32[8,128]{1,0:T(8,128)S(1)} %get-tuple-element.66.refs_0_, ...), custom_call_target="tpu_custom_call" | custom-call | flops 1024 | bytes 1024 | tf_op jit(solution)/shard_map/pallas_call | solution.py:28
  (8 shorter events, 0.0 us)
Async XLA Ops:
  0.6 16.1 %copy-start.2 = (f32[1,64,1536]{2,1,0:T(8,128)S(1)}, f32[1,64,1536]{2,1,0:T(8,128)}, u32[]{:S(2)}) copy-start(f32[1,64,1536]{2,1,0:T(8,128)} %stiffness.5) | copy-start | bytes 1179652
  2.0 9.3 %collective-permute-start = (f32[8,64,128]{2,1,0:T(8,128)S(1)}, f32[8,64,128]{2,1,0:T(8,128)S(1)}, u32[]{:S(2)}, u32[]{:S(2)}) collective-permute-start(f32[8,64,128]{2,1,0:T(8,128)S(1)} %get-tuple-element.38), channel_id=1, source_target_pairs={{0,2},{2,0},{1,3},{3,1},{4,6},{6,4},{5,7},{7,5},{8,10},{10,8},{9,1... | collective-permute-start | bytes 786440 | tf_op jit(solution)/shard_map/ppermute | solution.py:346
  5.0 12.5 %collective-permute-start.1 = (f32[4,64,128]{2,1,0:T(8,128)S(1)}, f32[4,64,128]{2,1,0:T(8,128)S(1)}, u32[]{:S(2)}, u32[]{:S(2)}) collective-permute-start(f32[4,64,128]{2,1,0:T(8,128)S(1)} %get-tuple-element.40), channel_id=1, source_target_pairs={{0,5},{1,8},{4,9},{5,12},{8,13},{9,0},{12,1},{13,4},{2,7},{3,10},{... | collective-permute-start | bytes 393224 | tf_op jit(solution)/shard_map/ppermute | solution.py:346
  5.7 11.8 %collective-permute-start.2 = (f32[4,64,128]{2,1,0:T(8,128)S(1)}, f32[4,64,128]{2,1,0:T(8,128)S(1)}, u32[]{:S(2)}, u32[]{:S(2)}) collective-permute-start(f32[4,64,128]{2,1,0:T(8,128)S(1)} %get-tuple-element.41), channel_id=1, source_target_pairs={{0,4},{1,5},{4,8},{5,9},{8,12},{9,13},{12,0},{13,1},{2,6},{3,7},{6... | collective-permute-start | bytes 393224 | tf_op jit(solution)/shard_map/ppermute | solution.py:346
  12.1 7.3 %copy-start = (f32[16,64,384]{2,1,0:T(8,128)S(1)}, f32[16,64,384]{2,1,0:T(8,128)}, u32[]{:S(2)}) copy-start(f32[16,64,384]{2,1,0:T(8,128)} %stiffness.7) | copy-start | bytes 4718596
  12.1 7.3 %copy-start.3 = (f32[16,64]{1,0:T(8,128)S(1)}, f32[16,64]{1,0:T(8,128)}, u32[]{:S(2)}) copy-start(f32[16,64]{1,0:T(8,128)} %kappa.5) | copy-start | bytes 12292
  12.2 7.3 %copy-start.4 = (s32[16,6]{0,1:T(8,128)S(1)}, s32[16,6]{0,1:T(8,128)}, u32[]{:S(2)}) copy-start(s32[16,6]{0,1:T(8,128)} %param.13) | copy-start | bytes 1156
  12.2 9.0 %collective-permute-start.3 = (f32[4,64,128]{2,1,0:T(8,128)S(1)}, f32[4,64,128]{2,1,0:T(8,128)S(1)}, u32[]{:S(2)}, u32[]{:S(2)}) collective-permute-start(f32[4,64,128]{2,1,0:T(8,128)S(1)} %get-tuple-element.43), channel_id=1, source_target_pairs={{0,12},{1,13},{4,0},{5,1},{8,4},{9,5},{12,8},{13,9},{2,14},{3,15},... | collective-permute-start | bytes 393224 | tf_op jit(solution)/shard_map/ppermute | solution.py:346
  16.1 5.8 %collective-permute-start.4 = (f32[4,64,128]{2,1,0:T(8,128)S(1)}, f32[4,64,128]{2,1,0:T(8,128)S(1)}, u32[]{:S(2)}, u32[]{:S(2)}) collective-permute-start(f32[4,64,128]{2,1,0:T(8,128)S(1)} %get-tuple-element.44), channel_id=1, source_target_pairs={{0,9},{1,12},{4,13},{5,0},{8,1},{9,4},{12,5},{13,8},{2,11},{3,14},... | collective-permute-start | bytes 393224 | tf_op jit(solution)/shard_map/ppermute | solution.py:346
  16.1 7.6 %collective-permute-start.5 = (f32[4,64,128]{2,1,0:T(8,128)S(1)}, f32[4,64,128]{2,1,0:T(8,128)S(1)}, u32[]{:S(2)}, u32[]{:S(2)}) collective-permute-start(f32[4,64,128]{2,1,0:T(8,128)S(1)} %get-tuple-element.45), channel_id=1, source_target_pairs={{0,13},{1,0},{4,1},{5,4},{8,5},{9,8},{12,9},{13,12},{2,15},{3,2},{... | collective-permute-start | bytes 393224 | tf_op jit(solution)/shard_map/ppermute | solution.py:346
  17.9 6.2 %collective-permute-start.6 = (f32[4,64,128]{2,1,0:T(8,128)S(1)}, f32[4,64,128]{2,1,0:T(8,128)S(1)}, u32[]{:S(2)}, u32[]{:S(2)}) collective-permute-start(f32[4,64,128]{2,1,0:T(8,128)S(1)} %get-tuple-element.46), channel_id=1, source_target_pairs={{0,2},{2,0},{1,3},{3,1},{4,6},{6,4},{5,7},{7,5},{8,10},{10,8},{9,1... | collective-permute-start | bytes 393224 | tf_op jit(solution)/shard_map/ppermute | solution.py:346
  19.4 6.3 %collective-permute-start.7 = (f32[4,64,128]{2,1,0:T(8,128)S(1)}, f32[4,64,128]{2,1,0:T(8,128)S(1)}, u32[]{:S(2)}, u32[]{:S(2)}) collective-permute-start(f32[4,64,128]{2,1,0:T(8,128)S(1)} %get-tuple-element.47), channel_id=1, source_target_pairs={{0,1},{1,4},{4,5},{5,8},{8,9},{9,12},{12,13},{13,0},{2,3},{3,6},{6... | collective-permute-start | bytes 393224 | tf_op jit(solution)/shard_map/ppermute | solution.py:346
  21.1 4.6 %copy-start.5 = (s32[1,6]{1,0:T(1,128)S(1)}, s32[1,6]{1,0:T(1,128)}, u32[]{:S(2)}) copy-start(s32[1,6]{1,0:T(1,128)} %counts.7) | copy-start | bytes 76
  27.4 9.3 %collective-permute-start.8 = (f32[8,64,128]{2,1,0:T(8,128)S(1)}, f32[8,64,128]{2,1,0:T(8,128)S(1)}, u32[]{:S(2)}, u32[]{:S(2)}) collective-permute-start(f32[8,64,128]{2,1,0:T(8,128)S(1)} %get-tuple-element.49), channel_id=1, source_target_pairs={{0,2},{2,0},{1,3},{3,1},{4,6},{6,4},{5,7},{7,5},{8,10},{10,8},{9,1... | collective-permute-start | bytes 786440 | tf_op jit(solution)/shard_map/ppermute | solution.py:346
  28.3 12.5 %collective-permute-start.12 = (f32[8,64,128]{2,1,0:T(8,128)S(1)}, f32[8,64,128]{2,1,0:T(8,128)S(1)}, u32[]{:S(2)}, u32[]{:S(2)}) collective-permute-start(f32[8,64,128]{2,1,0:T(8,128)S(1)} %get-tuple-element.55), channel_id=1, source_target_pairs={{0,2},{2,0},{1,3},{3,1},{4,6},{6,4},{5,7},{7,5},{8,10},{10,8},{9,1... | collective-permute-start | bytes 786440 | tf_op jit(solution)/shard_map/ppermute | solution.py:346
  29.5 11.3 %collective-permute-start.9 = (f32[4,64,128]{2,1,0:T(8,128)S(1)}, f32[4,64,128]{2,1,0:T(8,128)S(1)}, u32[]{:S(2)}, u32[]{:S(2)}) collective-permute-start(f32[4,64,128]{2,1,0:T(8,128)S(1)} %get-tuple-element.52), channel_id=1, source_target_pairs={{0,5},{1,8},{4,9},{5,12},{8,13},{9,0},{12,1},{13,4},{2,7},{3,10},{... | collective-permute-start | bytes 393224 | tf_op jit(solution)/shard_map/ppermute | solution.py:346
  29.7 11.1 %collective-permute-start.10 = (f32[4,64,128]{2,1,0:T(8,128)S(1)}, f32[4,64,128]{2,1,0:T(8,128)S(1)}, u32[]{:S(2)}, u32[]{:S(2)}) collective-permute-start(f32[4,64,128]{2,1,0:T(8,128)S(1)} %get-tuple-element.53), channel_id=1, source_target_pairs={{0,4},{1,5},{4,8},{5,9},{8,12},{9,13},{12,0},{13,1},{2,6},{3,7},{6... | collective-permute-start | bytes 393224 | tf_op jit(solution)/shard_map/ppermute | solution.py:346
  30.3 10.5 %collective-permute-start.11 = (f32[4,64,128]{2,1,0:T(8,128)S(1)}, f32[4,64,128]{2,1,0:T(8,128)S(1)}, u32[]{:S(2)}, u32[]{:S(2)}) collective-permute-start(f32[4,64,128]{2,1,0:T(8,128)S(1)} %get-tuple-element.54), channel_id=1, source_target_pairs={{0,1},{1,4},{4,5},{5,8},{8,9},{9,12},{12,13},{13,0},{2,3},{3,6},{6... | collective-permute-start | bytes 393224 | tf_op jit(solution)/shard_map/ppermute | solution.py:346
  39.1 10.3 %collective-permute-start.13 = (f32[4,64,128]{2,1,0:T(8,128)S(1)}, f32[4,64,128]{2,1,0:T(8,128)S(1)}, u32[]{:S(2)}, u32[]{:S(2)}) collective-permute-start(f32[4,64,128]{2,1,0:T(8,128)S(1)} %get-tuple-element.58), channel_id=1, source_target_pairs={{0,9},{1,12},{4,13},{5,0},{8,1},{9,4},{12,5},{13,8},{2,11},{3,14},... | collective-permute-start | bytes 393224 | tf_op jit(solution)/shard_map/ppermute | solution.py:346
  40.8 9.9 %collective-permute-start.14 = (f32[4,64,128]{2,1,0:T(8,128)S(1)}, f32[4,64,128]{2,1,0:T(8,128)S(1)}, u32[]{:S(2)}, u32[]{:S(2)}) collective-permute-start(f32[4,64,128]{2,1,0:T(8,128)S(1)} %get-tuple-element.59), channel_id=1, source_target_pairs={{0,12},{1,13},{4,0},{5,1},{8,4},{9,5},{12,8},{13,9},{2,14},{3,15},... | collective-permute-start | bytes 393224 | tf_op jit(solution)/shard_map/ppermute | solution.py:346
  41.9 1.7 %collective-permute-start.15 = (f32[8,128]{1,0:T(8,128)S(1)}, f32[8,128]{1,0:T(8,128)S(1)}, u32[]{:S(2)}, u32[]{:S(2)}) collective-permute-start(f32[8,128]{1,0:T(8,128)S(1)} %get-tuple-element.62.refs_0_), channel_id=1, source_target_pairs={{0,1},{1,0},{2,3},{3,2},{4,5},{5,4},{6,7},{7,6},{8,9},{9,8},{10,11... | collective-permute-start | bytes 12296 | tf_op jit(solution)/shard_map/ppermute | solution.py:374
  43.5 3.6 %collective-permute-start.18 = (f32[8,128]{1,0:T(8,128)S(1)}, f32[8,128]{1,0:T(8,128)S(1)}, u32[]{:S(2)}, u32[]{:S(2)}) collective-permute-start(f32[8,128]{1,0:T(8,128)S(1)} %get-tuple-element.65), channel_id=1, source_target_pairs={{0,2},{2,0},{1,3},{3,1},{4,6},{6,4},{5,7},{7,5},{8,10},{10,8},{9,1... | collective-permute-start | bytes 12296 | tf_op jit(solution)/shard_map/ppermute | solution.py:374
  45.3 7.8 %collective-permute-start.17 = (f32[4,64,128]{2,1,0:T(8,128)}, f32[4,64,128]{2,1,0:T(8,128)}, u32[]{:S(2)}, u32[]{:S(2)}) collective-permute-start(f32[4,64,128]{2,1,0:T(8,128)} %get-tuple-element.64), channel_id=1, source_target_pairs={{0,13},{1,0},{4,1},{5,4},{8,5},{9,8},{12,9},{13,12},{2,15},{3,2},{... | collective-permute-start | bytes 393224 | tf_op jit(solution)/shard_map/ppermute | solution.py:346
  46.1 7.6 %collective-permute-start.16 = (f32[6,64,128]{2,1,0:T(8,128)}, f32[6,64,128]{2,1,0:T(8,128)}, u32[]{:S(2)}, u32[]{:S(2)}) collective-permute-start(f32[6,64,128]{2,1,0:T(8,128)} %shard_map.107), channel_id=1, source_target_pairs={{0,2},{2,0},{1,3},{3,1},{4,6},{6,4},{5,7},{7,5},{8,10},{10,8},{9,1... | collective-permute-start | bytes 589832 | tf_op jit(solution)/shard_map/ppermute | solution.py:346
  47.7 7.3 %collective-permute-start.21 = (f32[8,128]{1,0:T(8,128)}, f32[8,128]{1,0:T(8,128)}, u32[]{:S(2)}, u32[]{:S(2)}) collective-permute-start(f32[8,128]{1,0:T(8,128)} %get-tuple-element.67), channel_id=1, source_target_pairs={{0,12},{4,8},{8,4},{12,0},{1,13},{5,9},{9,5},{13,1},{2,14},{6,10},... | collective-permute-start | bytes 12296 | tf_op jit(solution)/shard_map/ppermute | solution.py:374
  49.4 5.6 %collective-permute-start.20 = (f32[8,128]{1,0:T(8,128)}, f32[8,128]{1,0:T(8,128)}, u32[]{:S(2)}, u32[]{:S(2)}) collective-permute-start(f32[8,128]{1,0:T(8,128)} %get-tuple-element.67), channel_id=1, source_target_pairs={{0,8},{4,12},{8,0},{12,4},{1,9},{5,13},{9,1},{13,5},{2,10},{6,14},... | collective-permute-start | bytes 12296 | tf_op jit(solution)/shard_map/ppermute | solution.py:374
  50.7 4.3 %collective-permute-start.19 = (f32[8,128]{1,0:T(8,128)}, f32[8,128]{1,0:T(8,128)}, u32[]{:S(2)}, u32[]{:S(2)}) collective-permute-start(f32[8,128]{1,0:T(8,128)} %get-tuple-element.67), channel_id=1, source_target_pairs={{0,4},{4,0},{8,12},{12,8},{1,5},{5,1},{9,13},{13,9},{2,6},{6,2},{1... | collective-permute-start | bytes 12296 | tf_op jit(solution)/shard_map/ppermute | solution.py:374
  53.0 2.0 %copy-start.1 = (f32[1,16,64,128]{3,2,1,0:T(8,128)S(1)}, f32[1,16,64,128]{3,2,1,0:T(8,128)}, u32[]{:S(2)}) copy-start(f32[1,16,64,128]{3,2,1,0:T(8,128)} %param.8) | copy-start | bytes 1572868

commit v8 on v7

--- a/solution.py
+++ b/solution.py
@@ -10,10 +10,10 @@
 SPACE = ("mesh", "rep")
 F32 = jnp.float32
 BF16 = jnp.bfloat16
-PHASES = (((4, 2), (3, 5, 1, 0)), ((4, 2, 0), (5, 3, 1)))
+PHASES = (((4, 2), (3, 5, 1, 0)), ((2, 4, 0), (3, 5, 1)))
 STAGES = (("rep", (1,)), ("tm", (1,)), ("mesh", (1, 2, 3)))
 SPLIT = (3, 2)
-PIECES = 4
+PIECES = 8
 ORDER = (40, 160, 0, 0)
 
 

time: 57 us -> 57.3 us (level)
  no operation moved by 1% of the time
where the time goes in v8:
time: 57.3 us; the launch traced here: 57.1 us
  starting transfers between devices  24.1 us (42%)
  Pallas kernels  16.8 us (29%)
  waiting for transfers between devices  14.7 us (26%)
  between operations  1.51 us (3%)
    ppermute x17, starting transfers between devices, shifted(): return lax.ppermute(value, axes, route)  17.3 us
    pallas_call x16, Pallas kernels, call(): pl.pallas_call(body, out_shape=outs, in_specs=[pl.BlockSpec(memory_space=...  16.8 us
    ppermute x17, waiting for transfers between devices, shifted(): return lax.ppermute(value, axes, route)  13.8 us
    ppermute x5, starting transfers between devices, everywhere_sum(): terms += [lax.ppermute(sent, axis, route) for route in routes]  6.72 us
  transfers between devices with their start and end apart: 22, of which 9 were waited for; matrix products, arithmetic and copies ran while one was open for 0% of the time, Pallas kernels for 21%

profile of v8, /device:TPU:0, one launch (start us, length us, event | category | flops | bytes accessed | tf_op | source)
XLA Modules:
  0.0 57.1 jit_solution(18165292193889135753)
XLA Ops:
  0.6 1.4 %shard_map.95 = (f32[16,64,128]{2,1,0:T(8,128)S(1)}, s32[1,4,6]{2,1,0:T(4,128)S(1)}, f32[8,64,128]{2,1,0:T(8,128)S(1)}, f32[4,64,128]{2,1,0:T(8,128)S(1)}, f32[4,64,128]{2,1,0:T(8,128)S(1)}) custom-call(s32[1]{0:T(128)} %bitcast.1.hour, s32[1,4,6]{2,1,0:T(4,128)} %bitcast.11, f32[16,64,128]{2,1,0:T(8,128)} %bitcast.6), custom_call_target="tpu_custom_call" | custom-call | flops 1024 | bytes 1024 | tf_op jit(solution)/shard_map/pallas_call | solution.py:28
  2.0 3.0 %collective-permute-start = (f32[8,64,128]{2,1,0:T(8,128)S(1)}, f32[8,64,128]{2,1,0:T(8,128)S(1)}, u32[]{:S(2)}, u32[]{:S(2)}) collective-permute-start(f32[8,64,128]{2,1,0:T(8,128)S(1)} %get-tuple-element.38), channel_id=1, source_target_pairs={{0,2},{2,0},{1,3},{3,1},{4,6},{6,4},{5,7},{7,5},{8,10},{10,8},{9,1... | collective-permute-start | bytes 786440 | tf_op jit(solution)/shard_map/ppermute | solution.py:346
  5.0 0.7 %collective-permute-start.1 = (f32[4,64,128]{2,1,0:T(8,128)S(1)}, f32[4,64,128]{2,1,0:T(8,128)S(1)}, u32[]{:S(2)}, u32[]{:S(2)}) collective-permute-start(f32[4,64,128]{2,1,0:T(8,128)S(1)} %get-tuple-element.40), channel_id=1, source_target_pairs={{0,5},{1,8},{4,9},{5,12},{8,13},{9,0},{12,1},{13,4},{2,7},{3,10},{... | collective-permute-start | bytes 393224 | tf_op jit(solution)/shard_map/ppermute | solution.py:346
  5.7 1.6 %collective-permute-start.2 = (f32[4,64,128]{2,1,0:T(8,128)S(1)}, f32[4,64,128]{2,1,0:T(8,128)S(1)}, u32[]{:S(2)}, u32[]{:S(2)}) collective-permute-start(f32[4,64,128]{2,1,0:T(8,128)S(1)} %get-tuple-element.41), channel_id=1, source_target_pairs={{0,4},{1,5},{4,8},{5,9},{8,12},{9,13},{12,0},{13,1},{2,6},{3,7},{6... | collective-permute-start | bytes 393224 | tf_op jit(solution)/shard_map/ppermute | solution.py:346
  7.3 4.0 %collective-permute-done.refs_0_ = f32[8,64,128]{2,1,0:T(8,128)S(1)} collective-permute-done((f32[8,64,128]{2,1,0:T(8,128)S(1)}, f32[8,64,128]{2,1,0:T(8,128)S(1)}, u32[]{:S(2)}, u32[]{:S(2)}) %collective-permute-start) | collective-permute-done | bytes 262176 | tf_op jit(solution)/shard_map/ppermute | solution.py:346
  11.3 0.8 %shard_map.96 = (f32[16,64,128]{2,1,0:T(8,128)S(1)}, f32[4,64,128]{2,1,0:T(8,128)S(1)}, f32[4,64,128]{2,1,0:T(8,128)S(1)}, f32[4,64,128]{2,1,0:T(8,128)S(1)}, f32[4,64,128]{2,1,0:T(8,128)S(1)}) custom-call(s32[1,4,6]{2,1,0:T(4,128)S(1)} %get-tuple-element.36.faces, s32[1]{0:T(128)} %bitcast.1.hour, f32[16,64,128]{2,1,0:T(8,128)S(1)} %get-tuple-element.37.field, ...), custom_call_target="tpu_custom_call" | custom-call | flops 1024 | bytes 1024 | tf_op jit(solution)/shard_map/pallas_call | solution.py:28
  12.1 0.0 copy-start
  12.1 0.0 copy-start.3
  12.2 0.0 copy-start.4
  12.2 3.9 %collective-permute-start.3 = (f32[4,64,128]{2,1,0:T(8,128)S(1)}, f32[4,64,128]{2,1,0:T(8,128)S(1)}, u32[]{:S(2)}, u32[]{:S(2)}) collective-permute-start(f32[4,64,128]{2,1,0:T(8,128)S(1)} %get-tuple-element.43), channel_id=1, source_target_pairs={{0,12},{1,13},{4,0},{5,1},{8,4},{9,5},{12,8},{13,9},{2,14},{3,15},... | collective-permute-start | bytes 393224 | tf_op jit(solution)/shard_map/ppermute | solution.py:346
  16.1 0.0 collective-permute-start.4
  16.1 0.6 %collective-permute-start.5 = (f32[4,64,128]{2,1,0:T(8,128)S(1)}, f32[4,64,128]{2,1,0:T(8,128)S(1)}, u32[]{:S(2)}, u32[]{:S(2)}) collective-permute-start(f32[4,64,128]{2,1,0:T(8,128)S(1)} %get-tuple-element.45), channel_id=1, source_target_pairs={{0,13},{1,0},{4,1},{5,4},{8,5},{9,8},{12,9},{13,12},{2,15},{3,2},{... | collective-permute-start | bytes 393224 | tf_op jit(solution)/shard_map/ppermute | solution.py:346
  16.7 0.2 shard_map.98.stiffness
  17.5 0.0 collective-permute-done.1.refs_0_
  17.5 0.0 collective-permute-done.2.refs_1_
  17.5 0.3 shard_map.99
  17.9 1.6 %collective-permute-start.6 = (f32[4,64,128]{2,1,0:T(8,128)S(1)}, f32[4,64,128]{2,1,0:T(8,128)S(1)}, u32[]{:S(2)}, u32[]{:S(2)}) collective-permute-start(f32[4,64,128]{2,1,0:T(8,128)S(1)} %get-tuple-element.46), channel_id=1, source_target_pairs={{0,2},{2,0},{1,3},{3,1},{4,6},{6,4},{5,7},{7,5},{8,10},{10,8},{9,1... | collective-permute-start | bytes 393224 | tf_op jit(solution)/shard_map/ppermute | solution.py:346
  19.4 0.0 collective-permute-start.7
  19.5 1.6 %shard_map.97.near_part = f32[16,64,128]{2,1,0:T(8,128)S(1)} custom-call(s32[6,16]{1,0:T(8,128)S(1)} %bitcast.8, f32[16,64]{1,0:T(8,128)S(1)} %copy-done.3, f32[16,64,384]{2,1,0:T(8,128)S(1)} %copy-done, f32[16,64,128]{2,1,0:T(8,128)S(1)} %get-tuple-element.39.field.refs_2_.right), custom_call_target="tpu_custom_call" | custom-call | flops 1024 | bytes 1024 | tf_op jit(solution)/shard_map/pallas_call | solution.py:28
  21.1 0.0 copy-start.5
  21.1 0.0 collective-permute-done.3.refs_0_
  21.1 0.7 %collective-permute-done.4.refs_1_ = f32[4,64,128]{2,1,0:T(8,128)S(1)} collective-permute-done((f32[4,64,128]{2,1,0:T(8,128)S(1)}, f32[4,64,128]{2,1,0:T(8,128)S(1)}, u32[]{:S(2)}, u32[]{:S(2)}) %collective-permute-start.4) | collective-permute-done | bytes 131104 | tf_op jit(solution)/shard_map/ppermute | solution.py:346
  21.8 1.9 %collective-permute-done.5.refs_2_ = f32[4,64,128]{2,1,0:T(8,128)S(1)} collective-permute-done((f32[4,64,128]{2,1,0:T(8,128)S(1)}, f32[4,64,128]{2,1,0:T(8,128)S(1)}, u32[]{:S(2)}, u32[]{:S(2)}) %collective-permute-start.5) | collective-permute-done | bytes 131104 | tf_op jit(solution)/shard_map/ppermute | solution.py:346
  23.7 0.3 shard_map.100.done
  24.0 0.0 collective-permute-done.6.refs_0_
  24.0 1.7 %collective-permute-done.7.refs_1_ = f32[4,64,128]{2,1,0:T(8,128)S(1)} collective-permute-done((f32[4,64,128]{2,1,0:T(8,128)S(1)}, f32[4,64,128]{2,1,0:T(8,128)S(1)}, u32[]{:S(2)}, u32[]{:S(2)}) %collective-permute-start.7) | collective-permute-done | bytes 131104 | tf_op jit(solution)/shard_map/ppermute | solution.py:346
  25.7 1.7 %shard_map.101 = (f32[16,64,128]{2,1,0:T(8,128)S(1)}, f32[16,64,128]{2,1,0:T(8,128)S(1)}, f32[8,64,128]{2,1,0:T(8,128)S(1)}, f32[8,64,128]{2,1,0:T(8,128)S(1)}, ...) custom-call(s32[1,4,6]{2,1,0:T(4,128)S(1)} %get-tuple-element.36.faces, ...), custom_call_target="tpu_custom_call" | custom-call | flops 1024 | bytes 1024 | tf_op jit(solution)/shard_map/pallas_call | solution.py:28
  27.4 0.9 %collective-permute-start.8 = (f32[8,64,128]{2,1,0:T(8,128)S(1)}, f32[8,64,128]{2,1,0:T(8,128)S(1)}, u32[]{:S(2)}, u32[]{:S(2)}) collective-permute-start(f32[8,64,128]{2,1,0:T(8,128)S(1)} %get-tuple-element.49), channel_id=1, source_target_pairs={{0,2},{2,0},{1,3},{3,1},{4,6},{6,4},{5,7},{7,5},{8,10},{10,8},{9,1... | collective-permute-start | bytes 786440 | tf_op jit(solution)/shard_map/ppermute | solution.py:346
  28.3 1.2 %collective-permute-start.12 = (f32[8,64,128]{2,1,0:T(8,128)S(1)}, f32[8,64,128]{2,1,0:T(8,128)S(1)}, u32[]{:S(2)}, u32[]{:S(2)}) collective-permute-start(f32[8,64,128]{2,1,0:T(8,128)S(1)} %get-tuple-element.55), channel_id=1, source_target_pairs={{0,2},{2,0},{1,3},{3,1},{4,6},{6,4},{5,7},{7,5},{8,10},{10,8},{9,1... | collective-permute-start | bytes 786440 | tf_op jit(solution)/shard_map/ppermute | solution.py:346
  29.5 0.8 %collective-permute-start.9 = (f32[4,64,128]{2,1,0:T(8,128)S(1)}, f32[4,64,128]{2,1,0:T(8,128)S(1)}, u32[]{:S(2)}, u32[]{:S(2)}) collective-permute-start(f32[4,64,128]{2,1,0:T(8,128)S(1)} %get-tuple-element.52), channel_id=1, source_target_pairs={{0,4},{1,5},{4,8},{5,9},{8,12},{9,13},{12,0},{13,1},{2,6},{3,7},{6... | collective-permute-start | bytes 393224 | tf_op jit(solution)/shard_map/ppermute | solution.py:346
  30.3 0.0 collective-permute-start.10
  30.3 1.8 %collective-permute-start.11 = (f32[4,64,128]{2,1,0:T(8,128)S(1)}, f32[4,64,128]{2,1,0:T(8,128)S(1)}, u32[]{:S(2)}, u32[]{:S(2)}) collective-permute-start(f32[4,64,128]{2,1,0:T(8,128)S(1)} %get-tuple-element.54), channel_id=1, source_target_pairs={{0,1},{1,4},{4,5},{5,8},{8,9},{9,12},{12,13},{13,0},{2,3},{3,6},{6... | collective-permute-start | bytes 393224 | tf_op jit(solution)/shard_map/ppermute | solution.py:346
  32.1 1.6 %shard_map.102._.second = f32[16,64,128]{2,1,0:T(8,128)S(1)} custom-call(s32[6,16]{1,0:T(8,128)S(1)} %bitcast.9, f32[16,64]{1,0:T(8,128)S(1)} %copy-done.3, f32[16,64,384]{2,1,0:T(8,128)S(1)} %copy-done, f32[16,64,128]{2,1,0:T(8,128)S(1)} %get-tuple-element.48.field), custom_call_target="tpu_custom_call" | custom-call | flops 1024 | bytes 1024 | tf_op jit(solution)/shard_map/pallas_call | solution.py:28
  33.8 3.0 %collective-permute-done.8.refs_0_ = f32[8,64,128]{2,1,0:T(8,128)S(1)} collective-permute-done((f32[8,64,128]{2,1,0:T(8,128)S(1)}, f32[8,64,128]{2,1,0:T(8,128)S(1)}, u32[]{:S(2)}, u32[]{:S(2)}) %collective-permute-start.8) | collective-permute-done | bytes 262176 | tf_op jit(solution)/shard_map/ppermute | solution.py:346
  36.7 2.4 %shard_map.103 = (f32[16,64,128]{2,1,0:T(8,128)S(1)}, f32[16,64,128]{2,1,0:T(8,128)S(1)}, f32[4,64,128]{2,1,0:T(8,128)S(1)}, f32[4,64,128]{2,1,0:T(8,128)S(1)}, f32[4,64,128]{2,1,0:T(8,128)}) custom-call(s32[1,4,6]{2,1,0:T(4,128)S(1)} %get-tuple-element.36.faces, s32[1]{0:T(128)} %bitcast.1.hour, s32[6,16]{1,0:T(8,128)S(1)} %bitcast.10, ...), custom_call_target="tpu_custom_call" | custom-call | flops 1024 | bytes 1024 | tf_op jit(solution)/shard_map/pallas_call | solution.py:28
  39.1 0.0 collective-permute-start.13
  39.1 0.0 collective-permute-done.9.refs_0_
  39.1 0.4 collective-permute-start.14
  39.5 1.8 %collective-permute-done.10.refs_1_ = f32[4,64,128]{2,1,0:T(8,128)S(1)} collective-permute-done((f32[4,64,128]{2,1,0:T(8,128)S(1)}, f32[4,64,128]{2,1,0:T(8,128)S(1)}, u32[]{:S(2)}, u32[]{:S(2)}) %collective-permute-start.10) | collective-permute-done | bytes 131104 | tf_op jit(solution)/shard_map/ppermute | solution.py:346
  41.3 0.0 collective-permute-done.11.refs_2_
  41.3 0.0 collective-permute-done.12.refs_3_.refs_0_
  41.3 1.0 %shard_map.104 = (f32[12,64,128]{2,1,0:T(8,128)S(1)}, f32[8,128]{1,0:T(8,128)S(1)}) custom-call(s32[1,4,6]{2,1,0:T(4,128)S(1)} %get-tuple-element.36.faces, s32[1,6]{1,0:T(1,128)S(1)} %copy-done.5, s32[1]{0:T(128)} %bitcast.1.hour, f32[16,64,128]{2,1,0:T(8,128)S(1)} %get-tuple-element.39.field.refs_2_.right, f32[16,64,128]{2,1,0:T(8,128)S(1)} %get-tuple-element.51.first, ...), custom_call_target="tpu_custom_call" | custom-call | flops 1024 | bytes 1024 | tf_op jit(solution)/shard_map/pallas_call | solution.py:28
  42.4 0.6 %collective-permute-start.15 = (f32[8,128]{1,0:T(8,128)S(1)}, f32[8,128]{1,0:T(8,128)S(1)}, u32[]{:S(2)}, u32[]{:S(2)}) collective-permute-start(f32[8,128]{1,0:T(8,128)S(1)} %get-tuple-element.62.refs_0_), channel_id=1, source_target_pairs={{0,1},{1,0},{2,3},{3,2},{4,5},{5,4},{6,7},{7,6},{8,9},{9,8},{10,11... | collective-permute-start | bytes 12296 | tf_op jit(solution)/shard_map/ppermute | solution.py:374
  43.0 0.8 %collective-permute-done.15.refs_1_ = f32[8,128]{1,0:T(8,128)S(1)} collective-permute-done((f32[8,128]{1,0:T(8,128)S(1)}, f32[8,128]{1,0:T(8,128)S(1)}, u32[]{:S(2)}, u32[]{:S(2)}) %collective-permute-start.15) | collective-permute-done | bytes 4128 | tf_op jit(solution)/shard_map/ppermute | solution.py:374
  43.8 1.7 %collective-permute-start.18 = (f32[8,128]{1,0:T(8,128)S(1)}, f32[8,128]{1,0:T(8,128)S(1)}, u32[]{:S(2)}, u32[]{:S(2)}) collective-permute-start(f32[8,128]{1,0:T(8,128)S(1)} %get-tuple-element.65), channel_id=1, source_target_pairs={{0,2},{2,0},{1,3},{3,1},{4,6},{6,4},{5,7},{7,5},{8,10},{10,8},{9,1... | collective-permute-start | bytes 12296 | tf_op jit(solution)/shard_map/ppermute | solution.py:374
  45.5 0.0 collective-permute-start.17
  45.5 0.8 %shard_map.107 = f32[6,64,128]{2,1,0:T(8,128)} custom-call(s32[1]{0:T(128)} %bitcast.1.hour, f32[12,64,128]{2,1,0:T(8,128)S(1)} %get-tuple-element.57.own, f32[8,128]{1,0:T(8,128)S(1)} %get-tuple-element.63.refs_0_), custom_call_target="tpu_custom_call" | custom-call | flops 1024 | bytes 1024 | tf_op jit(solution)/shard_map/pallas_call | solution.py:28
  46.4 0.9 %collective-permute-start.16 = (f32[6,64,128]{2,1,0:T(8,128)}, f32[6,64,128]{2,1,0:T(8,128)}, u32[]{:S(2)}, u32[]{:S(2)}) collective-permute-start(f32[6,64,128]{2,1,0:T(8,128)} %shard_map.107), channel_id=1, source_target_pairs={{0,2},{2,0},{1,3},{3,1},{4,6},{6,4},{5,7},{7,5},{8,10},{10,8},{9,1... | collective-permute-start | bytes 589832 | tf_op jit(solution)/shard_map/ppermute | solution.py:346
  47.3 0.1 collective-permute-done.18.refs_1_
  47.4 0.6 %shard_map.109 = (f32[8,128]{1,0:T(8,128)}, f32[8,128]{1,0:T(8,128)S(1)}) custom-call(f32[8,128]{1,0:T(8,128)S(1)} %get-tuple-element.63.refs_0_, f32[8,128]{1,0:T(8,128)S(1)} %collective-permute-done.18.refs_1_), custom_call_target="tpu_custom_call" | custom-call | flops 1024 | bytes 1024 | tf_op jit(solution)/shard_map/pallas_call | solution.py:28
  48.0 2.0 %collective-permute-start.21 = (f32[8,128]{1,0:T(8,128)}, f32[8,128]{1,0:T(8,128)}, u32[]{:S(2)}, u32[]{:S(2)}) collective-permute-start(f32[8,128]{1,0:T(8,128)} %get-tuple-element.67), channel_id=1, source_target_pairs={{0,12},{4,8},{8,4},{12,0},{1,13},{5,9},{9,5},{13,1},{2,14},{6,10},... | collective-permute-start | bytes 12296 | tf_op jit(solution)/shard_map/ppermute | solution.py:374
  50.0 0.0 collective-permute-done.13.refs_1_
  50.0 0.4 collective-permute-start.20
  50.4 0.0 collective-permute-done.14.refs_2_
  50.4 2.0 %collective-permute-start.19 = (f32[8,128]{1,0:T(8,128)}, f32[8,128]{1,0:T(8,128)}, u32[]{:S(2)}, u32[]{:S(2)}) collective-permute-start(f32[8,128]{1,0:T(8,128)} %get-tuple-element.67), channel_id=1, source_target_pairs={{0,4},{4,0},{8,12},{12,8},{1,5},{5,1},{9,13},{13,9},{2,6},{6,2},{1... | collective-permute-start | bytes 12296 | tf_op jit(solution)/shard_map/ppermute | solution.py:374
  52.4 0.9 %shard_map.105 = (f32[16,64,128]{2,1,0:T(8,128)S(1)}, f32[16,64,128]{2,1,0:T(8,128)S(1)}) custom-call(s32[1,4,6]{2,1,0:T(4,128)S(1)} %get-tuple-element.36.faces, s32[1,6]{1,0:T(1,128)S(1)} %copy-done.5, s32[1]{0:T(128)} %bitcast.1.hour, f32[16,64,128]{2,1,0:T(8,128)S(1)} %get-tuple-element.50.near_part, f32[12,64,128]{2,1,0:T(8,128)S(1)} %get-tuple-element.57.own, ...), custom_call_target="tpu_custom_call" | custom-call | flops 171798691840 | bytes 1024 | tf_op jit(solution)/shard_map/pallas_call | solution.py:28
  53.3 0.0 copy-start.1
  53.3 0.0 collective-permute-done.17.refs_1_
  53.3 0.7 %collective-permute-done.16.refs_0_ = f32[6,64,128]{2,1,0:T(8,128)} collective-permute-done((f32[6,64,128]{2,1,0:T(8,128)}, f32[6,64,128]{2,1,0:T(8,128)}, u32[]{:S(2)}, u32[]{:S(2)}) %collective-permute-start.16) | collective-permute-done | bytes 196640 | tf_op jit(solution)/shard_map/ppermute | solution.py:346
  54.0 1.3 %shard_map.108.second = f32[16,64,128]{2,1,0:T(8,128)S(1)} custom-call(s32[1,4,6]{2,1,0:T(4,128)S(1)} %get-tuple-element.36.faces, s32[1,6]{1,0:T(1,128)S(1)} %copy-done.5, s32[1]{0:T(128)} %bitcast.1.hour, f32[16,64,128]{2,1,0:T(8,128)S(1)} %get-tuple-element.61.start, bf16[24,64,192]{2,1,0:T(8,128)(2,1)S(1)} %shard_map.98.stiffness, ...), custom_call_target="tpu_custom_call" | custom-call | flops 1024 | bytes 1024 | tf_op jit(solution)/shard_map/pallas_call | solution.py:28
  55.3 0.0 collective-permute-done.21.refs_3_
  55.3 0.0 collective-permute-done.20.refs_2_
  55.3 0.0 collective-permute-done.19.refs_1_
  55.3 1.8 %shard_map.110 = (f32[16,64,128]{2,1,0:T(8,128)}, f32[16,64,128]{2,1,0:T(8,128)}) custom-call(f32[16,64,128]{2,1,0:T(8,128)S(1)} %bitcast.7, f32[16,64,128]{2,1,0:T(8,128)S(1)} %get-tuple-element.60.first, f32[16,64,128]{2,1,0:T(8,128)S(1)} %shard_map.108.second, f32[8,128]{1,0:T(8,128)S(1)} %get-tuple-element.66.refs_0_, ...), custom_call_target="tpu_custom_call" | custom-call | flops 1024 | bytes 1024 | tf_op jit(solution)/shard_map/pallas_call | solution.py:28
  (8 shorter events, 0.0 us)
Async XLA Ops:
  0.6 16.1 %copy-start.2 = (f32[1,64,1536]{2,1,0:T(8,128)S(1)}, f32[1,64,1536]{2,1,0:T(8,128)}, u32[]{:S(2)}) copy-start(f32[1,64,1536]{2,1,0:T(8,128)} %stiffness.5) | copy-start | bytes 1179652
  2.0 9.3 %collective-permute-start = (f32[8,64,128]{2,1,0:T(8,128)S(1)}, f32[8,64,128]{2,1,0:T(8,128)S(1)}, u32[]{:S(2)}, u32[]{:S(2)}) collective-permute-start(f32[8,64,128]{2,1,0:T(8,128)S(1)} %get-tuple-element.38), channel_id=1, source_target_pairs={{0,2},{2,0},{1,3},{3,1},{4,6},{6,4},{5,7},{7,5},{8,10},{10,8},{9,1... | collective-permute-start | bytes 786440 | tf_op jit(solution)/shard_map/ppermute | solution.py:346
  5.0 12.5 %collective-permute-start.1 = (f32[4,64,128]{2,1,0:T(8,128)S(1)}, f32[4,64,128]{2,1,0:T(8,128)S(1)}, u32[]{:S(2)}, u32[]{:S(2)}) collective-permute-start(f32[4,64,128]{2,1,0:T(8,128)S(1)} %get-tuple-element.40), channel_id=1, source_target_pairs={{0,5},{1,8},{4,9},{5,12},{8,13},{9,0},{12,1},{13,4},{2,7},{3,10},{... | collective-permute-start | bytes 393224 | tf_op jit(solution)/shard_map/ppermute | solution.py:346
  5.7 11.8 %collective-permute-start.2 = (f32[4,64,128]{2,1,0:T(8,128)S(1)}, f32[4,64,128]{2,1,0:T(8,128)S(1)}, u32[]{:S(2)}, u32[]{:S(2)}) collective-permute-start(f32[4,64,128]{2,1,0:T(8,128)S(1)} %get-tuple-element.41), channel_id=1, source_target_pairs={{0,4},{1,5},{4,8},{5,9},{8,12},{9,13},{12,0},{13,1},{2,6},{3,7},{6... | collective-permute-start | bytes 393224 | tf_op jit(solution)/shard_map/ppermute | solution.py:346
  12.1 7.3 %copy-start = (f32[16,64,384]{2,1,0:T(8,128)S(1)}, f32[16,64,384]{2,1,0:T(8,128)}, u32[]{:S(2)}) copy-start(f32[16,64,384]{2,1,0:T(8,128)} %stiffness.7) | copy-start | bytes 4718596
  12.1 7.3 %copy-start.3 = (f32[16,64]{1,0:T(8,128)S(1)}, f32[16,64]{1,0:T(8,128)}, u32[]{:S(2)}) copy-start(f32[16,64]{1,0:T(8,128)} %kappa.5) | copy-start | bytes 12292
  12.2 7.3 %copy-start.4 = (s32[16,6]{0,1:T(8,128)S(1)}, s32[16,6]{0,1:T(8,128)}, u32[]{:S(2)}) copy-start(s32[16,6]{0,1:T(8,128)} %param.13) | copy-start | bytes 1156
  12.2 9.0 %collective-permute-start.3 = (f32[4,64,128]{2,1,0:T(8,128)S(1)}, f32[4,64,128]{2,1,0:T(8,128)S(1)}, u32[]{:S(2)}, u32[]{:S(2)}) collective-permute-start(f32[4,64,128]{2,1,0:T(8,128)S(1)} %get-tuple-element.43), channel_id=1, source_target_pairs={{0,12},{1,13},{4,0},{5,1},{8,4},{9,5},{12,8},{13,9},{2,14},{3,15},... | collective-permute-start | bytes 393224 | tf_op jit(solution)/shard_map/ppermute | solution.py:346
  16.1 5.8 %collective-permute-start.4 = (f32[4,64,128]{2,1,0:T(8,128)S(1)}, f32[4,64,128]{2,1,0:T(8,128)S(1)}, u32[]{:S(2)}, u32[]{:S(2)}) collective-permute-start(f32[4,64,128]{2,1,0:T(8,128)S(1)} %get-tuple-element.44), channel_id=1, source_target_pairs={{0,9},{1,12},{4,13},{5,0},{8,1},{9,4},{12,5},{13,8},{2,11},{3,14},... | collective-permute-start | bytes 393224 | tf_op jit(solution)/shard_map/ppermute | solution.py:346
  16.1 7.6 %collective-permute-start.5 = (f32[4,64,128]{2,1,0:T(8,128)S(1)}, f32[4,64,128]{2,1,0:T(8,128)S(1)}, u32[]{:S(2)}, u32[]{:S(2)}) collective-permute-start(f32[4,64,128]{2,1,0:T(8,128)S(1)} %get-tuple-element.45), channel_id=1, source_target_pairs={{0,13},{1,0},{4,1},{5,4},{8,5},{9,8},{12,9},{13,12},{2,15},{3,2},{... | collective-permute-start | bytes 393224 | tf_op jit(solution)/shard_map/ppermute | solution.py:346
  17.9 6.2 %collective-permute-start.6 = (f32[4,64,128]{2,1,0:T(8,128)S(1)}, f32[4,64,128]{2,1,0:T(8,128)S(1)}, u32[]{:S(2)}, u32[]{:S(2)}) collective-permute-start(f32[4,64,128]{2,1,0:T(8,128)S(1)} %get-tuple-element.46), channel_id=1, source_target_pairs={{0,2},{2,0},{1,3},{3,1},{4,6},{6,4},{5,7},{7,5},{8,10},{10,8},{9,1... | collective-permute-start | bytes 393224 | tf_op jit(solution)/shard_map/ppermute | solution.py:346
  19.4 6.3 %collective-permute-start.7 = (f32[4,64,128]{2,1,0:T(8,128)S(1)}, f32[4,64,128]{2,1,0:T(8,128)S(1)}, u32[]{:S(2)}, u32[]{:S(2)}) collective-permute-start(f32[4,64,128]{2,1,0:T(8,128)S(1)} %get-tuple-element.47), channel_id=1, source_target_pairs={{0,1},{1,4},{4,5},{5,8},{8,9},{9,12},{12,13},{13,0},{2,3},{3,6},{6... | collective-permute-start | bytes 393224 | tf_op jit(solution)/shard_map/ppermute | solution.py:346
  21.1 4.6 %copy-start.5 = (s32[1,6]{1,0:T(1,128)S(1)}, s32[1,6]{1,0:T(1,128)}, u32[]{:S(2)}) copy-start(s32[1,6]{1,0:T(1,128)} %counts.7) | copy-start | bytes 76
  27.4 9.3 %collective-permute-start.8 = (f32[8,64,128]{2,1,0:T(8,128)S(1)}, f32[8,64,128]{2,1,0:T(8,128)S(1)}, u32[]{:S(2)}, u32[]{:S(2)}) collective-permute-start(f32[8,64,128]{2,1,0:T(8,128)S(1)} %get-tuple-element.49), channel_id=1, source_target_pairs={{0,2},{2,0},{1,3},{3,1},{4,6},{6,4},{5,7},{7,5},{8,10},{10,8},{9,1... | collective-permute-start | bytes 786440 | tf_op jit(solution)/shard_map/ppermute | solution.py:346
  28.3 13.0 %collective-permute-start.12 = (f32[8,64,128]{2,1,0:T(8,128)S(1)}, f32[8,64,128]{2,1,0:T(8,128)S(1)}, u32[]{:S(2)}, u32[]{:S(2)}) collective-permute-start(f32[8,64,128]{2,1,0:T(8,128)S(1)} %get-tuple-element.55), channel_id=1, source_target_pairs={{0,2},{2,0},{1,3},{3,1},{4,6},{6,4},{5,7},{7,5},{8,10},{10,8},{9,1... | collective-permute-start | bytes 786440 | tf_op jit(solution)/shard_map/ppermute | solution.py:346
  29.5 9.6 %collective-permute-start.9 = (f32[4,64,128]{2,1,0:T(8,128)S(1)}, f32[4,64,128]{2,1,0:T(8,128)S(1)}, u32[]{:S(2)}, u32[]{:S(2)}) collective-permute-start(f32[4,64,128]{2,1,0:T(8,128)S(1)} %get-tuple-element.52), channel_id=1, source_target_pairs={{0,4},{1,5},{4,8},{5,9},{8,12},{9,13},{12,0},{13,1},{2,6},{3,7},{6... | collective-permute-start | bytes 393224 | tf_op jit(solution)/shard_map/ppermute | solution.py:346
  30.3 11.0 %collective-permute-start.10 = (f32[4,64,128]{2,1,0:T(8,128)S(1)}, f32[4,64,128]{2,1,0:T(8,128)S(1)}, u32[]{:S(2)}, u32[]{:S(2)}) collective-permute-start(f32[4,64,128]{2,1,0:T(8,128)S(1)} %get-tuple-element.53), channel_id=1, source_target_pairs={{0,5},{1,8},{4,9},{5,12},{8,13},{9,0},{12,1},{13,4},{2,7},{3,10},{... | collective-permute-start | bytes 393224 | tf_op jit(solution)/shard_map/ppermute | solution.py:346
  30.3 11.0 %collective-permute-start.11 = (f32[4,64,128]{2,1,0:T(8,128)S(1)}, f32[4,64,128]{2,1,0:T(8,128)S(1)}, u32[]{:S(2)}, u32[]{:S(2)}) collective-permute-start(f32[4,64,128]{2,1,0:T(8,128)S(1)} %get-tuple-element.54), channel_id=1, source_target_pairs={{0,1},{1,4},{4,5},{5,8},{8,9},{9,12},{12,13},{13,0},{2,3},{3,6},{6... | collective-permute-start | bytes 393224 | tf_op jit(solution)/shard_map/ppermute | solution.py:346
  39.1 10.9 %collective-permute-start.13 = (f32[4,64,128]{2,1,0:T(8,128)S(1)}, f32[4,64,128]{2,1,0:T(8,128)S(1)}, u32[]{:S(2)}, u32[]{:S(2)}) collective-permute-start(f32[4,64,128]{2,1,0:T(8,128)S(1)} %get-tuple-element.58), channel_id=1, source_target_pairs={{0,12},{1,13},{4,0},{5,1},{8,4},{9,5},{12,8},{13,9},{2,14},{3,15},... | collective-permute-start | bytes 393224 | tf_op jit(solution)/shard_map/ppermute | solution.py:346
  39.1 11.3 %collective-permute-start.14 = (f32[4,64,128]{2,1,0:T(8,128)S(1)}, f32[4,64,128]{2,1,0:T(8,128)S(1)}, u32[]{:S(2)}, u32[]{:S(2)}) collective-permute-start(f32[4,64,128]{2,1,0:T(8,128)S(1)} %get-tuple-element.59), channel_id=1, source_target_pairs={{0,9},{1,12},{4,13},{5,0},{8,1},{9,4},{12,5},{13,8},{2,11},{3,14},... | collective-permute-start | bytes 393224 | tf_op jit(solution)/shard_map/ppermute | solution.py:346
  42.4 1.4 %collective-permute-start.15 = (f32[8,128]{1,0:T(8,128)S(1)}, f32[8,128]{1,0:T(8,128)S(1)}, u32[]{:S(2)}, u32[]{:S(2)}) collective-permute-start(f32[8,128]{1,0:T(8,128)S(1)} %get-tuple-element.62.refs_0_), channel_id=1, source_target_pairs={{0,1},{1,0},{2,3},{3,2},{4,5},{5,4},{6,7},{7,6},{8,9},{9,8},{10,11... | collective-permute-start | bytes 12296 | tf_op jit(solution)/shard_map/ppermute | solution.py:374
  43.8 3.6 %collective-permute-start.18 = (f32[8,128]{1,0:T(8,128)S(1)}, f32[8,128]{1,0:T(8,128)S(1)}, u32[]{:S(2)}, u32[]{:S(2)}) collective-permute-start(f32[8,128]{1,0:T(8,128)S(1)} %get-tuple-element.65), channel_id=1, source_target_pairs={{0,2},{2,0},{1,3},{3,1},{4,6},{6,4},{5,7},{7,5},{8,10},{10,8},{9,1... | collective-permute-start | bytes 12296 | tf_op jit(solution)/shard_map/ppermute | solution.py:374
  45.5 7.8 %collective-permute-start.17 = (f32[4,64,128]{2,1,0:T(8,128)}, f32[4,64,128]{2,1,0:T(8,128)}, u32[]{:S(2)}, u32[]{:S(2)}) collective-permute-start(f32[4,64,128]{2,1,0:T(8,128)} %get-tuple-element.64), channel_id=1, source_target_pairs={{0,13},{1,0},{4,1},{5,4},{8,5},{9,8},{12,9},{13,12},{2,15},{3,2},{... | collective-permute-start | bytes 393224 | tf_op jit(solution)/shard_map/ppermute | solution.py:346
  46.4 7.6 %collective-permute-start.16 = (f32[6,64,128]{2,1,0:T(8,128)}, f32[6,64,128]{2,1,0:T(8,128)}, u32[]{:S(2)}, u32[]{:S(2)}) collective-permute-start(f32[6,64,128]{2,1,0:T(8,128)} %shard_map.107), channel_id=1, source_target_pairs={{0,2},{2,0},{1,3},{3,1},{4,6},{6,4},{5,7},{7,5},{8,10},{10,8},{9,1... | collective-permute-start | bytes 589832 | tf_op jit(solution)/shard_map/ppermute | solution.py:346
  48.0 7.3 %collective-permute-start.21 = (f32[8,128]{1,0:T(8,128)}, f32[8,128]{1,0:T(8,128)}, u32[]{:S(2)}, u32[]{:S(2)}) collective-permute-start(f32[8,128]{1,0:T(8,128)} %get-tuple-element.67), channel_id=1, source_target_pairs={{0,12},{4,8},{8,4},{12,0},{1,13},{5,9},{9,5},{13,1},{2,14},{6,10},... | collective-permute-start | bytes 12296 | tf_op jit(solution)/shard_map/ppermute | solution.py:374
  50.0 5.3 %collective-permute-start.20 = (f32[8,128]{1,0:T(8,128)}, f32[8,128]{1,0:T(8,128)}, u32[]{:S(2)}, u32[]{:S(2)}) collective-permute-start(f32[8,128]{1,0:T(8,128)} %get-tuple-element.67), channel_id=1, source_target_pairs={{0,8},{4,12},{8,0},{12,4},{1,9},{5,13},{9,1},{13,5},{2,10},{6,14},... | collective-permute-start | bytes 12296 | tf_op jit(solution)/shard_map/ppermute | solution.py:374
  50.4 4.9 %collective-permute-start.19 = (f32[8,128]{1,0:T(8,128)}, f32[8,128]{1,0:T(8,128)}, u32[]{:S(2)}, u32[]{:S(2)}) collective-permute-start(f32[8,128]{1,0:T(8,128)} %get-tuple-element.67), channel_id=1, source_target_pairs={{0,4},{4,0},{8,12},{12,8},{1,5},{5,1},{9,13},{13,9},{2,6},{6,2},{1... | collective-permute-start | bytes 12296 | tf_op jit(solution)/shard_map/ppermute | solution.py:374
  53.3 2.0 %copy-start.1 = (f32[1,16,64,128]{3,2,1,0:T(8,128)S(1)}, f32[1,16,64,128]{3,2,1,0:T(8,128)}, u32[]{:S(2)}) copy-start(f32[1,16,64,128]{3,2,1,0:T(8,128)} %param.8) | copy-start | bytes 1572868
